TPU v7x, 32 devices: a whole 2x2x4 slice. The times are simulated.
32 devices in a mesh: fsdp: 2 (over x), cp: 4 (over y, core), seq: 4 (over z).
Axes of the slice: x: 2, y: 2, z: 4, core: 2. Of those that a mesh axis runs over, the one named last changes fastest.
Arguments:
- inputs: bfloat16 [6, 2048, 1536], P('fsdp', ('cp', 'seq')), may hold values from -6 to 6
- cotangent: bfloat16 [6, 2048, 1536], P('fsdp', ('cp', 'seq')), may hold values from -6 to 6
- span_order: int32 [6, 8], P('fsdp'), may hold values from 0 to 7, each once within a row
- adapter_ids: int32 [6], P('fsdp'), may hold values from 0 to 7
- first_gain: bfloat16 [1536], replicated, may hold values from 0.5 to 1.5
- second_gain: bfloat16 [1536], replicated, may hold values from 0.5 to 1.5
- query_weight: bfloat16 [1536, 1536], P(('fsdp', 'cp')), may hold values from -0.15625 to 0.15625
- key_weight: bfloat16 [1536, 256], P(('fsdp', 'cp')), may hold values from -0.15625 to 0.15625
- value_weight: bfloat16 [1536, 256], P(('fsdp', 'cp')), may hold values from -0.15625 to 0.15625
- output_weight: bfloat16 [1536, 1536], P(('fsdp', 'cp')), may hold values from -1.25 to 1.25
- gate_weight: bfloat16 [1536, 8960], P(('fsdp', 'cp')), may hold values from -0.15625 to 0.15625
- up_weight: bfloat16 [1536, 8960], P(('fsdp', 'cp')), may hold values from -0.15625 to 0.15625
- down_weight: bfloat16 [8960, 1536], P(('fsdp', 'cp')), may hold values from -0.0625 to 0.0625
- query_bias: bfloat16 [1536], replicated, may hold values from -1.796875 to 1.796875
- key_bias: bfloat16 [256], replicated, may hold values from -1.796875 to 1.796875
- value_bias: bfloat16 [256], replicated, may hold values from -0.59765625 to 0.59765625
- query_reduce_factors: bfloat16 [1536, 128], replicated, may hold values from -0.15625 to 0.15625
- query_lift_factors: bfloat16 [128, 1536], replicated, may hold values from -1.5 to 1.5
- key_reduce_factors: bfloat16 [1536, 128], replicated, may hold values from -0.15625 to 0.15625
- key_lift_factors: bfloat16 [128, 256], replicated, may hold values from -1.5 to 1.5
- value_reduce_factors: bfloat16 [1536, 128], replicated, may hold values from -0.15625 to 0.15625
- value_lift_factors: bfloat16 [128, 256], replicated, may hold values from -1.5 to 1.5
- output_reduce_factors: bfloat16 [1536, 128], replicated, may hold values from -1.25 to 1.25
- output_lift_factors: bfloat16 [128, 1536], replicated, may hold values from -1.5 to 1.5
- gate_reduce_factors: bfloat16 [1536, 128], replicated, may hold values from -0.15625 to 0.15625
- gate_lift_factors: bfloat16 [128, 8960], replicated, may hold values from -1.5 to 1.5
- upper_reduce_factors: bfloat16 [1536, 128], replicated, may hold values from -0.15625 to 0.15625
- upper_lift_factors: bfloat16 [128, 8960], replicated, may hold values from -1.5 to 1.5
- down_reduce_factors: bfloat16 [8960, 128], replicated, may hold values from -0.0625 to 0.0625
- down_lift_factors: bfloat16 [128, 1536], replicated, may hold values from -1.5 to 1.5
Outputs:
- outputs: bfloat16 [6, 2048, 1536], P('fsdp', ('cp', 'seq'))
- input_grad: float32 [6, 2048, 1536], P('fsdp', ('cp', 'seq'))
- query_shrink_grad: float32 [1536, 128], replicated
- query_expand_grad: float32 [128, 1536], replicated
- key_shrink_grad: float32 [1536, 128], replicated
- key_expand_grad: float32 [128, 256], replicated
- value_shrink_grad: float32 [1536, 128], replicated
- value_expand_grad: float32 [128, 256], replicated
- output_shrink_grad: float32 [1536, 128], replicated
- output_expand_grad: float32 [128, 1536], replicated
- gate_shrink_grad: float32 [1536, 128], replicated
- gate_expand_grad: float32 [128, 8960], replicated
- up_shrink_grad: float32 [1536, 128], replicated
- up_expand_grad: float32 [128, 8960], replicated
- down_shrink_grad: float32 [8960, 128], replicated
- down_expand_grad: float32 [128, 1536], replicated
Inputs may be any that keep to these rules, and one draw needn't show every extreme that they name: `span_order`: each row is a permutation of the 8 block numbers.
All inputs are finite; a program needn't handle non-finite values.
Results may differ from a plain program's by a relative error of at most 0.018.
Values may be sent and summed in bfloat16 or wider, within the bound.
No kernel may reach another device: no remote copies, remote signals or barrier semaphores. Data moves between devices by JAX's collectives and lax.ppermute only.
A program may use at most 256 MiB of HBM per device.

v0:
```python
import math

import jax
import jax.numpy as jnp
from jax import lax
from jax.sharding import PartitionSpec as P

HEAD_DIM = 128
ADAPTER_RANK = 16


epsilon = 1e-06
adapter_scale = 0.5
rotary_base = 1000000.0
masked_score = -1e30


def rotary_tables(positions):
    halfway = HEAD_DIM // 2
    frequency = jnp.exp(
        jnp.arange(halfway, dtype=jnp.float32) * (-2.0 * math.log(rotary_base) / HEAD_DIM)
    )
    angles = positions.astype(jnp.float32)[..., None] * frequency
    angles = jnp.concatenate([angles, angles], axis=-1)
    return (jnp.cos(angles), jnp.sin(angles))


def rotate(values, cosine, sine_table):
    halfway = values.shape[-1] // 2
    turned = jnp.concatenate([-values[..., halfway:], values[..., :halfway]], axis=-1)
    return values * cosine + turned * sine_table


def unrotate(gradient, cosine, sine_table):
    halfway = gradient.shape[-1] // 2
    scaled = gradient * sine_table
    turned = jnp.concatenate([scaled[..., halfway:], -scaled[..., :halfway]], axis=-1)
    return gradient * cosine + turned


def project(inputs_low, weight):
    return jnp.dot(inputs_low, weight, preferred_element_type=jnp.float32)


def project_back(gradient, weight):
    return lax.dot_general(
        gradient, weight, (((1,), (1,)), ((), ())), preferred_element_type=jnp.float32
    )


def weight_grad(inputs_low, gradient):
    return lax.dot_general(
        inputs_low, gradient, (((0,), (0,)), ((), ())), preferred_element_type=jnp.float32
    )


def norm_forward(values, scales):
    return values * lax.rsqrt(jnp.mean(values * values, axis=-1, keepdims=True) + epsilon) * scales


def norm_backward(values, scales, gradient):
    inverse = lax.rsqrt(jnp.mean(values * values, axis=-1, keepdims=True) + epsilon)
    weighted = gradient * scales
    inner_sum = jnp.mean(weighted * values, axis=-1, keepdims=True)
    return inverse * weighted - values * (inverse * inverse * inverse) * inner_sum


def adapter_forward(inputs_low, shrink, expand, mixing):
    narrow = (project(inputs_low, shrink) * mixing).astype(jnp.bfloat16)
    return (project(narrow, expand), narrow)


def adapter_backward(inputs_low, shrink, expand, mixing, narrow, grad_low):
    narrow_grad = (project_back(grad_low, expand) * mixing).astype(jnp.bfloat16)
    return (
        project_back(narrow_grad, shrink),
        weight_grad(inputs_low, narrow_grad),
        weight_grad(narrow, grad_low),
    )


def body(
    inputs,
    cotangent,
    span_order,
    adapter_ids,
    first_gain,
    second_gain,
    query_weight,
    key_weight,
    value_weight,
    output_weight,
    gate_weight,
    up_weight,
    down_weight,
    query_bias,
    key_bias,
    value_bias,
    query_reduce_factors,
    query_lift_factors,
    key_reduce_factors,
    key_lift_factors,
    value_reduce_factors,
    value_lift_factors,
    output_reduce_factors,
    output_lift_factors,
    gate_reduce_factors,
    gate_lift_factors,
    upper_reduce_factors,
    upper_lift_factors,
    down_reduce_factors,
    down_lift_factors,
):
    seq_count = lax.axis_size("seq")
    cp_count = lax.axis_size("cp")
    seqs_here, tok_rows, model_width = inputs.shape
    tokens_num = seqs_here * tok_rows
    head_dim = HEAD_DIM
    head_count = model_width // head_dim
    kv_heads = key_weight.shape[1] // head_dim
    per_group = head_count // seq_count
    repeat_by = seq_count // kv_heads
    shard_rows = seq_count * tok_rows
    length = shard_rows * cp_count
    spans = span_order.shape[1]
    span_len = length // spans
    score_scale = 1.0 / math.sqrt(head_dim)
    all_rows = jnp.arange(length, dtype=jnp.int32)
    span_of = all_rows // span_len
    picked = jnp.sum(
        jnp.where(
            span_of[None, :, None] == jnp.arange(spans, dtype=jnp.int32)[None, None, :],
            span_order[:, None, :],
            0,
        ),
        axis=-1,
    )
    key_places = picked * span_len + all_rows % span_len
    query_places = lax.dynamic_slice_in_dim(
        key_places, lax.axis_index("cp") * shard_rows, shard_rows, 1
    )
    token_places = lax.dynamic_slice_in_dim(
        query_places, lax.axis_index("seq") * tok_rows, tok_rows, 1
    )
    cosine, sine_table = rotary_tables(token_places.reshape(tokens_num))
    cosine = cosine[:, None, :]
    sine_table = sine_table[:, None, :]
    column_count = jnp.arange(query_reduce_factors.shape[1], dtype=jnp.int32)
    mix_seq = jnp.where(
        column_count[None, :] // ADAPTER_RANK == adapter_ids[:, None], adapter_scale, 0.0
    ).astype(jnp.float32)
    mixing = jnp.broadcast_to(
        mix_seq[:, None, :], (seqs_here, tok_rows, column_count.shape[0])
    ).reshape(tokens_num, column_count.shape[0])
    resid_in = inputs.reshape(tokens_num, model_width).astype(jnp.float32)
    first_scales = first_gain.astype(jnp.float32)
    second_scales = second_gain.astype(jnp.float32)
    normed = norm_forward(resid_in, first_scales).astype(jnp.bfloat16)
    w_query, w_key, w_value, w_output = (
        lax.all_gather(query_weight, ("fsdp", "cp"), axis=0, tiled=True),
        lax.all_gather(key_weight, ("fsdp", "cp"), axis=0, tiled=True),
        lax.all_gather(value_weight, ("fsdp", "cp"), axis=0, tiled=True),
        lax.all_gather(output_weight, ("fsdp", "cp"), axis=0, tiled=True),
    )
    query_extra, query_narrow = adapter_forward(
        normed, query_reduce_factors, query_lift_factors, mixing
    )
    key_extra, key_narrow = adapter_forward(normed, key_reduce_factors, key_lift_factors, mixing)
    value_extra, value_narrow = adapter_forward(
        normed, value_reduce_factors, value_lift_factors, mixing
    )
    query_pre = project(normed, w_query) + query_bias.astype(jnp.float32) + query_extra
    key_pre = project(normed, w_key) + key_bias.astype(jnp.float32) + key_extra
    value_pre = project(normed, w_value) + value_bias.astype(jnp.float32) + value_extra
    query_rot = rotate(
        query_pre.reshape(tokens_num, head_count, head_dim), cosine, sine_table
    ).astype(jnp.bfloat16)
    key_rot = rotate(key_pre.reshape(tokens_num, kv_heads, head_dim), cosine, sine_table).astype(
        jnp.bfloat16
    )
    value_low = value_pre.reshape(tokens_num, kv_heads, head_dim).astype(jnp.bfloat16)
    pair_low = jnp.repeat(jnp.concatenate([key_rot, value_low], axis=-1), repeat_by, axis=1)
    query_send = query_rot.reshape(seqs_here, tok_rows, seq_count, per_group * head_dim)
    pair_send = pair_low.reshape(seqs_here, tok_rows, seq_count, 2 * head_dim)
    query_heads, pair_heads = (
        lax.all_to_all(query_send, "seq", split_axis=2, concat_axis=1, tiled=True),
        lax.all_to_all(pair_send, "seq", split_axis=2, concat_axis=1, tiled=True),
    )
    pair_all = lax.all_gather(pair_heads, "cp", axis=1, tiled=True)

    def attend(operand):
        queries, key_values, query_pos, key_pos = operand
        grouped = queries.reshape(shard_rows, per_group, head_dim)
        keys_here = key_values[:, 0, :head_dim]
        values_here = key_values[:, 0, head_dim:]
        scores = (
            jnp.einsum("qhd,kd->hqk", grouped, keys_here, preferred_element_type=jnp.float32)
            * score_scale
        )
        allowed = key_pos[None, None, :] <= query_pos[None, :, None]
        scores = jnp.where(allowed, scores, masked_score)
        top_score = jnp.max(scores, axis=-1, keepdims=True)
        exponent = jnp.exp(scores - top_score)
        total_mass = jnp.sum(exponent, axis=-1, keepdims=True)
        probability = exponent / total_mass
        log_total = top_score + jnp.log(total_mass)
        blended = jnp.einsum(
            "hqk,kd->qhd",
            probability.astype(jnp.bfloat16),
            values_here,
            preferred_element_type=jnp.float32,
        )
        return (
            blended.astype(jnp.bfloat16).reshape(shard_rows, 1, per_group * head_dim),
            log_total[..., 0],
        )

    attended_heads, log_totals = lax.map(attend, (query_heads, pair_all, query_places, key_places))
    attended = lax.all_to_all(
        attended_heads, "seq", split_axis=1, concat_axis=2, tiled=True
    ).reshape(tokens_num, model_width)
    output_extra, output_narrow = adapter_forward(
        attended, output_reduce_factors, output_lift_factors, mixing
    )
    middle = resid_in + (project(attended, w_output) + output_extra)
    normed_two = norm_forward(middle, second_scales).astype(jnp.bfloat16)
    w_gate, w_up, w_down = (
        lax.all_gather(gate_weight, ("fsdp", "cp"), axis=0, tiled=True),
        lax.all_gather(up_weight, ("fsdp", "cp"), axis=0, tiled=True),
        lax.all_gather(down_weight, ("fsdp", "cp"), axis=0, tiled=True),
    )
    gate_extra, gate_narrow = adapter_forward(
        normed_two, gate_reduce_factors, gate_lift_factors, mixing
    )
    upward_extra, upward_narrow = adapter_forward(
        normed_two, upper_reduce_factors, upper_lift_factors, mixing
    )
    gate_pre = project(normed_two, w_gate) + gate_extra
    upward = project(normed_two, w_up) + upward_extra
    sigmoid_gate = jax.nn.sigmoid(gate_pre)
    activated = gate_pre * sigmoid_gate
    hidden = (activated * upward).astype(jnp.bfloat16)
    down_extra, down_narrow = adapter_forward(
        hidden, down_reduce_factors, down_lift_factors, mixing
    )
    result = middle + (project(hidden, w_down) + down_extra)
    outputs = result.astype(jnp.bfloat16).reshape(seqs_here, tok_rows, model_width)
    grad_low = cotangent.reshape(tokens_num, model_width)
    grad_out = grad_low.astype(jnp.float32)
    w_gate, w_up, w_down = (
        lax.all_gather(gate_weight, ("fsdp", "cp"), axis=0, tiled=True),
        lax.all_gather(up_weight, ("fsdp", "cp"), axis=0, tiled=True),
        lax.all_gather(down_weight, ("fsdp", "cp"), axis=0, tiled=True),
    )
    down_in, down_shrink_grad, down_expand_grad = adapter_backward(
        hidden, down_reduce_factors, down_lift_factors, mixing, down_narrow, grad_low
    )
    hidden_grad = project_back(grad_low, w_down) + down_in
    gate_grad = (
        hidden_grad * upward * (sigmoid_gate * (1.0 + gate_pre * (1.0 - sigmoid_gate)))
    ).astype(jnp.bfloat16)
    upward_grad = (hidden_grad * activated).astype(jnp.bfloat16)
    gate_in, gate_shrink_grad, gate_expand_grad = adapter_backward(
        normed_two, gate_reduce_factors, gate_lift_factors, mixing, gate_narrow, gate_grad
    )
    upward_in, up_shrink_grad, up_expand_grad = adapter_backward(
        normed_two, upper_reduce_factors, upper_lift_factors, mixing, upward_narrow, upward_grad
    )
    normed_two_grad = (
        project_back(gate_grad, w_gate) + project_back(upward_grad, w_up) + gate_in + upward_in
    )
    middle_grad = grad_out + norm_backward(middle, second_scales, normed_two_grad)
    middle_low = middle_grad.astype(jnp.bfloat16)
    w_query, w_key, w_value, w_output = (
        lax.all_gather(query_weight, ("fsdp", "cp"), axis=0, tiled=True),
        lax.all_gather(key_weight, ("fsdp", "cp"), axis=0, tiled=True),
        lax.all_gather(value_weight, ("fsdp", "cp"), axis=0, tiled=True),
        lax.all_gather(output_weight, ("fsdp", "cp"), axis=0, tiled=True),
    )
    output_in, output_shrink_grad, output_expand_grad = adapter_backward(
        attended, output_reduce_factors, output_lift_factors, mixing, output_narrow, middle_low
    )
    attended_grad = (project_back(middle_low, w_output) + output_in).astype(jnp.bfloat16)
    grad_heads = lax.all_to_all(
        attended_grad.reshape(seqs_here, tok_rows, seq_count, per_group * head_dim),
        "seq",
        split_axis=2,
        concat_axis=1,
        tiled=True,
    )

    def attend_back(operand):
        queries, key_values, head_grads, log_total, query_pos, key_pos = operand
        grouped = queries.reshape(shard_rows, per_group, head_dim)
        grads_grouped = head_grads.reshape(shard_rows, per_group, head_dim)
        keys_here = key_values[:, 0, :head_dim]
        values_here = key_values[:, 0, head_dim:]
        scores = (
            jnp.einsum("qhd,kd->hqk", grouped, keys_here, preferred_element_type=jnp.float32)
            * score_scale
        )
        allowed = key_pos[None, None, :] <= query_pos[None, :, None]
        scores = jnp.where(allowed, scores, masked_score)
        probability = jnp.exp(scores - log_total[:, :, None])
        prob_grad = jnp.einsum(
            "qhd,kd->hqk", grads_grouped, values_here, preferred_element_type=jnp.float32
        )
        inner_sum = jnp.sum(probability * prob_grad, axis=-1, keepdims=True)
        score_grad = (probability * (prob_grad - inner_sum) * score_scale).astype(jnp.bfloat16)
        query_part = jnp.einsum(
            "hqk,kd->qhd", score_grad, keys_here, preferred_element_type=jnp.float32
        )
        key_part = jnp.einsum(
            "hqk,qhd->kd", score_grad, grouped, preferred_element_type=jnp.float32
        )
        value_part = jnp.einsum(
            "hqk,qhd->kd",
            probability.astype(jnp.bfloat16),
            grads_grouped,
            preferred_element_type=jnp.float32,
        )
        return (
            query_part.astype(jnp.bfloat16).reshape(shard_rows, 1, per_group * head_dim),
            jnp.concatenate([key_part, value_part], axis=-1),
        )

    query_grad_heads, pair_grad_all = lax.map(
        attend_back, (query_heads, pair_all, grad_heads, log_totals, query_places, key_places)
    )
    pair_grad = lax.psum_scatter(pair_grad_all, "cp", scatter_dimension=1, tiled=True).astype(
        jnp.bfloat16
    )
    query_grad_tok, pair_grad_tok = (
        lax.all_to_all(query_grad_heads, "seq", split_axis=1, concat_axis=2, tiled=True),
        lax.all_to_all(
            pair_grad.reshape(seqs_here, shard_rows, 1, 2 * head_dim),
            "seq",
            split_axis=1,
            concat_axis=2,
            tiled=True,
        ),
    )
    query_grad = unrotate(
        query_grad_tok.reshape(tokens_num, head_count, head_dim).astype(jnp.float32),
        cosine,
        sine_table,
    )
    query_grad = query_grad.reshape(tokens_num, model_width).astype(jnp.bfloat16)
    pair_summed = jnp.sum(
        pair_grad_tok.reshape(tokens_num, kv_heads, repeat_by, 2 * head_dim).astype(jnp.float32),
        axis=2,
    )
    key_grad = (
        unrotate(pair_summed[..., :head_dim], cosine, sine_table)
        .reshape(tokens_num, kv_heads * head_dim)
        .astype(jnp.bfloat16)
    )
    value_grad = (
        pair_summed[..., head_dim:].reshape(tokens_num, kv_heads * head_dim).astype(jnp.bfloat16)
    )
    query_in, query_shrink_grad, query_expand_grad = adapter_backward(
        normed, query_reduce_factors, query_lift_factors, mixing, query_narrow, query_grad
    )
    key_in, key_shrink_grad, key_expand_grad = adapter_backward(
        normed, key_reduce_factors, key_lift_factors, mixing, key_narrow, key_grad
    )
    value_in, value_shrink_grad, value_expand_grad = adapter_backward(
        normed, value_reduce_factors, value_lift_factors, mixing, value_narrow, value_grad
    )
    normed_grad = (
        project_back(query_grad, w_query)
        + project_back(key_grad, w_key)
        + project_back(value_grad, w_value)
        + query_in
        + key_in
        + value_in
    )
    input_grad = middle_grad + norm_backward(resid_in, first_scales, normed_grad)
    summed = lax.psum(
        (
            query_shrink_grad,
            query_expand_grad,
            key_shrink_grad,
            key_expand_grad,
            value_shrink_grad,
            value_expand_grad,
            output_shrink_grad,
            output_expand_grad,
            gate_shrink_grad,
            gate_expand_grad,
            up_shrink_grad,
            up_expand_grad,
            down_shrink_grad,
            down_expand_grad,
        ),
        ("fsdp", "cp", "seq"),
    )
    return (
        outputs,
        input_grad.reshape(seqs_here, tok_rows, model_width),
        summed[0],
        summed[1],
        summed[2],
        summed[3],
        summed[4],
        summed[5],
        summed[6],
        summed[7],
        summed[8],
        summed[9],
        summed[10],
        summed[11],
        summed[12],
        summed[13],
    )


def solution(mesh):
    placed = (
        P("fsdp", ("cp", "seq"), None),
        P("fsdp", ("cp", "seq"), None),
        P("fsdp", None),
        P("fsdp"),
        P(),
        P(),
        P(("fsdp", "cp"), None),
        P(("fsdp", "cp"), None),
        P(("fsdp", "cp"), None),
        P(("fsdp", "cp"), None),
        P(("fsdp", "cp"), None),
        P(("fsdp", "cp"), None),
        P(("fsdp", "cp"), None),
        P(),
        P(),
        P(),
        P(),
        P(),
        P(),
        P(),
        P(),
        P(),
        P(),
        P(),
        P(),
        P(),
        P(),
        P(),
        P(),
        P(),
    )
    return jax.shard_map(
        body,
        mesh=mesh,
        in_specs=placed,
        out_specs=(
            P("fsdp", ("cp", "seq"), None),
            P("fsdp", ("cp", "seq"), None),
            P(),
            P(),
            P(),
            P(),
            P(),
            P(),
            P(),
            P(),
            P(),
            P(),
            P(),
            P(),
            P(),
            P(),
        ),
        check_vma=False,
    )
```

profile of v0, /device:TPU:0, one launch (start us, length us, event | category | flops | bytes accessed | tf_op | source)
XLA Modules:
  0.0 2116.4 jit_solution(15718257371764512466)
XLA Ops:
  13.9 13.7 all_gather.31
  33.7 15.2 all_gather.32
  56.0 25.2 %all_to_all.87 = bf16[3,128,4,256]{3,1,0,2:T(8,128)(2,1)S(1)} all-to-all(bf16[3,128,4,256]{3,1,0,2:T(8,128)(2,1)S(1)} %bitcast.465), channel_id=1, replica_groups=mesh['fsdp'=2,'cp'=4,'seq'=4] {'seq'}, dimensions={2} | all-to-all | bytes 1572864 | tf_op jit(solution)/shard_map/all_to_all | solution.py:187
  118.3 4.6 reshape.461
  136.2 28.2 %all-to-all-done.1 = bf16[3,128,4,384]{3,1,0,2:T(8,128)(2,1)S(1)} async-done(((bf16[3,128,4,384]{3,1,0,2:T(8,128)(2,1)}), bf16[3,128,4,384]{3,1,0,2:T(8,128)(2,1)S(1)}, u32[]{:S(2)}, u32[]{:S(2)}) %all-to-all-start.1) | async-done | bytes 1179680 | tf_op jit(solution)/shard_map/all_to_all | solution.py:186
  168.4 74.9 %while.24 = (s32[]{:T(128)}, bf16[3,512,1,384]{1,3,2,0:T(8,128)(2,1)}, f32[3,3,512]{2,1,0:T(4,128)}, bf16[3,2048,1,256]{3,1,2,0:T(8,128)(2,1)}, s32[3,2048]{1,0:...) while((s32[]{:T(128)}, bf16[3,512,1,384]{1,3,2,0:T(8,128)(2,1)}, ...), condition=%wide.region_5.6_spmd, body=%wide.region_2.5_spmd.sunk | while | flops 1649605120 | bytes 47535204 | solution.py:218
  170.6 5.9 fusion.240
  176.5 7.3 fusion.241
  184.4 7.0 fusion.242
  194.3 5.9 fusion.240
  200.2 7.3 fusion.241
  208.2 10.1 fusion.242
  221.3 5.9 fusion.240
  227.2 7.7 fusion.241
  235.5 7.0 fusion.242
  247.8 4.8 all-to-all-start.2
  255.1 34.3 %all-to-all-done.2 = bf16[3,512,1,384]{3,0,2,1:T(4,128)(2,1)} async-done(((bf16[3,512,1,384]{3,0,2,1:T(4,128)(2,1)}), bf16[3,512,1,384]{3,0,2,1:T(4,128)(2,1)}, u32[]{:S(2)}, u32[]{:S(2)}) %all-to-all-start.2) | async-done | bytes 1179680 | tf_op jit(solution)/shard_map/all_to_all | solution.py:219
  294.2 6.2 fusion.89
  304.7 19.1 fusion.91
  323.8 11.8 convolution_add_fusion.1
  335.6 88.3 %all-gather.13.cloned.1.call-done = bf16[1536,8960]{1,0:T(8,128)(2,1)} async-done(((bf16[192,8960]{1,0:T(8,128)(2,1)}), bf16[1536,8960]{1,0:T(8,128)(2,1)}) %all-gather.13.cloned.1.call-update) | async-done | bytes 27525136 | tf_op jit(solution)/shard_map/all_gather | solution.py:228
  424.0 19.4 fusion.90
  443.4 11.8 convolution_add_fusion.2
  455.2 105.9 %all-gather.17.cloned.1.call-done = bf16[8960,1536]{1,0:T(8,128)(2,1)} async-done(((bf16[1120,1536]{1,0:T(8,128)(2,1)}), bf16[8960,1536]{1,0:T(8,128)(2,1)}) %all-gather.17.cloned.1.call-update) | async-done | bytes 27525136 | tf_op jit(solution)/shard_map/all_gather | solution.py:230
  561.0 19.8 fusion.93
  580.9 23.7 %multiply_convert_fusion = (bf16[384,8960]{1,0:T(8,128)(2,1)}, bf16[384,8960]{1,0:T(8,128)(2,1)}, bf16[384,8960]{1,0:T(8,128)(2,1)}) fusion(f32[384,8960]{1,0:T(8,128)} %convolution_add_fusion.2, f32[384,8960]{1,0:T(8,128)} %convolution_add_fusion.1, f32[384,8960]{1,0:T(8,128)} %fusion.93, bf16[384,128]{1,0:T(8,128)(2,1)} %fusion.62, ...), kind=kOutput, calls=%fused_computation.57 | convolution fusion | flops 935854080 | bytes 64323584 | tf_op jit(solution)/shard_map/dot_general | solution.py:46
  604.5 5.7 fusion.63
  612.7 17.9 fusion.94
  630.5 17.1 convolution_add_fusion.11
  661.8 4.6 all-to-all-start.3
  670.9 5.6 fusion.61
  682.0 6.5 fusion.107
  688.5 7.0 all-to-all-done.3
  699.0 353.7 %while.25 = (s32[]{:T(128)}, bf16[3,512,1,384]{1,3,2,0:T(8,128)(2,1)}, f32[3,2048,256]{2,0,1:T(4,128)}, bf16[3,2048,1,256]{3,1,2,0:T(8,128)(2,1)}, s32[3,2048]{1...) while((s32[]{:T(128)}, ...), condition=%wide.region_10.11_spmd, body=%wide.region_8.10_spmd.sunk | while | flops 4110097408 | bytes 150411984 | solution.py:327
  701.5 6.4 fusion.249
  709.1 6.3 fusion.248
  718.3 19.1 convolution_bitcast_fusion.2
  737.5 6.6 fusion.251
  745.7 4.7 copy.308
  750.4 45.1 %dynamic_update_slice.25 = f32[3,2048,256]{2,0,1:T(4,128)} dynamic-update-slice(f32[3,2048,256]{2,0,1:T(4,128)} %get-tuple-element.410, f32[1,2048,256]{2,0,1:T(1,128)S(1)} %copy.308, s32[]{:T(128)} %get-tuple-element.408, s32[]{:T(128)} %constant.116.clone.1..sunk, s32[]{:T(128)} %constant.116.clone.1..sunk) | dynamic-update-slice | bytes 4194308 | tf_op jit(solution)/shard_map/while/body/jit(dynamic_update_index_in_dim)/dynamic_update_slice | solution.py:327
  795.5 20.7 fusion.250
  819.3 6.4 fusion.249
  826.9 6.3 fusion.248
  836.1 19.1 convolution_bitcast_fusion.2
  855.3 6.6 fusion.251
  863.5 4.7 copy.308
  868.2 45.1 %dynamic_update_slice.25 = f32[3,2048,256]{2,0,1:T(4,128)} dynamic-update-slice(f32[3,2048,256]{2,0,1:T(4,128)} %get-tuple-element.410, f32[1,2048,256]{2,0,1:T(1,128)S(1)} %copy.308, s32[]{:T(128)} %get-tuple-element.408, s32[]{:T(128)} %constant.116.clone.1..sunk, s32[]{:T(128)} %constant.116.clone.1..sunk) | dynamic-update-slice | bytes 4194308 | tf_op jit(solution)/shard_map/while/body/jit(dynamic_update_index_in_dim)/dynamic_update_slice | solution.py:327
  913.3 20.7 fusion.250
  937.1 6.4 fusion.249
  944.7 6.3 fusion.248
  953.9 19.1 convolution_bitcast_fusion.2
  973.1 6.6 fusion.251
  981.3 4.7 copy.308
  986.0 45.1 %dynamic_update_slice.25 = f32[3,2048,256]{2,0,1:T(4,128)} dynamic-update-slice(f32[3,2048,256]{2,0,1:T(4,128)} %get-tuple-element.410, f32[1,2048,256]{2,0,1:T(1,128)S(1)} %copy.308, s32[]{:T(128)} %get-tuple-element.408, s32[]{:T(128)} %constant.116.clone.1..sunk, s32[]{:T(128)} %constant.116.clone.1..sunk) | dynamic-update-slice | bytes 4194308 | tf_op jit(solution)/shard_map/while/body/jit(dynamic_update_index_in_dim)/dynamic_update_slice | solution.py:327
  1031.1 20.7 fusion.250
  1052.7 146.6 %all-reduce.6 = bf16[3,2048,256]{2,0,1:T(4,128)(2,1)} all-reduce(f32[3,2048,256]{2,0,1:T(4,128)} %get-tuple-element.105), channel_id=2, replica_groups=mesh['fsdp'=2,'cp'=4,'seq'=4] {'cp'}, use_global_device_ids=true, to_apply=%region_11.12.clone | all-reduce | flops 1572864 | bytes 9437184
  1206.9 6.8 fusion.109
  1220.2 11.9 all-to-all-done.5
  1244.9 28.5 %all-to-all-done.4 = bf16[3,512,1,384]{3,0,2,1:T(4,128)(2,1)} async-done(((bf16[3,512,1,384]{3,0,2,1:T(4,128)(2,1)}), bf16[3,512,1,384]{3,0,2,1:T(4,128)(2,1)}, u32[]{:S(2)}, u32[]{:S(2)}) %all-to-all-start.4) | async-done | bytes 1179680 | tf_op jit(solution)/shard_map/all_to_all | solution.py:334
  1276.7 4.8 copy.293
  1281.5 4.6 copy.269
  1286.0 4.9 reshape.462
  1305.5 18.2 fusion.92
  1335.0 752.7 %all-reduce.5.cloned.1.call-done = (f32[1536,128]{1,0:T(8,128)}, f32[128,1536]{1,0:T(8,128)}, f32[1536,128]{1,0:T(8,128)}, f32[128,256]{1,0:T(8,128)}, f32[1536,...) async-done(((f32[1536,128]{1,0:T(8,128)}, ...) | async-done | bytes 21102608 | tf_op jit(solution)/shard_map/psum | solution.py:379
  (456 shorter events, 233.1 us)
Async XLA Ops:
  7.2 573.7 %copy-start = (bf16[8960,128]{1,0:T(8,128)(2,1)S(1)}, bf16[8960,128]{1,0:T(8,128)(2,1)}, u32[]{:S(2)}) copy-start(bf16[8960,128]{1,0:T(8,128)(2,1)} %param.62) | copy-start | bytes 6881284
  7.2 94.8 %all-gather.9.cloned.1.call-start = ((), (), s32[]{:S(2)}) async-start(), calls=%async_computation.7 | async-start | bytes 5308416 | tf_op jit(solution)/shard_map/all_gather | solution.py:160
  7.9 159.4 %all-gather.7.cloned.1.call-start = ((), (), s32[]{:S(2)}) async-start(), calls=%async_computation.6 | async-start | bytes 3932160 | tf_op jit(solution)/shard_map/all_gather | solution.py:189
  8.0 5.4 copy-start.49
  8.7 5.2 copy-start.96
  11.0 16.6 copy-start.98
  11.7 76.4 %copy-start.84 = (f32[3,128]{1,0:T(4,128)}, f32[3,128]{1,0:T(4,128)S(1)}, u32[]{:S(2)}) copy-start(f32[3,128]{1,0:T(4,128)S(1)} %compare_select_fusion) | copy-start | bytes 4612
  11.8 15.9 copy-start.100
  13.4 88.6 %copy-start.2 = (bf16[384,1536]{1,0:T(8,128)(2,1)}, bf16[384,1536]{1,0:T(8,128)(2,1)S(1)}, u32[]{:S(2)}) copy-start(bf16[384,1536]{1,0:T(8,128)(2,1)S(1)} %fusion.48) | copy-start | bytes 3538948
  13.4 15.8 copy-start.90
  13.9 16.3 copy-start.71
  28.5 5.1 copy-start.105
  32.1 18.2 copy-start.88
  33.6 17.7 copy-start.73
  33.6 19.5 copy-start.104
  82.2 212.1 %all-gather.11.cloned.1.call-start = ((), (), s32[]{:S(2)}) async-start(), calls=%async_computation.8 | async-start | bytes 5308416 | tf_op jit(solution)/shard_map/all_gather | solution.py:163
  82.9 221.8 %all-gather.15.cloned.1.call-start = ((), (), s32[]{:S(2)}) async-start(), calls=%async_computation.10 | async-start | bytes 30965760 | tf_op jit(solution)/shard_map/all_gather | solution.py:229
  83.5 340.5 %all-gather.13.cloned.1.call-start = ((), (), s32[]{:S(2)}) async-start(), calls=%async_computation.9 | async-start | bytes 30965760 | tf_op jit(solution)/shard_map/all_gather | solution.py:228
  84.1 6.3 copy-start.102
  84.1 477.0 %all-gather.17.cloned.1.call-start = ((), (), s32[]{:S(2)}) async-start(), calls=%async_computation.11 | async-start | bytes 30965760 | tf_op jit(solution)/shard_map/all_gather | solution.py:230
  132.4 32.0 %all-to-all-start.1 = ((bf16[3,128,4,384]{3,1,0,2:T(8,128)(2,1)}), bf16[3,128,4,384]{3,1,0,2:T(8,128)(2,1)S(1)}, u32[]{:S(2)}, u32[]{:S(2)}) async-start(bf16[3,128,4,384]{3,1,0,2:T(8,128)(2,1)} %copy.255), calls=%async_computation.1 | async-start | bytes 2359296 | tf_op jit(solution)/shard_map/all_to_all | solution.py:186
  243.9 8.7 copy-start.103
  243.9 8.7 copy-start.85
  247.8 41.6 %all-to-all-start.2 = ((bf16[3,512,1,384]{3,0,2,1:T(4,128)(2,1)}), bf16[3,512,1,384]{3,0,2,1:T(4,128)(2,1)}, u32[]{:S(2)}, u32[]{:S(2)}) async-start(bf16[3,512,1,384]{3,0,2,1:T(4,128)(2,1)} %copy.259), calls=%async_computation.2 | async-start | bytes 3145728 | tf_op jit(solution)/shard_map/all_to_all | solution.py:219
  294.2 6.2 copy-start.10
  294.2 6.2 copy-start.42
  294.2 6.2 copy-start.69
  304.7 19.2 copy-start.23
  304.7 19.2 copy-start.55
  424.0 19.4 copy-start.22
  424.0 19.4 copy-start.57
  604.5 5.7 copy-start.12
  604.5 6.2 copy-start.24
  610.2 37.4 %copy-start.63 = (bf16[384,128]{1,0:T(8,128)(2,1)}, bf16[384,128]{1,0:T(8,128)(2,1)S(1)}, u32[]{:S(2)}) copy-start(bf16[384,128]{1,0:T(8,128)(2,1)S(1)} %fusion.63) | copy-start | bytes 294916
  612.7 35.5 %copy-start.59 = (bf16[384,128]{1,0:T(8,128)(2,1)}, bf16[384,128]{1,0:T(8,128)(2,1)S(1)}, u32[]{:S(2)}) copy-start(bf16[384,128]{1,0:T(8,128)(2,1)S(1)} %fusion.64) | copy-start | bytes 294916
  630.5 17.1 copy-start.45
  661.8 33.7 %all-to-all-start.3 = ((bf16[3,128,4,384]{3,1,0,2:T(8,128)(2,1)}), bf16[3,128,4,384]{3,1,0,2:T(8,128)(2,1)}, u32[]{:S(2)}, u32[]{:S(2)}) async-start(bf16[3,128,4,384]{3,1,0,2:T(8,128)(2,1)} %copy.262), calls=%async_computation.3 | async-start | bytes 2359296 | tf_op jit(solution)/shard_map/all_to_all | solution.py:284
  670.8 5.7 copy-start.19
  670.8 5.7 copy-start.66
  670.8 7.1 copy-start.64
  717.6 19.9 copy-start.13
  737.5 6.7 copy-start.14
  835.4 19.9 copy-start.13
  855.3 6.7 copy-start.14
  953.1 19.9 copy-start.13
  973.1 6.7 copy-start.14
  1199.3 6.3 copy-start.17
  1199.3 6.3 copy-start.61
  1202.0 5.0 copy-start.56
  1202.0 30.1 %all-to-all-start.5 = ((bf16[3,512,1,256]{3,0,2,1:T(4,128)(2,1)}), bf16[3,512,1,256]{3,0,2,1:T(4,128)(2,1)S(1)}, u32[]{:S(2)}, u32[]{:S(2)}) async-start(bf16[3,512,1,256]{3,0,2,1:T(4,128)(2,1)} %fusion.69), calls=%async_computation.5 | async-start | bytes 2097152 | tf_op jit(solution)/shard_map/all_to_all | solution.py:335
  1205.7 8.0 slice-start
  1206.9 6.8 slice-start.1
  1206.9 6.8 copy-start.87
  1232.1 41.4 %all-to-all-start.4 = ((bf16[3,512,1,384]{3,0,2,1:T(4,128)(2,1)}), bf16[3,512,1,384]{3,0,2,1:T(4,128)(2,1)}, u32[]{:S(2)}, u32[]{:S(2)}) async-start(bf16[3,512,1,384]{3,0,2,1:T(4,128)(2,1)} %copy.267), calls=%async_computation.4 | async-start | bytes 3145728 | tf_op jit(solution)/shard_map/all_to_all | solution.py:334
  1236.5 851.2 %all-reduce.5.cloned.1.call-start = ((), (), s32[]{:S(2)}) async-start(), calls=%async_computation.12 | async-start | bytes 42205184 | tf_op jit(solution)/shard_map/psum | solution.py:379
  1240.1 4.9 copy-start.36
  1286.0 4.9 copy-start.39
  1305.5 18.3 copy-start.6
  1305.5 18.3 copy-start.48
  1305.5 18.3 copy-start.62
  2087.6 5.2 copy-start.93
  2087.6 5.9 copy-start.80
  2089.8 5.2 copy-start.79
  2096.8 4.9 slice-start.4
  (69 other events, 166.0 us)
Sparse Core Ops, SparseCore 0:
  9.9 46.2 all-gather.8
  82.3 26.6 all-gather.6
  110.9 38.9 all-gather.10
  151.5 135.2 all-gather.14
  288.6 135.3 all-gather.12
  425.7 135.2 all-gather.16
  1305.0 782.5 all-reduce.4
where the time goes:
time: 2130 us; the launch traced here: 2120 us
  waiting for transfers between devices  1060 us (50%)
  matrix products  461 us (22%)
  local copies, waits for them, and re-layouts  297 us (14%)
  blocking collectives  201 us (9%)
  other arithmetic  58.5 us (3%)
  starting transfers between devices  21.4 us (1%)
    psum x1, waiting for transfers between devices, body(): lax.psum((query_shrink_grad, query_expand_grad, key_shrink_grad, key_expa...  753 us
    dynamic_update_slice x6, local copies, waits for them, and re-layouts, body(): lax.map(attend_back, (query_heads, pair_all, grad_heads, log_totals, quer...  149 us
    unnamed x1, blocking collectives  147 us
    dot_general x21, matrix products, project(): return jnp.dot(inputs_low, weight, preferred_element_type=jnp.float32)  111 us
    all_gather x1, waiting for transfers between devices, body(): lax.all_gather(down_weight, ('fsdp', 'cp'), axis=0, tiled=True)  106 us
    dot_general x21, matrix products, project_back(): lax.dot_general(gradient, weight, (((1,), (1,)), ((), ())), preferred_ele...  99.5 us
    all_gather x1, waiting for transfers between devices, body(): lax.all_gather(gate_weight, ('fsdp', 'cp'), axis=0, tiled=True)  88.3 us
    dot_general x3, matrix products, attend_back(): jnp.einsum('hqk,kd->qhd', score_grad, keys_here, preferred_element_type=j...  62 us
  transfers between devices with their start and end apart: 12, of which 8 were waited for; matrix products, arithmetic and copies ran while one was open for 14% of the time, Pallas kernels for 0%

commit v1 on v0

v1 whole, which is shorter than its diff:
```python
import functools
import math

import jax
import jax.numpy as jnp
from jax import lax
from jax.experimental import pallas as pl
from jax.experimental.pallas import tpu as pltpu
from jax.sharding import PartitionSpec as P

HEAD_DIM = 128
ADAPTER_RANK = 16
epsilon = 1e-06
adapter_scale = 0.5
rotary_base = 1000000.0
masked_score = -1e30
PLANE = ("fsdp", "cp")
EVERY = ("fsdp", "cp", "seq")
BF = jnp.bfloat16
F32 = jnp.float32


def rotary_tables(positions):
    halfway = HEAD_DIM // 2
    frequency = jnp.exp(
        jnp.arange(halfway, dtype=jnp.float32) * (-2.0 * math.log(rotary_base) / HEAD_DIM)
    )
    angles = positions.astype(jnp.float32)[..., None] * frequency
    angles = jnp.concatenate([angles, angles], axis=-1)
    return (jnp.cos(angles), jnp.sin(angles))


def rotate(values, cosine, sine_table):
    halfway = values.shape[-1] // 2
    turned = jnp.concatenate([-values[..., halfway:], values[..., :halfway]], axis=-1)
    return values * cosine + turned * sine_table


def unrotate(gradient, cosine, sine_table):
    halfway = gradient.shape[-1] // 2
    scaled = gradient * sine_table
    turned = jnp.concatenate([scaled[..., halfway:], -scaled[..., :halfway]], axis=-1)
    return gradient * cosine + turned


def mm(left, right):
    return jnp.dot(left, right, preferred_element_type=jnp.float32)


def mm_nt(left, right):
    return lax.dot_general(
        left, right, (((1,), (1,)), ((), ())), preferred_element_type=jnp.float32
    )


def mm_tn(left, right):
    return lax.dot_general(
        left, right, (((0,), (0,)), ((), ())), preferred_element_type=jnp.float32
    )


def norm_forward(values, scales):
    return values * lax.rsqrt(jnp.mean(values * values, axis=-1, keepdims=True) + epsilon) * scales


def norm_backward(values, scales, gradient):
    inverse = lax.rsqrt(jnp.mean(values * values, axis=-1, keepdims=True) + epsilon)
    weighted = gradient * scales
    inner_sum = jnp.mean(weighted * values, axis=-1, keepdims=True)
    return inverse * weighted - values * (inverse * inverse * inverse) * inner_sum


def heads_to_rows(block):
    count = block.shape[1] // HEAD_DIM
    return jnp.concatenate(
        [block[:, HEAD_DIM * j : HEAD_DIM * (j + 1)] for j in range(count)], axis=0
    )


def rows_to_heads(rows, tokens):
    count = rows.shape[0] // tokens
    return jnp.concatenate([rows[tokens * j : tokens * (j + 1)] for j in range(count)], axis=1)


def attend_kernel(spans, span_len, tokens, info, q_ref, k_ref, v_ref, o_ref, lse_ref, m_ref, l_ref, acc_ref):
    seq = pl.program_id(0)
    seqs = pl.num_programs(0)
    own = info[seqs * spans + seq]
    shift = info[seqs * spans + seqs]
    scale = math.log2(math.e) / math.sqrt(HEAD_DIM)
    queries = heads_to_rows(q_ref[...])
    m_ref[...] = jnp.full(m_ref.shape, masked_score, F32)
    l_ref[...] = jnp.zeros(l_ref.shape, F32)
    acc_ref[...] = jnp.zeros(acc_ref.shape, F32)

    def update(j, masked):
        rows = pl.ds(pl.multiple_of(j * span_len, span_len), span_len)
        scores = mm_nt(k_ref[0, rows, :], queries) * scale
        if masked:
            key_at = lax.broadcasted_iota(jnp.int32, scores.shape, 0)
            query_at = shift + lax.rem(lax.broadcasted_iota(jnp.int32, scores.shape, 1), tokens)
            scores = jnp.where(key_at <= query_at, scores, masked_score)
        old = m_ref[...]
        top = jnp.maximum(old, jnp.max(scores, axis=0, keepdims=True))
        expo = jnp.exp2(scores - top)
        alpha = jnp.exp2(old - top)
        l_ref[...] = l_ref[...] * alpha + jnp.sum(expo, axis=0, keepdims=True)
        acc_ref[...] = acc_ref[...] * alpha + mm_tn(v_ref[0, rows, :], expo.astype(BF))
        m_ref[...] = top

    def step(j, carry):
        other = info[seq * spans + j]

        @pl.when(other < own)
        def _():
            update(j, False)

        @pl.when(other == own)
        def _():
            update(j, True)

        return carry

    lax.fori_loop(0, spans, step, 0)
    total = l_ref[...]
    out = jnp.transpose(acc_ref[...] / total)
    o_ref[...] = rows_to_heads(out.astype(BF), tokens)
    lse_ref[0] = jnp.broadcast_to(m_ref[...] + jnp.log2(total), lse_ref.shape[1:])


def attend(info, queries, pairs, seqs, spans, span_len):
    tokens = queries.shape[0] // seqs
    length = pairs.shape[1]
    kv_heads = pairs.shape[2] // (2 * HEAD_DIM)
    width = queries.shape[1] // kv_heads
    rows = tokens * (width // HEAD_DIM)
    grid_spec = pltpu.PrefetchScalarGridSpec(
        num_scalar_prefetch=1,
        grid=(seqs, kv_heads),
        in_specs=[
            pl.BlockSpec((tokens, width), lambda s, h, i: (s, h)),
            pl.BlockSpec((1, length, HEAD_DIM), lambda s, h, i: (s, 0, h)),
            pl.BlockSpec((1, length, HEAD_DIM), lambda s, h, i: (s, 0, kv_heads + h)),
        ],
        out_specs=[
            pl.BlockSpec((tokens, width), lambda s, h, i: (s, h)),
            pl.BlockSpec((1, 8, rows), lambda s, h, i: (s * kv_heads + h, 0, 0)),
        ],
        scratch_shapes=[pltpu.VMEM((1, rows), F32)] * 2 + [pltpu.VMEM((HEAD_DIM, rows), F32)],
    )
    work = seqs * kv_heads * rows * length
    return pl.pallas_call(
        functools.partial(attend_kernel, spans, span_len, tokens),
        grid_spec=grid_spec,
        out_shape=[
            jax.ShapeDtypeStruct(queries.shape, BF),
            jax.ShapeDtypeStruct((seqs * kv_heads, 8, rows), F32),
        ],
        name="attend",
        cost_estimate=pl.CostEstimate(
            flops=4 * work * HEAD_DIM, bytes_accessed=pairs.size * 2, transcendentals=work
        ),
    )(info, queries, pairs, pairs)


def attend_back_kernel(
    spans, span_len, tokens, kv_heads, info, q_ref, do_ref, o_ref, k_ref, v_ref, lse_ref, dq_ref, dkv_ref, acc_ref
):
    seq = pl.program_id(0)
    head = pl.program_id(1)
    seqs = pl.num_programs(0)
    own = info[seqs * spans + seq]
    shift = info[seqs * spans + seqs]
    root = 1.0 / math.sqrt(HEAD_DIM)
    scale = math.log2(math.e) * root
    queries = heads_to_rows(q_ref[...])
    grads = heads_to_rows(do_ref[...])
    results = heads_to_rows(o_ref[...])
    inner = jnp.sum(
        jnp.transpose(grads.astype(F32) * results.astype(F32)), axis=0, keepdims=True
    )
    lse = lse_ref[0, :1, :]
    acc_ref[...] = jnp.zeros(acc_ref.shape, F32)
    key_lane = pl.multiple_of(head * HEAD_DIM, HEAD_DIM)
    val_lane = pl.multiple_of((kv_heads + head) * HEAD_DIM, HEAD_DIM)

    def update(j, masked):
        rows = pl.ds(pl.multiple_of(j * span_len, span_len), span_len)
        keys = k_ref[0, rows, :]
        prob = jnp.exp2(mm_nt(keys, queries) * scale - lse)
        if masked:
            key_at = lax.broadcasted_iota(jnp.int32, prob.shape, 0)
            query_at = shift + lax.rem(lax.broadcasted_iota(jnp.int32, prob.shape, 1), tokens)
            prob = jnp.where(key_at <= query_at, prob, 0.0)
        prob_grad = mm_nt(v_ref[0, rows, :], grads)
        score_grad = (prob * (prob_grad - inner)).astype(BF)
        dkv_ref[0, rows, pl.ds(key_lane, HEAD_DIM)] = (mm(score_grad, queries) * root).astype(BF)
        dkv_ref[0, rows, pl.ds(val_lane, HEAD_DIM)] = mm(prob.astype(BF), grads).astype(BF)
        acc_ref[...] += mm_tn(score_grad, keys)

    def step(j, carry):
        other = info[seq * spans + j]

        @pl.when(other < own)
        def _():
            update(j, False)

        @pl.when(other == own)
        def _():
            update(j, True)

        @pl.when(other > own)
        def _():
            rows = pl.ds(pl.multiple_of(j * span_len, span_len), span_len)
            zero = jnp.zeros((span_len, HEAD_DIM), BF)
            dkv_ref[0, rows, pl.ds(key_lane, HEAD_DIM)] = zero
            dkv_ref[0, rows, pl.ds(val_lane, HEAD_DIM)] = zero

        return carry

    lax.fori_loop(0, spans, step, 0)
    dq_ref[...] = rows_to_heads((acc_ref[...] * root).astype(BF), tokens)


def attend_back(info, queries, grads, results, pairs, lse, seqs, spans, span_len):
    tokens = queries.shape[0] // seqs
    length = pairs.shape[1]
    kv_heads = pairs.shape[2] // (2 * HEAD_DIM)
    width = queries.shape[1] // kv_heads
    rows = tokens * (width // HEAD_DIM)
    grid_spec = pltpu.PrefetchScalarGridSpec(
        num_scalar_prefetch=1,
        grid=(seqs, kv_heads),
        in_specs=[
            pl.BlockSpec((tokens, width), lambda s, h, i: (s, h)),
            pl.BlockSpec((tokens, width), lambda s, h, i: (s, h)),
            pl.BlockSpec((tokens, width), lambda s, h, i: (s, h)),
            pl.BlockSpec((1, length, HEAD_DIM), lambda s, h, i: (s, 0, h)),
            pl.BlockSpec((1, length, HEAD_DIM), lambda s, h, i: (s, 0, kv_heads + h)),
            pl.BlockSpec((1, 8, rows), lambda s, h, i: (s * kv_heads + h, 0, 0)),
        ],
        out_specs=[
            pl.BlockSpec((tokens, width), lambda s, h, i: (s, h)),
            pl.BlockSpec((1, length, pairs.shape[2]), lambda s, h, i: (s, 0, 0)),
        ],
        scratch_shapes=[pltpu.VMEM((rows, HEAD_DIM), F32)],
    )
    work = seqs * kv_heads * rows * length
    return pl.pallas_call(
        functools.partial(attend_back_kernel, spans, span_len, tokens, kv_heads),
        grid_spec=grid_spec,
        out_shape=[
            jax.ShapeDtypeStruct(queries.shape, BF),
            jax.ShapeDtypeStruct(pairs.shape, BF),
        ],
        name="attend_back",
        cost_estimate=pl.CostEstimate(
            flops=10 * work * HEAD_DIM, bytes_accessed=pairs.size * 4, transcendentals=work
        ),
    )(info, queries, grads, results, pairs, pairs, lse)


def token_mask(tokens, lanes, seqs):
    row = lax.broadcasted_iota(jnp.int32, (tokens, lanes), 0) // (tokens // seqs)
    lane = lax.broadcasted_iota(jnp.int32, (tokens, lanes), 1) // ADAPTER_RANK
    return jnp.where(row == lane, adapter_scale, 0.0).astype(F32)


def feed_kernel(seqs, count, info, *refs):
    blocks = refs[:count]
    n2_ref, g0_ref, sgu_ref, ed_ref, wd_ref, eg_ref, eu_ref, sd_ref = refs[count : count + 8]
    peg_ref, peu_ref, psd_ref = refs[count + 8 : count + 11]
    out_ref, ng_ref, deg_ref, deu_ref, dsd_ref = refs[count + 11 : count + 16]
    acc_out, acc_ng, acc_nd, acc_bg, acc_bu, nar_g, nar_u, back_d, held, sems = refs[count + 16 :]
    chunk = pl.program_id(0)
    chunks = pl.num_programs(0)
    depth = blocks[0].shape[1]
    size = wd_ref.shape[0]

    def copies(at, slot):
        return [
            pltpu.make_async_copy(
                blocks[j].at[:, :, pl.ds(pl.multiple_of(at * size, 128), size)],
                held.at[slot, :, pl.ds(pl.multiple_of((info[0] ^ j) * depth, depth), depth), :],
                sems.at[slot, j],
            )
            for j in range(count)
        ]

    slot = lax.rem(chunk, 2)

    @pl.when(chunk == 0)
    def _():
        for copy in copies(chunk, slot):
            copy.start()

    @pl.when(chunk + 1 < chunks)
    def _():
        for copy in copies(chunk + 1, 1 - slot):
            copy.start()

    tokens = n2_ref.shape[0]
    model = n2_ref.shape[1]
    cols = sd_ref.shape[1]
    n2 = n2_ref[...]
    g0 = g0_ref[...]
    wg_ref = held.at[slot, 0]
    wu_ref = held.at[slot, 1]

    @pl.when(chunk == 0)
    def _():
        mix = token_mask(tokens, cols, seqs)
        narrow = mm(n2, sgu_ref[...])
        nar_g[...] = (narrow[:, :cols] * mix).astype(BF)
        nar_u[...] = (narrow[:, cols:] * mix).astype(BF)
        back_d[...] = (mm_nt(g0, ed_ref[...]) * mix).astype(BF)
        for acc in (acc_out, acc_ng, acc_nd, acc_bg, acc_bu):
            acc[...] = jnp.zeros(acc.shape, F32)

    for copy in copies(chunk, slot):
        copy.wait()
    narrow_g = nar_g[...]
    narrow_u = nar_u[...]
    narrow_b = back_d[...]
    gate = mm(n2, wg_ref[...]) + mm(narrow_g, eg_ref[...])
    upward = mm(n2, wu_ref[...]) + mm(narrow_u, eu_ref[...])
    sig = jax.nn.sigmoid(gate)
    act = gate * sig
    hidden = (act * upward).astype(BF)
    hidden_grad = mm_nt(g0, wd_ref[...]) + mm_nt(narrow_b, sd_ref[...])
    gate_grad = (hidden_grad * upward * (sig * (1.0 + gate * (1.0 - sig)))).astype(BF)
    up_grad = (hidden_grad * act).astype(BF)
    acc_out[...] += mm(hidden, wd_ref[...])
    acc_nd[...] += mm(hidden, sd_ref[...])
    acc_ng[...] += mm_nt(gate_grad, wg_ref[...]) + mm_nt(up_grad, wu_ref[...])
    acc_bg[...] += mm_nt(gate_grad, eg_ref[...])
    acc_bu[...] += mm_nt(up_grad, eu_ref[...])
    deg_ref[...] = peg_ref[...] + mm_tn(narrow_g, gate_grad)
    deu_ref[...] = peu_ref[...] + mm_tn(narrow_u, up_grad)
    dsd_ref[...] = psd_ref[...] + mm_tn(narrow_b, hidden)

    @pl.when(chunk == chunks - 1)
    def _():
        out_ref[:, :model] = acc_out[...].astype(BF)
        out_ref[:, model:] = jnp.concatenate([acc_nd[...], acc_nd[...]], axis=1).astype(BF)
        ng_ref[:, :model] = acc_ng[...].astype(BF)
        ng_ref[:, model:] = jnp.concatenate([acc_bg[...], acc_bu[...]], axis=1).astype(BF)


def feed(me, blocks, n2, g0, sgu, ed, wd, eg, eu, sd, previous, seqs, limit=768):
    tokens, model = n2.shape
    count = len(blocks)
    hidden = wd.shape[0]
    cols = ed.shape[0]
    size = max(c for c in range(128, limit + 1, 128) if hidden % c == 0)
    anywhere = pl.BlockSpec(memory_space=pl.ANY)
    whole = lambda a: pl.BlockSpec(
        a.shape, lambda h, i: (0,) * a.ndim, pipeline_mode=pl.Buffered(1)
    )
    part = lambda a: pl.BlockSpec((a.shape[0], size), lambda h, i: (0, h))
    tall = lambda a: pl.BlockSpec((size, a.shape[1]), lambda h, i: (h, 0))
    fixed = lambda c: pl.BlockSpec((tokens, c), lambda h, i: (0, 0))
    grads = jax.ShapeDtypeStruct((cols, hidden), F32)
    return pl.pallas_call(
        functools.partial(feed_kernel, seqs, count),
        grid_spec=pltpu.PrefetchScalarGridSpec(
            num_scalar_prefetch=1,
            grid=(hidden // size,),
            in_specs=[anywhere] * count
            + [whole(n2), whole(g0), whole(sgu), whole(ed), tall(wd)]
            + [part(eg), part(eu), tall(sd), part(grads), part(grads), part(grads)],
            out_specs=[fixed(model + 2 * cols), fixed(model + 2 * cols)] + [part(grads)] * 3,
            scratch_shapes=[
                pltpu.VMEM((tokens, model), F32),
                pltpu.VMEM((tokens, model), F32),
                pltpu.VMEM((tokens, cols), F32),
                pltpu.VMEM((tokens, cols), F32),
                pltpu.VMEM((tokens, cols), F32),
                pltpu.VMEM((tokens, cols), BF),
                pltpu.VMEM((tokens, cols), BF),
                pltpu.VMEM((tokens, cols), BF),
                pltpu.VMEM((2, 2, model, size), BF),
                pltpu.SemaphoreType.DMA((2, count)),
            ],
        ),
        out_shape=[
            jax.ShapeDtypeStruct((tokens, model + 2 * cols), BF),
            jax.ShapeDtypeStruct((tokens, model + 2 * cols), BF),
            grads, grads, grads,
        ],
        name="feed",
        cost_estimate=pl.CostEstimate(
            flops=12 * tokens * (model + cols) * hidden,
            bytes_accessed=6 * model * hidden,
            transcendentals=tokens * hidden,
        ),
    )(me.reshape(1).astype(jnp.int32), *blocks, n2, g0, sgu, ed, wd, eg, eu, sd, *previous)


def assemble_kernel(count, info, *refs):
    blocks = refs[:count]
    out_ref, held, blank, in_sem, out_sem = refs[count:]
    depth = blocks[0].shape[0]
    rest = out_ref.shape[0] - count * depth
    arrive = []
    leave = []
    for j in range(count):
        arrive.append(pltpu.make_async_copy(blocks[j], held.at[j], in_sem.at[j]))
        at = pl.multiple_of((info[0] ^ j) * depth, depth)
        leave.append(
            pltpu.make_async_copy(held.at[j], out_ref.at[pl.ds(at, depth), :], out_sem.at[j])
        )
    for copy in arrive:
        copy.start()
    if rest:
        blank[...] = jnp.zeros(blank.shape, BF)
        last = pltpu.make_async_copy(blank, out_ref.at[count * depth :, :], out_sem.at[count])
        last.start()
    for one, two in zip(arrive, leave):
        one.wait()
        two.start()
    for copy in leave:
        copy.wait()
    if rest:
        last.wait()


def assemble(index, blocks, rows):
    count = len(blocks)
    depth, lanes = blocks[0].shape
    anywhere = pl.BlockSpec(memory_space=pl.ANY)
    return pl.pallas_call(
        functools.partial(assemble_kernel, count),
        grid_spec=pltpu.PrefetchScalarGridSpec(
            num_scalar_prefetch=1,
            grid=(1,),
            in_specs=[anywhere] * count,
            out_specs=anywhere,
            scratch_shapes=[
                pltpu.VMEM((count, depth, lanes), BF),
                pltpu.VMEM((max(rows - count * depth, 16), lanes), BF),
                pltpu.SemaphoreType.DMA((count,)),
                pltpu.SemaphoreType.DMA((count + 1,)),
            ],
        ),
        out_shape=jax.ShapeDtypeStruct((rows, lanes), BF),
        name="assemble",
        cost_estimate=pl.CostEstimate(
            flops=0, bytes_accessed=4 * rows * lanes, transcendentals=0
        ),
    )(index.reshape(1).astype(jnp.int32), *blocks)


def expand_kernel(rank, hidden, padded, seq_n, early, kinds, both_ref, select_ref, *outs):
    pair = pl.program_id(0)
    select = select_ref[...]
    lanes = -(-hidden // 128) * 128
    width = both_ref.shape[2] - early
    for q in range(2):
        for i, out_ref in enumerate(outs[:3]):
            groups = []
            for f in range(2):
                at = i * padded
                left = lanes
                pieces = []
                while left:
                    z, low = divmod(at, width)
                    take = min(left, width - low)
                    device = pair * 4 * seq_n + (q * 2 + f) * seq_n + z
                    pieces.append(both_ref[device, :rank, early + low : early + low + take])
                    at += take
                    left -= take
                groups.append(jnp.concatenate(pieces, axis=1))
            rows = jnp.concatenate(groups, axis=0)
            if i < 2:
                out_ref[:, q * hidden : (q + 1) * hidden] = mm_tn(select, rows)[:, :hidden]
            else:
                out_ref[q * hidden : (q + 1) * hidden, :] = mm_tn(rows, select)[:hidden]

    @pl.when(pair == 0)
    def _():
        half = both_ref.shape[0] // 2
        for i, (out_ref, shrink) in enumerate(zip(outs[3:], kinds)):
            rows = jnp.concatenate(
                [
                    jnp.concatenate(
                        [both_ref[f * half + 2 * i + w, :rank, :early] for w in range(2)], axis=1
                    )
                    for f in range(2)
                ],
                axis=0,
            )
            out_ref[...] = mm_tn(rows, select) if shrink else mm_tn(select, rows)


def expand_all(both, select, rank, hidden, padded, seq_n, chips, early, kinds):
    cols = select.shape[1]
    model = 2 * early
    wide = lambda n: jax.ShapeDtypeStruct((cols, n), F32)
    tall = lambda n: jax.ShapeDtypeStruct((n, cols), F32)
    fixed = [tall(model) if shrink else wide(model) for shrink in kinds]
    return pl.pallas_call(
        functools.partial(expand_kernel, rank, hidden, padded, seq_n, early, kinds),
        grid=(chips // 2,),
        in_specs=[
            pl.BlockSpec(both.shape, lambda p: (0, 0, 0), pipeline_mode=pl.Buffered(1)),
            pl.BlockSpec(select.shape, lambda p: (0, 0)),
        ],
        out_specs=[
            pl.BlockSpec((cols, 2 * hidden), lambda p: (0, p)),
            pl.BlockSpec((cols, 2 * hidden), lambda p: (0, p)),
            pl.BlockSpec((2 * hidden, cols), lambda p: (p, 0)),
        ]
        + [pl.BlockSpec(one.shape, lambda p: (0, 0)) for one in fixed],
        out_shape=[wide(chips * hidden), wide(chips * hidden), tall(chips * hidden)] + fixed,
        name="expand",
        cost_estimate=pl.CostEstimate(
            flops=6 * cols * chips * hidden * select.shape[0],
            bytes_accessed=12 * cols * chips * hidden + both.size * 2,
            transcendentals=0,
        ),
    )(both, select)


def after(value, *needed):
    return lax.optimization_barrier((value, needed))[0]


def body(
    inputs, cotangent, span_order, adapter_ids, first_gain, second_gain,
    query_weight, key_weight, value_weight, output_weight, gate_weight, up_weight, down_weight,
    query_bias, key_bias, value_bias,
    query_reduce_factors, query_lift_factors, key_reduce_factors, key_lift_factors,
    value_reduce_factors, value_lift_factors, output_reduce_factors, output_lift_factors,
    gate_reduce_factors, gate_lift_factors, upper_reduce_factors, upper_lift_factors,
    down_reduce_factors, down_lift_factors,
):
    seq_n = lax.axis_size("seq")
    cp_n = lax.axis_size("cp")
    fsdp_n = lax.axis_size("fsdp")
    plane = fsdp_n * cp_n
    chips = plane // 2
    group = lax.axis_index("fsdp")
    me = group * cp_n + lax.axis_index("cp")
    chip = me // 2
    core = me % 2
    seqs, tok_rows, model = inputs.shape
    tokens = seqs * tok_rows
    cols = query_reduce_factors.shape[1]
    kv_width = key_weight.shape[1]
    length = tok_rows * seq_n * cp_n
    spans = span_order.shape[1]
    span_len = length // spans
    hidden_all = gate_weight.shape[1]
    hq = hidden_all // chips
    hp = -(-hq // 256) * 256
    pad = hp - hq
    rank = seqs * ADAPTER_RANK
    lanes = -(-rank // 64) * 64

    def swap(value, k):
        return lax.ppermute(value, PLANE, [(i, i ^ k) for i in range(plane)])

    first_row = (lax.axis_index("cp") * seq_n + lax.axis_index("seq")) * tok_rows
    own = lax.dynamic_slice_in_dim(span_order, first_row // span_len, 1, 1)[:, 0]
    shift = first_row % span_len
    info = jnp.concatenate([span_order.reshape(-1), own, shift.reshape(1)]).astype(jnp.int32)
    places = own[:, None] * span_len + shift + jnp.arange(tok_rows, dtype=jnp.int32)[None, :]
    cosine, sine_table = rotary_tables(places.reshape(tokens))
    cosine = cosine[:, None, :]
    sine_table = sine_table[:, None, :]
    lane = jnp.arange(lanes, dtype=jnp.int32)

    def chosen(ids):
        column = jnp.repeat(ids, ADAPTER_RANK) * ADAPTER_RANK + lane[:rank] % ADAPTER_RANK
        column = jnp.pad(column, (0, lanes - rank), constant_values=-1)
        return (jnp.arange(cols, dtype=jnp.int32)[:, None] == column[None, :]).astype(BF)

    ids_wide = jnp.broadcast_to(
        jnp.pad(adapter_ids, (0, -seqs % 8)).astype(F32)[:, None], (seqs + -seqs % 8, 128)
    )
    select = [chosen(adapter_ids)]
    for f in range(1, fsdp_n):
        select.append(chosen(swap(ids_wide, f * cp_n)[:seqs, 0].astype(jnp.int32)))
    mixing = token_mask(tokens, lanes, seqs)

    def shrink_of(value, f=0):
        return mm(value, select[f]).astype(BF)

    def expand_of(value, f=0):
        return mm_tn(select[f], value).astype(BF)

    w_kv = lax.all_gather(
        jnp.concatenate([key_weight, value_weight], axis=1), PLANE, axis=0, tiled=True
    )
    rows_q = [query_weight] + [swap(query_weight, 2 * k) for k in range(1, chips)]

    def by_chip(value):
        return jnp.stack(
            [
                jnp.pad(value[:, hq * c : hq * (c + 1)], ((0, 0), (0, pad)))
                for c in range(chips)
            ]
        )

    gate_up = jnp.stack([by_chip(gate_weight), by_chip(up_weight)], axis=1)
    depth = gate_weight.shape[0]
    parts = [lax.dynamic_index_in_dim(gate_up, chip ^ k, 0, keepdims=False) for k in range(chips)]

    resid_in = inputs.reshape(tokens, model).astype(F32)
    first_scales = first_gain.astype(F32)
    second_scales = second_gain.astype(F32)
    grad_low = cotangent.reshape(tokens, model)
    normed = norm_forward(resid_in, first_scales).astype(BF)
    w_kv, parts, rows_q = lax.optimization_barrier((w_kv, parts, rows_q))
    rows_o = [output_weight] + [swap(after(output_weight, rows_q), 2 * k) for k in range(1, chips)]
    crosses_cp = lambda k: 2 * k % cp_n != 0
    blocks = {
        k: swap(after(parts[k], rows_o), 2 * k) for k in range(1, chips) if not crosses_cp(k)
    }
    blocks[0] = parts[0]
    w_key = w_kv[:, :kv_width]
    w_value = w_kv[:, kv_width:]

    query_shrink, key_shrink, value_shrink, output_shrink, gate_shrink, up_shrink = [
        shrink_of(value)
        for value in (
            query_reduce_factors, key_reduce_factors, value_reduce_factors,
            output_reduce_factors, gate_reduce_factors, upper_reduce_factors,
        )
    ]
    query_expand, key_expand, value_expand, output_expand, down_expand = [
        expand_of(value)
        for value in (
            query_lift_factors, key_lift_factors, value_lift_factors,
            output_lift_factors, down_lift_factors,
        )
    ]

    def narrowed(value, shrink):
        return (mm(value, shrink) * mixing).astype(BF)

    key_narrow = narrowed(normed, key_shrink)
    value_narrow = narrowed(normed, value_shrink)
    key_pre = mm(normed, w_key) + key_bias.astype(F32) + mm(key_narrow, key_expand)
    value_low = (
        mm(normed, w_value) + value_bias.astype(F32) + mm(value_narrow, value_expand)
    ).astype(BF)
    key_rot = rotate(key_pre.reshape(tokens, -1, HEAD_DIM), cosine, sine_table).astype(BF)
    pair = jnp.concatenate([key_rot.reshape(tokens, kv_width), value_low], axis=1)
    pair_all = lax.all_gather(
        pair.reshape(seqs, tok_rows, 2 * kv_width), ("cp", "seq"), axis=1, tiled=True
    )

    def both_cores(rows):
        found = []
        for part in rows:
            found += [part, swap(part, 1)]
        return found

    w_query = assemble(me, after(both_cores(rows_q), pair), model)
    normed_later = after(normed, rows_o)
    query_narrow = narrowed(normed_later, query_shrink)
    query_pre = mm(normed_later, w_query) + query_bias.astype(F32) + mm(query_narrow, query_expand)
    query_rot = (
        rotate(query_pre.reshape(tokens, -1, HEAD_DIM), cosine, sine_table)
        .astype(BF)
        .reshape(tokens, model)
    )

    lift_g = lax.dynamic_index_in_dim(by_chip(gate_lift_factors), chip, 0, keepdims=False)
    lift_u = lax.dynamic_index_in_dim(by_chip(upper_lift_factors), chip, 0, keepdims=False)
    shrink_d = jnp.pad(
        lax.dynamic_slice_in_dim(down_reduce_factors, chip * hq, hq, 0), ((0, pad), (0, 0))
    )
    feed_factors = [
        (
            jnp.concatenate(
                [shrink_of(gate_reduce_factors, f), shrink_of(upper_reduce_factors, f)], axis=1
            ),
            expand_of(down_lift_factors, f),
            expand_of(lift_g, f),
            expand_of(lift_u, f),
            shrink_of(shrink_d, f),
        )
        for f in range(fsdp_n)
    ]

    down_rows = [down_weight, swap(after(down_weight, rows_o), 1)]
    w_output = assemble(me, after(both_cores(rows_o), query_rot), model)
    w_down = assemble(core, after(down_rows, query_rot), hp)
    query_rot = after(query_rot, [blocks[k] for k in blocks if k], w_output, w_down)
    for k in range(1, chips):
        if crosses_cp(k):
            blocks[k] = swap(after(parts[k], pair_all), 2 * k)
    blocks = [after(blocks[k], query_rot) for k in range(chips)]
    wide = []
    for part in blocks:
        wide += [part, swap(part, 1)]
    attended, lse = attend(info, query_rot, pair_all, seqs, spans, span_len)

    output_narrow = narrowed(attended, output_shrink)
    middle = resid_in + (mm(attended, w_output) + mm(output_narrow, output_expand))
    normed_two = norm_forward(middle, second_scales).astype(BF)

    g0_pieces = [grad_low] + [swap(after(grad_low, wide), 2 * k) for k in range(1, chips)]
    n2_pieces = [normed_two] + [swap(after(normed_two, wide), 2 * k) for k in range(1, chips)]
    if chips > 2:
        n2_pieces[1:3] = lax.optimization_barrier(n2_pieces[1:3])
    zero = jnp.zeros((lanes, hp), F32)
    sums = [(zero, zero, zero)] * fsdp_n
    out_raw = []
    grad_parts = []
    for k in range(chips):
        f = 2 * k // cp_n
        sgu, ed, eg, eu, sd = feed_factors[f]
        out_k, ng_k, *sums[f] = feed(
            me, wide, n2_pieces[k], g0_pieces[k], sgu, ed, w_down, eg, eu, sd, sums[f], seqs
        )
        out_raw.append(out_k)
        grad_parts.append(ng_k if k == 0 else swap(ng_k, 2 * k))

    grad_sum = grad_parts[0].astype(F32)
    for part in grad_parts[1:]:
        grad_sum = lax.optimization_barrier(grad_sum) + part.astype(F32)
    gate_back = (grad_sum[:, model : model + lanes] * mixing).astype(BF)
    up_back = (grad_sum[:, model + lanes :] * mixing).astype(BF)
    normed_two_grad = (
        grad_sum[:, :model] + mm_nt(gate_back, gate_shrink) + mm_nt(up_back, up_shrink)
    )
    middle_grad = grad_low.astype(F32) + norm_backward(middle, second_scales, normed_two_grad)
    middle_low = middle_grad.astype(BF)

    def narrowed_back(grad, expand):
        return (mm_nt(grad, expand) * mixing).astype(BF)

    output_back = narrowed_back(middle_low, output_expand)
    attended_grad = (mm_nt(middle_low, w_output) + mm_nt(output_back, output_shrink)).astype(BF)
    query_rot_grad, pair_part = attend_back(
        info, query_rot, attended_grad, attended, pair_all, lse, seqs, spans, span_len
    )

    out_raw = after(out_raw, grad_sum)
    out_parts = [part if k == 0 else swap(part, 2 * k) for k, part in enumerate(out_raw)]
    out_sum = sum(part.astype(F32) for part in out_parts)

    def pack(values, tiles):
        value = jnp.concatenate([value[:rank].astype(BF) for value in values], axis=1)
        return jnp.pad(value, ((0, 0), (0, -value.shape[1] % (128 * tiles))))

    sums = after(sums, attended_grad)
    stacked = jnp.stack([pack(sums[f], seq_n) for f in range(fsdp_n)])
    feed_wide = stacked.shape[2]

    def groups_of(parity):
        return jnp.stack(
            [
                lax.dynamic_index_in_dim(stacked, (2 * j + parity) ^ group, 0, keepdims=False)
                for j in range(fsdp_n // 2)
            ]
        )

    feed_half = groups_of(core).astype(F32) + swap(groups_of(1 - core), 1).astype(F32)
    feed_half = feed_half.reshape(fsdp_n // 2 * rank, seq_n, feed_wide // seq_n).astype(BF)
    feed_piece = lax.psum_scatter(
        feed_half.transpose(1, 0, 2), "seq", scatter_dimension=0, tiled=False
    )
    pair_grad = (
        lax.psum_scatter(
            after(pair_part, feed_piece, out_parts), ("cp", "seq"), scatter_dimension=1, tiled=True
        )
        .reshape(tokens, 2 * kv_width)
        .astype(F32)
    )

    down_narrow = (out_sum[:, model : model + lanes] * mixing).astype(BF)
    result = middle + (out_sum[:, :model] + mm(down_narrow, down_expand))
    outputs = result.astype(BF).reshape(seqs, tok_rows, model)

    query_grad = (
        unrotate(
            query_rot_grad.reshape(tokens, -1, HEAD_DIM).astype(F32), cosine, sine_table
        )
        .reshape(tokens, model)
        .astype(BF)
    )
    query_back = narrowed_back(query_grad, query_expand)
    query_in = mm_nt(query_grad, w_query) + mm_nt(query_back, query_shrink)

    def halves(value, index, exchange):
        span = 1
        while value.shape[0] > 1:
            split = value.reshape((value.shape[0] // 2, 2) + value.shape[1:])
            bit = index // span % 2
            keep = lax.dynamic_index_in_dim(split, bit, 1, keepdims=False)
            give = lax.dynamic_index_in_dim(split, 1 - bit, 1, keepdims=False)
            value = (keep.astype(F32) + exchange(give, span).astype(F32)).astype(BF)
            span *= 2
        return value[0]

    def swap_seq(value, k):
        return lax.ppermute(value, "seq", [(i, i ^ k) for i in range(seq_n)])

    ways = cp_n * seq_n
    cp_index = lax.axis_index("cp")
    early = pack(
        [
            mm_tn(output_back, attended),
            mm_tn(gate_back, normed_two),
            mm_tn(up_back, normed_two),
            mm_tn(output_narrow, middle_low),
            mm_tn(down_narrow, grad_low),
            mm_tn(query_back, normed),
            mm_tn(query_narrow, query_grad),
        ],
        ways,
    )
    early = early.reshape(rank, cp_n, seq_n, -1).transpose(1, 2, 0, 3)
    early = halves(early, cp_index, swap)
    early = halves(early, lax.axis_index("seq"), swap_seq)
    early_cols = early.shape[1]
    lines = feed_piece.shape[0]
    both = jnp.concatenate([jnp.pad(early, ((0, lines - rank), (0, 0))), feed_piece], axis=1)
    both = lax.all_gather(after(both, pair_grad), EVERY, axis=0, tiled=False)

    key_grad = (
        unrotate(pair_grad[:, :kv_width].reshape(tokens, -1, HEAD_DIM), cosine, sine_table)
        .reshape(tokens, kv_width)
        .astype(BF)
    )
    value_grad = pair_grad[:, kv_width:].astype(BF)
    key_back = narrowed_back(key_grad, key_expand)
    value_back = narrowed_back(value_grad, value_expand)

    late = pack(
        [
            mm_tn(key_back, normed),
            mm_tn(value_back, normed),
            mm_tn(key_narrow, key_grad),
            mm_tn(value_narrow, value_grad),
        ],
        cp_n,
    )
    late_wide = late.shape[1]
    late = late.reshape(rank, cp_n, late_wide // cp_n).transpose(1, 0, 2)
    late = halves(late, cp_index, swap)
    total = late.astype(F32)
    for k in range(1, seq_n):
        total = total + swap_seq(late, k).astype(F32)
    late = total.astype(BF)[None]
    for step in [span_k for span_k in (2**i for i in range(1, 30)) if span_k < plane] + [1]:
        late = jnp.concatenate([late, swap(late, step)], axis=0)

    normed_grad = (
        query_in
        + mm_nt(key_grad, w_key)
        + mm_nt(value_grad, w_value)
        + mm_nt(key_back, key_shrink)
        + mm_nt(value_back, value_shrink)
    )
    input_grad = middle_grad + norm_backward(resid_in, first_scales, normed_grad)

    came = [0]
    for step in [span_k for span_k in (2**i for i in range(1, 30)) if span_k < plane] + [1]:
        came = came + [c ^ step for c in came]
    inverse = [came.index(c) for c in range(plane)]
    late = jnp.take(
        late, jnp.asarray(inverse, jnp.int32)[jnp.arange(plane, dtype=jnp.int32) ^ me], axis=0
    )
    late = late.reshape(fsdp_n, cp_n, rank, late_wide // cp_n)
    late = late.transpose(0, 2, 1, 3).reshape(fsdp_n * rank, late_wide)

    order = jnp.arange(fsdp_n, dtype=jnp.int32) ^ group
    select_all = (
        jnp.take(jnp.stack(select), order, axis=0)[:, :, :rank]
        .transpose(0, 2, 1)
        .reshape(fsdp_n * rank, cols)
    )
    shrink_grad = lambda value: mm_tn(value, select_all)
    expand_grad = lambda value: mm_tn(select_all, value)

    late_of = lambda i: late[:, model * i : model * (i + 1)]
    tail_of = lambda i: late[:, model * 2 + kv_width * i : model * 2 + kv_width * (i + 1)]
    kinds = (True, True, True, False, False, True, False)
    if fsdp_n == 2 and 2 * hq % 128 == 0 and 2 * early_cols == model:
        expanded = expand_all(
            both, select_all, rank, hq, hp, seq_n, chips, early_cols, kinds
        )
    else:
        early_full = both[:, :rank, :early_cols].reshape(fsdp_n, ways, rank, early_cols)
        early_full = early_full.transpose(0, 2, 1, 3).reshape(fsdp_n * rank, ways * early_cols)
        feed_full = both[:, :, early_cols:].reshape(
            fsdp_n, cp_n // 2, 2, seq_n, fsdp_n // 2, rank, feed_wide // seq_n
        ).transpose(4, 2, 5, 0, 1, 3, 6)
        feed_full = feed_full.reshape(fsdp_n * rank, chips, feed_wide)
        expanded = []
        for i, shrink in enumerate((False, False, True) + kinds):
            if i < 3:
                rows = feed_full[:, :, i * hp : i * hp + hq].reshape(fsdp_n * rank, hidden_all)
            else:
                rows = early_full[:, model * (i - 3) : model * (i - 2)]
            expanded.append(shrink_grad(rows) if shrink else expand_grad(rows))

    return (
        outputs,
        input_grad.reshape(seqs, tok_rows, model),
        expanded[8],
        expanded[9],
        shrink_grad(late_of(0)),
        expand_grad(tail_of(0)),
        shrink_grad(late_of(1)),
        expand_grad(tail_of(1)),
        expanded[3],
        expanded[6],
        expanded[4],
        expanded[0],
        expanded[5],
        expanded[1],
        expanded[2],
        expanded[7],
    )


def solution(mesh):
    tokens_spec = P("fsdp", ("cp", "seq"), None)
    weight_spec = P(("fsdp", "cp"), None)
    placed = (
        (tokens_spec, tokens_spec, P("fsdp", None), P("fsdp"), P(), P())
        + (weight_spec,) * 7
        + (P(),) * 17
    )
    return jax.shard_map(
        body,
        mesh=mesh,
        in_specs=placed,
        out_specs=(tokens_spec, tokens_spec) + (P(),) * 14,
        check_vma=False,
    )
```

time: 2130 us -> 700 us (0.33)
  waiting for transfers between devices: 1060 us -> 207 us
  matrix products: 461 us -> 75.2 us
  local copies, waits for them, and re-layouts: 297 us -> 76.3 us
  blocking collectives: 201 us -> 0 us
  Pallas kernels: 0 us -> 189 us
  other arithmetic: 58.5 us -> 85.4 us
    psum x1 -> x0, waiting for transfers between devices: 753 us -> none  [body(): lax.psum((query_shrink_grad, query_expand_grad, key_shrink_grad, key_expa...]
    dot_general x77 -> x62, matrix products: 461 us -> 75.2 us  [the longest x23 34.3 us: mm(): return jnp.dot(left, right, preferred_element_type=jnp.float32)]
    pallas_call x0 -> x10, Pallas kernels: none -> 189 us  [the longest x4 117 us: feed(): pl.pallas_call(functools.partial(feed_kernel, seqs, count), grid_spec=plt...]
    all_gather x6 -> x3, waiting for transfers between devices: 194 us -> 14.1 us  [the longest x1 14.1 us: body(): both = lax.all_gather(after(both, pair_grad), EVERY, axis=0, tiled=False)]
    ppermute x0 -> x48, waiting for transfers between devices: none -> 174 us  [the longest x43 149 us: swap(): return lax.ppermute(value, PLANE, [(i, i ^ k) for i in range(plane)])]
    dynamic_update_slice x12 -> x0, local copies, waits for them, and re-layouts: 154 us -> none  [the longest x6 149 us: body(): lax.map(attend_back, (query_heads, pair_all, grad_heads, log_totals, quer...]
    unnamed x1 -> x0, blocking collectives: 147 us -> none
    all_to_all x5 -> x0, waiting for transfers between devices: 110 us -> none  [the longest x1 34.3 us: body(): lax.all_to_all(attended_heads, 'seq', split_axis=1, concat_axis=2, tiled=...]
  transfers between devices with their start and end apart: 12 -> 53, of which waited for: 8 -> 22; matrix products, arithmetic and copies ran while one was open for 14% -> 29% of each run, Pallas kernels for 0% -> 26%
where the time goes in v1:
time: 700 us; the launch traced here: 691 us
  waiting for transfers between devices  207 us (30%)
  Pallas kernels  189 us (27%)
  other arithmetic  85.4 us (12%)
  local copies, waits for them, and re-layouts  76.3 us (11%)
  matrix products  75.2 us (11%)
  starting transfers between devices  42.3 us (6%)
  between operations  16.2 us (2%)
    ppermute x43, waiting for transfers between devices, swap(): return lax.ppermute(value, PLANE, [(i, i ^ k) for i in range(plane)])  149 us
    pallas_call x4, Pallas kernels, feed(): pl.pallas_call(functools.partial(feed_kernel, seqs, count), grid_spec=plt...  117 us
    ppermute x43, starting transfers between devices, swap(): return lax.ppermute(value, PLANE, [(i, i ^ k) for i in range(plane)])  35.3 us
    dot_general x23, matrix products, mm(): return jnp.dot(left, right, preferred_element_type=jnp.float32)  34.3 us
    ppermute x5, waiting for transfers between devices, swap_seq(): return lax.ppermute(value, 'seq', [(i, i ^ k) for i in range(seq_n)])  25.4 us
    pallas_call x1, Pallas kernels, attend_back(): pl.pallas_call(functools.partial(attend_back_kernel, spans, span_len, tok...  24.9 us
    dot_general x25, matrix products, mm_tn(): lax.dot_general(left, right, (((0,), (0,)), ((), ())), preferred_element_...  24.9 us
    pallas_call x1, Pallas kernels, attend(): pl.pallas_call(functools.partial(attend_kernel, spans, span_len, tokens),...  21.1 us
  transfers between devices with their start and end apart: 53, of which 22 were waited for; matrix products, arithmetic and copies ran while one was open for 29% of the time, Pallas kernels for 26%

profile of v1, /device:TPU:0, one launch (start us, length us, event | category | flops | bytes accessed | tf_op | source)
XLA Modules:
  0.0 691.2 jit_solution(16382043647458234720)
XLA Ops:
  7.2 3.0 collective-permute-start
  18.5 4.1 fusion.156
  33.4 2.0 maximum_bitcast_fusion
  35.5 2.0 maximum_bitcast_fusion.1
  38.1 5.2 fusion.18
  69.6 2.5 mul.317
  72.2 3.1 copy.113
  76.4 2.1 fusion.159
  101.2 24.5 %collective-permute-done.3.refs_2_ = bf16[192,1536]{1,0:T(8,128)(2,1)} collective-permute-done((bf16[192,1536]{1,0:T(8,128)(2,1)}, bf16[192,1536]{1,0:T(8,128)(2,1)}, u32[]{:S(2)}, u32[]{:S(2)}) %collective-permute-start.3) | collective-permute-done | bytes 589856 | tf_op jit(solution)/shard_map/ppermute | solution.py:562
  130.8 3.0 collective-permute-done.6.refs_1_
  136.5 4.3 assemble.3
  142.1 5.9 fusion.3
  148.0 2.0 copy.114
  150.5 3.1 collective-permute-start.20
  156.2 3.2 copy.115
  159.4 3.9 add_convert_fusion.1.q_ref
  163.3 4.2 assemble.4
  167.5 5.0 assemble.5.refs_12_
  172.6 4.8 collective-permute-done.10.refs_4_
  178.0 21.1 %attend.1 = (bf16[384,1536]{1,0:T(8,128)(2,1)}, f32[6,8,768]{2,1,0:T(8,128)}) custom-call(s32[28]{0:T(128)} %pad_add_fusion.info, bf16[384,1536]{1,0:T(8,128)(2,1)} %add_convert_fusion.1.q_ref, bf16[3,2048,512]{2,1,0:T(8,128)(2,1)} %all-gather.7.cloned.1.call-done.k_ref.v_ref, bf16[3,2048,512]{2,1,0:T(8,128)(2,1)} %all-gather.7.cloned.1.call-done.k_ref.v_ref), custom_call_target="tpu_custom_call" | custom-call | flops 4831838208 | bytes 6291456 | tf_op jit(solution)/shard_map/attend/pallas_call | solution.py:152
  201.0 15.6 %collective-permute-done.20.refs_6_ = bf16[2,192,2304]{2,1,0:T(8,128)(2,1)} collective-permute-done((bf16[2,192,2304]{2,1,0:T(8,128)(2,1)}, bf16[2,192,2304]{2,1,0:T(8,128)(2,1)}, u32[]{:S(2)}, u32[]{:S(2)}) %collective-permute-start.20) | collective-permute-done | bytes 1769504 | tf_op jit(solution)/shard_map/ppermute | solution.py:562
  216.6 15.6 %collective-permute-done.17.refs_2_ = bf16[2,192,2304]{2,1,0:T(8,128)(2,1)} collective-permute-done((bf16[2,192,2304]{2,1,0:T(8,128)(2,1)}, bf16[2,192,2304]{2,1,0:T(8,128)(2,1)}, u32[]{:S(2)}, u32[]{:S(2)}) %collective-permute-start.17) | collective-permute-done | bytes 1769504 | tf_op jit(solution)/shard_map/ppermute | solution.py:562
  232.7 4.6 multiply_reduce_fusion.1
  244.8 29.0 %feed.4 = (bf16[384,1664]{1,0:T(8,128)(2,1)}, bf16[384,1664]{1,0:T(8,128)(2,1)}, f32[64,2304]{1,0:T(8,128)}, f32[64,2304]{1,0:T(8,128)}, f32[64,2304]{1,0:T(8,128)}) custom-call(s32[1]{0:T(128)} %bitcast.17.info, bf16[2,192,2304]{2,1,0:T(8,128)(2,1)} %get-tuple-element.135.refs_0_, bf16[2,192,2304]{2,1,0:T(8,128)(2,1)} %collective-permute-done.16.refs_1_, ...), custom_call_target="tpu_custom_call" | custom-call | flops 16986931200 | bytes 21233664 | tf_op jit(solution)/shard_map/feed/pallas_call | solution.py:364
  273.8 2.9 convert_element_type.427
  276.7 2.3 collective-permute-start.27
  279.0 14.2 %collective-permute-done.24.refs_9_ = bf16[384,1536]{1,0:T(8,128)(2,1)} collective-permute-done((bf16[384,1536]{1,0:T(8,128)(2,1)}, bf16[384,1536]{1,0:T(8,128)(2,1)}, u32[]{:S(2)}, u32[]{:S(2)}) %collective-permute-start.24) | collective-permute-done | bytes 1179680 | tf_op jit(solution)/shard_map/ppermute | solution.py:562
  293.3 29.2 %feed.5 = (bf16[384,1664]{1,0:T(8,128)(2,1)}, bf16[384,1664]{1,0:T(8,128)(2,1)}, f32[64,2304]{1,0:T(8,128)}, f32[64,2304]{1,0:T(8,128)}, f32[64,2304]{1,0:T(8,128)}) custom-call(s32[1]{0:T(128)} %bitcast.17.info, bf16[2,192,2304]{2,1,0:T(8,128)(2,1)} %get-tuple-element.135.refs_0_, bf16[2,192,2304]{2,1,0:T(8,128)(2,1)} %collective-permute-done.16.refs_1_, ...), custom_call_target="tpu_custom_call" | custom-call | flops 16986931200 | bytes 21233664 | tf_op jit(solution)/shard_map/feed/pallas_call | solution.py:364
  322.8 29.2 %feed.6 = (bf16[384,1664]{1,0:T(8,128)(2,1)}, bf16[384,1664]{1,0:T(8,128)(2,1)}, f32[64,2304]{1,0:T(8,128)}, f32[64,2304]{1,0:T(8,128)}, f32[64,2304]{1,0:T(8,128)}) custom-call(s32[1]{0:T(128)} %bitcast.17.info, bf16[2,192,2304]{2,1,0:T(8,128)(2,1)} %get-tuple-element.135.refs_0_, bf16[2,192,2304]{2,1,0:T(8,128)(2,1)} %collective-permute-done.16.refs_1_, ...), custom_call_target="tpu_custom_call" | custom-call | flops 16986931200 | bytes 21233664 | tf_op jit(solution)/shard_map/feed/pallas_call | solution.py:364
  353.0 29.7 %feed.7 = (bf16[384,1664]{1,0:T(8,128)(2,1)}, bf16[384,1664]{1,0:T(8,128)(2,1)}, f32[64,2304]{1,0:T(8,128)}, f32[64,2304]{1,0:T(8,128)}, f32[64,2304]{1,0:T(8,128)}) custom-call(s32[1]{0:T(128)} %bitcast.17.info, bf16[2,192,2304]{2,1,0:T(8,128)(2,1)} %get-tuple-element.135.refs_0_, bf16[2,192,2304]{2,1,0:T(8,128)(2,1)} %collective-permute-done.16.refs_1_, ...), custom_call_target="tpu_custom_call" | custom-call | flops 16986931200 | bytes 21233664 | tf_op jit(solution)/shard_map/feed/pallas_call | solution.py:364
  382.6 2.4 collective-permute-start.31
  385.0 2.3 convert_add_fusion.3
  389.0 24.1 %collective-permute-done.31 = bf16[384,1664]{1,0:T(8,128)(2,1)S(1)} collective-permute-done((bf16[384,1664]{1,0:T(8,128)(2,1)}, bf16[384,1664]{1,0:T(8,128)(2,1)S(1)}, u32[]{:S(2)}, u32[]{:S(2)}) %collective-permute-start.31) | collective-permute-done | bytes 1277984 | tf_op jit(solution)/shard_map/ppermute | solution.py:562
  415.6 2.2 subtract_add_fusion
  419.7 3.0 fusion.5.do_ref
  434.5 2.5 add_convert_fusion.2
  437.0 2.6 convert_element_type.451
  439.6 2.0 copy.162
  441.7 24.9 %attend_back.1 = (bf16[384,1536]{1,0:T(8,128)(2,1)}, bf16[3,2048,512]{2,1,0:T(8,128)(2,1)}) custom-call(s32[28]{0:T(128)} %pad_add_fusion.info, bf16[384,1536]{1,0:T(8,128)(2,1)} %add_convert_fusion.1.q_ref, bf16[384,1536]{1,0:T(8,128)(2,1)} %fusion.5.do_ref, bf16[384,1536]{1,0:T(8,128)(2,1)} %get-tuple-element.133.o_ref, ...), custom_call_target="tpu_custom_call" | custom-call | flops 12079595520 | bytes 12582912 | tf_op jit(solution)/shard_map/attend_back/pallas_call | solution.py:249
  466.6 2.7 copy.129
  469.3 2.4 fusion.167
  475.1 15.3 %collective-permute-done.34 = bf16[384,1664]{1,0:T(8,128)(2,1)} collective-permute-done((bf16[384,1664]{1,0:T(8,128)(2,1)}, bf16[384,1664]{1,0:T(8,128)(2,1)}, u32[]{:S(2)}, u32[]{:S(2)}) %collective-permute-start.34) | collective-permute-done | bytes 1277984 | tf_op jit(solution)/shard_map/ppermute | solution.py:562
  490.5 3.2 pad_maximum_fusion
  493.7 3.1 copy.130
  496.8 3.6 add_convert_fusion
  501.6 2.4 fusion.138
  504.1 2.2 fusion.144
  506.7 3.0 convert_add_fusion
  514.2 2.9 reshape.409
  520.6 2.3 collective-permute-done.36
  527.6 14.5 %collective-permute-done.37 = bf16[1,4,48,768]{3,2,1,0:T(8,128)(2,1)} collective-permute-done((bf16[1,4,48,768]{3,2,1,0:T(8,128)(2,1)}, bf16[1,4,48,768]{3,2,1,0:T(8,128)(2,1)}, u32[]{:S(2)}, u32[]{:S(2)}) %collective-permute-start.37) | collective-permute-done | bytes 294944 | tf_op jit(solution)/shard_map/ppermute | solution.py:562
  546.2 10.0 %collective-permute-done.38 = bf16[2,48,768]{2,1,0:T(8,128)(2,1)} collective-permute-done((bf16[2,48,768]{2,1,0:T(8,128)(2,1)}, bf16[2,48,768]{2,1,0:T(8,128)(2,1)}, u32[]{:S(2)}, u32[]{:S(2)}) %collective-permute-start.38) | collective-permute-done | bytes 147488 | tf_op jit(solution)/shard_map/ppermute | solution.py:802
  559.1 5.6 collective-permute-done.39
  567.3 18.6 %reduce-scatter.5.cloned.1.call-done = bf16[3,128,512]{2,1,0:T(8,128)(2,1)} async-done(((bf16[3,2048,512]{2,1,0:T(8,128)(2,1)}), bf16[3,128,512]{2,1,0:T(8,128)(2,1)}) %reduce-scatter.5.cloned.1.call-update) | async-done | bytes 393232 | tf_op jit(solution)/shard_map/reduce_scatter | solution.py:769
  601.5 5.9 convolution_add_fusion.2
  607.5 3.5 fusion.9
  619.3 2.7 collective-permute-done.41
  623.7 2.3 collective-permute-start.43
  626.9 3.2 collective-permute-done.42
  630.1 6.5 collective-permute-done.43
  639.2 2.1 collective-permute-done.45
  642.3 8.4 %collective-permute-done.46 = bf16[2,48,896]{2,1,0:T(8,128)(2,1)S(1)} collective-permute-done((bf16[2,48,896]{2,1,0:T(8,128)(2,1)S(1)}, bf16[2,48,896]{2,1,0:T(8,128)(2,1)S(1)}, u32[]{:S(2)}, u32[]{:S(2)}) %collective-permute-start.46) | collective-permute-done | bytes 172064 | tf_op jit(solution)/shard_map/ppermute | solution.py:562
  658.3 14.1 %all-gather.9.cloned.1.call-done = bf16[1536,2560]{1,0:T(8,128)(2,1)} async-done(((bf16[48,2560]{1,0:T(8,128)(2,1)}), bf16[1536,2560]{1,0:T(8,128)(2,1)}) %all-gather.9.cloned.1.call-update) | async-done | bytes 7864336 | tf_op jit(solution)/shard_map/all_gather | solution.py:824
  672.4 12.1 %expand.1 = (f32[128,8960]{1,0:T(8,128)}, f32[128,8960]{1,0:T(8,128)}, f32[8960,128]{1,0:T(8,128)}, f32[1536,128]{1,0:T(8,128)}, f32[1536,128]{1,0:T(8,128)}, /*...) custom-call(bf16[32,48,2560]{2,1,0:T(8,128)(2,1)} %bitcast.256, ...), custom_call_target="tpu_custom_call" | custom-call | flops 660602880 | bytes 21626880 | tf_op jit(solution)/shard_map/expand/pallas_call | solution.py:502
  (550 shorter events, 175.2 us)
Async XLA Ops:
  7.2 72.4 %copy-start = (bf16[8960,128]{1,0:T(8,128)(2,1)S(1)}, bf16[8960,128]{1,0:T(8,128)(2,1)}, u32[]{:S(2)}) copy-start(bf16[8960,128]{1,0:T(8,128)(2,1)} %param.59) | copy-start | bytes 6881284
  7.2 51.1 %all-gather.5.cloned.1.call-start = ((), (), s32[]{:S(2)}) async-start(), calls=%async_computation.2 | async-start | bytes 1769472 | tf_op jit(solution)/shard_map/all_gather | solution.py:593
  7.2 51.0 %collective-permute-start = (bf16[192,1536]{1,0:T(8,128)(2,1)}, bf16[192,1536]{1,0:T(8,128)(2,1)}, u32[]{:S(2)}, u32[]{:S(2)}) collective-permute-start(bf16[192,1536]{1,0:T(8,128)(2,1)} %refs_0_), channel_id=1, source_target_pairs={{0,8},{4,12},{8,0},{12,4},{16,24},{20,28},{24,16},{28,20},{1,9},{5... | collective-permute-start | bytes 1769480 | tf_op jit(solution)/shard_map/ppermute | solution.py:562
  10.3 48.0 %collective-permute-start.1 = (bf16[192,1536]{1,0:T(8,128)(2,1)}, bf16[192,1536]{1,0:T(8,128)(2,1)}, u32[]{:S(2)}, u32[]{:S(2)}) collective-permute-start(bf16[192,1536]{1,0:T(8,128)(2,1)} %refs_0_), channel_id=1, source_target_pairs={{0,16},{4,20},{8,24},{12,28},{16,0},{20,4},{24,8},{28,12},{1,17},{... | collective-permute-start | bytes 1769480 | tf_op jit(solution)/shard_map/ppermute | solution.py:562
  11.8 46.5 %collective-permute-start.2 = (bf16[192,1536]{1,0:T(8,128)(2,1)}, bf16[192,1536]{1,0:T(8,128)(2,1)}, u32[]{:S(2)}, u32[]{:S(2)}) collective-permute-start(bf16[192,1536]{1,0:T(8,128)(2,1)} %refs_0_), channel_id=1, source_target_pairs={{0,24},{4,28},{8,16},{12,20},{16,8},{20,12},{24,0},{28,4},{1,25},{... | collective-permute-start | bytes 1769480 | tf_op jit(solution)/shard_map/ppermute | solution.py:562
  13.5 137.1 %all-gather.7.cloned.1.call-start = ((), (), s32[]{:S(2)}) async-start(), calls=%async_computation.3 | async-start | bytes 6684672 | tf_op jit(solution)/shard_map/all_gather | solution.py:651
  14.8 33.7 %collective-permute-start.26 = (f32[8,128]{0,1:T(8,128)}, f32[8,128]{0,1:T(8,128)}, u32[]{:S(2)}, u32[]{:S(2)}) collective-permute-start(f32[8,128]{0,1:T(8,128)} %broadcast_in_dim.36), channel_id=1, source_target_pairs={{0,16},{4,20},{8,24},{12,28},{16,0},{20,4},{24,8},{28,12},{1,17},{... | collective-permute-start | bytes 12296 | tf_op jit(solution)/shard_map/ppermute | solution.py:562
  18.4 38.1 %copy-start.91 = (s32[64]{0:T(128)}, s32[64]{0:T(128)S(1)}, u32[]{:S(2)}) copy-start(s32[64]{0:T(128)S(1)} %get-tuple-element.243) | copy-start | bytes 772
  49.9 78.9 %copy-start.84 = (s32[64]{0:T(128)}, s32[64]{0:T(128)S(1)}, u32[]{:S(2)}) copy-start(s32[64]{0:T(128)S(1)} %pad.84) | copy-start | bytes 772
  68.7 421.7 %reduce-scatter.3.cloned.1.call-start = ((), (), s32[]{:S(2)}) async-start(), calls=%async_computation.4 | async-start | bytes 860160 | tf_op jit(solution)/shard_map/reduce_scatter | solution.py:765
  82.3 47.5 %copy-start.90 = (s32[64]{0:T(128)}, s32[64]{0:T(128)S(1)}, u32[]{:S(2)}) copy-start(s32[64]{0:T(128)S(1)} %pad.95) | copy-start | bytes 772
  91.2 34.5 %copy-start.19 = (bf16[64,1536]{0,1:T(8,128)(2,1)}, bf16[64,1536]{0,1:T(8,128)(2,1)S(1)}, u32[]{:S(2)}) copy-start(bf16[64,1536]{0,1:T(8,128)(2,1)S(1)} %convolution_convert_fusion.7) | copy-start | bytes 589828
  91.5 35.2 %copy-start.25 = (bf16[64,1536]{0,1:T(8,128)(2,1)}, bf16[64,1536]{0,1:T(8,128)(2,1)S(1)}, u32[]{:S(2)}) copy-start(bf16[64,1536]{0,1:T(8,128)(2,1)S(1)} %convolution_convert_fusion.6) | copy-start | bytes 589828
  91.5 34.2 %collective-permute-start.3 = (bf16[192,1536]{1,0:T(8,128)(2,1)}, bf16[192,1536]{1,0:T(8,128)(2,1)}, u32[]{:S(2)}, u32[]{:S(2)}) collective-permute-start(bf16[192,1536]{1,0:T(8,128)(2,1)} %refs_0_.1), channel_id=1, source_target_pairs={{0,8},{4,12},{8,0},{12,4},{16,24},{20,28},{24,16},{28,20},{1,9},{5... | collective-permute-start | bytes 1769480 | tf_op jit(solution)/shard_map/ppermute | solution.py:562
  93.1 32.6 %collective-permute-start.4 = (bf16[192,1536]{1,0:T(8,128)(2,1)}, bf16[192,1536]{1,0:T(8,128)(2,1)}, u32[]{:S(2)}, u32[]{:S(2)}) collective-permute-start(bf16[192,1536]{1,0:T(8,128)(2,1)} %refs_0_.1), channel_id=1, source_target_pairs={{0,16},{4,20},{8,24},{12,28},{16,0},{20,4},{24,8},{28,12},{1,17},{... | collective-permute-start | bytes 1769480 | tf_op jit(solution)/shard_map/ppermute | solution.py:562
  93.6 32.1 %collective-permute-start.5 = (bf16[192,1536]{1,0:T(8,128)(2,1)}, bf16[192,1536]{1,0:T(8,128)(2,1)}, u32[]{:S(2)}, u32[]{:S(2)}) collective-permute-start(bf16[192,1536]{1,0:T(8,128)(2,1)} %refs_0_.1), channel_id=1, source_target_pairs={{0,24},{4,28},{8,16},{12,20},{16,8},{20,12},{24,0},{28,4},{1,25},{... | collective-permute-start | bytes 1769480 | tf_op jit(solution)/shard_map/ppermute | solution.py:562
  125.7 41.8 %collective-permute-start.15 = (bf16[1120,1536]{1,0:T(8,128)(2,1)}, bf16[1120,1536]{1,0:T(8,128)(2,1)}, u32[]{:S(2)}, u32[]{:S(2)}) collective-permute-start(bf16[1120,1536]{1,0:T(8,128)(2,1)} %refs_0_.2), channel_id=1, source_target_pairs={{0,4},{4,0},{8,12},{12,8},{16,20},{20,16},{24,28},{28,24},{1,5},{5... | collective-permute-start | bytes 10321928 | tf_op jit(solution)/shard_map/ppermute | solution.py:562
  126.7 7.1 %collective-permute-start.6 = (bf16[192,1536]{1,0:T(8,128)(2,1)S(1)}, bf16[192,1536]{1,0:T(8,128)(2,1)S(1)}, u32[]{:S(2)}, u32[]{:S(2)}) collective-permute-start(bf16[192,1536]{1,0:T(8,128)(2,1)S(1)} %copy-done.61), channel_id=1, source_target_pairs={{0,4},{4,0},{8,12},{12,8},{16,20},{20,16},{24,28},{28,24},{1,5},{5... | collective-permute-start | bytes 1769480 | tf_op jit(solution)/shard_map/ppermute | solution.py:562
  127.2 6.8 collective-permute-start.7
  127.3 7.5 %collective-permute-start.8 = (bf16[192,1536]{1,0:T(8,128)(2,1)}, bf16[192,1536]{1,0:T(8,128)(2,1)S(1)}, u32[]{:S(2)}, u32[]{:S(2)}) collective-permute-start(bf16[192,1536]{1,0:T(8,128)(2,1)} %collective-permute-done.1.refs_4_), channel_id=1, source_target_pairs={{0,4},{4,0},{8,12},{12,8},{16,20},{20,16},{24,28},{28,24},{1,5},{5... | collective-permute-start | bytes 1769480 | tf_op jit(solution)/shard_map/ppermute | solution.py:562
  127.7 8.0 %collective-permute-start.9 = (bf16[192,1536]{1,0:T(8,128)(2,1)}, bf16[192,1536]{1,0:T(8,128)(2,1)S(1)}, u32[]{:S(2)}, u32[]{:S(2)}) collective-permute-start(bf16[192,1536]{1,0:T(8,128)(2,1)} %collective-permute-done.2.refs_6_), channel_id=1, source_target_pairs={{0,4},{4,0},{8,12},{12,8},{16,20},{20,16},{24,28},{28,24},{1,5},{5... | collective-permute-start | bytes 1769480 | tf_op jit(solution)/shard_map/ppermute | solution.py:562
  133.8 16.8 %collective-permute-start.11 = (bf16[192,1536]{1,0:T(8,128)(2,1)}, bf16[192,1536]{1,0:T(8,128)(2,1)}, u32[]{:S(2)}, u32[]{:S(2)}) collective-permute-start(bf16[192,1536]{1,0:T(8,128)(2,1)} %refs_0_.1), channel_id=1, source_target_pairs={{0,4},{4,0},{8,12},{12,8},{16,20},{20,16},{24,28},{28,24},{1,5},{5... | collective-permute-start | bytes 1769480 | tf_op jit(solution)/shard_map/ppermute | solution.py:562
  135.7 41.8 %collective-permute-start.10 = (bf16[2,192,2304]{2,1,0:T(8,128)(2,1)}, bf16[2,192,2304]{2,1,0:T(8,128)(2,1)}, u32[]{:S(2)}, u32[]{:S(2)}) collective-permute-start(bf16[2,192,2304]{2,1,0:T(8,128)(2,1)} %get-tuple-element.119), channel_id=1, source_target_pairs={{0,16},{4,20},{8,24},{12,28},{16,0},{20,4},{24,8},{28,12},{1,17},{... | collective-permute-start | bytes 5308424 | tf_op jit(solution)/shard_map/ppermute | solution.py:562
  140.8 12.8 %collective-permute-start.12 = (bf16[192,1536]{1,0:T(8,128)(2,1)}, bf16[192,1536]{1,0:T(8,128)(2,1)}, u32[]{:S(2)}, u32[]{:S(2)}) collective-permute-start(bf16[192,1536]{1,0:T(8,128)(2,1)} %collective-permute-done.3.refs_2_), channel_id=1, source_target_pairs={{0,4},{4,0},{8,12},{12,8},{16,20},{20,16},{24,28},{28,24},{1,5},{5... | collective-permute-start | bytes 1769480 | tf_op jit(solution)/shard_map/ppermute | solution.py:562
  150.1 9.3 %collective-permute-start.13 = (bf16[192,1536]{1,0:T(8,128)(2,1)}, bf16[192,1536]{1,0:T(8,128)(2,1)}, u32[]{:S(2)}, u32[]{:S(2)}) collective-permute-start(bf16[192,1536]{1,0:T(8,128)(2,1)} %collective-permute-done.4.refs_4_), channel_id=1, source_target_pairs={{0,4},{4,0},{8,12},{12,8},{16,20},{20,16},{24,28},{28,24},{1,5},{5... | collective-permute-start | bytes 1769480 | tf_op jit(solution)/shard_map/ppermute | solution.py:562
  150.5 66.0 %collective-permute-start.20 = (bf16[2,192,2304]{2,1,0:T(8,128)(2,1)}, bf16[2,192,2304]{2,1,0:T(8,128)(2,1)}, u32[]{:S(2)}, u32[]{:S(2)}) collective-permute-start(bf16[2,192,2304]{2,1,0:T(8,128)(2,1)} %get-tuple-element.141), channel_id=1, source_target_pairs={{0,24},{4,28},{8,16},{12,20},{16,8},{20,12},{24,0},{28,4},{1,25},{... | collective-permute-start | bytes 5308424 | tf_op jit(solution)/shard_map/ppermute | solution.py:562
  153.6 78.6 %collective-permute-start.17 = (bf16[2,192,2304]{2,1,0:T(8,128)(2,1)}, bf16[2,192,2304]{2,1,0:T(8,128)(2,1)}, u32[]{:S(2)}, u32[]{:S(2)}) collective-permute-start(bf16[2,192,2304]{2,1,0:T(8,128)(2,1)} %get-tuple-element.137), channel_id=1, source_target_pairs={{0,8},{4,12},{8,0},{12,4},{16,24},{20,28},{24,16},{28,20},{1,9},{5... | collective-permute-start | bytes 5308424 | tf_op jit(solution)/shard_map/ppermute | solution.py:562
  159.4 4.0 collective-permute-start.14
  172.6 59.6 %copy-start.36 = (bf16[64,1536]{1,0:T(8,128)(2,1)S(1)}, bf16[64,1536]{1,0:T(8,128)(2,1)}, u32[]{:S(2)}) copy-start(bf16[64,1536]{1,0:T(8,128)(2,1)} %convolution_convert_fusion.16) | copy-start | bytes 589828
  177.4 61.8 %collective-permute-start.19 = (bf16[2,192,2304]{2,1,0:T(8,128)(2,1)}, bf16[2,192,2304]{2,1,0:T(8,128)(2,1)}, u32[]{:S(2)}, u32[]{:S(2)}) collective-permute-start(bf16[2,192,2304]{2,1,0:T(8,128)(2,1)} %collective-permute-done.10.refs_4_), channel_id=1, source_target_pairs={{0,4},{4,0},{8,12},{12,8},{16,20},{20,16},{24,28},{28,24},{1,5},{5... | collective-permute-start | bytes 5308424 | tf_op jit(solution)/shard_map/ppermute | solution.py:562
  177.4 61.8 %collective-permute-start.16 = (bf16[2,192,2304]{2,1,0:T(8,128)(2,1)}, bf16[2,192,2304]{2,1,0:T(8,128)(2,1)}, u32[]{:S(2)}, u32[]{:S(2)}) collective-permute-start(bf16[2,192,2304]{2,1,0:T(8,128)(2,1)} %get-tuple-element.135.refs_0_), channel_id=1, source_target_pairs={{0,4},{4,0},{8,12},{12,8},{16,20},{20,16},{24,28},{28,24},{1,5},{5... | collective-permute-start | bytes 5308424 | tf_op jit(solution)/shard_map/ppermute | solution.py:562
  199.1 33.6 %copy-start.9 = (bf16[3,128,1536]{2,1,0:T(8,128)(2,1)S(1)}, bf16[3,128,1536]{2,1,0:T(8,128)(2,1)}, u32[]{:S(2)}) copy-start(bf16[3,128,1536]{2,1,0:T(8,128)(2,1)} %param.31) | copy-start | bytes 3538948
  199.1 33.6 %copy-start.46 = (bf16[384,1536]{1,0:T(8,128)(2,1)S(1)}, bf16[384,1536]{1,0:T(8,128)(2,1)}, u32[]{:S(2)}) copy-start(bf16[384,1536]{1,0:T(8,128)(2,1)} %get-tuple-element.133.o_ref) | copy-start | bytes 3538948
  216.6 22.6 %collective-permute-start.21 = (bf16[2,192,2304]{2,1,0:T(8,128)(2,1)}, bf16[2,192,2304]{2,1,0:T(8,128)(2,1)}, u32[]{:S(2)}, u32[]{:S(2)}) collective-permute-start(bf16[2,192,2304]{2,1,0:T(8,128)(2,1)} %collective-permute-done.20.refs_6_), channel_id=1, source_target_pairs={{0,4},{4,0},{8,12},{12,8},{16,20},{20,16},{24,28},{28,24},{1,5},{5... | collective-permute-start | bytes 5308424 | tf_op jit(solution)/shard_map/ppermute | solution.py:562
  232.2 7.0 %collective-permute-start.18 = (bf16[2,192,2304]{2,1,0:T(8,128)(2,1)}, bf16[2,192,2304]{2,1,0:T(8,128)(2,1)}, u32[]{:S(2)}, u32[]{:S(2)}) collective-permute-start(bf16[2,192,2304]{2,1,0:T(8,128)(2,1)} %collective-permute-done.17.refs_2_), channel_id=1, source_target_pairs={{0,4},{4,0},{8,12},{12,8},{16,20},{20,16},{24,28},{28,24},{1,5},{5... | collective-permute-start | bytes 5308424 | tf_op jit(solution)/shard_map/ppermute | solution.py:562
  239.2 37.5 %collective-permute-start.22 = (bf16[384,1536]{1,0:T(8,128)(2,1)}, bf16[384,1536]{1,0:T(8,128)(2,1)}, u32[]{:S(2)}, u32[]{:S(2)}) collective-permute-start(bf16[384,1536]{1,0:T(8,128)(2,1)} %multiply_convert_fusion.refs_8_), channel_id=1, source_target_pairs={{0,8},{4,12},{8,0},{12,4},{16,24},{20,28},{24,16},{28,20},{1,9},{5... | collective-permute-start | bytes 3538952 | tf_op jit(solution)/shard_map/ppermute | solution.py:562
  239.6 39.5 %collective-permute-start.23 = (bf16[384,1536]{1,0:T(8,128)(2,1)}, bf16[384,1536]{1,0:T(8,128)(2,1)}, u32[]{:S(2)}, u32[]{:S(2)}) collective-permute-start(bf16[384,1536]{1,0:T(8,128)(2,1)} %multiply_convert_fusion.refs_8_), channel_id=1, source_target_pairs={{0,16},{4,20},{8,24},{12,28},{16,0},{20,4},{24,8},{28,12},{1,17},{... | collective-permute-start | bytes 3538952 | tf_op jit(solution)/shard_map/ppermute | solution.py:562
  240.4 52.8 %collective-permute-start.24 = (bf16[384,1536]{1,0:T(8,128)(2,1)}, bf16[384,1536]{1,0:T(8,128)(2,1)}, u32[]{:S(2)}, u32[]{:S(2)}) collective-permute-start(bf16[384,1536]{1,0:T(8,128)(2,1)} %bitcast.25.refs_9_), channel_id=1, source_target_pairs={{0,8},{4,12},{8,0},{12,4},{16,24},{20,28},{24,16},{28,20},{1,9},{5... | collective-permute-start | bytes 3538952 | tf_op jit(solution)/shard_map/ppermute | solution.py:562
  242.2 80.6 %collective-permute-start.25 = (bf16[384,1536]{1,0:T(8,128)(2,1)}, bf16[384,1536]{1,0:T(8,128)(2,1)}, u32[]{:S(2)}, u32[]{:S(2)}) collective-permute-start(bf16[384,1536]{1,0:T(8,128)(2,1)} %bitcast.25.refs_9_), channel_id=1, source_target_pairs={{0,16},{4,20},{8,24},{12,28},{16,0},{20,4},{24,8},{28,12},{1,17},{... | collective-permute-start | bytes 3538952 | tf_op jit(solution)/shard_map/ppermute | solution.py:562
  243.3 109.6 %collective-permute-start.28 = (bf16[384,1536]{1,0:T(8,128)(2,1)}, bf16[384,1536]{1,0:T(8,128)(2,1)}, u32[]{:S(2)}, u32[]{:S(2)}) collective-permute-start(bf16[384,1536]{1,0:T(8,128)(2,1)} %bitcast.25.refs_9_), channel_id=1, source_target_pairs={{0,24},{4,28},{8,16},{12,20},{16,8},{20,12},{24,0},{28,4},{1,25},{... | collective-permute-start | bytes 3538952 | tf_op jit(solution)/shard_map/ppermute | solution.py:562
  276.7 76.2 %collective-permute-start.27 = (bf16[384,1536]{1,0:T(8,128)(2,1)}, bf16[384,1536]{1,0:T(8,128)(2,1)}, u32[]{:S(2)}, u32[]{:S(2)}) collective-permute-start(bf16[384,1536]{1,0:T(8,128)(2,1)} %multiply_convert_fusion.refs_8_), channel_id=1, source_target_pairs={{0,24},{4,28},{8,16},{12,20},{16,8},{20,12},{24,0},{28,4},{1,25},{... | collective-permute-start | bytes 3538952 | tf_op jit(solution)/shard_map/ppermute | solution.py:562
  322.4 62.6 %collective-permute-start.29 = (bf16[384,1664]{1,0:T(8,128)(2,1)}, bf16[384,1664]{1,0:T(8,128)(2,1)}, u32[]{:S(2)}, u32[]{:S(2)}) collective-permute-start(bf16[384,1664]{1,0:T(8,128)(2,1)} %get-tuple-element.158), channel_id=1, source_target_pairs={{0,8},{4,12},{8,0},{12,4},{16,24},{20,28},{24,16},{28,20},{1,9},{5... | collective-permute-start | bytes 3833864 | tf_op jit(solution)/shard_map/ppermute | solution.py:562
  352.0 35.3 %collective-permute-start.30 = (bf16[384,1664]{1,0:T(8,128)(2,1)}, bf16[384,1664]{1,0:T(8,128)(2,1)}, u32[]{:S(2)}, u32[]{:S(2)}) collective-permute-start(bf16[384,1664]{1,0:T(8,128)(2,1)} %get-tuple-element.159), channel_id=1, source_target_pairs={{0,16},{4,20},{8,24},{12,28},{16,0},{20,4},{24,8},{28,12},{1,17},{... | collective-permute-start | bytes 3833864 | tf_op jit(solution)/shard_map/ppermute | solution.py:562
  382.6 30.4 %collective-permute-start.31 = (bf16[384,1664]{1,0:T(8,128)(2,1)}, bf16[384,1664]{1,0:T(8,128)(2,1)S(1)}, u32[]{:S(2)}, u32[]{:S(2)}) collective-permute-start(bf16[384,1664]{1,0:T(8,128)(2,1)} %get-tuple-element.160), channel_id=1, source_target_pairs={{0,24},{4,28},{8,16},{12,20},{16,8},{20,12},{24,0},{28,4},{1,25},{... | collective-permute-start | bytes 3833864 | tf_op jit(solution)/shard_map/ppermute | solution.py:562
  431.0 3.5 collective-permute-start.35
  431.0 44.1 %collective-permute-start.32 = (bf16[384,1664]{1,0:T(8,128)(2,1)}, bf16[384,1664]{1,0:T(8,128)(2,1)}, u32[]{:S(2)}, u32[]{:S(2)}) collective-permute-start(bf16[384,1664]{1,0:T(8,128)(2,1)} %get-tuple-element.162), channel_id=1, source_target_pairs={{0,8},{4,12},{8,0},{12,4},{16,24},{20,28},{24,16},{28,20},{1,9},{5... | collective-permute-start | bytes 3833864 | tf_op jit(solution)/shard_map/ppermute | solution.py:562
  432.7 42.4 %collective-permute-start.33 = (bf16[384,1664]{1,0:T(8,128)(2,1)}, bf16[384,1664]{1,0:T(8,128)(2,1)}, u32[]{:S(2)}, u32[]{:S(2)}) collective-permute-start(bf16[384,1664]{1,0:T(8,128)(2,1)} %get-tuple-element.163), channel_id=1, source_target_pairs={{0,16},{4,20},{8,24},{12,28},{16,0},{20,4},{24,8},{28,12},{1,17},{... | collective-permute-start | bytes 3833864 | tf_op jit(solution)/shard_map/ppermute | solution.py:562
  433.9 56.5 %collective-permute-start.34 = (bf16[384,1664]{1,0:T(8,128)(2,1)}, bf16[384,1664]{1,0:T(8,128)(2,1)}, u32[]{:S(2)}, u32[]{:S(2)}) collective-permute-start(bf16[384,1664]{1,0:T(8,128)(2,1)} %get-tuple-element.164), channel_id=1, source_target_pairs={{0,24},{4,28},{8,16},{12,20},{16,8},{20,12},{24,0},{28,4},{1,25},{... | collective-permute-start | bytes 3833864 | tf_op jit(solution)/shard_map/ppermute | solution.py:562
  441.6 144.2 %reduce-scatter.5.cloned.1.call-start = ((), (), s32[]{:S(2)}) async-start(), calls=%async_computation.5 | async-start | bytes 6684672 | tf_op jit(solution)/shard_map/reduce_scatter | solution.py:769
  490.4 181.9 %all-gather.9.cloned.1.call-start = ((), (), s32[]{:S(2)}) async-start(), calls=%async_computation.6 | async-start | bytes 8110080 | tf_op jit(solution)/shard_map/all_gather | solution.py:824
  520.6 2.3 collective-permute-start.36
  525.2 63.3 %copy-start.2 = (s32[8]{0:T(128)S(1)}, s32[8]{0:T(128)}, u32[]{:S(2)}) copy-start(s32[8]{0:T(128)} %constant.283.clone) | copy-start | bytes 100
  525.9 69.4 %copy-start.85 = (s32[64]{0:T(128)S(1)}, s32[64]{0:T(128)}, u32[]{:S(2)}) copy-start(s32[64]{0:T(128)} %copy-done.84) | copy-start | bytes 772
  525.9 16.2 %collective-permute-start.37 = (bf16[1,4,48,768]{3,2,1,0:T(8,128)(2,1)}, bf16[1,4,48,768]{3,2,1,0:T(8,128)(2,1)}, u32[]{:S(2)}, u32[]{:S(2)}) collective-permute-start(bf16[1,4,48,768]{3,2,1,0:T(8,128)(2,1)} %constant_dynamic-slice_fusion.2), channel_id=1, source_target_pairs={{0,8},{4,12},{8,0},{12,4},{16,24},{20,28},{24,16},{28,20},{1,9},{5... | collective-permute-start | bytes 884744 | tf_op jit(solution)/shard_map/ppermute | solution.py:562
  544.6 11.5 %collective-permute-start.38 = (bf16[2,48,768]{2,1,0:T(8,128)(2,1)}, bf16[2,48,768]{2,1,0:T(8,128)(2,1)}, u32[]{:S(2)}, u32[]{:S(2)}) collective-permute-start(bf16[2,48,768]{2,1,0:T(8,128)(2,1)} %dynamic-slice_bitcast_fusion.2), channel_id=1, source_target_pairs={{0,1},{1,0},{2,3},{3,2},{4,5},{5,4},{6,7},{7,6},{8,9},{9,8},{10,11... | collective-permute-start | bytes 442376 | tf_op jit(solution)/shard_map/ppermute | solution.py:802
  558.5 6.2 collective-permute-start.39
  615.7 1.7 collective-permute-start.40
  617.5 4.6 collective-permute-start.41
  622.0 8.1 %collective-permute-start.42 = (bf16[48,896]{1,0:T(8,128)(2,1)S(1)}, bf16[48,896]{1,0:T(8,128)(2,1)S(1)}, u32[]{:S(2)}, u32[]{:S(2)}) collective-permute-start(bf16[48,896]{1,0:T(8,128)(2,1)S(1)} %fusion.87), channel_id=1, source_target_pairs={{0,1},{1,0},{2,3},{3,2},{4,5},{5,4},{6,7},{7,6},{8,9},{9,8},{10,11... | collective-permute-start | bytes 258056 | tf_op jit(solution)/shard_map/ppermute | solution.py:802
  623.7 13.0 %collective-permute-start.43 = (bf16[48,896]{1,0:T(8,128)(2,1)S(1)}, bf16[48,896]{1,0:T(8,128)(2,1)S(1)}, u32[]{:S(2)}, u32[]{:S(2)}) collective-permute-start(bf16[48,896]{1,0:T(8,128)(2,1)S(1)} %fusion.87), channel_id=1, source_target_pairs={{0,2},{1,3},{2,0},{3,1},{4,6},{5,7},{6,4},{7,5},{8,10},{9,11},{10,... | collective-permute-start | bytes 258056 | tf_op jit(solution)/shard_map/ppermute | solution.py:802
  626.0 10.7 %collective-permute-start.44 = (bf16[48,896]{1,0:T(8,128)(2,1)S(1)}, bf16[48,896]{1,0:T(8,128)(2,1)S(1)}, u32[]{:S(2)}, u32[]{:S(2)}) collective-permute-start(bf16[48,896]{1,0:T(8,128)(2,1)S(1)} %fusion.87), channel_id=1, source_target_pairs={{0,3},{1,2},{2,1},{3,0},{4,7},{5,6},{6,5},{7,4},{8,11},{9,10},{10,... | collective-permute-start | bytes 258056 | tf_op jit(solution)/shard_map/ppermute | solution.py:802
  636.8 4.6 collective-permute-start.45
  641.3 9.3 %collective-permute-start.46 = (bf16[2,48,896]{2,1,0:T(8,128)(2,1)S(1)}, bf16[2,48,896]{2,1,0:T(8,128)(2,1)S(1)}, u32[]{:S(2)}, u32[]{:S(2)}) collective-permute-start(bf16[2,48,896]{2,1,0:T(8,128)(2,1)S(1)} %pad_maximum_fusion.11), channel_id=1, source_target_pairs={{0,16},{4,20},{8,24},{12,28},{16,0},{20,4},{24,8},{28,12},{1,17},{... | collective-permute-start | bytes 516104 | tf_op jit(solution)/shard_map/ppermute | solution.py:562
  650.7 2.1 collective-permute-start.47
  (124 other events, 703.1 us)
Sparse Core Ops, SparseCore 0:
  13.6 32.9 all-gather.4
  68.8 80.3 all-gather.6
  441.7 23.7 reduce-scatter.2
  490.6 95.2 reduce-scatter.4
  589.2 83.1 all-gather.8

commit v2 on v1

--- a/solution.py
+++ b/solution.py
@@ -164,7 +164,8 @@
 
 
 def attend_back_kernel(
-    spans, span_len, tokens, kv_heads, info, q_ref, do_ref, o_ref, k_ref, v_ref, lse_ref, dq_ref, dkv_ref, acc_ref
+    spans, span_len, tokens, kv_heads,
+    info, q_ref, do_ref, o_ref, k_ref, v_ref, lse_ref, dq_ref, dkv_ref, acc_ref,
 ):
     seq = pl.program_id(0)
     head = pl.program_id(1)
@@ -184,6 +185,11 @@
     key_lane = pl.multiple_of(head * HEAD_DIM, HEAD_DIM)
     val_lane = pl.multiple_of((kv_heads + head) * HEAD_DIM, HEAD_DIM)
 
+    def store(j, key_grad, value_grad):
+        rows = pl.ds(pl.multiple_of(j * span_len, span_len), span_len)
+        dkv_ref[0, rows, pl.ds(key_lane, HEAD_DIM)] = key_grad
+        dkv_ref[0, rows, pl.ds(val_lane, HEAD_DIM)] = value_grad
+
     def update(j, masked):
         rows = pl.ds(pl.multiple_of(j * span_len, span_len), span_len)
         keys = k_ref[0, rows, :]
@@ -194,9 +200,10 @@
             prob = jnp.where(key_at <= query_at, prob, 0.0)
         prob_grad = mm_nt(v_ref[0, rows, :], grads)
         score_grad = (prob * (prob_grad - inner)).astype(BF)
-        dkv_ref[0, rows, pl.ds(key_lane, HEAD_DIM)] = (mm(score_grad, queries) * root).astype(BF)
-        dkv_ref[0, rows, pl.ds(val_lane, HEAD_DIM)] = mm(prob.astype(BF), grads).astype(BF)
         acc_ref[...] += mm_tn(score_grad, keys)
+        store(
+            j, (mm(score_grad, queries) * root).astype(BF), mm(prob.astype(BF), grads).astype(BF)
+        )
 
     def step(j, carry):
         other = info[seq * spans + j]
@@ -211,10 +218,8 @@
 
         @pl.when(other > own)
         def _():
-            rows = pl.ds(pl.multiple_of(j * span_len, span_len), span_len)
             zero = jnp.zeros((span_len, HEAD_DIM), BF)
-            dkv_ref[0, rows, pl.ds(key_lane, HEAD_DIM)] = zero
-            dkv_ref[0, rows, pl.ds(val_lane, HEAD_DIM)] = zero
+            store(j, zero, zero)
 
         return carry
 
@@ -228,21 +233,20 @@
     kv_heads = pairs.shape[2] // (2 * HEAD_DIM)
     width = queries.shape[1] // kv_heads
     rows = tokens * (width // HEAD_DIM)
+    row = pl.BlockSpec((tokens, width), lambda s, h, i: (s, h))
+    block = (1, length, pairs.shape[2])
     grid_spec = pltpu.PrefetchScalarGridSpec(
         num_scalar_prefetch=1,
         grid=(seqs, kv_heads),
         in_specs=[
-            pl.BlockSpec((tokens, width), lambda s, h, i: (s, h)),
-            pl.BlockSpec((tokens, width), lambda s, h, i: (s, h)),
-            pl.BlockSpec((tokens, width), lambda s, h, i: (s, h)),
+            row,
+            row,
+            row,
             pl.BlockSpec((1, length, HEAD_DIM), lambda s, h, i: (s, 0, h)),
             pl.BlockSpec((1, length, HEAD_DIM), lambda s, h, i: (s, 0, kv_heads + h)),
             pl.BlockSpec((1, 8, rows), lambda s, h, i: (s * kv_heads + h, 0, 0)),
         ],
-        out_specs=[
-            pl.BlockSpec((tokens, width), lambda s, h, i: (s, h)),
-            pl.BlockSpec((1, length, pairs.shape[2]), lambda s, h, i: (s, 0, 0)),
-        ],
+        out_specs=[row, pl.BlockSpec(block, lambda s, h, i: (s, 0, 0))],
         scratch_shapes=[pltpu.VMEM((rows, HEAD_DIM), F32)],
     )
     work = seqs * kv_heads * rows * length
@@ -260,13 +264,246 @@
     )(info, queries, grads, results, pairs, pairs, lse)
 
 
+def turned(values, cosine, sine_signed):
+    return values * cosine + pltpu.roll(values, HEAD_DIM // 2, axis=1) * sine_signed
+
+
+def fetch_rows(index, blocks, out_ref, sems):
+    depth = blocks[0].shape[0]
+    return [
+        pltpu.make_async_copy(
+            block,
+            out_ref.at[pl.ds(pl.multiple_of((index ^ j) * depth, depth), depth), :],
+            sems.at[j],
+        )
+        for j, block in enumerate(blocks)
+    ]
+
+
+def keys_kernel(
+    seqs, x_ref, gain_ref, w_ref, shrink_ref, ek_ref, ev_ref, bias_ref, cos_ref, sin_ref,
+    normed_ref, nk_ref, nv_ref, pair_ref,
+):
+    tokens, width = pair_ref.shape
+    kv = width // 2
+    lanes = ek_ref.shape[0]
+    normed = norm_forward(x_ref[...].astype(F32), gain_ref[...]).astype(BF)
+    normed_ref[...] = normed
+    mix = token_mask(tokens, lanes, seqs)
+    narrow = mm(normed, shrink_ref[...])
+    narrow_k = (narrow[:, :lanes] * mix).astype(BF)
+    narrow_v = (narrow[:, lanes:] * mix).astype(BF)
+    nk_ref[...] = narrow_k
+    nv_ref[...] = narrow_v
+    raw = mm(normed, w_ref[...]) + bias_ref[...]
+    keys = raw[:, :kv] + mm(narrow_k, ek_ref[...])
+    vals = raw[:, kv:] + mm(narrow_v, ev_ref[...])
+    cosine = cos_ref[...]
+    sine = sin_ref[...]
+    for h in range(kv // HEAD_DIM):
+        at = slice(h * HEAD_DIM, (h + 1) * HEAD_DIM)
+        pair_ref[:, at] = turned(keys[:, at], cosine, sine).astype(BF)
+    pair_ref[:, kv:] = vals.astype(BF)
+
+
+def keys_values(x, gain, w_kv, shrink, expand_k, expand_v, bias, cosine, sine, seqs):
+    tokens, model = x.shape
+    lanes = expand_k.shape[0]
+    low = lambda n: jax.ShapeDtypeStruct((tokens, n), BF)
+    return pl.pallas_call(
+        functools.partial(keys_kernel, seqs),
+        out_shape=[low(model), low(lanes), low(lanes), low(w_kv.shape[1])],
+        name="keys_values",
+        cost_estimate=pl.CostEstimate(
+            flops=2 * tokens * model * w_kv.shape[1],
+            bytes_accessed=8 * tokens * model,
+            transcendentals=tokens,
+        ),
+    )(x, gain, w_kv, shrink, expand_k, expand_v, bias, cosine, sine)
+
+
+def queries_kernel(
+    seqs, count, info, normed_ref, shrink_ref, eq_ref, bias_ref, cos_ref, sin_ref, *refs
+):
+    blocks = refs[:count]
+    query_ref, narrow_ref, w_ref, sems = refs[count:]
+    copies = fetch_rows(info[0], blocks, w_ref, sems)
+    for copy in copies:
+        copy.start()
+    tokens, model = query_ref.shape
+    lanes = eq_ref.shape[0]
+    normed = normed_ref[...]
+    narrow = (mm(normed, shrink_ref[...]) * token_mask(tokens, lanes, seqs)).astype(BF)
+    narrow_ref[...] = narrow
+    for copy in copies:
+        copy.wait()
+    cosine = cos_ref[...]
+    sine = sin_ref[...]
+    step = 2 * HEAD_DIM
+    for c in range(0, model, step):
+        raw = mm(normed, w_ref[:, c : c + step]) + bias_ref[:, c : c + step]
+        raw = raw + mm(narrow, eq_ref[:, c : c + step])
+        for h in range(0, step, HEAD_DIM):
+            query_ref[:, c + h : c + h + HEAD_DIM] = turned(
+                raw[:, h : h + HEAD_DIM], cosine, sine
+            ).astype(BF)
+
+
+def outputs_kernel(seqs, count, info, attended_ref, x_ref, gain_ref, shrink_ref, eo_ref, *refs):
+    blocks = refs[:count]
+    middle_ref, normed_ref, narrow_ref, w_ref, sems = refs[count:]
+    copies = fetch_rows(info[0], blocks, w_ref, sems)
+    for copy in copies:
+        copy.start()
+    tokens, model = middle_ref.shape
+    lanes = eo_ref.shape[0]
+    attended = attended_ref[...]
+    narrow = (mm(attended, shrink_ref[...]) * token_mask(tokens, lanes, seqs)).astype(BF)
+    narrow_ref[...] = narrow
+    for copy in copies:
+        copy.wait()
+    middle = x_ref[...].astype(F32) + (mm(attended, w_ref[...]) + mm(narrow, eo_ref[...]))
+    middle_ref[...] = middle
+    normed_ref[...] = norm_forward(middle, gain_ref[...]).astype(BF)
+
+
+def before_attention_kernel(
+    seqs, most_ref, last_ref, grad_ref, middle_ref, gain_ref, gs_ref, us_ref, os_ref, oe_ref, w_ref,
+    mg_ref, low_ref, gb_ref, ub_ref, ob_ref, ag_ref,
+):
+    tokens, model = mg_ref.shape
+    lanes = oe_ref.shape[0]
+    mix = token_mask(tokens, lanes, seqs)
+    total = most_ref[...] + last_ref[...].astype(F32)
+    gate_back = (total[:, model : model + lanes] * mix).astype(BF)
+    up_back = (total[:, model + lanes :] * mix).astype(BF)
+    gb_ref[...] = gate_back
+    ub_ref[...] = up_back
+    normed_grad = total[:, :model] + mm_nt(gate_back, gs_ref[...]) + mm_nt(up_back, us_ref[...])
+    middle_grad = grad_ref[...].astype(F32) + norm_backward(
+        middle_ref[...], gain_ref[...], normed_grad
+    )
+    mg_ref[...] = middle_grad
+    low = middle_grad.astype(BF)
+    low_ref[...] = low
+    output_back = (mm_nt(low, oe_ref[...]) * mix).astype(BF)
+    ob_ref[...] = output_back
+    ag_ref[...] = (mm_nt(low, w_ref[...]) + mm_nt(output_back, os_ref[...])).astype(BF)
+
+
+def before_attention(most, last, grad, middle, gain, gs, us, os, oe, w_output, seqs):
+    tokens, model = middle.shape
+    lanes = oe.shape[0]
+    low = lambda n: jax.ShapeDtypeStruct((tokens, n), BF)
+    return pl.pallas_call(
+        functools.partial(before_attention_kernel, seqs),
+        out_shape=[
+            jax.ShapeDtypeStruct((tokens, model), F32),
+            low(model), low(lanes), low(lanes), low(lanes), low(model),
+        ],
+        name="before_attention",
+        cost_estimate=pl.CostEstimate(
+            flops=2 * tokens * model * model, bytes_accessed=30 * tokens * model, transcendentals=0
+        ),
+    )(most, last, grad, middle, gain, gs, us, os, oe, w_output)
+
+
+def last_grads_kernel(
+    seqs, rank, info, pair_ref, cos_ref, sin_ref, ke_ref, ve_ref, normed_ref, nk_ref, nv_ref,
+    kg_ref, vg_ref, kb_ref, vb_ref, late_ref, rows_ref,
+):
+    tokens, width = pair_ref.shape
+    kv = width // 2
+    lanes = ke_ref.shape[0]
+    model = normed_ref.shape[1]
+    mix = token_mask(tokens, lanes, seqs)
+    cosine = cos_ref[...]
+    sine = -sin_ref[...]
+    for h in range(kv // HEAD_DIM):
+        at = slice(h * HEAD_DIM, (h + 1) * HEAD_DIM)
+        kg_ref[:, at] = turned(pair_ref[:, at].astype(F32), cosine, sine).astype(BF)
+    vg_ref[...] = pair_ref[:, kv:]
+    key_grad = kg_ref[...]
+    value_grad = vg_ref[...]
+    key_back = (mm_nt(key_grad, ke_ref[...]) * mix).astype(BF)
+    value_back = (mm_nt(value_grad, ve_ref[...]) * mix).astype(BF)
+    kb_ref[...] = key_back
+    vb_ref[...] = value_back
+    normed = normed_ref[...]
+    rows_ref[:, :model] = mm_tn(key_back, normed)[:rank].astype(BF)
+    rows_ref[:, model : 2 * model] = mm_tn(value_back, normed)[:rank].astype(BF)
+    rows_ref[:, 2 * model : 2 * model + kv] = mm_tn(nk_ref[...], key_grad)[:rank].astype(BF)
+    rows_ref[:, 2 * model + kv :] = mm_tn(nv_ref[...], value_grad)[:rank].astype(BF)
+    parts = 2 * late_ref.shape[1]
+    size = late_ref.shape[3]
+    for p in range(parts):
+        at = p ^ info[0]
+        late_ref[lax.rem(at, 2), at // 2] = rows_ref[:, p * size : (p + 1) * size]
+
+
+def last_grads(mine, pair_grad, cosine, sine, ke, ve, normed, nk, nv, seqs, rank, parts):
+    tokens, width = pair_grad.shape
+    lanes = ke.shape[0]
+    model = normed.shape[1]
+    low = lambda n: jax.ShapeDtypeStruct((tokens, n), BF)
+    total = 2 * model + width
+    operands = [pair_grad, cosine, sine, ke, ve, normed, nk, nv]
+    results = [
+        low(width // 2), low(width // 2), low(lanes), low(lanes),
+        jax.ShapeDtypeStruct((2, parts // 2, rank, total // parts), BF),
+    ]
+    return pl.pallas_call(
+        functools.partial(last_grads_kernel, seqs, rank),
+        grid_spec=pltpu.PrefetchScalarGridSpec(
+            num_scalar_prefetch=1,
+            grid=(1,),
+            in_specs=[pl.BlockSpec(a.shape, lambda g, i, n=a.ndim: (0,) * n) for a in operands],
+            out_specs=[
+                pl.BlockSpec(r.shape, lambda g, i, n=len(r.shape): (0,) * n) for r in results
+            ],
+            scratch_shapes=[pltpu.VMEM((rank, total), BF)],
+        ),
+        out_shape=results,
+        name="last_grads",
+        cost_estimate=pl.CostEstimate(
+            flops=4 * tokens * model * 128, bytes_accessed=6 * tokens * model, transcendentals=0
+        ),
+    )(mine.reshape(1).astype(jnp.int32), *operands)
+
+
+def with_blocks(kernel, name, seqs, index, blocks, operands, results):
+    count = len(blocks)
+    depth, lanes = blocks[0].shape
+    inside = pl.BlockSpec(memory_space=pltpu.VMEM)
+    results = list(results) + [jax.ShapeDtypeStruct((count * depth, lanes), BF)]
+    return pl.pallas_call(
+        functools.partial(kernel, seqs, count),
+        grid_spec=pltpu.PrefetchScalarGridSpec(
+            num_scalar_prefetch=1,
+            grid=(1,),
+            in_specs=[pl.BlockSpec(a.shape, lambda g, i, n=a.ndim: (0,) * n) for a in operands]
+            + [pl.BlockSpec(memory_space=pl.ANY)] * count,
+            out_specs=[pl.BlockSpec(r.shape, lambda g, i: (0, 0)) for r in results],
+            scratch_shapes=[pltpu.SemaphoreType.DMA((count,))],
+        ),
+        out_shape=results,
+        name=name,
+        cost_estimate=pl.CostEstimate(
+            flops=2 * operands[0].shape[0] * count * depth * lanes,
+            bytes_accessed=4 * count * depth * lanes,
+            transcendentals=0,
+        ),
+    )(index.reshape(1).astype(jnp.int32), *operands, *blocks)
+
+
 def token_mask(tokens, lanes, seqs):
     row = lax.broadcasted_iota(jnp.int32, (tokens, lanes), 0) // (tokens // seqs)
     lane = lax.broadcasted_iota(jnp.int32, (tokens, lanes), 1) // ADAPTER_RANK
     return jnp.where(row == lane, adapter_scale, 0.0).astype(F32)
 
 
-def feed_kernel(seqs, count, info, *refs):
+def feed_kernel(seqs, kinds, info, *refs):
+    count = len(kinds)
     blocks = refs[:count]
     n2_ref, g0_ref, sgu_ref, ed_ref, wd_ref, eg_ref, eu_ref, sd_ref = refs[count : count + 8]
     peg_ref, peu_ref, psd_ref = refs[count + 8 : count + 11]
@@ -274,18 +511,20 @@
     acc_out, acc_ng, acc_nd, acc_bg, acc_bu, nar_g, nar_u, back_d, held, sems = refs[count + 16 :]
     chunk = pl.program_id(0)
     chunks = pl.num_programs(0)
-    depth = blocks[0].shape[1]
+    depth = blocks[0].shape[-2]
     size = wd_ref.shape[0]
 
     def copies(at, slot):
-        return [
-            pltpu.make_async_copy(
-                blocks[j].at[:, :, pl.ds(pl.multiple_of(at * size, 128), size)],
-                held.at[slot, :, pl.ds(pl.multiple_of((info[0] ^ j) * depth, depth), depth), :],
-                sems.at[slot, j],
-            )
-            for j in range(count)
-        ]
+        found = []
+        for n, (j, which) in enumerate(kinds):
+            rows = pl.ds(pl.multiple_of((info[0] ^ j) * depth, depth), depth)
+            lanes = pl.ds(pl.multiple_of(at * size, 128), size)
+            if which is None:
+                source, target = blocks[n].at[:, :, lanes], held.at[slot, :, rows, :]
+            else:
+                source, target = blocks[n].at[:, lanes], held.at[slot, info[1] ^ which, rows, :]
+            found.append(pltpu.make_async_copy(source, target, sems.at[slot, n]))
+        return found
 
     slot = lax.rem(chunk, 2)
 
@@ -347,7 +586,7 @@
         ng_ref[:, model:] = jnp.concatenate([acc_bg[...], acc_bu[...]], axis=1).astype(BF)
 
 
-def feed(me, blocks, n2, g0, sgu, ed, wd, eg, eu, sd, previous, seqs, limit=768):
+def feed(index, kinds, blocks, n2, g0, sgu, ed, wd, eg, eu, sd, previous, seqs, limit=768):
     tokens, model = n2.shape
     count = len(blocks)
     hidden = wd.shape[0]
@@ -362,7 +601,7 @@
     fixed = lambda c: pl.BlockSpec((tokens, c), lambda h, i: (0, 0))
     grads = jax.ShapeDtypeStruct((cols, hidden), F32)
     return pl.pallas_call(
-        functools.partial(feed_kernel, seqs, count),
+        functools.partial(feed_kernel, seqs, tuple(kinds)),
         grid_spec=pltpu.PrefetchScalarGridSpec(
             num_scalar_prefetch=1,
             grid=(hidden // size,),
@@ -394,7 +633,7 @@
             bytes_accessed=6 * model * hidden,
             transcendentals=tokens * hidden,
         ),
-    )(me.reshape(1).astype(jnp.int32), *blocks, n2, g0, sgu, ed, wd, eg, eu, sd, *previous)
+    )(index, *blocks, n2, g0, sgu, ed, wd, eg, eu, sd, *previous)
 
 
 def assemble_kernel(count, info, *refs):
@@ -516,7 +755,7 @@
         name="expand",
         cost_estimate=pl.CostEstimate(
             flops=6 * cols * chips * hidden * select.shape[0],
-            bytes_accessed=12 * cols * chips * hidden + both.size * 2,
+            bytes_accessed=12 * cols * chips * hidden,
             transcendentals=0,
         ),
     )(both, select)
@@ -561,12 +800,23 @@
     def swap(value, k):
         return lax.ppermute(value, PLANE, [(i, i ^ k) for i in range(plane)])
 
+    def swap_seq(value, k):
+        return lax.ppermute(value, "seq", [(i, i ^ k) for i in range(seq_n)])
+
     first_row = (lax.axis_index("cp") * seq_n + lax.axis_index("seq")) * tok_rows
     own = lax.dynamic_slice_in_dim(span_order, first_row // span_len, 1, 1)[:, 0]
     shift = first_row % span_len
-    info = jnp.concatenate([span_order.reshape(-1), own, shift.reshape(1)]).astype(jnp.int32)
+    cp_index = lax.axis_index("cp")
+    seq_index = lax.axis_index("seq")
+    info = jnp.concatenate(
+        [span_order.reshape(-1), own, jnp.stack([shift, cp_index])]
+    ).astype(jnp.int32)
     places = own[:, None] * span_len + shift + jnp.arange(tok_rows, dtype=jnp.int32)[None, :]
     cosine, sine_table = rotary_tables(places.reshape(tokens))
+    sine_signed = jnp.where(
+        jnp.arange(HEAD_DIM, dtype=jnp.int32) < HEAD_DIM // 2, -sine_table, sine_table
+    )
+    flat_cosine = cosine
     cosine = cosine[:, None, :]
     sine_table = sine_table[:, None, :]
     lane = jnp.arange(lanes, dtype=jnp.int32)
@@ -607,18 +857,17 @@
     depth = gate_weight.shape[0]
     parts = [lax.dynamic_index_in_dim(gate_up, chip ^ k, 0, keepdims=False) for k in range(chips)]
 
-    resid_in = inputs.reshape(tokens, model).astype(F32)
+    low_in = inputs.reshape(tokens, model)
+    resid_in = low_in.astype(F32)
     first_scales = first_gain.astype(F32)
     second_scales = second_gain.astype(F32)
     grad_low = cotangent.reshape(tokens, model)
-    normed = norm_forward(resid_in, first_scales).astype(BF)
     w_kv, parts, rows_q = lax.optimization_barrier((w_kv, parts, rows_q))
     rows_o = [output_weight] + [swap(after(output_weight, rows_q), 2 * k) for k in range(1, chips)]
-    crosses_cp = lambda k: 2 * k % cp_n != 0
-    blocks = {
-        k: swap(after(parts[k], rows_o), 2 * k) for k in range(1, chips) if not crosses_cp(k)
+    blocks = {}
+    g0_pieces = {
+        k: swap(after(grad_low, rows_q), 2 * k) for k in range(1, chips) if 2 * k % cp_n == 0
     }
-    blocks[0] = parts[0]
     w_key = w_kv[:, :kv_width]
     w_value = w_kv[:, kv_width:]
 
@@ -640,14 +889,11 @@
     def narrowed(value, shrink):
         return (mm(value, shrink) * mixing).astype(BF)
 
-    key_narrow = narrowed(normed, key_shrink)
-    value_narrow = narrowed(normed, value_shrink)
-    key_pre = mm(normed, w_key) + key_bias.astype(F32) + mm(key_narrow, key_expand)
-    value_low = (
-        mm(normed, w_value) + value_bias.astype(F32) + mm(value_narrow, value_expand)
-    ).astype(BF)
-    key_rot = rotate(key_pre.reshape(tokens, -1, HEAD_DIM), cosine, sine_table).astype(BF)
-    pair = jnp.concatenate([key_rot.reshape(tokens, kv_width), value_low], axis=1)
+    normed, key_narrow, value_narrow, pair = keys_values(
+        low_in, first_scales[None], w_kv, jnp.concatenate([key_shrink, value_shrink], axis=1),
+        key_expand, value_expand,
+        jnp.concatenate([key_bias, value_bias]).astype(F32)[None], flat_cosine, sine_signed, seqs,
+    )
     pair_all = lax.all_gather(
         pair.reshape(seqs, tok_rows, 2 * kv_width), ("cp", "seq"), axis=1, tiled=True
     )
@@ -658,20 +904,28 @@
             found += [part, swap(part, 1)]
         return found
 
-    w_query = assemble(me, after(both_cores(rows_q), pair), model)
-    normed_later = after(normed, rows_o)
-    query_narrow = narrowed(normed_later, query_shrink)
-    query_pre = mm(normed_later, w_query) + query_bias.astype(F32) + mm(query_narrow, query_expand)
-    query_rot = (
-        rotate(query_pre.reshape(tokens, -1, HEAD_DIM), cosine, sine_table)
-        .astype(BF)
-        .reshape(tokens, model)
-    )
-
-    lift_g = lax.dynamic_index_in_dim(by_chip(gate_lift_factors), chip, 0, keepdims=False)
-    lift_u = lax.dynamic_index_in_dim(by_chip(upper_lift_factors), chip, 0, keepdims=False)
+    query_rot, query_narrow, w_query = with_blocks(
+        queries_kernel, "queries", seqs, me, after(both_cores(rows_q), pair),
+        [
+            after(normed, rows_o, g0_pieces), query_shrink, query_expand, query_bias.astype(F32)[None], flat_cosine,
+            sine_signed,
+        ],
+        [
+            jax.ShapeDtypeStruct((tokens, model), BF),
+            jax.ShapeDtypeStruct((tokens, lanes), BF),
+        ],
+    )
+
+    attended, lse = attend(info, query_rot, pair_all, seqs, spans, span_len)
+    for k in range(1, chips):
+        blocks[k] = swap(after(parts[k], pair_all, query_rot), 2 * k)
+    late_lift = after(
+        (gate_lift_factors, upper_lift_factors, down_reduce_factors), attended, blocks
+    )
+    lift_g = lax.dynamic_index_in_dim(by_chip(late_lift[0]), chip, 0, keepdims=False)
+    lift_u = lax.dynamic_index_in_dim(by_chip(late_lift[1]), chip, 0, keepdims=False)
     shrink_d = jnp.pad(
-        lax.dynamic_slice_in_dim(down_reduce_factors, chip * hq, hq, 0), ((0, pad), (0, 0))
+        lax.dynamic_slice_in_dim(late_lift[2], chip * hq, hq, 0), ((0, pad), (0, 0))
     )
     feed_factors = [
         (
@@ -686,97 +940,88 @@
         for f in range(fsdp_n)
     ]
 
-    down_rows = [down_weight, swap(after(down_weight, rows_o), 1)]
-    w_output = assemble(me, after(both_cores(rows_o), query_rot), model)
-    w_down = assemble(core, after(down_rows, query_rot), hp)
-    query_rot = after(query_rot, [blocks[k] for k in blocks if k], w_output, w_down)
+    output_blocks = both_cores(after(rows_o, query_rot))
+    down_rows = [down_weight, swap(after(down_weight, query_rot), 1)]
+    w_down = assemble(core, after(down_rows, attended), hp)
+    kinds = [(0, None), (1, None)]
+    wide = [parts[0], swap(after(parts[0], query_rot), 1)]
     for k in range(1, chips):
-        if crosses_cp(k):
-            blocks[k] = swap(after(parts[k], pair_all), 2 * k)
-    blocks = [after(blocks[k], query_rot) for k in range(chips)]
-    wide = []
-    for part in blocks:
-        wide += [part, swap(part, 1)]
-    attended, lse = attend(info, query_rot, pair_all, seqs, spans, span_len)
-
-    output_narrow = narrowed(attended, output_shrink)
-    middle = resid_in + (mm(attended, w_output) + mm(output_narrow, output_expand))
-    normed_two = norm_forward(middle, second_scales).astype(BF)
-
-    g0_pieces = [grad_low] + [swap(after(grad_low, wide), 2 * k) for k in range(1, chips)]
-    n2_pieces = [normed_two] + [swap(after(normed_two, wide), 2 * k) for k in range(1, chips)]
+        kinds += [(2 * k, None), (2 * k + 1, None)]
+        wide += [blocks[k], swap(blocks[k], 1)]
+    feed_index = jnp.stack([me, core]).astype(jnp.int32)
+
+    middle, normed_two, output_narrow, w_output = with_blocks(
+        outputs_kernel, "outputs", seqs, me, output_blocks,
+        [attended, low_in, second_scales[None], output_shrink, output_expand],
+        [
+            jax.ShapeDtypeStruct((tokens, model), F32),
+            jax.ShapeDtypeStruct((tokens, model), BF),
+            jax.ShapeDtypeStruct((tokens, lanes), BF),
+        ],
+    )
+
+    g0_pieces[0] = grad_low
+    n2_pieces = [normed_two]
+    for k in range(1, chips):
+        if k < 3 and k not in g0_pieces:
+            g0_pieces[k] = swap(after(grad_low, wide), 2 * k)
+        if k < 3:
+            n2_pieces.append(swap(after(normed_two, wide), 2 * k))
     if chips > 2:
         n2_pieces[1:3] = lax.optimization_barrier(n2_pieces[1:3])
     zero = jnp.zeros((lanes, hp), F32)
     sums = [(zero, zero, zero)] * fsdp_n
     out_raw = []
     grad_parts = []
-    for k in range(chips):
+    early_first = [0] + sorted(range(1, chips), key=lambda k: (k > 2, -k if k < 3 else k))
+    for k in early_first:
         f = 2 * k // cp_n
         sgu, ed, eg, eu, sd = feed_factors[f]
+        if len(out_raw) == 1:
+            for other in range(3, chips):
+                n2_pieces.append(swap(after(normed_two, out_raw[0]), 2 * other))
+                g0_pieces[other] = swap(after(grad_low, out_raw[0]), 2 * other)
+        if out_raw:
+            sums[f] = after(sums[f], out_raw[-1])
         out_k, ng_k, *sums[f] = feed(
-            me, wide, n2_pieces[k], g0_pieces[k], sgu, ed, w_down, eg, eu, sd, sums[f], seqs
+            feed_index, kinds, wide, n2_pieces[k], g0_pieces[k], sgu, ed, w_down, eg, eu, sd, sums[f], seqs
         )
         out_raw.append(out_k)
         grad_parts.append(ng_k if k == 0 else swap(ng_k, 2 * k))
 
-    grad_sum = grad_parts[0].astype(F32)
-    for part in grad_parts[1:]:
-        grad_sum = lax.optimization_barrier(grad_sum) + part.astype(F32)
-    gate_back = (grad_sum[:, model : model + lanes] * mixing).astype(BF)
-    up_back = (grad_sum[:, model + lanes :] * mixing).astype(BF)
-    normed_two_grad = (
-        grad_sum[:, :model] + mm_nt(gate_back, gate_shrink) + mm_nt(up_back, up_shrink)
-    )
-    middle_grad = grad_low.astype(F32) + norm_backward(middle, second_scales, normed_two_grad)
-    middle_low = middle_grad.astype(BF)
-
-    def narrowed_back(grad, expand):
-        return (mm_nt(grad, expand) * mixing).astype(BF)
-
-    output_back = narrowed_back(middle_low, output_expand)
-    attended_grad = (mm_nt(middle_low, w_output) + mm_nt(output_back, output_shrink)).astype(BF)
-    query_rot_grad, pair_part = attend_back(
-        info, query_rot, attended_grad, attended, pair_all, lse, seqs, spans, span_len
-    )
-
-    out_raw = after(out_raw, grad_sum)
-    out_parts = [part if k == 0 else swap(part, 2 * k) for k, part in enumerate(out_raw)]
-    out_sum = sum(part.astype(F32) for part in out_parts)
+    grad_most = grad_parts[0].astype(F32)
+    for part in grad_parts[1:-1]:
+        grad_most = lax.optimization_barrier(grad_most) + part.astype(F32)
 
     def pack(values, tiles):
         value = jnp.concatenate([value[:rank].astype(BF) for value in values], axis=1)
         return jnp.pad(value, ((0, 0), (0, -value.shape[1] % (128 * tiles))))
 
-    sums = after(sums, attended_grad)
-    stacked = jnp.stack([pack(sums[f], seq_n) for f in range(fsdp_n)])
-    feed_wide = stacked.shape[2]
-
-    def groups_of(parity):
-        return jnp.stack(
-            [
-                lax.dynamic_index_in_dim(stacked, (2 * j + parity) ^ group, 0, keepdims=False)
-                for j in range(fsdp_n // 2)
-            ]
-        )
-
-    feed_half = groups_of(core).astype(F32) + swap(groups_of(1 - core), 1).astype(F32)
-    feed_half = feed_half.reshape(fsdp_n // 2 * rank, seq_n, feed_wide // seq_n).astype(BF)
-    feed_piece = lax.psum_scatter(
-        feed_half.transpose(1, 0, 2), "seq", scatter_dimension=0, tiled=False
-    )
-    pair_grad = (
-        lax.psum_scatter(
-            after(pair_part, feed_piece, out_parts), ("cp", "seq"), scatter_dimension=1, tiled=True
-        )
-        .reshape(tokens, 2 * kv_width)
-        .astype(F32)
-    )
+    middle_grad, middle_low, gate_back, up_back, output_back, attended_grad = before_attention(
+        grad_most, grad_parts[-1], grad_low, middle, second_scales[None],
+        gate_shrink, up_shrink, output_shrink, output_expand, w_output, seqs,
+    )
+
+    def narrowed_back(grad, expand):
+        return (mm_nt(grad, expand) * mixing).astype(BF)
+
+    out_raw = after(out_raw, middle_low)
+    out_parts = [swap(part, 2 * k) if k else part for k, part in zip(early_first, out_raw)]
+    query_rot_grad, pair_part = attend_back(
+        info, query_rot, attended_grad, attended, pair_all, lse, seqs, spans, span_len
+    )
+    pair_grad = lax.psum_scatter(
+        after(pair_part, out_parts[:3]), ("cp", "seq"), scatter_dimension=1, tiled=True
+    ).reshape(tokens, 2 * kv_width)
+    out_sum = sum(part.astype(F32) for part in out_parts)
 
     down_narrow = (out_sum[:, model : model + lanes] * mixing).astype(BF)
     result = middle + (out_sum[:, :model] + mm(down_narrow, down_expand))
     outputs = result.astype(BF).reshape(seqs, tok_rows, model)
 
+    query_rot_grad, sums, middle_late, output_back, gate_back, up_back = after(
+        (query_rot_grad, sums, middle_low, output_back, gate_back, up_back), out_parts[:3]
+    )
     query_grad = (
         unrotate(
             query_rot_grad.reshape(tokens, -1, HEAD_DIM).astype(F32), cosine, sine_table
@@ -798,17 +1043,28 @@
             span *= 2
         return value[0]
 
-    def swap_seq(value, k):
-        return lax.ppermute(value, "seq", [(i, i ^ k) for i in range(seq_n)])
-
+    stacked = jnp.stack([pack(sums[f], seq_n) for f in range(fsdp_n)])
+    feed_wide = stacked.shape[2]
+
+    def groups_of(parity):
+        return jnp.stack(
+            [
+                lax.dynamic_index_in_dim(stacked, (2 * j + parity) ^ group, 0, keepdims=False)
+                for j in range(fsdp_n // 2)
+            ]
+        )
+
+    feed_half = groups_of(core).astype(F32) + swap(groups_of(1 - core), 1).astype(F32)
+    feed_half = feed_half.reshape(fsdp_n // 2 * rank, seq_n, feed_wide // seq_n).astype(BF)
+    feed_half = feed_half.transpose(1, 0, 2)
+    feed_piece = halves(feed_half, seq_index, swap_seq)
     ways = cp_n * seq_n
-    cp_index = lax.axis_index("cp")
     early = pack(
         [
             mm_tn(output_back, attended),
             mm_tn(gate_back, normed_two),
             mm_tn(up_back, normed_two),
-            mm_tn(output_narrow, middle_low),
+            mm_tn(output_narrow, middle_late),
             mm_tn(down_narrow, grad_low),
             mm_tn(query_back, normed),
             mm_tn(query_narrow, query_grad),
@@ -817,33 +1073,22 @@
     )
     early = early.reshape(rank, cp_n, seq_n, -1).transpose(1, 2, 0, 3)
     early = halves(early, cp_index, swap)
-    early = halves(early, lax.axis_index("seq"), swap_seq)
+    early = halves(early, seq_index, swap_seq)
     early_cols = early.shape[1]
-    lines = feed_piece.shape[0]
-    both = jnp.concatenate([jnp.pad(early, ((0, lines - rank), (0, 0))), feed_piece], axis=1)
+    both = jnp.concatenate([jnp.pad(early, ((0, feed_piece.shape[0] - rank), (0, 0))), feed_piece], axis=1)
     both = lax.all_gather(after(both, pair_grad), EVERY, axis=0, tiled=False)
 
-    key_grad = (
-        unrotate(pair_grad[:, :kv_width].reshape(tokens, -1, HEAD_DIM), cosine, sine_table)
-        .reshape(tokens, kv_width)
-        .astype(BF)
-    )
-    value_grad = pair_grad[:, kv_width:].astype(BF)
-    key_back = narrowed_back(key_grad, key_expand)
-    value_back = narrowed_back(value_grad, value_expand)
-
-    late = pack(
-        [
-            mm_tn(key_back, normed),
-            mm_tn(value_back, normed),
-            mm_tn(key_narrow, key_grad),
-            mm_tn(value_narrow, value_grad),
-        ],
-        cp_n,
-    )
-    late_wide = late.shape[1]
-    late = late.reshape(rank, cp_n, late_wide // cp_n).transpose(1, 0, 2)
-    late = halves(late, cp_index, swap)
+    key_grad, value_grad, key_back, value_back, late = last_grads(
+        cp_index, pair_grad, flat_cosine, sine_signed, key_expand, value_expand, normed,
+        key_narrow, value_narrow, seqs, rank, cp_n,
+    )
+    late_wide = late.shape[3] * cp_n
+    total = late[0].astype(F32) + swap(late[1], 1).astype(F32)
+    span = 2
+    while span < cp_n:
+        total = total[0::2] + swap(total[1::2].astype(BF), span).astype(F32)
+        span *= 2
+    late = total[0].astype(BF)
     total = late.astype(F32)
     for k in range(1, seq_n):
         total = total + swap_seq(late, k).astype(F32)
@@ -881,10 +1126,10 @@
 
     late_of = lambda i: late[:, model * i : model * (i + 1)]
     tail_of = lambda i: late[:, model * 2 + kv_width * i : model * 2 + kv_width * (i + 1)]
-    kinds = (True, True, True, False, False, True, False)
+    order_kinds = (True, True, True, False, False, True, False)
     if fsdp_n == 2 and 2 * hq % 128 == 0 and 2 * early_cols == model:
         expanded = expand_all(
-            both, select_all, rank, hq, hp, seq_n, chips, early_cols, kinds
+            both, select_all, rank, hq, hp, seq_n, chips, early_cols, order_kinds
         )
     else:
         early_full = both[:, :rank, :early_cols].reshape(fsdp_n, ways, rank, early_cols)
@@ -894,7 +1139,7 @@
         ).transpose(4, 2, 5, 0, 1, 3, 6)
         feed_full = feed_full.reshape(fsdp_n * rank, chips, feed_wide)
         expanded = []
-        for i, shrink in enumerate((False, False, True) + kinds):
+        for i, shrink in enumerate((False, False, True) + order_kinds):
             if i < 3:
                 rows = feed_full[:, :, i * hp : i * hp + hq].reshape(fsdp_n * rank, hidden_all)
             else:

time: 700 us -> 713 us (1.019)
  waiting for transfers between devices: 207 us -> 283 us
  other arithmetic: 85.4 us -> 51 us
  matrix products: 75.2 us -> 47 us
  local copies, waits for them, and re-layouts: 76.3 us -> 52.5 us
  Pallas kernels: 189 us -> 212 us
    ppermute x43, waiting for transfers between devices: 149 us -> 208 us  [swap(): return lax.ppermute(value, PLANE, [(i, i ^ k) for i in range(plane)])]
    pallas_call x4 -> x9, Pallas kernels: 117 us -> 155 us  [the longest x4 120 us: feed(): pl.pallas_call(functools.partial(feed_kernel, seqs, tuple(kinds)), grid_s...]
    dot_general x23 -> x11, matrix products: 34.3 us -> 13.7 us  [mm(): return jnp.dot(left, right, preferred_element_type=jnp.float32)]
    ppermute x5 -> x7, waiting for transfers between devices: 25.4 us -> 41 us  [swap_seq(): return lax.ppermute(value, 'seq', [(i, i ^ k) for i in range(seq_n)])]
    convert_element_type x11 -> x3, other arithmetic: 13 us -> 2.07 us  [the longest x1 1.47 us: body(): grad_most = grad_parts[0].astype(F32)]
    pallas_call x3 -> x1, Pallas kernels: 13.5 us -> 4.91 us  [assemble(): pl.pallas_call(functools.partial(assemble_kernel, count), grid_spec=pltpu...]
    dot_general x14 -> x7, matrix products: 16.1 us -> 9.21 us  [mm_nt(): lax.dot_general(left, right, (((1,), (1,)), ((), ())), preferred_element_...]
    reduce_scatter x2 -> x1, waiting for transfers between devices: 18.6 us -> 12.8 us  [body(): lax.psum_scatter(after(pair_part, out_parts[:3]), ('cp', 'seq'), scatter_...]
  transfers between devices with their start and end apart: 53 -> 54, of which waited for: 22 -> 27; matrix products, arithmetic and copies ran while one was open for 29% -> 20% of each run, Pallas kernels for 26% -> 26%
where the time goes in v2:
time: 713 us; the launch traced here: 705 us
  waiting for transfers between devices  283 us (40%)
  Pallas kernels  212 us (30%)
  local copies, waits for them, and re-layouts  52.5 us (7%)
  other arithmetic  51 us (7%)
  matrix products  47 us (7%)
  starting transfers between devices  43.7 us (6%)
  between operations  15.8 us (2%)
    ppermute x43, waiting for transfers between devices, swap(): return lax.ppermute(value, PLANE, [(i, i ^ k) for i in range(plane)])  208 us
    pallas_call x4, Pallas kernels, feed(): pl.pallas_call(functools.partial(feed_kernel, seqs, tuple(kinds)), grid_s...  120 us
    ppermute x7, waiting for transfers between devices, swap_seq(): return lax.ppermute(value, 'seq', [(i, i ^ k) for i in range(seq_n)])  41 us
    ppermute x43, starting transfers between devices, swap(): return lax.ppermute(value, PLANE, [(i, i ^ k) for i in range(plane)])  36.6 us
    dot_general x21, matrix products, mm_tn(): lax.dot_general(left, right, (((0,), (0,)), ((), ())), preferred_element_...  24.1 us
    pallas_call x1, Pallas kernels, attend_back(): pl.pallas_call(functools.partial(attend_back_kernel, spans, span_len, tok...  22.3 us
    pallas_call x1, Pallas kernels, attend(): pl.pallas_call(functools.partial(attend_kernel, spans, span_len, tokens),...  17.3 us
    all_gather x1, waiting for transfers between devices, body(): both = lax.all_gather(after(both, pair_grad), EVERY, axis=0, tiled=False)  16.8 us
  transfers between devices with their start and end apart: 54, of which 27 were waited for; matrix products, arithmetic and copies ran while one was open for 20% of the time, Pallas kernels for 26%

profile of v2, /device:TPU:0, one launch (start us, length us, event | category | flops | bytes accessed | tf_op | source)
XLA Modules:
  0.0 705.4 jit_solution(13054939661253011496)
XLA Ops:
  7.2 3.0 collective-permute-start
  14.2 2.0 collective-permute-start.25
  16.8 4.1 fusion.117
  20.9 1.9 fusion.116
  25.0 1.9 select_bitcast_fusion
  29.7 3.3 fusion.10
  34.4 11.3 %collective-permute-done.25 = f32[8,128]{0,1:T(8,128)} collective-permute-done((f32[8,128]{0,1:T(8,128)S(1)}, f32[8,128]{0,1:T(8,128)}, u32[]{:S(2)}, u32[]{:S(2)}) %collective-permute-start.25) | collective-permute-done | bytes 4128 | tf_op jit(solution)/shard_map/ppermute | solution.py:801
  50.6 4.3 keys_values.1
  63.5 2.0 convolution_convert_fusion.6
  65.6 11.9 %collective-permute-done.3.refs_2_ = bf16[192,1536]{1,0:T(8,128)(2,1)S(1)} collective-permute-done((bf16[192,1536]{1,0:T(8,128)(2,1)}, bf16[192,1536]{1,0:T(8,128)(2,1)S(1)}, u32[]{:S(2)}, u32[]{:S(2)}) %collective-permute-start.3) | collective-permute-done | bytes 589856 | tf_op jit(solution)/shard_map/ppermute | solution.py:801
  77.5 20.0 %collective-permute-done.4.refs_4_ = bf16[192,1536]{1,0:T(8,128)(2,1)S(1)} collective-permute-done((bf16[192,1536]{1,0:T(8,128)(2,1)}, bf16[192,1536]{1,0:T(8,128)(2,1)S(1)}, u32[]{:S(2)}, u32[]{:S(2)}) %collective-permute-start.4) | collective-permute-done | bytes 589856 | tf_op jit(solution)/shard_map/ppermute | solution.py:801
  97.4 12.0 %collective-permute-done.5.refs_6_ = bf16[192,1536]{1,0:T(8,128)(2,1)S(1)} collective-permute-done((bf16[192,1536]{1,0:T(8,128)(2,1)}, bf16[192,1536]{1,0:T(8,128)(2,1)S(1)}, u32[]{:S(2)}, u32[]{:S(2)}) %collective-permute-start.5) | collective-permute-done | bytes 589856 | tf_op jit(solution)/shard_map/ppermute | solution.py:801
  110.6 7.5 %queries.1 = (bf16[384,1536]{1,0:T(8,128)(2,1)}, bf16[384,64]{1,0:T(8,128)(2,1)}, bf16[1536,1536]{1,0:T(8,128)(2,1)}) custom-call(s32[1]{0:T(128)} %bitcast.info, bf16[384,1536]{1,0:T(8,128)(2,1)} %get-tuple-element.146.normed_ref, bf16[1536,64]{1,0:T(8,128)(2,1)} %bitcast.193, bf16[64,1536]{1,0:T(8,128)(2,1)} %convolution_convert_fusion.17.eq_ref, ...), custom_call_target="tpu_custom_call" | custom-call | flops 1811939328 | bytes 9437184 | tf_op jit(solution)/shard_map/queries/pallas_call | solution.py:479
  125.9 2.1 convolution_convert_fusion.13
  128.0 4.7 all-gather.7.cloned.1.call-done.k_ref.v_ref
  136.2 1.9 convolution_convert_fusion.15.refs_11_
  141.9 1.8 copy.103
  143.7 1.9 convolution_convert_fusion.14.refs_11_
  145.7 1.9 convolution_convert_fusion.16.eo_ref.oe_ref
  148.2 2.1 pad_maximum_fusion.4.refs_10_
  150.3 17.3 %attend.1 = (bf16[384,1536]{1,0:T(8,128)(2,1)}, f32[6,8,768]{2,1,0:T(8,128)}) custom-call(s32[29]{0:T(128)} %pad_add_fusion.info, bf16[384,1536]{1,0:T(8,128)(2,1)} %get-tuple-element.156.q_ref, bf16[3,2048,512]{2,1,0:T(8,128)(2,1)} %all-gather.7.cloned.1.call-done.k_ref.v_ref, bf16[3,2048,512]{2,1,0:T(8,128)(2,1)} %all-gather.7.cloned.1.call-done.k_ref.v_ref), custom_call_target="tpu_custom_call" | custom-call | flops 4831838208 | bytes 6291456 | tf_op jit(solution)/shard_map/attend/pallas_call | solution.py:152
  167.6 4.9 assemble.1.refs_12_
  173.4 8.7 %outputs.1 = (f32[384,1536]{1,0:T(8,128)}, bf16[384,1536]{1,0:T(8,128)(2,1)}, bf16[384,64]{1,0:T(8,128)(2,1)}, bf16[1536,1536]{1,0:T(8,128)(2,1)}) custom-call(s32[1]{0:T(128)} %bitcast.info, bf16[384,1536]{1,0:T(8,128)(2,1)} %get-tuple-element.157.attended_ref.o_ref, bf16[384,1536]{1,0:T(8,128)(2,1)} %bitcast.184, f32[1,1536]{1,0:T(1,128)} %reshape.390.gain_ref, ...), custom_call_target="tpu_custom_call" | custom-call | flops 1811939328 | bytes 9437184 | tf_op jit(solution)/shard_map/outputs/pallas_call | solution.py:479
  182.1 29.7 %collective-permute-done.18.refs_4_ = bf16[2,192,2304]{2,1,0:T(8,128)(2,1)} collective-permute-done((bf16[2,192,2304]{2,1,0:T(8,128)(2,1)}, bf16[2,192,2304]{2,1,0:T(8,128)(2,1)}, u32[]{:S(2)}, u32[]{:S(2)}) %collective-permute-start.18) | collective-permute-done | bytes 1769504 | tf_op jit(solution)/shard_map/ppermute | solution.py:801
  212.6 1.9 fusion.119
  224.3 2.1 collective-permute-done.21.refs_7_
  226.6 2.5 collective-permute-done.17.refs_3_
  232.1 29.9 %feed.4 = (bf16[384,1664]{1,0:T(8,128)(2,1)}, bf16[384,1664]{1,0:T(8,128)(2,1)}, f32[64,2304]{1,0:T(8,128)}, f32[64,2304]{1,0:T(8,128)}, f32[64,2304]{1,0:T(8,128)}) custom-call(s32[2]{0:T(128)} %pad_add_fusion.1.info, bf16[2,192,2304]{2,1,0:T(8,128)(2,1)} %get-tuple-element.164.refs_0_, bf16[2,192,2304]{2,1,0:T(8,128)(2,1)} %collective-permute-done.15.refs_1_, ...), custom_call_target="tpu_custom_call" | custom-call | flops 16986931200 | bytes 21233664 | tf_op jit(solution)/shard_map/feed/pallas_call | solution.py:603
  265.5 2.3 collective-permute-start.28
  267.9 29.9 %feed.5 = (bf16[384,1664]{1,0:T(8,128)(2,1)}, bf16[384,1664]{1,0:T(8,128)(2,1)}, f32[64,2304]{1,0:T(8,128)}, f32[64,2304]{1,0:T(8,128)}, f32[64,2304]{1,0:T(8,128)}) custom-call(s32[2]{0:T(128)} %pad_add_fusion.1.info, bf16[2,192,2304]{2,1,0:T(8,128)(2,1)} %get-tuple-element.164.refs_0_, bf16[2,192,2304]{2,1,0:T(8,128)(2,1)} %collective-permute-done.15.refs_1_, ...), custom_call_target="tpu_custom_call" | custom-call | flops 16986931200 | bytes 21233664 | tf_op jit(solution)/shard_map/feed/pallas_call | solution.py:603
  298.4 43.4 %collective-permute-done.26.refs_9_ = bf16[384,1536]{1,0:T(8,128)(2,1)} collective-permute-done((bf16[384,1536]{1,0:T(8,128)(2,1)}, bf16[384,1536]{1,0:T(8,128)(2,1)}, u32[]{:S(2)}, u32[]{:S(2)}) %collective-permute-start.26) | collective-permute-done | bytes 1179680 | tf_op jit(solution)/shard_map/ppermute | solution.py:801
  341.8 30.2 %feed.6 = (bf16[384,1664]{1,0:T(8,128)(2,1)}, bf16[384,1664]{1,0:T(8,128)(2,1)}, f32[64,2304]{1,0:T(8,128)}, f32[64,2304]{1,0:T(8,128)}, f32[64,2304]{1,0:T(8,128)}) custom-call(s32[2]{0:T(128)} %pad_add_fusion.1.info, bf16[2,192,2304]{2,1,0:T(8,128)(2,1)} %get-tuple-element.164.refs_0_, bf16[2,192,2304]{2,1,0:T(8,128)(2,1)} %collective-permute-done.15.refs_1_, ...), custom_call_target="tpu_custom_call" | custom-call | flops 16986931200 | bytes 21233664 | tf_op jit(solution)/shard_map/feed/pallas_call | solution.py:603
  373.5 30.0 %feed.7 = (bf16[384,1664]{1,0:T(8,128)(2,1)}, bf16[384,1664]{1,0:T(8,128)(2,1)}, f32[64,2304]{1,0:T(8,128)}, f32[64,2304]{1,0:T(8,128)}, f32[64,2304]{1,0:T(8,128)}) custom-call(s32[2]{0:T(128)} %pad_add_fusion.1.info, bf16[2,192,2304]{2,1,0:T(8,128)(2,1)} %get-tuple-element.164.refs_0_, bf16[2,192,2304]{2,1,0:T(8,128)(2,1)} %collective-permute-done.15.refs_1_, ...), custom_call_target="tpu_custom_call" | custom-call | flops 16986931200 | bytes 21233664 | tf_op jit(solution)/shard_map/feed/pallas_call | solution.py:603
  405.7 3.0 convert_add_fusion.1.most_ref
  408.8 24.3 %collective-permute-done.31.last_ref = bf16[384,1664]{1,0:T(8,128)(2,1)S(1)} collective-permute-done((bf16[384,1664]{1,0:T(8,128)(2,1)}, bf16[384,1664]{1,0:T(8,128)(2,1)S(1)}, u32[]{:S(2)}, u32[]{:S(2)}) %collective-permute-start.31) | collective-permute-done | bytes 1277984 | tf_op jit(solution)/shard_map/ppermute | solution.py:801
  434.2 11.5 %before_attention.1 = (f32[384,1536]{1,0:T(8,128)}, bf16[384,1536]{1,0:T(8,128)(2,1)}, bf16[384,64]{1,0:T(8,128)(2,1)}, bf16[384,64]{1,0:T(8,128)(2,1)}, bf16[38...) custom-call(f32[384,1664]{1,0:T(8,128)} %convert_add_fusion.1.most_ref, bf16[384,1664]{1,0:T(8,128)(2,1)} %copy-done.31, ...), custom_call_target="tpu_custom_call" | custom-call | flops 1811939328 | bytes 17694720 | tf_op jit(solution)/shard_map/before_attention/pallas_call | solution.py:398
  449.9 2.0 copy.106
  452.0 2.4 collective-permute-start.34
  454.4 22.3 %attend_back.1 = (bf16[384,1536]{1,0:T(8,128)(2,1)}, bf16[3,2048,512]{2,1,0:T(8,128)(2,1)}) custom-call(s32[29]{0:T(128)} %pad_add_fusion.info, bf16[384,1536]{1,0:T(8,128)(2,1)} %get-tuple-element.156.q_ref, bf16[384,1536]{1,0:T(8,128)(2,1)} %get-tuple-element.214.do_ref, bf16[384,1536]{1,0:T(8,128)(2,1)} %get-tuple-element.157.attended_ref.o_ref, ...), custom_call_target="tpu_custom_call" | custom-call | flops 12079595520 | bytes 12582912 | tf_op jit(solution)/shard_map/attend_back/pallas_call | solution.py:253
  477.0 24.1 %collective-permute-done.33 = bf16[384,1664]{1,0:T(8,128)(2,1)} collective-permute-done((bf16[384,1664]{1,0:T(8,128)(2,1)}, bf16[384,1664]{1,0:T(8,128)(2,1)}, u32[]{:S(2)}, u32[]{:S(2)}) %collective-permute-start.33) | collective-permute-done | bytes 1277984 | tf_op jit(solution)/shard_map/ppermute | solution.py:801
  504.1 2.1 broadcast_multiply_fusion
  508.1 3.2 copy.109
  511.3 2.5 add_convert_fusion
  515.9 1.9 fusion.126
  520.0 2.8 convert_add_fusion
  522.8 2.8 fusion.109
  541.0 12.9 %collective-permute-done.36 = bf16[1,4,48,768]{3,2,1,0:T(8,128)(2,1)S(1)} collective-permute-done((bf16[1,4,48,768]{3,2,1,0:T(8,128)(2,1)S(1)}, bf16[1,4,48,768]{3,2,1,0:T(8,128)(2,1)S(1)}, u32[]{:S(2)}, u32[]{:S(2)}) %collective-permute-start.36) | collective-permute-done | bytes 294944 | tf_op jit(solution)/shard_map/ppermute | solution.py:801
  556.2 13.0 %collective-permute-done.37 = bf16[2,48,768]{2,1,0:T(8,128)(2,1)S(1)} collective-permute-done((bf16[2,48,768]{2,1,0:T(8,128)(2,1)S(1)}, bf16[2,48,768]{2,1,0:T(8,128)(2,1)S(1)}, u32[]{:S(2)}, u32[]{:S(2)}) %collective-permute-start.37) | collective-permute-done | bytes 147488 | tf_op jit(solution)/shard_map/ppermute | solution.py:804
  569.3 9.3 %collective-permute-done.40 = bf16[2,48,1792]{2,1,0:T(8,128)(2,1)S(1)} collective-permute-done((bf16[2,48,1792]{2,1,0:T(8,128)(2,1)S(1)}, bf16[2,48,1792]{2,1,0:T(8,128)(2,1)S(1)}, u32[]{:S(2)}, u32[]{:S(2)}) %collective-permute-start.40) | collective-permute-done | bytes 344096 | tf_op jit(solution)/shard_map/ppermute | solution.py:804
  578.8 9.1 %collective-permute-done.41 = bf16[1,48,1792]{2,1,0:T(8,128)(2,1)S(1)} collective-permute-done((bf16[1,48,1792]{2,1,0:T(8,128)(2,1)S(1)}, bf16[1,48,1792]{2,1,0:T(8,128)(2,1)S(1)}, u32[]{:S(2)}, u32[]{:S(2)}) %collective-permute-start.41) | collective-permute-done | bytes 172064 | tf_op jit(solution)/shard_map/ppermute | solution.py:804
  588.6 12.8 %reduce-scatter.2.cloned.1.call-done = bf16[3,128,512]{2,1,0:T(8,128)(2,1)} async-done(((bf16[3,2048,512]{2,1,0:T(8,128)(2,1)}), bf16[3,128,512]{2,1,0:T(8,128)(2,1)}) %reduce-scatter.2.cloned.1.call-update) | async-done | bytes 393232 | tf_op jit(solution)/shard_map/reduce_scatter | solution.py:1013
  609.3 2.0 gather_fusion
  612.9 3.6 fusion.8
  616.5 4.4 fusion.121
  621.5 3.3 last_grads.1
  629.6 3.6 collective-permute-done.43
  635.1 2.6 collective-permute-start.46
  638.1 4.3 collective-permute-done.44
  642.4 5.4 collective-permute-done.45
  647.9 3.4 collective-permute-start.47
  655.3 6.5 collective-permute-done.48
  661.9 2.0 fusion.5
  669.5 16.8 %all-gather.9.cloned.1.call-done = bf16[1536,2560]{1,0:T(8,128)(2,1)} async-done(((bf16[48,2560]{1,0:T(8,128)(2,1)}), bf16[1536,2560]{1,0:T(8,128)(2,1)}) %all-gather.9.cloned.1.call-update) | async-done | bytes 7864336 | tf_op jit(solution)/shard_map/all_gather | solution.py:1079
  686.3 12.1 %expand.1 = (f32[128,8960]{1,0:T(8,128)}, f32[128,8960]{1,0:T(8,128)}, f32[8960,128]{1,0:T(8,128)}, f32[1536,128]{1,0:T(8,128)}, f32[1536,128]{1,0:T(8,128)}, /*...) custom-call(bf16[32,48,2560]{2,1,0:T(8,128)(2,1)} %bitcast.188, ...), custom_call_target="tpu_custom_call" | custom-call | flops 660602880 | bytes 13762560 | tf_op jit(solution)/shard_map/expand/pallas_call | solution.py:741
  (400 shorter events, 123.0 us)
Async XLA Ops:
  7.2 211.7 %copy-start = (bf16[8960,128]{1,0:T(8,128)(2,1)S(1)}, bf16[8960,128]{1,0:T(8,128)(2,1)}, u32[]{:S(2)}) copy-start(bf16[8960,128]{1,0:T(8,128)(2,1)} %param.59) | copy-start | bytes 6881284
  7.2 43.4 %all-gather.5.cloned.1.call-start = ((), (), s32[]{:S(2)}) async-start(), calls=%async_computation.1 | async-start | bytes 1769472 | tf_op jit(solution)/shard_map/all_gather | solution.py:843
  7.2 43.3 %collective-permute-start = (bf16[192,1536]{1,0:T(8,128)(2,1)}, bf16[192,1536]{1,0:T(8,128)(2,1)}, u32[]{:S(2)}, u32[]{:S(2)}) collective-permute-start(bf16[192,1536]{1,0:T(8,128)(2,1)} %refs_0_), channel_id=1, source_target_pairs={{0,8},{4,12},{8,0},{12,4},{16,24},{20,28},{24,16},{28,20},{1,9},{5... | collective-permute-start | bytes 1769480 | tf_op jit(solution)/shard_map/ppermute | solution.py:801
  10.3 40.2 %collective-permute-start.1 = (bf16[192,1536]{1,0:T(8,128)(2,1)}, bf16[192,1536]{1,0:T(8,128)(2,1)}, u32[]{:S(2)}, u32[]{:S(2)}) collective-permute-start(bf16[192,1536]{1,0:T(8,128)(2,1)} %refs_0_), channel_id=1, source_target_pairs={{0,16},{4,20},{8,24},{12,28},{16,0},{20,4},{24,8},{28,12},{1,17},{... | collective-permute-start | bytes 1769480 | tf_op jit(solution)/shard_map/ppermute | solution.py:801
  11.8 38.8 %collective-permute-start.2 = (bf16[192,1536]{1,0:T(8,128)(2,1)}, bf16[192,1536]{1,0:T(8,128)(2,1)}, u32[]{:S(2)}, u32[]{:S(2)}) collective-permute-start(bf16[192,1536]{1,0:T(8,128)(2,1)} %refs_0_), channel_id=1, source_target_pairs={{0,24},{4,28},{8,16},{12,20},{16,8},{20,12},{24,0},{28,4},{1,25},{... | collective-permute-start | bytes 1769480 | tf_op jit(solution)/shard_map/ppermute | solution.py:801
  13.5 119.3 %all-gather.7.cloned.1.call-start = ((), (), s32[]{:S(2)}) async-start(), calls=%async_computation.2 | async-start | bytes 6684672 | tf_op jit(solution)/shard_map/all_gather | solution.py:897
  14.2 31.5 %collective-permute-start.25 = (f32[8,128]{0,1:T(8,128)S(1)}, f32[8,128]{0,1:T(8,128)}, u32[]{:S(2)}, u32[]{:S(2)}) collective-permute-start(f32[8,128]{0,1:T(8,128)S(1)} %broadcast_in_dim.86), channel_id=1, source_target_pairs={{0,16},{4,20},{8,24},{12,28},{16,0},{20,4},{24,8},{28,12},{1,17},{... | collective-permute-start | bytes 12296 | tf_op jit(solution)/shard_map/ppermute | solution.py:801
  54.9 546.5 %reduce-scatter.2.cloned.1.call-start = ((), (), s32[]{:S(2)}) async-start(), calls=%async_computation.3 | async-start | bytes 6684672 | tf_op jit(solution)/shard_map/reduce_scatter | solution.py:1013
  55.1 2.3 collective-permute-start.10
  55.2 3.7 collective-permute-start.7
  55.7 4.7 collective-permute-start.8
  55.8 53.6 %collective-permute-start.6 = (bf16[384,1536]{1,0:T(8,128)(2,1)}, bf16[384,1536]{1,0:T(8,128)(2,1)S(1)}, u32[]{:S(2)}, u32[]{:S(2)}) collective-permute-start(bf16[384,1536]{1,0:T(8,128)(2,1)} %bitcast.21.refs_9_.grad_ref), channel_id=1, source_target_pairs={{0,16},{4,20},{8,24},{12,28},{16,0},{20,4},{24,8},{28,12},{1,17},{... | collective-permute-start | bytes 3538952 | tf_op jit(solution)/shard_map/ppermute | solution.py:801
  57.3 8.3 %collective-permute-start.9 = (bf16[192,1536]{1,0:T(8,128)(2,1)}, bf16[192,1536]{1,0:T(8,128)(2,1)S(1)}, u32[]{:S(2)}, u32[]{:S(2)}) collective-permute-start(bf16[192,1536]{1,0:T(8,128)(2,1)} %collective-permute-done.1.refs_4_), channel_id=1, source_target_pairs={{0,4},{4,0},{8,12},{12,8},{16,20},{20,16},{24,28},{28,24},{1,5},{5... | collective-permute-start | bytes 1769480 | tf_op jit(solution)/shard_map/ppermute | solution.py:801
  57.5 20.0 %collective-permute-start.3 = (bf16[192,1536]{1,0:T(8,128)(2,1)}, bf16[192,1536]{1,0:T(8,128)(2,1)S(1)}, u32[]{:S(2)}, u32[]{:S(2)}) collective-permute-start(bf16[192,1536]{1,0:T(8,128)(2,1)} %refs_0_.1), channel_id=1, source_target_pairs={{0,8},{4,12},{8,0},{12,4},{16,24},{20,28},{24,16},{28,20},{1,9},{5... | collective-permute-start | bytes 1769480 | tf_op jit(solution)/shard_map/ppermute | solution.py:801
  58.9 38.5 %collective-permute-start.4 = (bf16[192,1536]{1,0:T(8,128)(2,1)}, bf16[192,1536]{1,0:T(8,128)(2,1)S(1)}, u32[]{:S(2)}, u32[]{:S(2)}) collective-permute-start(bf16[192,1536]{1,0:T(8,128)(2,1)} %refs_0_.1), channel_id=1, source_target_pairs={{0,16},{4,20},{8,24},{12,28},{16,0},{20,4},{24,8},{28,12},{1,17},{... | collective-permute-start | bytes 1769480 | tf_op jit(solution)/shard_map/ppermute | solution.py:801
  61.2 48.2 %collective-permute-start.5 = (bf16[192,1536]{1,0:T(8,128)(2,1)}, bf16[192,1536]{1,0:T(8,128)(2,1)S(1)}, u32[]{:S(2)}, u32[]{:S(2)}) collective-permute-start(bf16[192,1536]{1,0:T(8,128)(2,1)} %refs_0_.1), channel_id=1, source_target_pairs={{0,24},{4,28},{8,16},{12,20},{16,8},{20,12},{24,0},{28,4},{1,25},{... | collective-permute-start | bytes 1769480 | tf_op jit(solution)/shard_map/ppermute | solution.py:801
  65.6 43.8 %copy-start.43 = (bf16[192,1536]{1,0:T(8,128)(2,1)}, bf16[192,1536]{1,0:T(8,128)(2,1)S(1)}, u32[]{:S(2)}) copy-start(bf16[192,1536]{1,0:T(8,128)(2,1)S(1)} %collective-permute-done.9.refs_5_) | copy-start | bytes 1769476
  118.1 30.0 %collective-permute-start.22 = (bf16[1120,1536]{1,0:T(8,128)(2,1)}, bf16[1120,1536]{1,0:T(8,128)(2,1)}, u32[]{:S(2)}, u32[]{:S(2)}) collective-permute-start(bf16[1120,1536]{1,0:T(8,128)(2,1)} %refs_0_.2), channel_id=1, source_target_pairs={{0,4},{4,0},{8,12},{12,8},{16,20},{20,16},{24,28},{28,24},{1,5},{5... | collective-permute-start | bytes 10321928 | tf_op jit(solution)/shard_map/ppermute | solution.py:801
  118.9 403.8 %copy-start.70 = (pred[64]{0:T(512)(128)(4,1)}, pred[64]{0:T(512)(128)(4,1)S(1)}, u32[]{:S(2)}) copy-start(pred[64]{0:T(512)(128)(4,1)S(1)} %compare_and_fusion.2) | copy-start | bytes 196
  120.7 102.6 %copy-start.61 = (s32[64]{0:T(128)}, s32[64]{0:T(128)S(1)}, u32[]{:S(2)}) copy-start(s32[64]{0:T(128)S(1)} %pad.95) | copy-start | bytes 772
  122.9 15.2 %collective-permute-start.11 = (bf16[192,1536]{1,0:T(8,128)(2,1)}, bf16[192,1536]{1,0:T(8,128)(2,1)}, u32[]{:S(2)}, u32[]{:S(2)}) collective-permute-start(bf16[192,1536]{1,0:T(8,128)(2,1)} %refs_0_.1), channel_id=1, source_target_pairs={{0,4},{4,0},{8,12},{12,8},{16,20},{20,16},{24,28},{28,24},{1,5},{5... | collective-permute-start | bytes 1769480 | tf_op jit(solution)/shard_map/ppermute | solution.py:801
  132.7 49.3 %collective-permute-start.20 = (bf16[2,192,2304]{2,1,0:T(8,128)(2,1)}, bf16[2,192,2304]{2,1,0:T(8,128)(2,1)}, u32[]{:S(2)}, u32[]{:S(2)}) collective-permute-start(bf16[2,192,2304]{2,1,0:T(8,128)(2,1)} %get-tuple-element.170), channel_id=1, source_target_pairs={{0,24},{4,28},{8,16},{12,20},{16,8},{20,12},{24,0},{28,4},{1,25},{... | collective-permute-start | bytes 5308424 | tf_op jit(solution)/shard_map/ppermute | solution.py:801
  134.2 77.6 %collective-permute-start.18 = (bf16[2,192,2304]{2,1,0:T(8,128)(2,1)}, bf16[2,192,2304]{2,1,0:T(8,128)(2,1)}, u32[]{:S(2)}, u32[]{:S(2)}) collective-permute-start(bf16[2,192,2304]{2,1,0:T(8,128)(2,1)} %get-tuple-element.168), channel_id=1, source_target_pairs={{0,16},{4,20},{8,24},{12,28},{16,0},{20,4},{24,8},{28,12},{1,17},{... | collective-permute-start | bytes 5308424 | tf_op jit(solution)/shard_map/ppermute | solution.py:801
  134.7 77.9 %collective-permute-start.16 = (bf16[2,192,2304]{2,1,0:T(8,128)(2,1)}, bf16[2,192,2304]{2,1,0:T(8,128)(2,1)}, u32[]{:S(2)}, u32[]{:S(2)}) collective-permute-start(bf16[2,192,2304]{2,1,0:T(8,128)(2,1)} %get-tuple-element.166), channel_id=1, source_target_pairs={{0,8},{4,12},{8,0},{12,4},{16,24},{20,28},{24,16},{28,20},{1,9},{5... | collective-permute-start | bytes 5308424 | tf_op jit(solution)/shard_map/ppermute | solution.py:801
  138.1 9.5 %collective-permute-start.12 = (bf16[192,1536]{1,0:T(8,128)(2,1)}, bf16[192,1536]{1,0:T(8,128)(2,1)}, u32[]{:S(2)}, u32[]{:S(2)}) collective-permute-start(bf16[192,1536]{1,0:T(8,128)(2,1)} %copy-done.37), channel_id=1, source_target_pairs={{0,4},{4,0},{8,12},{12,8},{16,20},{20,16},{24,28},{28,24},{1,5},{5... | collective-permute-start | bytes 1769480 | tf_op jit(solution)/shard_map/ppermute | solution.py:801
  147.6 24.9 %collective-permute-start.13 = (bf16[192,1536]{1,0:T(8,128)(2,1)}, bf16[192,1536]{1,0:T(8,128)(2,1)S(1)}, u32[]{:S(2)}, u32[]{:S(2)}) collective-permute-start(bf16[192,1536]{1,0:T(8,128)(2,1)} %copy-done.38), channel_id=1, source_target_pairs={{0,4},{4,0},{8,12},{12,8},{16,20},{20,16},{24,28},{28,24},{1,5},{5... | collective-permute-start | bytes 1769480 | tf_op jit(solution)/shard_map/ppermute | solution.py:801
  148.1 24.5 %collective-permute-start.14 = (bf16[192,1536]{1,0:T(8,128)(2,1)}, bf16[192,1536]{1,0:T(8,128)(2,1)}, u32[]{:S(2)}, u32[]{:S(2)}) collective-permute-start(bf16[192,1536]{1,0:T(8,128)(2,1)} %copy-done.39), channel_id=1, source_target_pairs={{0,4},{4,0},{8,12},{12,8},{16,20},{20,16},{24,28},{28,24},{1,5},{5... | collective-permute-start | bytes 1769480 | tf_op jit(solution)/shard_map/ppermute | solution.py:801
  172.6 51.7 %collective-permute-start.15 = (bf16[2,192,2304]{2,1,0:T(8,128)(2,1)}, bf16[2,192,2304]{2,1,0:T(8,128)(2,1)}, u32[]{:S(2)}, u32[]{:S(2)}) collective-permute-start(bf16[2,192,2304]{2,1,0:T(8,128)(2,1)} %get-tuple-element.164.refs_0_), channel_id=1, source_target_pairs={{0,4},{4,0},{8,12},{12,8},{16,20},{20,16},{24,28},{28,24},{1,5},{5... | collective-permute-start | bytes 5308424 | tf_op jit(solution)/shard_map/ppermute | solution.py:801
  182.1 32.5 %copy-start.24 = (bf16[128,8960]{1,0:T(8,128)(2,1)S(1)}, bf16[128,8960]{1,0:T(8,128)(2,1)}, u32[]{:S(2)}) copy-start(bf16[128,8960]{1,0:T(8,128)(2,1)} %param.56) | copy-start | bytes 6881284
  220.1 6.3 collective-permute-start.21
  220.1 6.6 collective-permute-start.19
  220.6 8.6 %collective-permute-start.17 = (bf16[2,192,2304]{2,1,0:T(8,128)(2,1)}, bf16[2,192,2304]{2,1,0:T(8,128)(2,1)}, u32[]{:S(2)}, u32[]{:S(2)}) collective-permute-start(bf16[2,192,2304]{2,1,0:T(8,128)(2,1)} %collective-permute-done.16.refs_2_), channel_id=1, source_target_pairs={{0,4},{4,0},{8,12},{12,8},{16,20},{20,16},{24,28},{28,24},{1,5},{5... | collective-permute-start | bytes 5308424 | tf_op jit(solution)/shard_map/ppermute | solution.py:801
  229.2 38.7 %collective-permute-start.23 = (bf16[384,1536]{1,0:T(8,128)(2,1)}, bf16[384,1536]{1,0:T(8,128)(2,1)}, u32[]{:S(2)}, u32[]{:S(2)}) collective-permute-start(bf16[384,1536]{1,0:T(8,128)(2,1)} %get-tuple-element.194.refs_8_), channel_id=1, source_target_pairs={{0,8},{4,12},{8,0},{12,4},{16,24},{20,28},{24,16},{28,20},{1,9},{5... | collective-permute-start | bytes 3538952 | tf_op jit(solution)/shard_map/ppermute | solution.py:801
  229.8 38.1 %collective-permute-start.24 = (bf16[384,1536]{1,0:T(8,128)(2,1)}, bf16[384,1536]{1,0:T(8,128)(2,1)}, u32[]{:S(2)}, u32[]{:S(2)}) collective-permute-start(bf16[384,1536]{1,0:T(8,128)(2,1)} %get-tuple-element.194.refs_8_), channel_id=1, source_target_pairs={{0,16},{4,20},{8,24},{12,28},{16,0},{20,4},{24,8},{28,12},{1,17},{... | collective-permute-start | bytes 3538952 | tf_op jit(solution)/shard_map/ppermute | solution.py:801
  263.4 78.4 %collective-permute-start.26 = (bf16[384,1536]{1,0:T(8,128)(2,1)}, bf16[384,1536]{1,0:T(8,128)(2,1)}, u32[]{:S(2)}, u32[]{:S(2)}) collective-permute-start(bf16[384,1536]{1,0:T(8,128)(2,1)} %bitcast.21.refs_9_.grad_ref), channel_id=1, source_target_pairs={{0,8},{4,12},{8,0},{12,4},{16,24},{20,28},{24,16},{28,20},{1,9},{5... | collective-permute-start | bytes 3538952 | tf_op jit(solution)/shard_map/ppermute | solution.py:801
  264.9 108.6 %collective-permute-start.27 = (bf16[384,1536]{1,0:T(8,128)(2,1)}, bf16[384,1536]{1,0:T(8,128)(2,1)}, u32[]{:S(2)}, u32[]{:S(2)}) collective-permute-start(bf16[384,1536]{1,0:T(8,128)(2,1)} %get-tuple-element.194.refs_8_), channel_id=1, source_target_pairs={{0,24},{4,28},{8,16},{12,20},{16,8},{20,12},{24,0},{28,4},{1,25},{... | collective-permute-start | bytes 3538952 | tf_op jit(solution)/shard_map/ppermute | solution.py:801
  265.5 108.0 %collective-permute-start.28 = (bf16[384,1536]{1,0:T(8,128)(2,1)}, bf16[384,1536]{1,0:T(8,128)(2,1)}, u32[]{:S(2)}, u32[]{:S(2)}) collective-permute-start(bf16[384,1536]{1,0:T(8,128)(2,1)} %bitcast.21.refs_9_.grad_ref), channel_id=1, source_target_pairs={{0,24},{4,28},{8,16},{12,20},{16,8},{20,12},{24,0},{28,4},{1,25},{... | collective-permute-start | bytes 3538952 | tf_op jit(solution)/shard_map/ppermute | solution.py:801
  297.8 106.4 %collective-permute-start.29 = (bf16[384,1664]{1,0:T(8,128)(2,1)}, bf16[384,1664]{1,0:T(8,128)(2,1)}, u32[]{:S(2)}, u32[]{:S(2)}) collective-permute-start(bf16[384,1664]{1,0:T(8,128)(2,1)} %get-tuple-element.204), channel_id=1, source_target_pairs={{0,16},{4,20},{8,24},{12,28},{16,0},{20,4},{24,8},{28,12},{1,17},{... | collective-permute-start | bytes 3833864 | tf_op jit(solution)/shard_map/ppermute | solution.py:801
  372.0 33.7 %collective-permute-start.30 = (bf16[384,1664]{1,0:T(8,128)(2,1)}, bf16[384,1664]{1,0:T(8,128)(2,1)}, u32[]{:S(2)}, u32[]{:S(2)}) collective-permute-start(bf16[384,1664]{1,0:T(8,128)(2,1)} %get-tuple-element.205), channel_id=1, source_target_pairs={{0,8},{4,12},{8,0},{12,4},{16,24},{20,28},{24,16},{28,20},{1,9},{5... | collective-permute-start | bytes 3833864 | tf_op jit(solution)/shard_map/ppermute | solution.py:801
  403.5 29.6 %collective-permute-start.31 = (bf16[384,1664]{1,0:T(8,128)(2,1)}, bf16[384,1664]{1,0:T(8,128)(2,1)S(1)}, u32[]{:S(2)}, u32[]{:S(2)}) collective-permute-start(bf16[384,1664]{1,0:T(8,128)(2,1)} %get-tuple-element.206), channel_id=1, source_target_pairs={{0,24},{4,28},{8,16},{12,20},{16,8},{20,12},{24,0},{28,4},{1,25},{... | collective-permute-start | bytes 3833864 | tf_op jit(solution)/shard_map/ppermute | solution.py:801
  445.7 31.3 %collective-permute-start.32 = (bf16[384,1664]{1,0:T(8,128)(2,1)}, bf16[384,1664]{1,0:T(8,128)(2,1)}, u32[]{:S(2)}, u32[]{:S(2)}) collective-permute-start(bf16[384,1664]{1,0:T(8,128)(2,1)} %get-tuple-element.210), channel_id=1, source_target_pairs={{0,16},{4,20},{8,24},{12,28},{16,0},{20,4},{24,8},{28,12},{1,17},{... | collective-permute-start | bytes 3833864 | tf_op jit(solution)/shard_map/ppermute | solution.py:801
  446.2 54.9 %collective-permute-start.33 = (bf16[384,1664]{1,0:T(8,128)(2,1)}, bf16[384,1664]{1,0:T(8,128)(2,1)}, u32[]{:S(2)}, u32[]{:S(2)}) collective-permute-start(bf16[384,1664]{1,0:T(8,128)(2,1)} %get-tuple-element.211), channel_id=1, source_target_pairs={{0,8},{4,12},{8,0},{12,4},{16,24},{20,28},{24,16},{28,20},{1,9},{5... | collective-permute-start | bytes 3833864 | tf_op jit(solution)/shard_map/ppermute | solution.py:801
  452.0 70.8 %copy-start.62 = (s32[384]{0:T(512)}, s32[384]{0:T(512)S(1)}, u32[]{:S(2)}) copy-start(s32[384]{0:T(512)S(1)} %get-tuple-element.296) | copy-start | bytes 4612
  452.0 70.8 %copy-start.63 = (s32[384]{0:T(512)}, s32[384]{0:T(512)S(1)}, u32[]{:S(2)}) copy-start(s32[384]{0:T(512)S(1)} %get-tuple-element.297) | copy-start | bytes 4612
  452.0 67.9 %collective-permute-start.34 = (bf16[384,1664]{1,0:T(8,128)(2,1)}, bf16[384,1664]{1,0:T(8,128)(2,1)}, u32[]{:S(2)}, u32[]{:S(2)}) collective-permute-start(bf16[384,1664]{1,0:T(8,128)(2,1)} %get-tuple-element.212), channel_id=1, source_target_pairs={{0,24},{4,28},{8,16},{12,20},{16,8},{20,12},{24,0},{28,4},{1,25},{... | collective-permute-start | bytes 3833864 | tf_op jit(solution)/shard_map/ppermute | solution.py:801
  501.2 185.1 %all-gather.9.cloned.1.call-start = ((), (), s32[]{:S(2)}) async-start(), calls=%async_computation.4 | async-start | bytes 8110080 | tf_op jit(solution)/shard_map/all_gather | solution.py:1079
  528.6 8.1 %collective-permute-start.35 = (bf16[2,4,48,768]{3,2,1,0:T(8,128)(2,1)}, bf16[2,4,48,768]{3,2,1,0:T(8,128)(2,1)}, u32[]{:S(2)}, u32[]{:S(2)}) collective-permute-start(bf16[2,4,48,768]{3,2,1,0:T(8,128)(2,1)} %dynamic-slice_bitcast_fusion), channel_id=1, source_target_pairs={{0,4},{4,0},{8,12},{12,8},{16,20},{20,16},{24,28},{28,24},{1,5},{5... | collective-permute-start | bytes 1769480 | tf_op jit(solution)/shard_map/ppermute | solution.py:801
  536.2 2.6 collective-permute-start.39
  537.9 15.9 %collective-permute-start.36 = (bf16[1,4,48,768]{3,2,1,0:T(8,128)(2,1)S(1)}, bf16[1,4,48,768]{3,2,1,0:T(8,128)(2,1)S(1)}, u32[]{:S(2)}, u32[]{:S(2)}) collective-permute-start(bf16[1,4,48,768]{3,2,1,0:T(8,128)(2,1)S(1)} %constant_dynamic-slice_fusion.2), channel_id=1, source_target_pairs={{0,8},{4,12},{8,0},{12,4},{16,24},{20,28},{24,16},{28,20},{1,9},{5... | collective-permute-start | bytes 884744 | tf_op jit(solution)/shard_map/ppermute | solution.py:801
  553.9 48.8 %copy-start.2 = (s32[8]{0:T(128)S(1)}, s32[8]{0:T(128)}, u32[]{:S(2)}) copy-start(s32[8]{0:T(128)} %constant.283.clone) | copy-start | bytes 100
  554.0 15.2 %collective-permute-start.37 = (bf16[2,48,768]{2,1,0:T(8,128)(2,1)S(1)}, bf16[2,48,768]{2,1,0:T(8,128)(2,1)S(1)}, u32[]{:S(2)}, u32[]{:S(2)}) collective-permute-start(bf16[2,48,768]{2,1,0:T(8,128)(2,1)S(1)} %dynamic-slice_bitcast_fusion.2), channel_id=1, source_target_pairs={{0,1},{1,0},{2,3},{3,2},{4,5},{5,4},{6,7},{7,6},{8,9},{9,8},{10,11... | collective-permute-start | bytes 442376 | tf_op jit(solution)/shard_map/ppermute | solution.py:804
  555.4 51.1 %copy-start.3 = (bf16[3,128,1536]{2,1,0:T(8,128)(2,1)S(1)}, bf16[3,128,1536]{2,1,0:T(8,128)(2,1)}, u32[]{:S(2)}) copy-start(bf16[3,128,1536]{2,1,0:T(8,128)(2,1)} %param.31) | copy-start | bytes 3538948
  555.5 23.1 %collective-permute-start.40 = (bf16[2,48,1792]{2,1,0:T(8,128)(2,1)S(1)}, bf16[2,48,1792]{2,1,0:T(8,128)(2,1)S(1)}, u32[]{:S(2)}, u32[]{:S(2)}) collective-permute-start(bf16[2,48,1792]{2,1,0:T(8,128)(2,1)S(1)} %dynamic-slice_bitcast_fusion.1), channel_id=1, source_target_pairs={{0,1},{1,0},{2,3},{3,2},{4,5},{5,4},{6,7},{7,6},{8,9},{9,8},{10,11... | collective-permute-start | bytes 1032200 | tf_op jit(solution)/shard_map/ppermute | solution.py:804
  569.2 43.7 %copy-start.5 = (f32[384,1536]{1,0:T(8,128)S(1)}, f32[384,1536]{1,0:T(8,128)}, u32[]{:S(2)}) copy-start(f32[384,1536]{1,0:T(8,128)} %get-tuple-element.162.middle_ref) | copy-start | bytes 7077892
  569.2 9.5 %collective-permute-start.38 = (bf16[1,48,768]{2,1,0:T(8,128)(2,1)S(1)}, bf16[1,48,768]{2,1,0:T(8,128)(2,1)S(1)}, u32[]{:S(2)}, u32[]{:S(2)}) collective-permute-start(bf16[1,48,768]{2,1,0:T(8,128)(2,1)S(1)} %constant_dynamic-slice_fusion.1), channel_id=1, source_target_pairs={{0,2},{1,3},{2,0},{3,1},{4,6},{5,7},{6,4},{7,5},{8,10},{9,11},{10,... | collective-permute-start | bytes 221192 | tf_op jit(solution)/shard_map/ppermute | solution.py:804
  578.7 9.2 %collective-permute-start.41 = (bf16[1,48,1792]{2,1,0:T(8,128)(2,1)S(1)}, bf16[1,48,1792]{2,1,0:T(8,128)(2,1)S(1)}, u32[]{:S(2)}, u32[]{:S(2)}) collective-permute-start(bf16[1,48,1792]{2,1,0:T(8,128)(2,1)S(1)} %constant_dynamic-slice_fusion), channel_id=1, source_target_pairs={{0,2},{1,3},{2,0},{3,1},{4,6},{5,7},{6,4},{7,5},{8,10},{9,11},{10,... | collective-permute-start | bytes 516104 | tf_op jit(solution)/shard_map/ppermute | solution.py:804
  625.7 2.0 collective-permute-start.42
  627.7 5.4 collective-permute-start.43
  633.2 9.2 %collective-permute-start.44 = (bf16[48,896]{1,0:T(8,128)(2,1)S(1)}, bf16[48,896]{1,0:T(8,128)(2,1)S(1)}, u32[]{:S(2)}, u32[]{:S(2)}) collective-permute-start(bf16[48,896]{1,0:T(8,128)(2,1)S(1)} %fusion.64), channel_id=1, source_target_pairs={{0,1},{1,0},{2,3},{3,2},{4,5},{5,4},{6,7},{7,6},{8,9},{9,8},{10,11... | collective-permute-start | bytes 258056 | tf_op jit(solution)/shard_map/ppermute | solution.py:804
  634.1 13.8 %collective-permute-start.45 = (bf16[48,896]{1,0:T(8,128)(2,1)S(1)}, bf16[48,896]{1,0:T(8,128)(2,1)S(1)}, u32[]{:S(2)}, u32[]{:S(2)}) collective-permute-start(bf16[48,896]{1,0:T(8,128)(2,1)S(1)} %fusion.64), channel_id=1, source_target_pairs={{0,2},{1,3},{2,0},{3,1},{4,6},{5,7},{6,4},{7,5},{8,10},{9,11},{10,... | collective-permute-start | bytes 258056 | tf_op jit(solution)/shard_map/ppermute | solution.py:804
  635.1 12.8 %collective-permute-start.46 = (bf16[48,896]{1,0:T(8,128)(2,1)S(1)}, bf16[48,896]{1,0:T(8,128)(2,1)S(1)}, u32[]{:S(2)}, u32[]{:S(2)}) collective-permute-start(bf16[48,896]{1,0:T(8,128)(2,1)S(1)} %fusion.64), channel_id=1, source_target_pairs={{0,3},{1,2},{2,1},{3,0},{4,7},{5,6},{6,5},{7,4},{8,11},{9,10},{10,... | collective-permute-start | bytes 258056 | tf_op jit(solution)/shard_map/ppermute | solution.py:804
  647.9 5.8 collective-permute-start.47
  653.8 8.0 %collective-permute-start.48 = (bf16[2,48,896]{2,1,0:T(8,128)(2,1)S(1)}, bf16[2,48,896]{2,1,0:T(8,128)(2,1)S(1)}, u32[]{:S(2)}, u32[]{:S(2)}) collective-permute-start(bf16[2,48,896]{2,1,0:T(8,128)(2,1)S(1)} %pad_maximum_fusion.9), channel_id=1, source_target_pairs={{0,16},{4,20},{8,24},{12,28},{16,0},{20,4},{24,8},{28,12},{1,17},{... | collective-permute-start | bytes 516104 | tf_op jit(solution)/shard_map/ppermute | solution.py:801
  661.8 2.1 collective-permute-start.49
  (69 other events, 473.3 us)
Sparse Core Ops, SparseCore 0:
  13.6 32.9 all-gather.4
  55.0 77.6 all-gather.6
  501.3 100.0 reduce-scatter.1
  605.1 81.0 all-gather.8

commit v3 on v2

--- a/solution.py
+++ b/solution.py
@@ -871,20 +871,21 @@
     w_key = w_kv[:, :kv_width]
     w_value = w_kv[:, kv_width:]
 
-    query_shrink, key_shrink, value_shrink, output_shrink, gate_shrink, up_shrink = [
+    query_shrink, key_shrink, value_shrink, output_shrink = [
         shrink_of(value)
         for value in (
-            query_reduce_factors, key_reduce_factors, value_reduce_factors,
-            output_reduce_factors, gate_reduce_factors, upper_reduce_factors,
+            query_reduce_factors, key_reduce_factors, value_reduce_factors, output_reduce_factors,
         )
     ]
-    query_expand, key_expand, value_expand, output_expand, down_expand = [
+    query_expand, key_expand, value_expand, output_expand = [
         expand_of(value)
         for value in (
-            query_lift_factors, key_lift_factors, value_lift_factors,
-            output_lift_factors, down_lift_factors,
+            query_lift_factors, key_lift_factors, value_lift_factors, output_lift_factors,
         )
     ]
+    w_kv, output_shrink, output_expand, query_shrink, query_expand = lax.optimization_barrier(
+        (w_kv, output_shrink, output_expand, query_shrink, query_expand)
+    )
 
     def narrowed(value, shrink):
         return (mm(value, shrink) * mixing).astype(BF)
@@ -904,10 +905,23 @@
             found += [part, swap(part, 1)]
         return found
 
+    late_lift = (
+        gate_lift_factors, upper_lift_factors, down_reduce_factors, down_lift_factors,
+        gate_reduce_factors, upper_reduce_factors,
+    )
+    gate_shrink, up_shrink = shrink_of(late_lift[4]), shrink_of(late_lift[5])
+    down_expand = expand_of(late_lift[3])
+    reduce_factors = [
+        (
+            jnp.concatenate([shrink_of(late_lift[4], f), shrink_of(late_lift[5], f)], axis=1),
+            expand_of(late_lift[3], f),
+        )
+        for f in range(fsdp_n)
+    ]
     query_rot, query_narrow, w_query = with_blocks(
         queries_kernel, "queries", seqs, me, after(both_cores(rows_q), pair),
         [
-            after(normed, rows_o, g0_pieces), query_shrink, query_expand, query_bias.astype(F32)[None], flat_cosine,
+            after(normed, rows_o, g0_pieces, reduce_factors, gate_shrink, up_shrink, down_expand), query_shrink, query_expand, query_bias.astype(F32)[None], flat_cosine,
             sine_signed,
         ],
         [
@@ -919,27 +933,18 @@
     attended, lse = attend(info, query_rot, pair_all, seqs, spans, span_len)
     for k in range(1, chips):
         blocks[k] = swap(after(parts[k], pair_all, query_rot), 2 * k)
-    late_lift = after(
-        (gate_lift_factors, upper_lift_factors, down_reduce_factors), attended, blocks
-    )
-    lift_g = lax.dynamic_index_in_dim(by_chip(late_lift[0]), chip, 0, keepdims=False)
-    lift_u = lax.dynamic_index_in_dim(by_chip(late_lift[1]), chip, 0, keepdims=False)
+    late_down, late_gate, late_up = after(
+        (down_reduce_factors, gate_lift_factors, upper_lift_factors), attended, blocks
+    )
     shrink_d = jnp.pad(
-        lax.dynamic_slice_in_dim(late_lift[2], chip * hq, hq, 0), ((0, pad), (0, 0))
-    )
+        lax.dynamic_slice_in_dim(late_down, chip * hq, hq, 0), ((0, pad), (0, 0))
+    )
+    lift_g = lax.dynamic_index_in_dim(by_chip(late_gate), chip, 0, keepdims=False)
+    lift_u = lax.dynamic_index_in_dim(by_chip(late_up), chip, 0, keepdims=False)
+    lift_factors = [(expand_of(lift_g, f), expand_of(lift_u, f)) for f in range(fsdp_n)]
     feed_factors = [
-        (
-            jnp.concatenate(
-                [shrink_of(gate_reduce_factors, f), shrink_of(upper_reduce_factors, f)], axis=1
-            ),
-            expand_of(down_lift_factors, f),
-            expand_of(lift_g, f),
-            expand_of(lift_u, f),
-            shrink_of(shrink_d, f),
-        )
-        for f in range(fsdp_n)
+        reduce_factors[f] + lift_factors[f] + (shrink_of(shrink_d, f),) for f in range(fsdp_n)
     ]
-
     output_blocks = both_cores(after(rows_o, query_rot))
     down_rows = [down_weight, swap(after(down_weight, query_rot), 1)]
     w_down = assemble(core, after(down_rows, attended), hp)
@@ -977,10 +982,21 @@
     for k in early_first:
         f = 2 * k // cp_n
         sgu, ed, eg, eu, sd = feed_factors[f]
-        if len(out_raw) == 1:
+        if len(out_raw) == 2 or (len(out_raw) == 1 and chips == 2):
+            middle_row = tokens // 2
             for other in range(3, chips):
-                n2_pieces.append(swap(after(normed_two, out_raw[0]), 2 * other))
-                g0_pieces[other] = swap(after(grad_low, out_raw[0]), 2 * other)
+                for pieces in (n2_pieces, g0_pieces):
+                    first, second = after((pieces[2], pieces[1]), out_raw[0])
+                    if other == 3:
+                        piece = jnp.concatenate(
+                            [swap(first[:middle_row], 2), swap(second[middle_row:], 4)], axis=0
+                        )
+                    else:
+                        piece = swap(after(pieces[0], out_raw[0]), 2 * other)
+                    if pieces is n2_pieces:
+                        n2_pieces.append(piece)
+                    else:
+                        g0_pieces[other] = piece
         if out_raw:
             sums[f] = after(sums[f], out_raw[-1])
         out_k, ng_k, *sums[f] = feed(
@@ -1006,10 +1022,13 @@
         return (mm_nt(grad, expand) * mixing).astype(BF)
 
     out_raw = after(out_raw, middle_low)
-    out_parts = [swap(part, 2 * k) if k else part for k, part in zip(early_first, out_raw)]
+    out_parts = [swap(part, 2 * k) if k else part for k, part in zip(early_first[:3], out_raw)]
     query_rot_grad, pair_part = attend_back(
         info, query_rot, attended_grad, attended, pair_all, lse, seqs, spans, span_len
     )
+    out_parts += [
+        swap(after(part, pair_part), 2 * k) for k, part in zip(early_first[3:], out_raw[3:])
+    ]
     pair_grad = lax.psum_scatter(
         after(pair_part, out_parts[:3]), ("cp", "seq"), scatter_dimension=1, tiled=True
     ).reshape(tokens, 2 * kv_width)
@@ -1022,6 +1041,7 @@
     query_rot_grad, sums, middle_late, output_back, gate_back, up_back = after(
         (query_rot_grad, sums, middle_low, output_back, gate_back, up_back), out_parts[:3]
     )
+    cosine, sine_table = after((cosine, sine_table), pair_part)
     query_grad = (
         unrotate(
             query_rot_grad.reshape(tokens, -1, HEAD_DIM).astype(F32), cosine, sine_table

time: 713 us -> 691 us (0.969)
  waiting for transfers between devices: 283 us -> 234 us
  Pallas kernels: 212 us -> 224 us
  starting transfers between devices: 43.7 us -> 55.7 us
    ppermute x43 -> x45, waiting for transfers between devices: 208 us -> 153 us  [swap(): return lax.ppermute(value, PLANE, [(i, i ^ k) for i in range(plane)])]
    ppermute x43 -> x45, starting transfers between devices: 36.6 us -> 45.7 us  [swap(): return lax.ppermute(value, PLANE, [(i, i ^ k) for i in range(plane)])]
    all_gather x1, waiting for transfers between devices: 4.73 us -> 12.7 us  [body(): lax.all_gather(pair.reshape(seqs, tok_rows, 2 * kv_width), ('cp', 'seq'),...]
  transfers between devices with their start and end apart: 54 -> 56, of which waited for: 27 -> 26; matrix products, arithmetic and copies ran while one was open for 20% -> 22% of each run, Pallas kernels for 26% -> 29%
where the time goes in v3:
time: 691 us; the launch traced here: 684 us
  waiting for transfers between devices  234 us (34%)
  Pallas kernels  224 us (32%)
  other arithmetic  57.1 us (8%)
  local copies, waits for them, and re-layouts  55.8 us (8%)
  starting transfers between devices  55.7 us (8%)
  matrix products  42.5 us (6%)
  between operations  15.7 us (2%)
    ppermute x45, waiting for transfers between devices, swap(): return lax.ppermute(value, PLANE, [(i, i ^ k) for i in range(plane)])  153 us
    pallas_call x4, Pallas kernels, feed(): pl.pallas_call(functools.partial(feed_kernel, seqs, tuple(kinds)), grid_s...  120 us
    ppermute x45, starting transfers between devices, swap(): return lax.ppermute(value, PLANE, [(i, i ^ k) for i in range(plane)])  45.7 us
    ppermute x7, waiting for transfers between devices, swap_seq(): return lax.ppermute(value, 'seq', [(i, i ^ k) for i in range(seq_n)])  44.8 us
    pallas_call x1, Pallas kernels, attend_back(): pl.pallas_call(functools.partial(attend_back_kernel, spans, span_len, tok...  29 us
    dot_general x21, matrix products, mm_tn(): lax.dot_general(left, right, (((0,), (0,)), ((), ())), preferred_element_...  23.2 us
    pallas_call x1, Pallas kernels, attend(): pl.pallas_call(functools.partial(attend_kernel, spans, span_len, tokens),...  22.3 us
    pallas_call x2, Pallas kernels, with_blocks(): pl.pallas_call(functools.partial(kernel, seqs, count), grid_spec=pltpu.Pr...  16.2 us
  transfers between devices with their start and end apart: 56, of which 26 were waited for; matrix products, arithmetic and copies ran while one was open for 22% of the time, Pallas kernels for 29%

profile of v3, /device:TPU:0, one launch (start us, length us, event | category | flops | bytes accessed | tf_op | source)
XLA Modules:
  0.0 684.0 jit_solution(13964596481347579133)
XLA Ops:
  7.2 3.0 collective-permute-start
  14.8 1.9 collective-permute-start.7
  16.8 4.1 fusion.120
  20.8 1.9 fusion.119
  30.8 3.3 fusion.10
  36.0 9.8 %collective-permute-done.7 = f32[8,128]{0,1:T(8,128)} collective-permute-done((f32[8,128]{0,1:T(8,128)}, f32[8,128]{0,1:T(8,128)}, u32[]{:S(2)}, u32[]{:S(2)}) %collective-permute-start.7) | collective-permute-done | bytes 4128 | tf_op jit(solution)/shard_map/ppermute | solution.py:801
  54.6 2.0 convolution_convert_fusion.17.eo_ref.oe_ref
  56.6 4.3 keys_values.1
  68.1 2.7 collective-permute-start.5
  74.3 2.0 copy.101
  77.2 1.9 convolution_convert_fusion.14.refs_11_
  79.1 2.5 pad_maximum_fusion.5
  81.6 5.8 collective-permute-done.3.refs_2_
  87.4 18.6 %collective-permute-done.4.refs_4_ = bf16[192,1536]{1,0:T(8,128)(2,1)} collective-permute-done((bf16[192,1536]{1,0:T(8,128)(2,1)}, bf16[192,1536]{1,0:T(8,128)(2,1)}, u32[]{:S(2)}, u32[]{:S(2)}) %collective-permute-start.4) | collective-permute-done | bytes 589856 | tf_op jit(solution)/shard_map/ppermute | solution.py:801
  106.0 12.0 %collective-permute-done.5.refs_6_ = bf16[192,1536]{1,0:T(8,128)(2,1)} collective-permute-done((bf16[192,1536]{1,0:T(8,128)(2,1)}, bf16[192,1536]{1,0:T(8,128)(2,1)}, u32[]{:S(2)}, u32[]{:S(2)}) %collective-permute-start.5) | collective-permute-done | bytes 589856 | tf_op jit(solution)/shard_map/ppermute | solution.py:801
  118.1 7.5 %queries.1 = (bf16[384,1536]{1,0:T(8,128)(2,1)}, bf16[384,64]{1,0:T(8,128)(2,1)}, bf16[1536,1536]{1,0:T(8,128)(2,1)}) custom-call(s32[1]{0:T(128)} %bitcast.info, bf16[384,1536]{1,0:T(8,128)(2,1)} %get-tuple-element.157.normed_ref, bf16[1536,64]{1,0:T(8,128)(2,1)} %bitcast.195, bf16[64,1536]{1,0:T(8,128)(2,1)} %convolution_convert_fusion.16.eq_ref, ...), custom_call_target="tpu_custom_call" | custom-call | flops 1811939328 | bytes 9437184 | tf_op jit(solution)/shard_map/queries/pallas_call | solution.py:479
  126.1 12.7 %all-gather.7.cloned.1.call-done.k_ref.v_ref = bf16[3,2048,512]{2,1,0:T(8,128)(2,1)} async-done(((bf16[3,128,512]{2,1,0:T(8,128)(2,1)}), bf16[3,2048,512]{2,1,0:T(8,128)(2,1)}) %all-gather.7.cloned.1.call-update) | async-done | bytes 6291472 | tf_op jit(solution)/shard_map/all_gather | solution.py:898
  146.2 22.3 %attend.1 = (bf16[384,1536]{1,0:T(8,128)(2,1)}, f32[6,8,768]{2,1,0:T(8,128)}) custom-call(s32[29]{0:T(128)} %pad_add_fusion.info, bf16[384,1536]{1,0:T(8,128)(2,1)} %get-tuple-element.169.q_ref, bf16[3,2048,512]{2,1,0:T(8,128)(2,1)} %all-gather.7.cloned.1.call-done.k_ref.v_ref, bf16[3,2048,512]{2,1,0:T(8,128)(2,1)} %all-gather.7.cloned.1.call-done.k_ref.v_ref), custom_call_target="tpu_custom_call" | custom-call | flops 4831838208 | bytes 6291456 | tf_op jit(solution)/shard_map/attend/pallas_call | solution.py:152
  168.5 5.0 assemble.1.refs_12_
  175.0 8.7 %outputs.1 = (f32[384,1536]{1,0:T(8,128)}, bf16[384,1536]{1,0:T(8,128)(2,1)}, bf16[384,64]{1,0:T(8,128)(2,1)}, bf16[1536,1536]{1,0:T(8,128)(2,1)}) custom-call(s32[1]{0:T(128)} %bitcast.info, bf16[384,1536]{1,0:T(8,128)(2,1)} %get-tuple-element.170.attended_ref.o_ref, bf16[384,1536]{1,0:T(8,128)(2,1)} %bitcast.188, f32[1,1536]{1,0:T(1,128)} %reshape.458.gain_ref, ...), custom_call_target="tpu_custom_call" | custom-call | flops 1811939328 | bytes 9437184 | tf_op jit(solution)/shard_map/outputs/pallas_call | solution.py:479
  183.7 34.1 %collective-permute-done.19.refs_4_ = bf16[2,192,2304]{2,1,0:T(8,128)(2,1)} collective-permute-done((bf16[2,192,2304]{2,1,0:T(8,128)(2,1)}, bf16[2,192,2304]{2,1,0:T(8,128)(2,1)}, u32[]{:S(2)}, u32[]{:S(2)}) %collective-permute-start.19) | collective-permute-done | bytes 1769504 | tf_op jit(solution)/shard_map/ppermute | solution.py:801
  230.4 2.1 collective-permute-done.22.refs_7_
  232.7 2.5 collective-permute-done.18.refs_3_
  238.2 29.9 %feed.4 = (bf16[384,1664]{1,0:T(8,128)(2,1)}, bf16[384,1664]{1,0:T(8,128)(2,1)}, f32[64,2304]{1,0:T(8,128)}, f32[64,2304]{1,0:T(8,128)}, f32[64,2304]{1,0:T(8,128)}) custom-call(s32[2]{0:T(128)} %pad_add_fusion.1.info, bf16[2,192,2304]{2,1,0:T(8,128)(2,1)} %get-tuple-element.179.refs_0_, bf16[2,192,2304]{2,1,0:T(8,128)(2,1)} %collective-permute-done.16.refs_1_, ...), custom_call_target="tpu_custom_call" | custom-call | flops 16986931200 | bytes 21233664 | tf_op jit(solution)/shard_map/feed/pallas_call | solution.py:603
  271.1 29.9 %feed.5 = (bf16[384,1664]{1,0:T(8,128)(2,1)}, bf16[384,1664]{1,0:T(8,128)(2,1)}, f32[64,2304]{1,0:T(8,128)}, f32[64,2304]{1,0:T(8,128)}, f32[64,2304]{1,0:T(8,128)}) custom-call(s32[2]{0:T(128)} %pad_add_fusion.1.info, bf16[2,192,2304]{2,1,0:T(8,128)(2,1)} %get-tuple-element.179.refs_0_, bf16[2,192,2304]{2,1,0:T(8,128)(2,1)} %collective-permute-done.16.refs_1_, ...), custom_call_target="tpu_custom_call" | custom-call | flops 16986931200 | bytes 21233664 | tf_op jit(solution)/shard_map/feed/pallas_call | solution.py:603
  301.6 1.9 slice.193
  304.1 1.9 slice.194
  310.1 1.9 slice.192
  312.6 30.1 %feed.6 = (bf16[384,1664]{1,0:T(8,128)(2,1)}, bf16[384,1664]{1,0:T(8,128)(2,1)}, f32[64,2304]{1,0:T(8,128)}, f32[64,2304]{1,0:T(8,128)}, f32[64,2304]{1,0:T(8,128)}) custom-call(s32[2]{0:T(128)} %pad_add_fusion.1.info, bf16[2,192,2304]{2,1,0:T(8,128)(2,1)} %get-tuple-element.179.refs_0_, bf16[2,192,2304]{2,1,0:T(8,128)(2,1)} %collective-permute-done.16.refs_1_, ...), custom_call_target="tpu_custom_call" | custom-call | flops 16986931200 | bytes 21233664 | tf_op jit(solution)/shard_map/feed/pallas_call | solution.py:603
  345.0 2.4 pad_maximum_fusion.2.refs_9_
  347.4 8.5 %collective-permute-done.28 = bf16[192,1536]{1,0:T(8,128)(2,1)} collective-permute-done((bf16[192,1536]{1,0:T(8,128)(2,1)}, bf16[192,1536]{1,0:T(8,128)(2,1)}, u32[]{:S(2)}, u32[]{:S(2)}) %collective-permute-start.28) | collective-permute-done | bytes 589856 | tf_op jit(solution)/shard_map/ppermute | solution.py:801
  355.9 2.3 pad_maximum_fusion.1.refs_8_
  358.2 30.0 %feed.7 = (bf16[384,1664]{1,0:T(8,128)(2,1)}, bf16[384,1664]{1,0:T(8,128)(2,1)}, f32[64,2304]{1,0:T(8,128)}, f32[64,2304]{1,0:T(8,128)}, f32[64,2304]{1,0:T(8,128)}) custom-call(s32[2]{0:T(128)} %pad_add_fusion.1.info, bf16[2,192,2304]{2,1,0:T(8,128)(2,1)} %get-tuple-element.179.refs_0_, bf16[2,192,2304]{2,1,0:T(8,128)(2,1)} %collective-permute-done.16.refs_1_, ...), custom_call_target="tpu_custom_call" | custom-call | flops 16986931200 | bytes 21233664 | tf_op jit(solution)/shard_map/feed/pallas_call | solution.py:603
  390.4 3.0 convert_add_fusion.1.most_ref
  393.5 24.4 %collective-permute-done.33.last_ref = bf16[384,1664]{1,0:T(8,128)(2,1)} collective-permute-done((bf16[384,1664]{1,0:T(8,128)(2,1)}, bf16[384,1664]{1,0:T(8,128)(2,1)}, u32[]{:S(2)}, u32[]{:S(2)}) %collective-permute-start.33) | collective-permute-done | bytes 1277984 | tf_op jit(solution)/shard_map/ppermute | solution.py:801
  417.8 11.5 %before_attention.1 = (f32[384,1536]{1,0:T(8,128)}, bf16[384,1536]{1,0:T(8,128)(2,1)}, bf16[384,64]{1,0:T(8,128)(2,1)}, bf16[384,64]{1,0:T(8,128)(2,1)}, bf16[38...) custom-call(f32[384,1664]{1,0:T(8,128)} %convert_add_fusion.1.most_ref, bf16[384,1664]{1,0:T(8,128)(2,1)} %collective-permute-done.33.last_ref, ...), custom_call_target="tpu_custom_call" | custom-call | flops 1811939328 | bytes 17694720 | tf_op jit(solution)/shard_map/before_attention/pallas_call | solution.py:398
  431.3 29.0 %attend_back.1 = (bf16[384,1536]{1,0:T(8,128)(2,1)}, bf16[3,2048,512]{2,1,0:T(8,128)(2,1)}) custom-call(s32[29]{0:T(128)} %pad_add_fusion.info, bf16[384,1536]{1,0:T(8,128)(2,1)} %get-tuple-element.169.q_ref, bf16[384,1536]{1,0:T(8,128)(2,1)} %get-tuple-element.230.do_ref, bf16[384,1536]{1,0:T(8,128)(2,1)} %get-tuple-element.170.attended_ref.o_ref, ...), custom_call_target="tpu_custom_call" | custom-call | flops 12079595520 | bytes 12582912 | tf_op jit(solution)/shard_map/attend_back/pallas_call | solution.py:253
  462.8 2.0 copy.106
  464.9 7.2 %collective-permute-start.36 = (bf16[384,1664]{1,0:T(8,128)(2,1)}, bf16[384,1664]{1,0:T(8,128)(2,1)}, u32[]{:S(2)}, u32[]{:S(2)}) collective-permute-start(bf16[384,1664]{1,0:T(8,128)(2,1)} %get-tuple-element.233), channel_id=1, source_target_pairs={{0,24},{4,28},{8,16},{12,20},{16,8},{20,12},{24,0},{28,4},{1,25},{... | collective-permute-start | bytes 3833864 | tf_op jit(solution)/shard_map/ppermute | solution.py:801
  477.6 3.0 copy.109
  480.7 2.6 add_convert_fusion
  489.4 7.2 %collective-permute-done.36 = bf16[384,1664]{1,0:T(8,128)(2,1)} collective-permute-done((bf16[384,1664]{1,0:T(8,128)(2,1)}, bf16[384,1664]{1,0:T(8,128)(2,1)}, u32[]{:S(2)}, u32[]{:S(2)}) %collective-permute-start.36) | collective-permute-done | bytes 1277984 | tf_op jit(solution)/shard_map/ppermute | solution.py:801
  496.6 2.8 convert_add_fusion
  499.4 2.8 fusion.112
  514.5 2.8 collective-permute-start.38
  519.4 11.7 %collective-permute-done.38 = bf16[1,4,48,768]{3,2,1,0:T(8,128)(2,1)S(1)} collective-permute-done((bf16[1,4,48,768]{3,2,1,0:T(8,128)(2,1)S(1)}, bf16[1,4,48,768]{3,2,1,0:T(8,128)(2,1)S(1)}, u32[]{:S(2)}, u32[]{:S(2)}) %collective-permute-start.38) | collective-permute-done | bytes 294944 | tf_op jit(solution)/shard_map/ppermute | solution.py:801
  533.5 11.0 %collective-permute-done.39 = bf16[2,48,768]{2,1,0:T(8,128)(2,1)S(1)} collective-permute-done((bf16[2,48,768]{2,1,0:T(8,128)(2,1)S(1)}, bf16[2,48,768]{2,1,0:T(8,128)(2,1)S(1)}, u32[]{:S(2)}, u32[]{:S(2)}) %collective-permute-start.39) | collective-permute-done | bytes 147488 | tf_op jit(solution)/shard_map/ppermute | solution.py:804
  546.3 9.1 %collective-permute-done.42 = bf16[2,48,1792]{2,1,0:T(8,128)(2,1)S(1)} collective-permute-done((bf16[2,48,1792]{2,1,0:T(8,128)(2,1)S(1)}, bf16[2,48,1792]{2,1,0:T(8,128)(2,1)S(1)}, u32[]{:S(2)}, u32[]{:S(2)}) %collective-permute-start.42) | collective-permute-done | bytes 344096 | tf_op jit(solution)/shard_map/ppermute | solution.py:804
  556.8 13.1 %collective-permute-done.43 = bf16[1,48,1792]{2,1,0:T(8,128)(2,1)S(1)} collective-permute-done((bf16[1,48,1792]{2,1,0:T(8,128)(2,1)S(1)}, bf16[1,48,1792]{2,1,0:T(8,128)(2,1)S(1)}, u32[]{:S(2)}, u32[]{:S(2)}) %collective-permute-start.43) | collective-permute-done | bytes 172064 | tf_op jit(solution)/shard_map/ppermute | solution.py:804
  570.6 8.1 %reduce-scatter.2.cloned.1.call-done = bf16[3,128,512]{2,1,0:T(8,128)(2,1)} async-done(((bf16[3,2048,512]{2,1,0:T(8,128)(2,1)}), bf16[3,128,512]{2,1,0:T(8,128)(2,1)}) %reduce-scatter.2.cloned.1.call-update) | async-done | bytes 393232 | tf_op jit(solution)/shard_map/reduce_scatter | solution.py:1032
  586.7 2.0 gather_fusion
  590.2 3.7 fusion.8
  593.9 4.4 fusion.124
  598.9 3.3 last_grads.1
  606.9 3.2 collective-permute-done.45
  610.1 2.2 collective-permute-start.46
  615.2 5.0 collective-permute-done.46
  620.2 6.7 collective-permute-done.47
  628.1 3.3 collective-permute-done.49
  631.5 4.0 collective-permute-start.50
  635.5 6.6 collective-permute-done.50
  642.2 2.0 fusion.5
  649.8 15.1 %all-gather.9.cloned.1.call-done = bf16[1536,2560]{1,0:T(8,128)(2,1)} async-done(((bf16[48,2560]{1,0:T(8,128)(2,1)}), bf16[1536,2560]{1,0:T(8,128)(2,1)}) %all-gather.9.cloned.1.call-update) | async-done | bytes 7864336 | tf_op jit(solution)/shard_map/all_gather | solution.py:1099
  664.9 12.1 %expand.1 = (f32[128,8960]{1,0:T(8,128)}, f32[128,8960]{1,0:T(8,128)}, f32[8960,128]{1,0:T(8,128)}, f32[1536,128]{1,0:T(8,128)}, f32[1536,128]{1,0:T(8,128)}, /*...) custom-call(bf16[32,48,2560]{2,1,0:T(8,128)(2,1)} %bitcast.192, ...), custom_call_target="tpu_custom_call" | custom-call | flops 660602880 | bytes 13762560 | tf_op jit(solution)/shard_map/expand/pallas_call | solution.py:741
  (407 shorter events, 134.0 us)
Async XLA Ops:
  7.2 217.8 %copy-start = (bf16[8960,128]{1,0:T(8,128)(2,1)S(1)}, bf16[8960,128]{1,0:T(8,128)(2,1)}, u32[]{:S(2)}) copy-start(bf16[8960,128]{1,0:T(8,128)(2,1)} %param.59) | copy-start | bytes 6881284
  7.2 49.4 %all-gather.5.cloned.1.call-start = ((), (), s32[]{:S(2)}) async-start(), calls=%async_computation.1 | async-start | bytes 1769472 | tf_op jit(solution)/shard_map/all_gather | solution.py:843
  7.2 49.3 %collective-permute-start = (bf16[192,1536]{1,0:T(8,128)(2,1)}, bf16[192,1536]{1,0:T(8,128)(2,1)}, u32[]{:S(2)}, u32[]{:S(2)}) collective-permute-start(bf16[192,1536]{1,0:T(8,128)(2,1)} %refs_0_), channel_id=1, source_target_pairs={{0,8},{4,12},{8,0},{12,4},{16,24},{20,28},{24,16},{28,20},{1,9},{5... | collective-permute-start | bytes 1769480 | tf_op jit(solution)/shard_map/ppermute | solution.py:801
  10.3 46.3 %collective-permute-start.1 = (bf16[192,1536]{1,0:T(8,128)(2,1)}, bf16[192,1536]{1,0:T(8,128)(2,1)}, u32[]{:S(2)}, u32[]{:S(2)}) collective-permute-start(bf16[192,1536]{1,0:T(8,128)(2,1)} %refs_0_), channel_id=1, source_target_pairs={{0,16},{4,20},{8,24},{12,28},{16,0},{20,4},{24,8},{28,12},{1,17},{... | collective-permute-start | bytes 1769480 | tf_op jit(solution)/shard_map/ppermute | solution.py:801
  11.8 44.8 %collective-permute-start.2 = (bf16[192,1536]{1,0:T(8,128)(2,1)}, bf16[192,1536]{1,0:T(8,128)(2,1)}, u32[]{:S(2)}, u32[]{:S(2)}) collective-permute-start(bf16[192,1536]{1,0:T(8,128)(2,1)} %refs_0_), channel_id=1, source_target_pairs={{0,24},{4,28},{8,16},{12,20},{16,8},{20,12},{24,0},{28,4},{1,25},{... | collective-permute-start | bytes 1769480 | tf_op jit(solution)/shard_map/ppermute | solution.py:801
  13.5 125.3 %all-gather.7.cloned.1.call-start = ((), (), s32[]{:S(2)}) async-start(), calls=%async_computation.2 | async-start | bytes 6684672 | tf_op jit(solution)/shard_map/all_gather | solution.py:898
  14.8 30.9 %collective-permute-start.7 = (f32[8,128]{0,1:T(8,128)}, f32[8,128]{0,1:T(8,128)}, u32[]{:S(2)}, u32[]{:S(2)}) collective-permute-start(f32[8,128]{0,1:T(8,128)} %broadcast_in_dim.81), channel_id=1, source_target_pairs={{0,16},{4,20},{8,24},{12,28},{16,0},{20,4},{24,8},{28,12},{1,17},{... | collective-permute-start | bytes 12296 | tf_op jit(solution)/shard_map/ppermute | solution.py:801
  61.0 517.7 %reduce-scatter.2.cloned.1.call-start = ((), (), s32[]{:S(2)}) async-start(), calls=%async_computation.3 | async-start | bytes 6684672 | tf_op jit(solution)/shard_map/reduce_scatter | solution.py:1032
  62.8 4.5 collective-permute-start.10
  62.8 5.0 collective-permute-start.11
  63.3 4.8 collective-permute-start.8
  64.3 165.1 %copy-start.58 = (s32[64]{0:T(128)}, s32[64]{0:T(128)S(1)}, u32[]{:S(2)}) copy-start(s32[64]{0:T(128)S(1)} %pad.86) | copy-start | bytes 772
  64.3 53.8 %collective-permute-start.6 = (bf16[384,1536]{1,0:T(8,128)(2,1)}, bf16[384,1536]{1,0:T(8,128)(2,1)}, u32[]{:S(2)}, u32[]{:S(2)}) collective-permute-start(bf16[384,1536]{1,0:T(8,128)(2,1)} %bitcast.23.refs_9_.grad_ref), channel_id=1, source_target_pairs={{0,16},{4,20},{8,24},{12,28},{16,0},{20,4},{24,8},{28,12},{1,17},{... | collective-permute-start | bytes 3538952 | tf_op jit(solution)/shard_map/ppermute | solution.py:801
  67.0 14.6 %collective-permute-start.9 = (bf16[192,1536]{1,0:T(8,128)(2,1)}, bf16[192,1536]{1,0:T(8,128)(2,1)}, u32[]{:S(2)}, u32[]{:S(2)}) collective-permute-start(bf16[192,1536]{1,0:T(8,128)(2,1)} %collective-permute-done.refs_2_), channel_id=1, source_target_pairs={{0,4},{4,0},{8,12},{12,8},{16,20},{20,16},{24,28},{28,24},{1,5},{5... | collective-permute-start | bytes 1769480 | tf_op jit(solution)/shard_map/ppermute | solution.py:801
  67.3 20.1 %collective-permute-start.3 = (bf16[192,1536]{1,0:T(8,128)(2,1)}, bf16[192,1536]{1,0:T(8,128)(2,1)}, u32[]{:S(2)}, u32[]{:S(2)}) collective-permute-start(bf16[192,1536]{1,0:T(8,128)(2,1)} %refs_0_.1), channel_id=1, source_target_pairs={{0,8},{4,12},{8,0},{12,4},{16,24},{20,28},{24,16},{28,20},{1,9},{5... | collective-permute-start | bytes 1769480 | tf_op jit(solution)/shard_map/ppermute | solution.py:801
  67.8 38.2 %collective-permute-start.4 = (bf16[192,1536]{1,0:T(8,128)(2,1)}, bf16[192,1536]{1,0:T(8,128)(2,1)}, u32[]{:S(2)}, u32[]{:S(2)}) collective-permute-start(bf16[192,1536]{1,0:T(8,128)(2,1)} %refs_0_.1), channel_id=1, source_target_pairs={{0,16},{4,20},{8,24},{12,28},{16,0},{20,4},{24,8},{28,12},{1,17},{... | collective-permute-start | bytes 1769480 | tf_op jit(solution)/shard_map/ppermute | solution.py:801
  68.1 49.9 %collective-permute-start.5 = (bf16[192,1536]{1,0:T(8,128)(2,1)}, bf16[192,1536]{1,0:T(8,128)(2,1)}, u32[]{:S(2)}, u32[]{:S(2)}) collective-permute-start(bf16[192,1536]{1,0:T(8,128)(2,1)} %refs_0_.1), channel_id=1, source_target_pairs={{0,24},{4,28},{8,16},{12,20},{16,8},{20,12},{24,0},{28,4},{1,25},{... | collective-permute-start | bytes 1769480 | tf_op jit(solution)/shard_map/ppermute | solution.py:801
  74.2 51.3 %copy-start.20 = (bf16[64,1536]{0,1:T(8,128)(2,1)}, bf16[64,1536]{0,1:T(8,128)(2,1)S(1)}, u32[]{:S(2)}) copy-start(bf16[64,1536]{0,1:T(8,128)(2,1)S(1)} %copy.100) | copy-start | bytes 589828
  125.5 19.1 %collective-permute-start.23 = (bf16[1120,1536]{1,0:T(8,128)(2,1)}, bf16[1120,1536]{1,0:T(8,128)(2,1)}, u32[]{:S(2)}, u32[]{:S(2)}) collective-permute-start(bf16[1120,1536]{1,0:T(8,128)(2,1)} %refs_0_.2), channel_id=1, source_target_pairs={{0,4},{4,0},{8,12},{12,8},{16,20},{20,16},{24,28},{28,24},{1,5},{5... | collective-permute-start | bytes 10321928 | tf_op jit(solution)/shard_map/ppermute | solution.py:801
  125.6 16.7 %collective-permute-start.12 = (bf16[192,1536]{1,0:T(8,128)(2,1)}, bf16[192,1536]{1,0:T(8,128)(2,1)S(1)}, u32[]{:S(2)}, u32[]{:S(2)}) collective-permute-start(bf16[192,1536]{1,0:T(8,128)(2,1)} %refs_0_.1), channel_id=1, source_target_pairs={{0,4},{4,0},{8,12},{12,8},{16,20},{20,16},{24,28},{28,24},{1,5},{5... | collective-permute-start | bytes 1769480 | tf_op jit(solution)/shard_map/ppermute | solution.py:801
  138.8 44.9 %collective-permute-start.21 = (bf16[2,192,2304]{2,1,0:T(8,128)(2,1)}, bf16[2,192,2304]{2,1,0:T(8,128)(2,1)}, u32[]{:S(2)}, u32[]{:S(2)}) collective-permute-start(bf16[2,192,2304]{2,1,0:T(8,128)(2,1)} %get-tuple-element.185), channel_id=1, source_target_pairs={{0,24},{4,28},{8,16},{12,20},{16,8},{20,12},{24,0},{28,4},{1,25},{... | collective-permute-start | bytes 5308424 | tf_op jit(solution)/shard_map/ppermute | solution.py:801
  140.3 77.6 %collective-permute-start.19 = (bf16[2,192,2304]{2,1,0:T(8,128)(2,1)}, bf16[2,192,2304]{2,1,0:T(8,128)(2,1)}, u32[]{:S(2)}, u32[]{:S(2)}) collective-permute-start(bf16[2,192,2304]{2,1,0:T(8,128)(2,1)} %get-tuple-element.183), channel_id=1, source_target_pairs={{0,16},{4,20},{8,24},{12,28},{16,0},{20,4},{24,8},{28,12},{1,17},{... | collective-permute-start | bytes 5308424 | tf_op jit(solution)/shard_map/ppermute | solution.py:801
  140.8 77.9 %collective-permute-start.17 = (bf16[2,192,2304]{2,1,0:T(8,128)(2,1)}, bf16[2,192,2304]{2,1,0:T(8,128)(2,1)}, u32[]{:S(2)}, u32[]{:S(2)}) collective-permute-start(bf16[2,192,2304]{2,1,0:T(8,128)(2,1)} %get-tuple-element.181), channel_id=1, source_target_pairs={{0,8},{4,12},{8,0},{12,4},{16,24},{20,28},{24,16},{28,20},{1,9},{5... | collective-permute-start | bytes 5308424 | tf_op jit(solution)/shard_map/ppermute | solution.py:801
  142.3 2.2 collective-permute-start.13
  144.5 29.0 %collective-permute-start.14 = (bf16[192,1536]{1,0:T(8,128)(2,1)}, bf16[192,1536]{1,0:T(8,128)(2,1)}, u32[]{:S(2)}, u32[]{:S(2)}) collective-permute-start(bf16[192,1536]{1,0:T(8,128)(2,1)} %collective-permute-done.4.refs_4_), channel_id=1, source_target_pairs={{0,4},{4,0},{8,12},{12,8},{16,20},{20,16},{24,28},{28,24},{1,5},{5... | collective-permute-start | bytes 1769480 | tf_op jit(solution)/shard_map/ppermute | solution.py:801
  144.7 30.4 %collective-permute-start.15 = (bf16[192,1536]{1,0:T(8,128)(2,1)}, bf16[192,1536]{1,0:T(8,128)(2,1)}, u32[]{:S(2)}, u32[]{:S(2)}) collective-permute-start(bf16[192,1536]{1,0:T(8,128)(2,1)} %collective-permute-done.5.refs_6_), channel_id=1, source_target_pairs={{0,4},{4,0},{8,12},{12,8},{16,20},{20,16},{24,28},{28,24},{1,5},{5... | collective-permute-start | bytes 1769480 | tf_op jit(solution)/shard_map/ppermute | solution.py:801
  146.2 353.1 %copy-start.59 = (s32[384]{0:T(512)}, s32[384]{0:T(512)S(1)}, u32[]{:S(2)}) copy-start(s32[384]{0:T(512)S(1)} %get-tuple-element.321) | copy-start | bytes 4612
  146.2 353.1 %copy-start.60 = (s32[384]{0:T(512)}, s32[384]{0:T(512)S(1)}, u32[]{:S(2)}) copy-start(s32[384]{0:T(512)S(1)} %get-tuple-element.322) | copy-start | bytes 4612
  173.5 56.9 %collective-permute-start.16 = (bf16[2,192,2304]{2,1,0:T(8,128)(2,1)}, bf16[2,192,2304]{2,1,0:T(8,128)(2,1)}, u32[]{:S(2)}, u32[]{:S(2)}) collective-permute-start(bf16[2,192,2304]{2,1,0:T(8,128)(2,1)} %get-tuple-element.179.refs_0_), channel_id=1, source_target_pairs={{0,4},{4,0},{8,12},{12,8},{16,20},{20,16},{24,28},{28,24},{1,5},{5... | collective-permute-start | bytes 5308424 | tf_op jit(solution)/shard_map/ppermute | solution.py:801
  226.2 6.3 collective-permute-start.22
  226.2 6.6 collective-permute-start.20
  226.7 8.6 %collective-permute-start.18 = (bf16[2,192,2304]{2,1,0:T(8,128)(2,1)}, bf16[2,192,2304]{2,1,0:T(8,128)(2,1)}, u32[]{:S(2)}, u32[]{:S(2)}) collective-permute-start(bf16[2,192,2304]{2,1,0:T(8,128)(2,1)} %collective-permute-done.17.refs_2_), channel_id=1, source_target_pairs={{0,4},{4,0},{8,12},{12,8},{16,20},{20,16},{24,28},{28,24},{1,5},{5... | collective-permute-start | bytes 5308424 | tf_op jit(solution)/shard_map/ppermute | solution.py:801
  235.2 35.8 %collective-permute-start.24 = (bf16[384,1536]{1,0:T(8,128)(2,1)}, bf16[384,1536]{1,0:T(8,128)(2,1)}, u32[]{:S(2)}, u32[]{:S(2)}) collective-permute-start(bf16[384,1536]{1,0:T(8,128)(2,1)} %get-tuple-element.194.refs_8_), channel_id=1, source_target_pairs={{0,8},{4,12},{8,0},{12,4},{16,24},{20,28},{24,16},{28,20},{1,9},{5... | collective-permute-start | bytes 3538952 | tf_op jit(solution)/shard_map/ppermute | solution.py:801
  235.9 35.2 %collective-permute-start.25 = (bf16[384,1536]{1,0:T(8,128)(2,1)}, bf16[384,1536]{1,0:T(8,128)(2,1)}, u32[]{:S(2)}, u32[]{:S(2)}) collective-permute-start(bf16[384,1536]{1,0:T(8,128)(2,1)} %get-tuple-element.194.refs_8_), channel_id=1, source_target_pairs={{0,16},{4,20},{8,24},{12,28},{16,0},{20,4},{24,8},{28,12},{1,17},{... | collective-permute-start | bytes 3538952 | tf_op jit(solution)/shard_map/ppermute | solution.py:801
  269.6 32.0 %collective-permute-start.26 = (bf16[384,1536]{1,0:T(8,128)(2,1)}, bf16[384,1536]{1,0:T(8,128)(2,1)}, u32[]{:S(2)}, u32[]{:S(2)}) collective-permute-start(bf16[384,1536]{1,0:T(8,128)(2,1)} %bitcast.23.refs_9_.grad_ref), channel_id=1, source_target_pairs={{0,8},{4,12},{8,0},{12,4},{16,24},{20,28},{24,16},{28,20},{1,9},{5... | collective-permute-start | bytes 3538952 | tf_op jit(solution)/shard_map/ppermute | solution.py:801
  301.0 87.9 %collective-permute-start.31 = (bf16[384,1664]{1,0:T(8,128)(2,1)}, bf16[384,1664]{1,0:T(8,128)(2,1)}, u32[]{:S(2)}, u32[]{:S(2)}) collective-permute-start(bf16[384,1664]{1,0:T(8,128)(2,1)} %get-tuple-element.221), channel_id=1, source_target_pairs={{0,16},{4,20},{8,24},{12,28},{16,0},{20,4},{24,8},{28,12},{1,17},{... | collective-permute-start | bytes 3833864 | tf_op jit(solution)/shard_map/ppermute | solution.py:801
  303.5 39.2 %collective-permute-start.29 = (bf16[192,1536]{1,0:T(8,128)(2,1)}, bf16[192,1536]{1,0:T(8,128)(2,1)}, u32[]{:S(2)}, u32[]{:S(2)}) collective-permute-start(bf16[192,1536]{1,0:T(8,128)(2,1)} %slice.193), channel_id=1, source_target_pairs={{0,8},{4,12},{8,0},{12,4},{16,24},{20,28},{24,16},{28,20},{1,9},{5... | collective-permute-start | bytes 1769480 | tf_op jit(solution)/shard_map/ppermute | solution.py:801
  306.1 39.0 %collective-permute-start.30 = (bf16[192,1536]{1,0:T(8,128)(2,1)}, bf16[192,1536]{1,0:T(8,128)(2,1)}, u32[]{:S(2)}, u32[]{:S(2)}) collective-permute-start(bf16[192,1536]{1,0:T(8,128)(2,1)} %slice.194), channel_id=1, source_target_pairs={{0,16},{4,20},{8,24},{12,28},{16,0},{20,4},{24,8},{28,12},{1,17},{... | collective-permute-start | bytes 1769480 | tf_op jit(solution)/shard_map/ppermute | solution.py:801
  308.6 38.8 %collective-permute-start.27 = (bf16[192,1536]{1,0:T(8,128)(2,1)S(1)}, bf16[192,1536]{1,0:T(8,128)(2,1)}, u32[]{:S(2)}, u32[]{:S(2)}) collective-permute-start(bf16[192,1536]{1,0:T(8,128)(2,1)S(1)} %slice.191), channel_id=1, source_target_pairs={{0,8},{4,12},{8,0},{12,4},{16,24},{20,28},{24,16},{28,20},{1,9},{5... | collective-permute-start | bytes 1769480 | tf_op jit(solution)/shard_map/ppermute | solution.py:801
  312.0 43.9 %collective-permute-start.28 = (bf16[192,1536]{1,0:T(8,128)(2,1)}, bf16[192,1536]{1,0:T(8,128)(2,1)}, u32[]{:S(2)}, u32[]{:S(2)}) collective-permute-start(bf16[192,1536]{1,0:T(8,128)(2,1)} %slice.192), channel_id=1, source_target_pairs={{0,16},{4,20},{8,24},{12,28},{16,0},{20,4},{24,8},{28,12},{1,17},{... | collective-permute-start | bytes 1769480 | tf_op jit(solution)/shard_map/ppermute | solution.py:801
  342.7 47.7 %collective-permute-start.32 = (bf16[384,1664]{1,0:T(8,128)(2,1)}, bf16[384,1664]{1,0:T(8,128)(2,1)}, u32[]{:S(2)}, u32[]{:S(2)}) collective-permute-start(bf16[384,1664]{1,0:T(8,128)(2,1)} %get-tuple-element.222), channel_id=1, source_target_pairs={{0,8},{4,12},{8,0},{12,4},{16,24},{20,28},{24,16},{28,20},{1,9},{5... | collective-permute-start | bytes 3833864 | tf_op jit(solution)/shard_map/ppermute | solution.py:801
  388.2 29.6 %collective-permute-start.33 = (bf16[384,1664]{1,0:T(8,128)(2,1)}, bf16[384,1664]{1,0:T(8,128)(2,1)}, u32[]{:S(2)}, u32[]{:S(2)}) collective-permute-start(bf16[384,1664]{1,0:T(8,128)(2,1)} %get-tuple-element.223), channel_id=1, source_target_pairs={{0,24},{4,28},{8,16},{12,20},{16,8},{20,12},{24,0},{28,4},{1,25},{... | collective-permute-start | bytes 3833864 | tf_op jit(solution)/shard_map/ppermute | solution.py:801
  429.4 42.7 %collective-permute-start.34 = (bf16[384,1664]{1,0:T(8,128)(2,1)}, bf16[384,1664]{1,0:T(8,128)(2,1)}, u32[]{:S(2)}, u32[]{:S(2)}) collective-permute-start(bf16[384,1664]{1,0:T(8,128)(2,1)} %get-tuple-element.227), channel_id=1, source_target_pairs={{0,16},{4,20},{8,24},{12,28},{16,0},{20,4},{24,8},{28,12},{1,17},{... | collective-permute-start | bytes 3833864 | tf_op jit(solution)/shard_map/ppermute | solution.py:801
  429.9 42.1 %collective-permute-start.35 = (bf16[384,1664]{1,0:T(8,128)(2,1)}, bf16[384,1664]{1,0:T(8,128)(2,1)}, u32[]{:S(2)}, u32[]{:S(2)}) collective-permute-start(bf16[384,1664]{1,0:T(8,128)(2,1)} %get-tuple-element.228), channel_id=1, source_target_pairs={{0,8},{4,12},{8,0},{12,4},{16,24},{20,28},{24,16},{28,20},{1,9},{5... | collective-permute-start | bytes 3833864 | tf_op jit(solution)/shard_map/ppermute | solution.py:801
  430.5 68.8 %copy-start.70 = (pred[384]{0:T(512)(128)(4,1)}, pred[384]{0:T(512)(128)(4,1)S(1)}, u32[]{:S(2)}) copy-start(pred[384]{0:T(512)(128)(4,1)S(1)} %fusion.102) | copy-start | bytes 1156
  464.9 31.7 %collective-permute-start.36 = (bf16[384,1664]{1,0:T(8,128)(2,1)}, bf16[384,1664]{1,0:T(8,128)(2,1)}, u32[]{:S(2)}, u32[]{:S(2)}) collective-permute-start(bf16[384,1664]{1,0:T(8,128)(2,1)} %get-tuple-element.233), channel_id=1, source_target_pairs={{0,24},{4,28},{8,16},{12,20},{16,8},{20,12},{24,0},{28,4},{1,25},{... | collective-permute-start | bytes 3833864 | tf_op jit(solution)/shard_map/ppermute | solution.py:801
  472.1 192.8 %all-gather.9.cloned.1.call-start = ((), (), s32[]{:S(2)}) async-start(), calls=%async_computation.4 | async-start | bytes 8110080 | tf_op jit(solution)/shard_map/all_gather | solution.py:1099
  505.1 8.1 %collective-permute-start.37 = (bf16[2,4,48,768]{3,2,1,0:T(8,128)(2,1)}, bf16[2,4,48,768]{3,2,1,0:T(8,128)(2,1)}, u32[]{:S(2)}, u32[]{:S(2)}) collective-permute-start(bf16[2,4,48,768]{3,2,1,0:T(8,128)(2,1)} %dynamic-slice_bitcast_fusion), channel_id=1, source_target_pairs={{0,4},{4,0},{8,12},{12,8},{16,20},{20,16},{24,28},{28,24},{1,5},{5... | collective-permute-start | bytes 1769480 | tf_op jit(solution)/shard_map/ppermute | solution.py:801
  512.8 4.5 collective-permute-start.41
  514.5 16.7 %collective-permute-start.38 = (bf16[1,4,48,768]{3,2,1,0:T(8,128)(2,1)S(1)}, bf16[1,4,48,768]{3,2,1,0:T(8,128)(2,1)S(1)}, u32[]{:S(2)}, u32[]{:S(2)}) collective-permute-start(bf16[1,4,48,768]{3,2,1,0:T(8,128)(2,1)S(1)} %constant_dynamic-slice_fusion.2), channel_id=1, source_target_pairs={{0,8},{4,12},{8,0},{12,4},{16,24},{20,28},{24,16},{28,20},{1,9},{5... | collective-permute-start | bytes 884744 | tf_op jit(solution)/shard_map/ppermute | solution.py:801
  531.3 48.7 %copy-start.2 = (s32[8]{0:T(128)S(1)}, s32[8]{0:T(128)}, u32[]{:S(2)}) copy-start(s32[8]{0:T(128)} %constant.283.clone) | copy-start | bytes 100
  531.3 13.1 %collective-permute-start.39 = (bf16[2,48,768]{2,1,0:T(8,128)(2,1)S(1)}, bf16[2,48,768]{2,1,0:T(8,128)(2,1)S(1)}, u32[]{:S(2)}, u32[]{:S(2)}) collective-permute-start(bf16[2,48,768]{2,1,0:T(8,128)(2,1)S(1)} %dynamic-slice_bitcast_fusion.2), channel_id=1, source_target_pairs={{0,1},{1,0},{2,3},{3,2},{4,5},{5,4},{6,7},{7,6},{8,9},{9,8},{10,11... | collective-permute-start | bytes 442376 | tf_op jit(solution)/shard_map/ppermute | solution.py:804
  532.9 50.9 %copy-start.3 = (bf16[3,128,1536]{2,1,0:T(8,128)(2,1)S(1)}, bf16[3,128,1536]{2,1,0:T(8,128)(2,1)}, u32[]{:S(2)}) copy-start(bf16[3,128,1536]{2,1,0:T(8,128)(2,1)} %param.31) | copy-start | bytes 3538948
  532.9 22.5 %collective-permute-start.42 = (bf16[2,48,1792]{2,1,0:T(8,128)(2,1)S(1)}, bf16[2,48,1792]{2,1,0:T(8,128)(2,1)S(1)}, u32[]{:S(2)}, u32[]{:S(2)}) collective-permute-start(bf16[2,48,1792]{2,1,0:T(8,128)(2,1)S(1)} %dynamic-slice_bitcast_fusion.1), channel_id=1, source_target_pairs={{0,1},{1,0},{2,3},{3,2},{4,5},{5,4},{6,7},{7,6},{8,9},{9,8},{10,11... | collective-permute-start | bytes 1032200 | tf_op jit(solution)/shard_map/ppermute | solution.py:804
  544.5 12.2 %collective-permute-start.40 = (bf16[1,48,768]{2,1,0:T(8,128)(2,1)S(1)}, bf16[1,48,768]{2,1,0:T(8,128)(2,1)S(1)}, u32[]{:S(2)}, u32[]{:S(2)}) collective-permute-start(bf16[1,48,768]{2,1,0:T(8,128)(2,1)S(1)} %constant_dynamic-slice_fusion.1), channel_id=1, source_target_pairs={{0,2},{1,3},{2,0},{3,1},{4,6},{5,7},{6,4},{7,5},{8,10},{9,11},{10,... | collective-permute-start | bytes 221192 | tf_op jit(solution)/shard_map/ppermute | solution.py:804
  555.5 14.3 %collective-permute-start.43 = (bf16[1,48,1792]{2,1,0:T(8,128)(2,1)S(1)}, bf16[1,48,1792]{2,1,0:T(8,128)(2,1)S(1)}, u32[]{:S(2)}, u32[]{:S(2)}) collective-permute-start(bf16[1,48,1792]{2,1,0:T(8,128)(2,1)S(1)} %constant_dynamic-slice_fusion), channel_id=1, source_target_pairs={{0,2},{1,3},{2,0},{3,1},{4,6},{5,7},{6,4},{7,5},{8,10},{9,11},{10,... | collective-permute-start | bytes 516104 | tf_op jit(solution)/shard_map/ppermute | solution.py:804
  603.1 2.0 collective-permute-start.44
  605.1 5.0 collective-permute-start.45
  610.1 10.1 %collective-permute-start.46 = (bf16[48,896]{1,0:T(8,128)(2,1)S(1)}, bf16[48,896]{1,0:T(8,128)(2,1)S(1)}, u32[]{:S(2)}, u32[]{:S(2)}) collective-permute-start(bf16[48,896]{1,0:T(8,128)(2,1)S(1)} %fusion.65), channel_id=1, source_target_pairs={{0,1},{1,0},{2,3},{3,2},{4,5},{5,4},{6,7},{7,6},{8,9},{9,8},{10,11... | collective-permute-start | bytes 258056 | tf_op jit(solution)/shard_map/ppermute | solution.py:804
  612.3 14.6 %collective-permute-start.47 = (bf16[48,896]{1,0:T(8,128)(2,1)S(1)}, bf16[48,896]{1,0:T(8,128)(2,1)S(1)}, u32[]{:S(2)}, u32[]{:S(2)}) collective-permute-start(bf16[48,896]{1,0:T(8,128)(2,1)S(1)} %fusion.65), channel_id=1, source_target_pairs={{0,2},{1,3},{2,0},{3,1},{4,6},{5,7},{6,4},{7,5},{8,10},{9,11},{10,... | collective-permute-start | bytes 258056 | tf_op jit(solution)/shard_map/ppermute | solution.py:804
  613.9 12.9 %collective-permute-start.48 = (bf16[48,896]{1,0:T(8,128)(2,1)S(1)}, bf16[48,896]{1,0:T(8,128)(2,1)S(1)}, u32[]{:S(2)}, u32[]{:S(2)}) collective-permute-start(bf16[48,896]{1,0:T(8,128)(2,1)S(1)} %fusion.65), channel_id=1, source_target_pairs={{0,3},{1,2},{2,1},{3,0},{4,7},{5,6},{6,5},{7,4},{8,11},{9,10},{10,... | collective-permute-start | bytes 258056 | tf_op jit(solution)/shard_map/ppermute | solution.py:804
  626.9 4.6 collective-permute-start.49
  631.5 10.6 %collective-permute-start.50 = (bf16[2,48,896]{2,1,0:T(8,128)(2,1)S(1)}, bf16[2,48,896]{2,1,0:T(8,128)(2,1)S(1)}, u32[]{:S(2)}, u32[]{:S(2)}) collective-permute-start(bf16[2,48,896]{2,1,0:T(8,128)(2,1)S(1)} %pad_maximum_fusion.12), channel_id=1, source_target_pairs={{0,16},{4,20},{8,24},{12,28},{16,0},{20,4},{24,8},{28,12},{1,17},{... | collective-permute-start | bytes 516104 | tf_op jit(solution)/shard_map/ppermute | solution.py:801
  642.1 2.1 collective-permute-start.51
  (69 other events, 588.8 us)
Sparse Core Ops, SparseCore 0:
  13.6 32.9 all-gather.4
  61.1 77.6 all-gather.6
  472.2 106.4 reduce-scatter.1
  582.4 82.4 all-gather.8

commit v4 on v3

--- a/solution.py
+++ b/solution.py
@@ -351,7 +351,7 @@
 
 def outputs_kernel(seqs, count, info, attended_ref, x_ref, gain_ref, shrink_ref, eo_ref, *refs):
     blocks = refs[:count]
-    middle_ref, normed_ref, narrow_ref, w_ref, sems = refs[count:]
+    middle_ref, normed_ref, top_ref, bottom_ref, narrow_ref, w_ref, sems = refs[count:]
     copies = fetch_rows(info[0], blocks, w_ref, sems)
     for copy in copies:
         copy.start()
@@ -364,7 +364,10 @@
         copy.wait()
     middle = x_ref[...].astype(F32) + (mm(attended, w_ref[...]) + mm(narrow, eo_ref[...]))
     middle_ref[...] = middle
-    normed_ref[...] = norm_forward(middle, gain_ref[...]).astype(BF)
+    normed = norm_forward(middle, gain_ref[...]).astype(BF)
+    normed_ref[...] = normed
+    top_ref[...] = normed[: tokens // 2]
+    bottom_ref[...] = normed[tokens // 2 :]
 
 
 def before_attention_kernel(
@@ -505,10 +508,12 @@
 def feed_kernel(seqs, kinds, info, *refs):
     count = len(kinds)
     blocks = refs[:count]
-    n2_ref, g0_ref, sgu_ref, ed_ref, wd_ref, eg_ref, eu_ref, sd_ref = refs[count : count + 8]
-    peg_ref, peu_ref, psd_ref = refs[count + 8 : count + 11]
-    out_ref, ng_ref, deg_ref, deu_ref, dsd_ref = refs[count + 11 : count + 16]
-    acc_out, acc_ng, acc_nd, acc_bg, acc_bu, nar_g, nar_u, back_d, held, sems = refs[count + 16 :]
+    top_ref, bottom_ref, grad_top_ref, grad_bottom_ref = refs[count : count + 4]
+    count += 4
+    sgu_ref, ed_ref, wd_ref, eg_ref, eu_ref, sd_ref = refs[count : count + 6]
+    peg_ref, peu_ref, psd_ref = refs[count + 6 : count + 9]
+    out_ref, ng_ref, deg_ref, deu_ref, dsd_ref = refs[count + 9 : count + 14]
+    acc_out, acc_ng, acc_nd, acc_bg, acc_bu, nar_g, nar_u, back_d, held, sems = refs[count + 14 :]
     chunk = pl.program_id(0)
     chunks = pl.num_programs(0)
     depth = blocks[0].shape[-2]
@@ -538,11 +543,11 @@
         for copy in copies(chunk + 1, 1 - slot):
             copy.start()
 
-    tokens = n2_ref.shape[0]
-    model = n2_ref.shape[1]
+    tokens = out_ref.shape[0]
+    model = top_ref.shape[1]
     cols = sd_ref.shape[1]
-    n2 = n2_ref[...]
-    g0 = g0_ref[...]
+    n2 = jnp.concatenate([top_ref[...], bottom_ref[...]], axis=0)
+    g0 = jnp.concatenate([grad_top_ref[...], grad_bottom_ref[...]], axis=0)
     wg_ref = held.at[slot, 0]
     wu_ref = held.at[slot, 1]
 
@@ -587,7 +592,7 @@
 
 
 def feed(index, kinds, blocks, n2, g0, sgu, ed, wd, eg, eu, sd, previous, seqs, limit=768):
-    tokens, model = n2.shape
+    tokens, model = 2 * n2[0].shape[0], n2[0].shape[1]
     count = len(blocks)
     hidden = wd.shape[0]
     cols = ed.shape[0]
@@ -606,7 +611,7 @@
             num_scalar_prefetch=1,
             grid=(hidden // size,),
             in_specs=[anywhere] * count
-            + [whole(n2), whole(g0), whole(sgu), whole(ed), tall(wd)]
+            + [whole(n2[0]), whole(n2[1]), whole(g0[0]), whole(g0[1]), whole(sgu), whole(ed), tall(wd)]
             + [part(eg), part(eu), tall(sd), part(grads), part(grads), part(grads)],
             out_specs=[fixed(model + 2 * cols), fixed(model + 2 * cols)] + [part(grads)] * 3,
             scratch_shapes=[
@@ -633,7 +638,7 @@
             bytes_accessed=6 * model * hidden,
             transcendentals=tokens * hidden,
         ),
-    )(index, *blocks, n2, g0, sgu, ed, wd, eg, eu, sd, *previous)
+    )(index, *blocks, *n2, *g0, sgu, ed, wd, eg, eu, sd, *previous)
 
 
 def assemble_kernel(count, info, *refs):
@@ -865,9 +870,6 @@
     w_kv, parts, rows_q = lax.optimization_barrier((w_kv, parts, rows_q))
     rows_o = [output_weight] + [swap(after(output_weight, rows_q), 2 * k) for k in range(1, chips)]
     blocks = {}
-    g0_pieces = {
-        k: swap(after(grad_low, rows_q), 2 * k) for k in range(1, chips) if 2 * k % cp_n == 0
-    }
     w_key = w_kv[:, :kv_width]
     w_value = w_kv[:, kv_width:]
 
@@ -883,9 +885,19 @@
             query_lift_factors, key_lift_factors, value_lift_factors, output_lift_factors,
         )
     ]
-    w_kv, output_shrink, output_expand, query_shrink, query_expand = lax.optimization_barrier(
-        (w_kv, output_shrink, output_expand, query_shrink, query_expand)
-    )
+    grad_halves = (grad_low[: tokens // 2], grad_low[tokens // 2 :])
+    w_kv, output_shrink, output_expand, query_shrink, query_expand, grad_halves = (
+        lax.optimization_barrier(
+            (w_kv, output_shrink, output_expand, query_shrink, query_expand, grad_halves)
+        )
+    )
+
+    def swap_both(pair, k):
+        return tuple(swap(half, k) for half in pair)
+
+    g0_pieces = {
+        k: swap_both(after(grad_halves, rows_q), 2 * k) for k in range(1, chips) if 2 * k % cp_n == 0
+    }
 
     def narrowed(value, shrink):
         return (mm(value, shrink) * mixing).astype(BF)
@@ -918,10 +930,20 @@
         )
         for f in range(fsdp_n)
     ]
+    late_down, late_gate, late_up = down_reduce_factors, gate_lift_factors, upper_lift_factors
+    shrink_d = jnp.pad(
+        lax.dynamic_slice_in_dim(late_down, chip * hq, hq, 0), ((0, pad), (0, 0))
+    )
+    lift_g = lax.dynamic_index_in_dim(by_chip(late_gate), chip, 0, keepdims=False)
+    lift_u = lax.dynamic_index_in_dim(by_chip(late_up), chip, 0, keepdims=False)
+    lift_factors = [(expand_of(lift_g, f), expand_of(lift_u, f)) for f in range(fsdp_n)]
+    feed_factors = [
+        reduce_factors[f] + lift_factors[f] + (shrink_of(shrink_d, f),) for f in range(fsdp_n)
+    ]
     query_rot, query_narrow, w_query = with_blocks(
         queries_kernel, "queries", seqs, me, after(both_cores(rows_q), pair),
         [
-            after(normed, rows_o, g0_pieces, reduce_factors, gate_shrink, up_shrink, down_expand), query_shrink, query_expand, query_bias.astype(F32)[None], flat_cosine,
+            after(normed, rows_o, g0_pieces, feed_factors, gate_shrink, up_shrink, down_expand), query_shrink, query_expand, query_bias.astype(F32)[None], flat_cosine,
             sine_signed,
         ],
         [
@@ -930,48 +952,37 @@
         ],
     )
 
-    attended, lse = attend(info, query_rot, pair_all, seqs, spans, span_len)
+    down_rows = [down_weight, swap(after(down_weight, query_rot), 1)]
+    w_down = assemble(core, after(down_rows, query_rot), hp)
+    attended, lse = attend(info, after(query_rot, w_down), pair_all, seqs, spans, span_len)
     for k in range(1, chips):
         blocks[k] = swap(after(parts[k], pair_all, query_rot), 2 * k)
-    late_down, late_gate, late_up = after(
-        (down_reduce_factors, gate_lift_factors, upper_lift_factors), attended, blocks
-    )
-    shrink_d = jnp.pad(
-        lax.dynamic_slice_in_dim(late_down, chip * hq, hq, 0), ((0, pad), (0, 0))
-    )
-    lift_g = lax.dynamic_index_in_dim(by_chip(late_gate), chip, 0, keepdims=False)
-    lift_u = lax.dynamic_index_in_dim(by_chip(late_up), chip, 0, keepdims=False)
-    lift_factors = [(expand_of(lift_g, f), expand_of(lift_u, f)) for f in range(fsdp_n)]
-    feed_factors = [
-        reduce_factors[f] + lift_factors[f] + (shrink_of(shrink_d, f),) for f in range(fsdp_n)
-    ]
     output_blocks = both_cores(after(rows_o, query_rot))
-    down_rows = [down_weight, swap(after(down_weight, query_rot), 1)]
-    w_down = assemble(core, after(down_rows, attended), hp)
-    kinds = [(0, None), (1, None)]
-    wide = [parts[0], swap(after(parts[0], query_rot), 1)]
-    for k in range(1, chips):
-        kinds += [(2 * k, None), (2 * k + 1, None)]
-        wide += [blocks[k], swap(blocks[k], 1)]
-    feed_index = jnp.stack([me, core]).astype(jnp.int32)
-
-    middle, normed_two, output_narrow, w_output = with_blocks(
+    middle, normed_two, normed_top, normed_bottom, output_narrow, w_output = with_blocks(
         outputs_kernel, "outputs", seqs, me, output_blocks,
         [attended, low_in, second_scales[None], output_shrink, output_expand],
         [
             jax.ShapeDtypeStruct((tokens, model), F32),
             jax.ShapeDtypeStruct((tokens, model), BF),
+            jax.ShapeDtypeStruct((tokens // 2, model), BF),
+            jax.ShapeDtypeStruct((tokens // 2, model), BF),
             jax.ShapeDtypeStruct((tokens, lanes), BF),
         ],
     )
 
-    g0_pieces[0] = grad_low
-    n2_pieces = [normed_two]
+    kinds = [(0, None), (1, None)]
+    wide = [parts[0], swap(after(parts[0], query_rot), 1)]
     for k in range(1, chips):
-        if k < 3 and k not in g0_pieces:
-            g0_pieces[k] = swap(after(grad_low, wide), 2 * k)
+        kinds += [(2 * k, None), (2 * k + 1, None)]
+        wide += [blocks[k], swap(after(blocks[k], middle), 1)]
+    feed_index = jnp.stack([me, core]).astype(jnp.int32)
+
+    g0_pieces[0] = grad_halves
+    normed_halves = (normed_top, normed_bottom)
+    n2_pieces = [normed_halves]
+    for k in range(1, chips):
         if k < 3:
-            n2_pieces.append(swap(after(normed_two, wide), 2 * k))
+            n2_pieces.append(swap_both(after(normed_halves, wide), 2 * k))
     if chips > 2:
         n2_pieces[1:3] = lax.optimization_barrier(n2_pieces[1:3])
     zero = jnp.zeros((lanes, hp), F32)
@@ -982,17 +993,18 @@
     for k in early_first:
         f = 2 * k // cp_n
         sgu, ed, eg, eu, sd = feed_factors[f]
-        if len(out_raw) == 2 or (len(out_raw) == 1 and chips == 2):
-            middle_row = tokens // 2
+        if len(out_raw) == 1:
+            for other in range(1, min(chips, 3)):
+                if other not in g0_pieces:
+                    g0_pieces[other] = swap_both(after(grad_halves, out_raw[0]), 2 * other)
+        if len(out_raw) == 2:
             for other in range(3, chips):
                 for pieces in (n2_pieces, g0_pieces):
-                    first, second = after((pieces[2], pieces[1]), out_raw[0])
+                    first, second, own_pair = after((pieces[2], pieces[1], pieces[0]), out_raw[-1])
                     if other == 3:
-                        piece = jnp.concatenate(
-                            [swap(first[:middle_row], 2), swap(second[middle_row:], 4)], axis=0
-                        )
+                        piece = (swap(first[0], 2), swap(second[1], 4))
                     else:
-                        piece = swap(after(pieces[0], out_raw[0]), 2 * other)
+                        piece = swap_both(own_pair, 2 * other)
                     if pieces is n2_pieces:
                         n2_pieces.append(piece)
                     else:

time: 691 us -> 663 us (0.959)
  starting transfers between devices: 55.7 us -> 97 us
  waiting for transfers between devices: 234 us -> 194 us
  Pallas kernels: 224 us -> 209 us
  other arithmetic: 57.1 us -> 49.5 us
    ppermute x45 -> x49, starting transfers between devices: 45.7 us -> 71.6 us  [swap(): return lax.ppermute(value, PLANE, [(i, i ^ k) for i in range(plane)])]
    ppermute x45 -> x49, waiting for transfers between devices: 153 us -> 134 us  [swap(): return lax.ppermute(value, PLANE, [(i, i ^ k) for i in range(plane)])]
    ppermute x7, starting transfers between devices: 9.69 us -> 25.1 us  [swap_seq(): return lax.ppermute(value, 'seq', [(i, i ^ k) for i in range(seq_n)])]
    all_gather x1, waiting for transfers between devices: 12.7 us -> 0.01 us  [body(): lax.all_gather(pair.reshape(seqs, tok_rows, 2 * kv_width), ('cp', 'seq'),...]
    pallas_call x1, Pallas kernels: 29 us -> 19.9 us  [attend_back(): pl.pallas_call(functools.partial(attend_back_kernel, spans, span_len, tok...]
    pallas_call x1, Pallas kernels: 22.3 us -> 14.9 us  [attend(): pl.pallas_call(functools.partial(attend_kernel, spans, span_len, tokens),...]
    ppermute x7, waiting for transfers between devices: 44.8 us -> 37.8 us  [swap_seq(): return lax.ppermute(value, 'seq', [(i, i ^ k) for i in range(seq_n)])]
  transfers between devices with their start and end apart: 56 -> 60, of which waited for: 26 -> 27; matrix products, arithmetic and copies ran while one was open for 22% -> 21% of each run, Pallas kernels for 29% -> 28%
where the time goes in v4:
time: 663 us; the launch traced here: 657 us
  Pallas kernels  209 us (32%)
  waiting for transfers between devices  194 us (29%)
  starting transfers between devices  97 us (15%)
  local copies, waits for them, and re-layouts  52.2 us (8%)
  other arithmetic  49.5 us (7%)
  matrix products  39.1 us (6%)
  between operations  16 us (2%)
    ppermute x49, waiting for transfers between devices, swap(): return lax.ppermute(value, PLANE, [(i, i ^ k) for i in range(plane)])  134 us
    pallas_call x4, Pallas kernels, feed(): pl.pallas_call(functools.partial(feed_kernel, seqs, tuple(kinds)), grid_s...  120 us
    ppermute x49, starting transfers between devices, swap(): return lax.ppermute(value, PLANE, [(i, i ^ k) for i in range(plane)])  71.6 us
    ppermute x7, waiting for transfers between devices, swap_seq(): return lax.ppermute(value, 'seq', [(i, i ^ k) for i in range(seq_n)])  37.8 us
    ppermute x7, starting transfers between devices, swap_seq(): return lax.ppermute(value, 'seq', [(i, i ^ k) for i in range(seq_n)])  25.1 us
    dot_general x21, matrix products, mm_tn(): lax.dot_general(left, right, (((0,), (0,)), ((), ())), preferred_element_...  21.9 us
    pallas_call x1, Pallas kernels, attend_back(): pl.pallas_call(functools.partial(attend_back_kernel, spans, span_len, tok...  19.9 us
    pallas_call x2, Pallas kernels, with_blocks(): pl.pallas_call(functools.partial(kernel, seqs, count), grid_spec=pltpu.Pr...  18.2 us
  transfers between devices with their start and end apart: 60, of which 27 were waited for; matrix products, arithmetic and copies ran while one was open for 21% of the time, Pallas kernels for 28%

profile of v4, /device:TPU:0, one launch (start us, length us, event | category | flops | bytes accessed | tf_op | source)
XLA Modules:
  0.0 656.9 jit_solution(1339424930146720375)
XLA Ops:
  7.2 3.0 collective-permute-start.1
  13.1 1.9 collective-permute-start.8
  17.8 2.3 fusion.124
  20.1 4.1 fusion.120
  24.2 1.9 fusion.119
  28.6 2.1 select_bitcast_fusion
  33.4 3.2 fusion.10
  48.6 1.9 convolution_convert_fusion.17.eo_ref.oe_ref
  50.6 3.1 all-gather.5.cloned.1.call-done.w_ref
  53.7 4.3 keys_values.1
  58.8 1.9 fusion.123
  83.6 7.2 %collective-permute-done.5.refs_6_ = bf16[192,1536]{1,0:T(8,128)(2,1)} collective-permute-done((bf16[192,1536]{1,0:T(8,128)(2,1)}, bf16[192,1536]{1,0:T(8,128)(2,1)}, u32[]{:S(2)}, u32[]{:S(2)}) %collective-permute-start.5) | collective-permute-done | bytes 589856 | tf_op jit(solution)/shard_map/ppermute | solution.py:806
  90.8 12.5 %collective-permute-done.4.refs_4_ = bf16[192,1536]{1,0:T(8,128)(2,1)S(1)} collective-permute-done((bf16[192,1536]{1,0:T(8,128)(2,1)}, bf16[192,1536]{1,0:T(8,128)(2,1)S(1)}, u32[]{:S(2)}, u32[]{:S(2)}) %collective-permute-start.4) | collective-permute-done | bytes 589856 | tf_op jit(solution)/shard_map/ppermute | solution.py:806
  103.4 12.0 %collective-permute-done.3.refs_2_ = bf16[192,1536]{1,0:T(8,128)(2,1)} collective-permute-done((bf16[192,1536]{1,0:T(8,128)(2,1)}, bf16[192,1536]{1,0:T(8,128)(2,1)}, u32[]{:S(2)}, u32[]{:S(2)}) %collective-permute-start.3) | collective-permute-done | bytes 589856 | tf_op jit(solution)/shard_map/ppermute | solution.py:806
  116.1 11.9 %collective-permute-done.7.refs_11_ = bf16[192,1536]{1,0:T(8,128)(2,1)} collective-permute-done((bf16[192,1536]{1,0:T(8,128)(2,1)}, bf16[192,1536]{1,0:T(8,128)(2,1)}, u32[]{:S(2)}, u32[]{:S(2)}) %collective-permute-start.7) | collective-permute-done | bytes 589856 | tf_op jit(solution)/shard_map/ppermute | solution.py:806
  128.0 7.7 %queries.1 = (bf16[384,1536]{1,0:T(8,128)(2,1)}, bf16[384,64]{1,0:T(8,128)(2,1)}, bf16[1536,1536]{1,0:T(8,128)(2,1)}) custom-call(s32[1]{0:T(128)} %bitcast.info, bf16[384,1536]{1,0:T(8,128)(2,1)} %get-tuple-element.170.normed_ref, bf16[1536,64]{1,0:T(8,128)(2,1)} %bitcast.198, bf16[64,1536]{1,0:T(8,128)(2,1)} %convolution_convert_fusion.16.eq_ref, ...), custom_call_target="tpu_custom_call" | custom-call | flops 1811939328 | bytes 9437184 | tf_op jit(solution)/shard_map/queries/pallas_call | solution.py:482
  139.8 2.9 collective-permute-done.14.refs_1_
  143.1 1.8 collective-permute-done.15.refs_3_
  147.7 5.0 assemble.1.refs_14_
  152.8 14.9 %attend.1 = (bf16[384,1536]{1,0:T(8,128)(2,1)}, f32[6,8,768]{2,1,0:T(8,128)}) custom-call(s32[29]{0:T(128)} %pad_add_fusion.info, bf16[384,1536]{1,0:T(8,128)(2,1)} %get-tuple-element.186.q_ref, bf16[3,2048,512]{2,1,0:T(8,128)(2,1)} %all-gather.7.cloned.1.call-done.k_ref.v_ref, bf16[3,2048,512]{2,1,0:T(8,128)(2,1)} %all-gather.7.cloned.1.call-done.k_ref.v_ref), custom_call_target="tpu_custom_call" | custom-call | flops 4831838208 | bytes 6291456 | tf_op jit(solution)/shard_map/attend/pallas_call | solution.py:152
  167.7 15.4 %collective-permute-start.18 = (bf16[2,192,2304]{2,1,0:T(8,128)(2,1)S(1)}, bf16[2,192,2304]{2,1,0:T(8,128)(2,1)S(1)}, u32[]{:S(2)}, u32[]{:S(2)}) collective-permute-start(bf16[2,192,2304]{2,1,0:T(8,128)(2,1)S(1)} %copy-done.30), channel_id=1, source_target_pairs={{0,4},{4,0},{8,12},{12,8},{16,20},{20,16},{24,28},{28,24},{1,5},{5... | collective-permute-start | bytes 5308424 | tf_op jit(solution)/shard_map/ppermute | solution.py:806
  183.1 10.6 %outputs.1 = (f32[384,1536]{1,0:T(8,128)}, bf16[384,1536]{1,0:T(8,128)(2,1)}, bf16[192,1536]{1,0:T(8,128)(2,1)}, bf16[192,1536]{1,0:T(8,128)(2,1)}, bf16[384,64]{1,0:T(8,128)(2,1)}, /*index=5*/bf16[1536,1536]{1,0:T(8,128)(2,1)}) custom-call(s32[1]{0:T(128)} %bitcast.info, bf16[384,1536]{1,0:T(8,128)(2,1)} %get-tuple-element.187.attended_ref.o_ref, ...), custom_call_target="tpu_custom_call" | custom-call | flops 1811939328 | bytes 9437184 | tf_op jit(solution)/shard_map/outputs/pallas_call | solution.py:482
  193.7 21.4 %collective-permute-done.21.refs_4_ = bf16[2,192,2304]{2,1,0:T(8,128)(2,1)} collective-permute-done((bf16[2,192,2304]{2,1,0:T(8,128)(2,1)}, bf16[2,192,2304]{2,1,0:T(8,128)(2,1)}, u32[]{:S(2)}, u32[]{:S(2)}) %collective-permute-start.21) | collective-permute-done | bytes 1769504 | tf_op jit(solution)/shard_map/ppermute | solution.py:806
  217.8 2.3 collective-permute-done.20.refs_3_
  220.1 2.5 collective-permute-done.22.refs_5_
  222.6 2.5 collective-permute-done.24.refs_7_
  230.0 29.7 %feed.4 = (bf16[384,1664]{1,0:T(8,128)(2,1)}, bf16[384,1664]{1,0:T(8,128)(2,1)}, f32[64,2304]{1,0:T(8,128)}, f32[64,2304]{1,0:T(8,128)}, f32[64,2304]{1,0:T(8,128)}) custom-call(s32[2]{0:T(128)} %pad_add_fusion.1.info, bf16[2,192,2304]{2,1,0:T(8,128)(2,1)} %get-tuple-element.196.refs_0_, bf16[2,192,2304]{2,1,0:T(8,128)(2,1)} %copy-done.82, ...), custom_call_target="tpu_custom_call" | custom-call | flops 16986931200 | bytes 21233664 | tf_op jit(solution)/shard_map/feed/pallas_call | solution.py:608
  263.4 29.9 %feed.5 = (bf16[384,1664]{1,0:T(8,128)(2,1)}, bf16[384,1664]{1,0:T(8,128)(2,1)}, f32[64,2304]{1,0:T(8,128)}, f32[64,2304]{1,0:T(8,128)}, f32[64,2304]{1,0:T(8,128)}) custom-call(s32[2]{0:T(128)} %pad_add_fusion.1.info, bf16[2,192,2304]{2,1,0:T(8,128)(2,1)} %get-tuple-element.196.refs_0_, bf16[2,192,2304]{2,1,0:T(8,128)(2,1)} %copy-done.82, ...), custom_call_target="tpu_custom_call" | custom-call | flops 16986931200 | bytes 21233664 | tf_op jit(solution)/shard_map/feed/pallas_call | solution.py:608
  297.4 30.2 %feed.6 = (bf16[384,1664]{1,0:T(8,128)(2,1)}, bf16[384,1664]{1,0:T(8,128)(2,1)}, f32[64,2304]{1,0:T(8,128)}, f32[64,2304]{1,0:T(8,128)}, f32[64,2304]{1,0:T(8,128)}) custom-call(s32[2]{0:T(128)} %pad_add_fusion.1.info, bf16[2,192,2304]{2,1,0:T(8,128)(2,1)} %get-tuple-element.196.refs_0_, bf16[2,192,2304]{2,1,0:T(8,128)(2,1)} %copy-done.82, ...), custom_call_target="tpu_custom_call" | custom-call | flops 16986931200 | bytes 21233664 | tf_op jit(solution)/shard_map/feed/pallas_call | solution.py:608
  329.8 30.0 %feed.7 = (bf16[384,1664]{1,0:T(8,128)(2,1)}, bf16[384,1664]{1,0:T(8,128)(2,1)}, f32[64,2304]{1,0:T(8,128)}, f32[64,2304]{1,0:T(8,128)}, f32[64,2304]{1,0:T(8,128)}) custom-call(s32[2]{0:T(128)} %pad_add_fusion.1.info, bf16[2,192,2304]{2,1,0:T(8,128)(2,1)} %get-tuple-element.196.refs_0_, bf16[2,192,2304]{2,1,0:T(8,128)(2,1)} %copy-done.82, ...), custom_call_target="tpu_custom_call" | custom-call | flops 16986931200 | bytes 21233664 | tf_op jit(solution)/shard_map/feed/pallas_call | solution.py:608
  362.8 3.0 convert_add_fusion.1.most_ref
  365.9 22.0 %collective-permute-done.37.last_ref = bf16[384,1664]{1,0:T(8,128)(2,1)} collective-permute-done((bf16[384,1664]{1,0:T(8,128)(2,1)}, bf16[384,1664]{1,0:T(8,128)(2,1)}, u32[]{:S(2)}, u32[]{:S(2)}) %collective-permute-start.37) | collective-permute-done | bytes 1277984 | tf_op jit(solution)/shard_map/ppermute | solution.py:806
  387.9 11.5 %before_attention.1 = (f32[384,1536]{1,0:T(8,128)}, bf16[384,1536]{1,0:T(8,128)(2,1)}, bf16[384,64]{1,0:T(8,128)(2,1)}, bf16[384,64]{1,0:T(8,128)(2,1)}, bf16[38...) custom-call(f32[384,1664]{1,0:T(8,128)} %convert_add_fusion.1.most_ref, bf16[384,1664]{1,0:T(8,128)(2,1)} %collective-permute-done.37.last_ref, ...), custom_call_target="tpu_custom_call" | custom-call | flops 1811939328 | bytes 17694720 | tf_op jit(solution)/shard_map/before_attention/pallas_call | solution.py:401
  402.6 19.9 %attend_back.1 = (bf16[384,1536]{1,0:T(8,128)(2,1)}, bf16[3,2048,512]{2,1,0:T(8,128)(2,1)}) custom-call(s32[29]{0:T(128)} %pad_add_fusion.info, bf16[384,1536]{1,0:T(8,128)(2,1)} %get-tuple-element.186.q_ref, bf16[384,1536]{1,0:T(8,128)(2,1)} %get-tuple-element.249.do_ref, bf16[384,1536]{1,0:T(8,128)(2,1)} %get-tuple-element.187.attended_ref.o_ref, ...), custom_call_target="tpu_custom_call" | custom-call | flops 12079595520 | bytes 12582912 | tf_op jit(solution)/shard_map/attend_back/pallas_call | solution.py:253
  423.5 8.0 %collective-permute-start.40 = (bf16[384,1664]{1,0:T(8,128)(2,1)}, bf16[384,1664]{1,0:T(8,128)(2,1)}, u32[]{:S(2)}, u32[]{:S(2)}) collective-permute-start(bf16[384,1664]{1,0:T(8,128)(2,1)} %get-tuple-element.252), channel_id=1, source_target_pairs={{0,24},{4,28},{8,16},{12,20},{16,8},{20,12},{24,0},{28,4},{1,25},{... | collective-permute-start | bytes 3833864 | tf_op jit(solution)/shard_map/ppermute | solution.py:806
  433.1 2.0 copy.106
  435.2 2.4 fusion.128
  439.4 1.9 broadcast_multiply_fusion
  443.1 3.0 copy.109
  450.3 4.4 collective-permute-done.40
  454.7 2.7 convert_add_fusion
  473.1 5.9 collective-permute-start.41
  482.3 4.2 collective-permute-start.42
  488.6 11.9 %collective-permute-done.42 = bf16[1,4,48,768]{3,2,1,0:T(8,128)(2,1)S(1)} collective-permute-done((bf16[1,4,48,768]{3,2,1,0:T(8,128)(2,1)S(1)}, bf16[1,4,48,768]{3,2,1,0:T(8,128)(2,1)S(1)}, u32[]{:S(2)}, u32[]{:S(2)}) %collective-permute-start.42) | collective-permute-done | bytes 294944 | tf_op jit(solution)/shard_map/ppermute | solution.py:806
  502.9 6.2 collective-permute-done.43
  509.2 11.7 %collective-permute-start.44 = (bf16[1,48,768]{2,1,0:T(8,128)(2,1)S(1)}, bf16[1,48,768]{2,1,0:T(8,128)(2,1)S(1)}, u32[]{:S(2)}, u32[]{:S(2)}) collective-permute-start(bf16[1,48,768]{2,1,0:T(8,128)(2,1)S(1)} %constant_dynamic-slice_fusion.1), channel_id=1, source_target_pairs={{0,2},{1,3},{2,0},{3,1},{4,6},{5,7},{6,4},{7,5},{8,10},{9,11},{10,... | collective-permute-start | bytes 221192 | tf_op jit(solution)/shard_map/ppermute | solution.py:809
  520.8 6.4 collective-permute-done.46
  527.3 4.3 collective-permute-start.47
  531.7 12.8 %collective-permute-done.47 = bf16[1,48,1792]{2,1,0:T(8,128)(2,1)S(1)} collective-permute-done((bf16[1,48,1792]{2,1,0:T(8,128)(2,1)S(1)}, bf16[1,48,1792]{2,1,0:T(8,128)(2,1)S(1)}, u32[]{:S(2)}, u32[]{:S(2)}) %collective-permute-start.47) | collective-permute-done | bytes 172064 | tf_op jit(solution)/shard_map/ppermute | solution.py:809
  545.2 7.9 %reduce-scatter.2.cloned.1.call-done = bf16[3,128,512]{2,1,0:T(8,128)(2,1)} async-done(((bf16[3,2048,512]{2,1,0:T(8,128)(2,1)}), bf16[3,128,512]{2,1,0:T(8,128)(2,1)}) %reduce-scatter.2.cloned.1.call-update) | async-done | bytes 393232 | tf_op jit(solution)/shard_map/reduce_scatter | solution.py:1044
  561.0 2.0 gather_fusion
  564.6 3.6 fusion.8
  568.3 4.4 fusion.125
  573.2 3.3 last_grads.1
  580.9 3.5 collective-permute-done.49
  584.4 4.2 collective-permute-start.52
  588.7 2.7 collective-permute-start.51
  591.9 1.9 collective-permute-done.52
  593.8 10.5 %collective-permute-done.51 = bf16[48,896]{1,0:T(8,128)(2,1)S(1)} collective-permute-done((bf16[48,896]{1,0:T(8,128)(2,1)S(1)}, bf16[48,896]{1,0:T(8,128)(2,1)S(1)}, u32[]{:S(2)}, u32[]{:S(2)}) %collective-permute-start.51) | collective-permute-done | bytes 86048 | tf_op jit(solution)/shard_map/ppermute | solution.py:809
  606.5 2.4 collective-permute-done.53
  609.4 9.6 %collective-permute-done.54 = bf16[2,48,896]{2,1,0:T(8,128)(2,1)S(1)} collective-permute-done((bf16[2,48,896]{2,1,0:T(8,128)(2,1)S(1)}, bf16[2,48,896]{2,1,0:T(8,128)(2,1)S(1)}, u32[]{:S(2)}, u32[]{:S(2)}) %collective-permute-start.54) | collective-permute-done | bytes 172064 | tf_op jit(solution)/shard_map/ppermute | solution.py:806
  619.2 2.0 fusion.5
  626.8 11.0 %all-gather.9.cloned.1.call-done = bf16[1536,2560]{1,0:T(8,128)(2,1)} async-done(((bf16[48,2560]{1,0:T(8,128)(2,1)}), bf16[1536,2560]{1,0:T(8,128)(2,1)}) %all-gather.9.cloned.1.call-update) | async-done | bytes 7864336 | tf_op jit(solution)/shard_map/all_gather | solution.py:1111
  637.7 12.1 %expand.1 = (f32[128,8960]{1,0:T(8,128)}, f32[128,8960]{1,0:T(8,128)}, f32[8960,128]{1,0:T(8,128)}, f32[1536,128]{1,0:T(8,128)}, f32[1536,128]{1,0:T(8,128)}, /*...) custom-call(bf16[32,48,2560]{2,1,0:T(8,128)(2,1)} %bitcast.195, ...), custom_call_target="tpu_custom_call" | custom-call | flops 660602880 | bytes 13762560 | tf_op jit(solution)/shard_map/expand/pallas_call | solution.py:746
  (429 shorter events, 135.0 us)
Async XLA Ops:
  7.2 46.5 %all-gather.5.cloned.1.call-start = ((), (), s32[]{:S(2)}) async-start(), calls=%async_computation.1 | async-start | bytes 1769472 | tf_op jit(solution)/shard_map/all_gather | solution.py:848
  7.2 43.3 %collective-permute-start.1 = (bf16[192,1536]{1,0:T(8,128)(2,1)}, bf16[192,1536]{1,0:T(8,128)(2,1)}, u32[]{:S(2)}, u32[]{:S(2)}) collective-permute-start(bf16[192,1536]{1,0:T(8,128)(2,1)} %refs_0_), channel_id=1, source_target_pairs={{0,16},{4,20},{8,24},{12,28},{16,0},{20,4},{24,8},{28,12},{1,17},{... | collective-permute-start | bytes 1769480 | tf_op jit(solution)/shard_map/ppermute | solution.py:806
  10.2 40.3 %collective-permute-start = (bf16[192,1536]{1,0:T(8,128)(2,1)}, bf16[192,1536]{1,0:T(8,128)(2,1)}, u32[]{:S(2)}, u32[]{:S(2)}) collective-permute-start(bf16[192,1536]{1,0:T(8,128)(2,1)} %refs_0_), channel_id=1, source_target_pairs={{0,8},{4,12},{8,0},{12,4},{16,24},{20,28},{24,16},{28,20},{1,9},{5... | collective-permute-start | bytes 1769480 | tf_op jit(solution)/shard_map/ppermute | solution.py:806
  11.8 38.8 %collective-permute-start.2 = (bf16[192,1536]{1,0:T(8,128)(2,1)}, bf16[192,1536]{1,0:T(8,128)(2,1)}, u32[]{:S(2)}, u32[]{:S(2)}) collective-permute-start(bf16[192,1536]{1,0:T(8,128)(2,1)} %refs_0_), channel_id=1, source_target_pairs={{0,24},{4,28},{8,16},{12,20},{16,8},{20,12},{24,0},{28,4},{1,25},{... | collective-permute-start | bytes 1769480 | tf_op jit(solution)/shard_map/ppermute | solution.py:806
  13.1 27.0 %collective-permute-start.8 = (f32[8,128]{0,1:T(8,128)}, f32[8,128]{0,1:T(8,128)}, u32[]{:S(2)}, u32[]{:S(2)}) collective-permute-start(f32[8,128]{0,1:T(8,128)} %broadcast_in_dim.81), channel_id=1, source_target_pairs={{0,16},{4,20},{8,24},{12,28},{16,0},{20,4},{24,8},{28,12},{1,17},{... | collective-permute-start | bytes 12296 | tf_op jit(solution)/shard_map/ppermute | solution.py:806
  16.7 119.6 %all-gather.7.cloned.1.call-start = ((), (), s32[]{:S(2)}) async-start(), calls=%async_computation.2 | async-start | bytes 6684672 | tf_op jit(solution)/shard_map/all_gather | solution.py:910
  58.0 495.1 %reduce-scatter.2.cloned.1.call-start = ((), (), s32[]{:S(2)}) async-start(), calls=%async_computation.3 | async-start | bytes 6684672 | tf_op jit(solution)/shard_map/reduce_scatter | solution.py:1044
  69.3 5.6 collective-permute-start.9
  69.5 6.8 %collective-permute-start.10 = (bf16[192,1536]{1,0:T(8,128)(2,1)}, bf16[192,1536]{1,0:T(8,128)(2,1)S(1)}, u32[]{:S(2)}, u32[]{:S(2)}) collective-permute-start(bf16[192,1536]{1,0:T(8,128)(2,1)} %collective-permute-done.refs_2_), channel_id=1, source_target_pairs={{0,4},{4,0},{8,12},{12,8},{16,20},{20,16},{24,28},{28,24},{1,5},{5... | collective-permute-start | bytes 1769480 | tf_op jit(solution)/shard_map/ppermute | solution.py:806
  69.8 7.2 %collective-permute-start.11 = (bf16[192,1536]{1,0:T(8,128)(2,1)}, bf16[192,1536]{1,0:T(8,128)(2,1)S(1)}, u32[]{:S(2)}, u32[]{:S(2)}) collective-permute-start(bf16[192,1536]{1,0:T(8,128)(2,1)} %collective-permute-done.1.refs_4_), channel_id=1, source_target_pairs={{0,4},{4,0},{8,12},{12,8},{16,20},{20,16},{24,28},{28,24},{1,5},{5... | collective-permute-start | bytes 1769480 | tf_op jit(solution)/shard_map/ppermute | solution.py:806
  70.1 8.4 %collective-permute-start.12 = (bf16[192,1536]{1,0:T(8,128)(2,1)}, bf16[192,1536]{1,0:T(8,128)(2,1)S(1)}, u32[]{:S(2)}, u32[]{:S(2)}) collective-permute-start(bf16[192,1536]{1,0:T(8,128)(2,1)} %collective-permute-done.2.refs_6_), channel_id=1, source_target_pairs={{0,4},{4,0},{8,12},{12,8},{16,20},{20,16},{24,28},{28,24},{1,5},{5... | collective-permute-start | bytes 1769480 | tf_op jit(solution)/shard_map/ppermute | solution.py:806
  73.4 17.4 %collective-permute-start.5 = (bf16[192,1536]{1,0:T(8,128)(2,1)}, bf16[192,1536]{1,0:T(8,128)(2,1)}, u32[]{:S(2)}, u32[]{:S(2)}) collective-permute-start(bf16[192,1536]{1,0:T(8,128)(2,1)} %refs_0_.2), channel_id=1, source_target_pairs={{0,24},{4,28},{8,16},{12,20},{16,8},{20,12},{24,0},{28,4},{1,25},{... | collective-permute-start | bytes 1769480 | tf_op jit(solution)/shard_map/ppermute | solution.py:806
  74.9 28.5 %collective-permute-start.4 = (bf16[192,1536]{1,0:T(8,128)(2,1)}, bf16[192,1536]{1,0:T(8,128)(2,1)S(1)}, u32[]{:S(2)}, u32[]{:S(2)}) collective-permute-start(bf16[192,1536]{1,0:T(8,128)(2,1)} %refs_0_.2), channel_id=1, source_target_pairs={{0,16},{4,20},{8,24},{12,28},{16,0},{20,4},{24,8},{28,12},{1,17},{... | collective-permute-start | bytes 1769480 | tf_op jit(solution)/shard_map/ppermute | solution.py:806
  76.3 39.0 %collective-permute-start.3 = (bf16[192,1536]{1,0:T(8,128)(2,1)}, bf16[192,1536]{1,0:T(8,128)(2,1)}, u32[]{:S(2)}, u32[]{:S(2)}) collective-permute-start(bf16[192,1536]{1,0:T(8,128)(2,1)} %refs_0_.2), channel_id=1, source_target_pairs={{0,8},{4,12},{8,0},{12,4},{16,24},{20,28},{24,16},{28,20},{1,9},{5... | collective-permute-start | bytes 1769480 | tf_op jit(solution)/shard_map/ppermute | solution.py:806
  76.9 39.2 %collective-permute-start.6 = (bf16[192,1536]{1,0:T(8,128)(2,1)}, bf16[192,1536]{1,0:T(8,128)(2,1)}, u32[]{:S(2)}, u32[]{:S(2)}) collective-permute-start(bf16[192,1536]{1,0:T(8,128)(2,1)} %get-tuple-element.219.refs_10_), channel_id=1, source_target_pairs={{0,16},{4,20},{8,24},{12,28},{16,0},{20,4},{24,8},{28,12},{1,17},{... | collective-permute-start | bytes 1769480 | tf_op jit(solution)/shard_map/ppermute | solution.py:806
  78.4 49.6 %collective-permute-start.7 = (bf16[192,1536]{1,0:T(8,128)(2,1)}, bf16[192,1536]{1,0:T(8,128)(2,1)}, u32[]{:S(2)}, u32[]{:S(2)}) collective-permute-start(bf16[192,1536]{1,0:T(8,128)(2,1)} %get-tuple-element.220.refs_11_), channel_id=1, source_target_pairs={{0,16},{4,20},{8,24},{12,28},{16,0},{20,4},{24,8},{28,12},{1,17},{... | collective-permute-start | bytes 1769480 | tf_op jit(solution)/shard_map/ppermute | solution.py:806
  135.7 9.6 %collective-permute-start.13 = (bf16[1120,1536]{1,0:T(8,128)(2,1)}, bf16[1120,1536]{1,0:T(8,128)(2,1)S(1)}, u32[]{:S(2)}, u32[]{:S(2)}) collective-permute-start(bf16[1120,1536]{1,0:T(8,128)(2,1)} %refs_0_.1), channel_id=1, source_target_pairs={{0,4},{4,0},{8,12},{12,8},{16,20},{20,16},{24,28},{28,24},{1,5},{5... | collective-permute-start | bytes 10321928 | tf_op jit(solution)/shard_map/ppermute | solution.py:806
  135.8 6.9 %collective-permute-start.14 = (bf16[192,1536]{1,0:T(8,128)(2,1)}, bf16[192,1536]{1,0:T(8,128)(2,1)}, u32[]{:S(2)}, u32[]{:S(2)}) collective-permute-start(bf16[192,1536]{1,0:T(8,128)(2,1)} %refs_0_.2), channel_id=1, source_target_pairs={{0,4},{4,0},{8,12},{12,8},{16,20},{20,16},{24,28},{28,24},{1,5},{5... | collective-permute-start | bytes 1769480 | tf_op jit(solution)/shard_map/ppermute | solution.py:806
  136.3 57.4 %collective-permute-start.23 = (bf16[2,192,2304]{2,1,0:T(8,128)(2,1)}, bf16[2,192,2304]{2,1,0:T(8,128)(2,1)}, u32[]{:S(2)}, u32[]{:S(2)}) collective-permute-start(bf16[2,192,2304]{2,1,0:T(8,128)(2,1)} %get-tuple-element.204), channel_id=1, source_target_pairs={{0,24},{4,28},{8,16},{12,20},{16,8},{20,12},{24,0},{28,4},{1,25},{... | collective-permute-start | bytes 5308424 | tf_op jit(solution)/shard_map/ppermute | solution.py:806
  137.8 77.3 %collective-permute-start.21 = (bf16[2,192,2304]{2,1,0:T(8,128)(2,1)}, bf16[2,192,2304]{2,1,0:T(8,128)(2,1)}, u32[]{:S(2)}, u32[]{:S(2)}) collective-permute-start(bf16[2,192,2304]{2,1,0:T(8,128)(2,1)} %get-tuple-element.201), channel_id=1, source_target_pairs={{0,16},{4,20},{8,24},{12,28},{16,0},{20,4},{24,8},{28,12},{1,17},{... | collective-permute-start | bytes 5308424 | tf_op jit(solution)/shard_map/ppermute | solution.py:806
  138.2 77.8 %collective-permute-start.19 = (bf16[2,192,2304]{2,1,0:T(8,128)(2,1)}, bf16[2,192,2304]{2,1,0:T(8,128)(2,1)}, u32[]{:S(2)}, u32[]{:S(2)}) collective-permute-start(bf16[2,192,2304]{2,1,0:T(8,128)(2,1)} %get-tuple-element.198), channel_id=1, source_target_pairs={{0,8},{4,12},{8,0},{12,4},{16,24},{20,28},{24,16},{28,20},{1,9},{5... | collective-permute-start | bytes 5308424 | tf_op jit(solution)/shard_map/ppermute | solution.py:806
  142.7 2.2 collective-permute-start.15
  144.9 22.8 %collective-permute-start.16 = (bf16[192,1536]{1,0:T(8,128)(2,1)}, bf16[192,1536]{1,0:T(8,128)(2,1)}, u32[]{:S(2)}, u32[]{:S(2)}) collective-permute-start(bf16[192,1536]{1,0:T(8,128)(2,1)} %copy-done.47), channel_id=1, source_target_pairs={{0,4},{4,0},{8,12},{12,8},{16,20},{20,16},{24,28},{28,24},{1,5},{5... | collective-permute-start | bytes 1769480 | tf_op jit(solution)/shard_map/ppermute | solution.py:806
  145.7 37.4 %collective-permute-start.17 = (bf16[192,1536]{1,0:T(8,128)(2,1)}, bf16[192,1536]{1,0:T(8,128)(2,1)}, u32[]{:S(2)}, u32[]{:S(2)}) collective-permute-start(bf16[192,1536]{1,0:T(8,128)(2,1)} %collective-permute-done.5.refs_6_), channel_id=1, source_target_pairs={{0,4},{4,0},{8,12},{12,8},{16,20},{20,16},{24,28},{28,24},{1,5},{5... | collective-permute-start | bytes 1769480 | tf_op jit(solution)/shard_map/ppermute | solution.py:806
  167.7 50.1 %collective-permute-start.18 = (bf16[2,192,2304]{2,1,0:T(8,128)(2,1)S(1)}, bf16[2,192,2304]{2,1,0:T(8,128)(2,1)S(1)}, u32[]{:S(2)}, u32[]{:S(2)}) collective-permute-start(bf16[2,192,2304]{2,1,0:T(8,128)(2,1)S(1)} %copy-done.30), channel_id=1, source_target_pairs={{0,4},{4,0},{8,12},{12,8},{16,20},{20,16},{24,28},{28,24},{1,5},{5... | collective-permute-start | bytes 5308424 | tf_op jit(solution)/shard_map/ppermute | solution.py:806
  216.0 4.0 collective-permute-start.20
  216.0 6.5 collective-permute-start.22
  216.5 8.6 %collective-permute-start.24 = (bf16[2,192,2304]{2,1,0:T(8,128)(2,1)}, bf16[2,192,2304]{2,1,0:T(8,128)(2,1)}, u32[]{:S(2)}, u32[]{:S(2)}) collective-permute-start(bf16[2,192,2304]{2,1,0:T(8,128)(2,1)} %collective-permute-done.23.refs_6_), channel_id=1, source_target_pairs={{0,4},{4,0},{8,12},{12,8},{16,20},{20,16},{24,28},{28,24},{1,5},{5... | collective-permute-start | bytes 5308424 | tf_op jit(solution)/shard_map/ppermute | solution.py:806
  217.2 240.9 %copy-start.77 = (pred[64]{0:T(512)(128)(4,1)}, pred[64]{0:T(512)(128)(4,1)S(1)}, u32[]{:S(2)}) copy-start(pred[64]{0:T(512)(128)(4,1)S(1)} %compare_and_fusion.2) | copy-start | bytes 196
  217.8 240.4 %copy-start.69 = (s32[384]{0:T(512)}, s32[384]{0:T(512)S(1)}, u32[]{:S(2)}) copy-start(s32[384]{0:T(512)S(1)} %get-tuple-element.345) | copy-start | bytes 4612
  217.8 240.4 %copy-start.70 = (s32[384]{0:T(512)}, s32[384]{0:T(512)S(1)}, u32[]{:S(2)}) copy-start(s32[384]{0:T(512)S(1)} %get-tuple-element.346) | copy-start | bytes 4612
  225.1 36.7 %collective-permute-start.27 = (bf16[192,1536]{1,0:T(8,128)(2,1)}, bf16[192,1536]{1,0:T(8,128)(2,1)}, u32[]{:S(2)}, u32[]{:S(2)}) collective-permute-start(bf16[192,1536]{1,0:T(8,128)(2,1)} %get-tuple-element.209.refs_8_), channel_id=1, source_target_pairs={{0,16},{4,20},{8,24},{12,28},{16,0},{20,4},{24,8},{28,12},{1,17},{... | collective-permute-start | bytes 1769480 | tf_op jit(solution)/shard_map/ppermute | solution.py:806
  225.8 37.5 %collective-permute-start.25 = (bf16[192,1536]{1,0:T(8,128)(2,1)}, bf16[192,1536]{1,0:T(8,128)(2,1)}, u32[]{:S(2)}, u32[]{:S(2)}) collective-permute-start(bf16[192,1536]{1,0:T(8,128)(2,1)} %get-tuple-element.209.refs_8_), channel_id=1, source_target_pairs={{0,8},{4,12},{8,0},{12,4},{16,24},{20,28},{24,16},{28,20},{1,9},{5... | collective-permute-start | bytes 1769480 | tf_op jit(solution)/shard_map/ppermute | solution.py:806
  227.2 36.1 %collective-permute-start.28 = (bf16[192,1536]{1,0:T(8,128)(2,1)}, bf16[192,1536]{1,0:T(8,128)(2,1)}, u32[]{:S(2)}, u32[]{:S(2)}) collective-permute-start(bf16[192,1536]{1,0:T(8,128)(2,1)} %get-tuple-element.210.refs_9_), channel_id=1, source_target_pairs={{0,16},{4,20},{8,24},{12,28},{16,0},{20,4},{24,8},{28,12},{1,17},{... | collective-permute-start | bytes 1769480 | tf_op jit(solution)/shard_map/ppermute | solution.py:806
  227.8 35.6 %collective-permute-start.26 = (bf16[192,1536]{1,0:T(8,128)(2,1)}, bf16[192,1536]{1,0:T(8,128)(2,1)}, u32[]{:S(2)}, u32[]{:S(2)}) collective-permute-start(bf16[192,1536]{1,0:T(8,128)(2,1)} %get-tuple-element.210.refs_9_), channel_id=1, source_target_pairs={{0,8},{4,12},{8,0},{12,4},{16,24},{20,28},{24,16},{28,20},{1,9},{5... | collective-permute-start | bytes 1769480 | tf_op jit(solution)/shard_map/ppermute | solution.py:806
  259.7 33.6 %collective-permute-start.29 = (bf16[192,1536]{1,0:T(8,128)(2,1)}, bf16[192,1536]{1,0:T(8,128)(2,1)}, u32[]{:S(2)}, u32[]{:S(2)}) collective-permute-start(bf16[192,1536]{1,0:T(8,128)(2,1)} %get-tuple-element.219.refs_10_), channel_id=1, source_target_pairs={{0,8},{4,12},{8,0},{12,4},{16,24},{20,28},{24,16},{28,20},{1,9},{5... | collective-permute-start | bytes 1769480 | tf_op jit(solution)/shard_map/ppermute | solution.py:806
  261.9 31.4 %collective-permute-start.30 = (bf16[192,1536]{1,0:T(8,128)(2,1)}, bf16[192,1536]{1,0:T(8,128)(2,1)S(1)}, u32[]{:S(2)}, u32[]{:S(2)}) collective-permute-start(bf16[192,1536]{1,0:T(8,128)(2,1)} %get-tuple-element.220.refs_11_), channel_id=1, source_target_pairs={{0,8},{4,12},{8,0},{12,4},{16,24},{20,28},{24,16},{28,20},{1,9},{5... | collective-permute-start | bytes 1769480 | tf_op jit(solution)/shard_map/ppermute | solution.py:806
  293.3 35.0 %collective-permute-start.31 = (bf16[192,1536]{1,0:T(8,128)(2,1)}, bf16[192,1536]{1,0:T(8,128)(2,1)}, u32[]{:S(2)}, u32[]{:S(2)}) collective-permute-start(bf16[192,1536]{1,0:T(8,128)(2,1)} %collective-permute-done.27.refs_8_), channel_id=1, source_target_pairs={{0,8},{4,12},{8,0},{12,4},{16,24},{20,28},{24,16},{28,20},{1,9},{5... | collective-permute-start | bytes 1769480 | tf_op jit(solution)/shard_map/ppermute | solution.py:806
  294.0 35.8 %collective-permute-start.32 = (bf16[192,1536]{1,0:T(8,128)(2,1)}, bf16[192,1536]{1,0:T(8,128)(2,1)}, u32[]{:S(2)}, u32[]{:S(2)}) collective-permute-start(bf16[192,1536]{1,0:T(8,128)(2,1)} %collective-permute-done.26.refs_9_), channel_id=1, source_target_pairs={{0,16},{4,20},{8,24},{12,28},{16,0},{20,4},{24,8},{28,12},{1,17},{... | collective-permute-start | bytes 1769480 | tf_op jit(solution)/shard_map/ppermute | solution.py:806
  295.5 34.3 %collective-permute-start.33 = (bf16[192,1536]{1,0:T(8,128)(2,1)}, bf16[192,1536]{1,0:T(8,128)(2,1)}, u32[]{:S(2)}, u32[]{:S(2)}) collective-permute-start(bf16[192,1536]{1,0:T(8,128)(2,1)} %collective-permute-done.6.refs_10_), channel_id=1, source_target_pairs={{0,8},{4,12},{8,0},{12,4},{16,24},{20,28},{24,16},{28,20},{1,9},{5... | collective-permute-start | bytes 1769480 | tf_op jit(solution)/shard_map/ppermute | solution.py:806
  296.1 33.7 %collective-permute-start.34 = (bf16[192,1536]{1,0:T(8,128)(2,1)S(1)}, bf16[192,1536]{1,0:T(8,128)(2,1)}, u32[]{:S(2)}, u32[]{:S(2)}) collective-permute-start(bf16[192,1536]{1,0:T(8,128)(2,1)S(1)} %collective-permute-done.30.refs_11_), channel_id=1, source_target_pairs={{0,16},{4,20},{8,24},{12,28},{16,0},{20,4},{24,8},{28,12},{1,17},{... | collective-permute-start | bytes 1769480 | tf_op jit(solution)/shard_map/ppermute | solution.py:806
  327.6 35.2 %collective-permute-start.36 = (bf16[384,1664]{1,0:T(8,128)(2,1)}, bf16[384,1664]{1,0:T(8,128)(2,1)}, u32[]{:S(2)}, u32[]{:S(2)}) collective-permute-start(bf16[384,1664]{1,0:T(8,128)(2,1)} %get-tuple-element.241), channel_id=1, source_target_pairs={{0,8},{4,12},{8,0},{12,4},{16,24},{20,28},{24,16},{28,20},{1,9},{5... | collective-permute-start | bytes 3833864 | tf_op jit(solution)/shard_map/ppermute | solution.py:806
  328.3 33.0 %collective-permute-start.35 = (bf16[384,1664]{1,0:T(8,128)(2,1)}, bf16[384,1664]{1,0:T(8,128)(2,1)}, u32[]{:S(2)}, u32[]{:S(2)}) collective-permute-start(bf16[384,1664]{1,0:T(8,128)(2,1)} %get-tuple-element.240), channel_id=1, source_target_pairs={{0,16},{4,20},{8,24},{12,28},{16,0},{20,4},{24,8},{28,12},{1,17},{... | collective-permute-start | bytes 3833864 | tf_op jit(solution)/shard_map/ppermute | solution.py:806
  359.8 28.0 %collective-permute-start.37 = (bf16[384,1664]{1,0:T(8,128)(2,1)}, bf16[384,1664]{1,0:T(8,128)(2,1)}, u32[]{:S(2)}, u32[]{:S(2)}) collective-permute-start(bf16[384,1664]{1,0:T(8,128)(2,1)} %get-tuple-element.242), channel_id=1, source_target_pairs={{0,24},{4,28},{8,16},{12,20},{16,8},{20,12},{24,0},{28,4},{1,25},{... | collective-permute-start | bytes 3833864 | tf_op jit(solution)/shard_map/ppermute | solution.py:806
  399.4 35.7 %collective-permute-start.38 = (bf16[384,1664]{1,0:T(8,128)(2,1)}, bf16[384,1664]{1,0:T(8,128)(2,1)}, u32[]{:S(2)}, u32[]{:S(2)}) collective-permute-start(bf16[384,1664]{1,0:T(8,128)(2,1)} %get-tuple-element.246), channel_id=1, source_target_pairs={{0,16},{4,20},{8,24},{12,28},{16,0},{20,4},{24,8},{28,12},{1,17},{... | collective-permute-start | bytes 3833864 | tf_op jit(solution)/shard_map/ppermute | solution.py:806
  399.9 35.2 %collective-permute-start.39 = (bf16[384,1664]{1,0:T(8,128)(2,1)}, bf16[384,1664]{1,0:T(8,128)(2,1)}, u32[]{:S(2)}, u32[]{:S(2)}) collective-permute-start(bf16[384,1664]{1,0:T(8,128)(2,1)} %get-tuple-element.247), channel_id=1, source_target_pairs={{0,8},{4,12},{8,0},{12,4},{16,24},{20,28},{24,16},{28,20},{1,9},{5... | collective-permute-start | bytes 3833864 | tf_op jit(solution)/shard_map/ppermute | solution.py:806
  423.5 31.3 %collective-permute-start.40 = (bf16[384,1664]{1,0:T(8,128)(2,1)}, bf16[384,1664]{1,0:T(8,128)(2,1)}, u32[]{:S(2)}, u32[]{:S(2)}) collective-permute-start(bf16[384,1664]{1,0:T(8,128)(2,1)} %get-tuple-element.252), channel_id=1, source_target_pairs={{0,24},{4,28},{8,16},{12,20},{16,8},{20,12},{24,0},{28,4},{1,25},{... | collective-permute-start | bytes 3833864 | tf_op jit(solution)/shard_map/ppermute | solution.py:806
  435.2 202.6 %all-gather.9.cloned.1.call-start = ((), (), s32[]{:S(2)}) async-start(), calls=%async_computation.4 | async-start | bytes 8110080 | tf_op jit(solution)/shard_map/all_gather | solution.py:1111
  473.1 8.0 %collective-permute-start.41 = (bf16[2,4,48,768]{3,2,1,0:T(8,128)(2,1)S(1)}, bf16[2,4,48,768]{3,2,1,0:T(8,128)(2,1)}, u32[]{:S(2)}, u32[]{:S(2)}) collective-permute-start(bf16[2,4,48,768]{3,2,1,0:T(8,128)(2,1)S(1)} %dynamic-slice_bitcast_fusion), channel_id=1, source_target_pairs={{0,4},{4,0},{8,12},{12,8},{16,20},{20,16},{24,28},{28,24},{1,5},{5... | collective-permute-start | bytes 1769480 | tf_op jit(solution)/shard_map/ppermute | solution.py:806
  480.3 6.2 collective-permute-start.45
  482.3 18.2 %collective-permute-start.42 = (bf16[1,4,48,768]{3,2,1,0:T(8,128)(2,1)S(1)}, bf16[1,4,48,768]{3,2,1,0:T(8,128)(2,1)S(1)}, u32[]{:S(2)}, u32[]{:S(2)}) collective-permute-start(bf16[1,4,48,768]{3,2,1,0:T(8,128)(2,1)S(1)} %constant_dynamic-slice_fusion.2), channel_id=1, source_target_pairs={{0,8},{4,12},{8,0},{12,4},{16,24},{20,28},{24,16},{28,20},{1,9},{5... | collective-permute-start | bytes 884744 | tf_op jit(solution)/shard_map/ppermute | solution.py:806
  500.7 57.6 %copy-start.3 = (bf16[3,128,1536]{2,1,0:T(8,128)(2,1)S(1)}, bf16[3,128,1536]{2,1,0:T(8,128)(2,1)}, u32[]{:S(2)}) copy-start(bf16[3,128,1536]{2,1,0:T(8,128)(2,1)} %param.31) | copy-start | bytes 3538948
  500.7 8.4 %collective-permute-start.43 = (bf16[2,48,768]{2,1,0:T(8,128)(2,1)S(1)}, bf16[2,48,768]{2,1,0:T(8,128)(2,1)S(1)}, u32[]{:S(2)}, u32[]{:S(2)}) collective-permute-start(bf16[2,48,768]{2,1,0:T(8,128)(2,1)S(1)} %dynamic-slice_bitcast_fusion.2), channel_id=1, source_target_pairs={{0,1},{1,0},{2,3},{3,2},{4,5},{5,4},{6,7},{7,6},{8,9},{9,8},{10,11... | collective-permute-start | bytes 442376 | tf_op jit(solution)/shard_map/ppermute | solution.py:809
  502.3 24.9 %collective-permute-start.46 = (bf16[2,48,1792]{2,1,0:T(8,128)(2,1)S(1)}, bf16[2,48,1792]{2,1,0:T(8,128)(2,1)S(1)}, u32[]{:S(2)}, u32[]{:S(2)}) collective-permute-start(bf16[2,48,1792]{2,1,0:T(8,128)(2,1)S(1)} %dynamic-slice_bitcast_fusion.1), channel_id=1, source_target_pairs={{0,1},{1,0},{2,3},{3,2},{4,5},{5,4},{6,7},{7,6},{8,9},{9,8},{10,11... | collective-permute-start | bytes 1032200 | tf_op jit(solution)/shard_map/ppermute | solution.py:809
  509.2 22.5 %collective-permute-start.44 = (bf16[1,48,768]{2,1,0:T(8,128)(2,1)S(1)}, bf16[1,48,768]{2,1,0:T(8,128)(2,1)S(1)}, u32[]{:S(2)}, u32[]{:S(2)}) collective-permute-start(bf16[1,48,768]{2,1,0:T(8,128)(2,1)S(1)} %constant_dynamic-slice_fusion.1), channel_id=1, source_target_pairs={{0,2},{1,3},{2,0},{3,1},{4,6},{5,7},{6,4},{7,5},{8,10},{9,11},{10,... | collective-permute-start | bytes 221192 | tf_op jit(solution)/shard_map/ppermute | solution.py:809
  527.3 17.1 %collective-permute-start.47 = (bf16[1,48,1792]{2,1,0:T(8,128)(2,1)S(1)}, bf16[1,48,1792]{2,1,0:T(8,128)(2,1)S(1)}, u32[]{:S(2)}, u32[]{:S(2)}) collective-permute-start(bf16[1,48,1792]{2,1,0:T(8,128)(2,1)S(1)} %constant_dynamic-slice_fusion), channel_id=1, source_target_pairs={{0,2},{1,3},{2,0},{3,1},{4,6},{5,7},{6,4},{7,5},{8,10},{9,11},{10,... | collective-permute-start | bytes 516104 | tf_op jit(solution)/shard_map/ppermute | solution.py:809
  577.4 2.0 collective-permute-start.48
  579.4 5.0 collective-permute-start.49
  584.4 9.3 %collective-permute-start.52 = (bf16[48,896]{1,0:T(8,128)(2,1)S(1)}, bf16[48,896]{1,0:T(8,128)(2,1)S(1)}, u32[]{:S(2)}, u32[]{:S(2)}) collective-permute-start(bf16[48,896]{1,0:T(8,128)(2,1)S(1)} %fusion.65), channel_id=1, source_target_pairs={{0,3},{1,2},{2,1},{3,0},{4,7},{5,6},{6,5},{7,4},{8,11},{9,10},{10,... | collective-permute-start | bytes 258056 | tf_op jit(solution)/shard_map/ppermute | solution.py:809
  588.7 15.6 %collective-permute-start.51 = (bf16[48,896]{1,0:T(8,128)(2,1)S(1)}, bf16[48,896]{1,0:T(8,128)(2,1)S(1)}, u32[]{:S(2)}, u32[]{:S(2)}) collective-permute-start(bf16[48,896]{1,0:T(8,128)(2,1)S(1)} %fusion.65), channel_id=1, source_target_pairs={{0,2},{1,3},{2,0},{3,1},{4,6},{5,7},{6,4},{7,5},{8,10},{9,11},{10,... | collective-permute-start | bytes 258056 | tf_op jit(solution)/shard_map/ppermute | solution.py:809
  591.4 12.9 %collective-permute-start.50 = (bf16[48,896]{1,0:T(8,128)(2,1)S(1)}, bf16[48,896]{1,0:T(8,128)(2,1)S(1)}, u32[]{:S(2)}, u32[]{:S(2)}) collective-permute-start(bf16[48,896]{1,0:T(8,128)(2,1)S(1)} %fusion.65), channel_id=1, source_target_pairs={{0,1},{1,0},{2,3},{3,2},{4,5},{5,4},{6,7},{7,6},{8,9},{9,8},{10,11... | collective-permute-start | bytes 258056 | tf_op jit(solution)/shard_map/ppermute | solution.py:809
  604.4 4.6 collective-permute-start.53
  608.9 10.1 %collective-permute-start.54 = (bf16[2,48,896]{2,1,0:T(8,128)(2,1)S(1)}, bf16[2,48,896]{2,1,0:T(8,128)(2,1)S(1)}, u32[]{:S(2)}, u32[]{:S(2)}) collective-permute-start(bf16[2,48,896]{2,1,0:T(8,128)(2,1)S(1)} %pad_maximum_fusion.10), channel_id=1, source_target_pairs={{0,16},{4,20},{8,24},{12,28},{16,0},{20,4},{24,8},{28,12},{1,17},{... | collective-permute-start | bytes 516104 | tf_op jit(solution)/shard_map/ppermute | solution.py:806
  619.1 2.1 collective-permute-start.55
  (83 other events, 730.0 us)
Sparse Core Ops, SparseCore 0:
  16.8 36.8 all-gather.4
  58.1 75.2 all-gather.6
  435.3 117.7 reduce-scatter.1
  556.9 80.8 all-gather.8

commit v5 on v4

--- a/solution.py
+++ b/solution.py
@@ -917,9 +917,24 @@
             found += [part, swap(part, 1)]
         return found
 
-    late_lift = (
+    query_rot, query_narrow, w_query = with_blocks(
+        queries_kernel, "queries", seqs, me, after(both_cores(rows_q), pair),
+        [
+            after(normed, rows_o, g0_pieces), query_shrink, query_expand, query_bias.astype(F32)[None], flat_cosine,
+            sine_signed,
+        ],
+        [
+            jax.ShapeDtypeStruct((tokens, model), BF),
+            jax.ShapeDtypeStruct((tokens, lanes), BF),
+        ],
+    )
+
+    late_lift = after(
+        (
         gate_lift_factors, upper_lift_factors, down_reduce_factors, down_lift_factors,
         gate_reduce_factors, upper_reduce_factors,
+        ),
+        query_rot,
     )
     gate_shrink, up_shrink = shrink_of(late_lift[4]), shrink_of(late_lift[5])
     down_expand = expand_of(late_lift[3])
@@ -930,7 +945,7 @@
         )
         for f in range(fsdp_n)
     ]
-    late_down, late_gate, late_up = down_reduce_factors, gate_lift_factors, upper_lift_factors
+    late_down, late_gate, late_up = late_lift[2], late_lift[0], late_lift[1]
     shrink_d = jnp.pad(
         lax.dynamic_slice_in_dim(late_down, chip * hq, hq, 0), ((0, pad), (0, 0))
     )
@@ -940,23 +955,14 @@
     feed_factors = [
         reduce_factors[f] + lift_factors[f] + (shrink_of(shrink_d, f),) for f in range(fsdp_n)
     ]
-    query_rot, query_narrow, w_query = with_blocks(
-        queries_kernel, "queries", seqs, me, after(both_cores(rows_q), pair),
-        [
-            after(normed, rows_o, g0_pieces, feed_factors, gate_shrink, up_shrink, down_expand), query_shrink, query_expand, query_bias.astype(F32)[None], flat_cosine,
-            sine_signed,
-        ],
-        [
-            jax.ShapeDtypeStruct((tokens, model), BF),
-            jax.ShapeDtypeStruct((tokens, lanes), BF),
-        ],
-    )
-
     down_rows = [down_weight, swap(after(down_weight, query_rot), 1)]
     w_down = assemble(core, after(down_rows, query_rot), hp)
-    attended, lse = attend(info, after(query_rot, w_down), pair_all, seqs, spans, span_len)
+    attended, lse = attend(
+        info, after(query_rot, w_down, feed_factors, gate_shrink, up_shrink, down_expand),
+        pair_all, seqs, spans, span_len,
+    )
     for k in range(1, chips):
-        blocks[k] = swap(after(parts[k], pair_all, query_rot), 2 * k)
+        blocks[k] = swap(after(parts[k], rows_o), 2 * k)
     output_blocks = both_cores(after(rows_o, query_rot))
     middle, normed_two, normed_top, normed_bottom, output_narrow, w_output = with_blocks(
         outputs_kernel, "outputs", seqs, me, output_blocks,

time: 663 us -> 647 us (0.976)
  starting transfers between devices: 97 us -> 61.5 us
  Pallas kernels: 209 us -> 221 us
    ppermute x7, starting transfers between devices: 25.1 us -> 6.74 us  [swap_seq(): return lax.ppermute(value, 'seq', [(i, i ^ k) for i in range(seq_n)])]
    ppermute x49, starting transfers between devices: 71.6 us -> 54.4 us  [swap(): return lax.ppermute(value, PLANE, [(i, i ^ k) for i in range(plane)])]
    ppermute x7, waiting for transfers between devices: 37.8 us -> 53.1 us  [swap_seq(): return lax.ppermute(value, 'seq', [(i, i ^ k) for i in range(seq_n)])]
    ppermute x49, waiting for transfers between devices: 134 us -> 124 us  [swap(): return lax.ppermute(value, PLANE, [(i, i ^ k) for i in range(plane)])]
  transfers between devices with their start and end apart: 60 -> 60, of which waited for: 27 -> 26; matrix products, arithmetic and copies ran while one was open for 21% -> 22% of each run, Pallas kernels for 28% -> 30%
where the time goes in v5:
time: 647 us; the launch traced here: 643 us
  Pallas kernels  221 us (34%)
  waiting for transfers between devices  195 us (30%)
  starting transfers between devices  61.5 us (10%)
  local copies, waits for them, and re-layouts  56 us (9%)
  other arithmetic  51.2 us (8%)
  matrix products  42.2 us (7%)
  between operations  16 us (2%)
    ppermute x49, waiting for transfers between devices, swap(): return lax.ppermute(value, PLANE, [(i, i ^ k) for i in range(plane)])  124 us
    pallas_call x4, Pallas kernels, feed(): pl.pallas_call(functools.partial(feed_kernel, seqs, tuple(kinds)), grid_s...  120 us
    ppermute x49, starting transfers between devices, swap(): return lax.ppermute(value, PLANE, [(i, i ^ k) for i in range(plane)])  54.4 us
    ppermute x7, waiting for transfers between devices, swap_seq(): return lax.ppermute(value, 'seq', [(i, i ^ k) for i in range(seq_n)])  53.1 us
    pallas_call x1, Pallas kernels, attend_back(): pl.pallas_call(functools.partial(attend_back_kernel, spans, span_len, tok...  26.4 us
    dot_general x21, matrix products, mm_tn(): lax.dot_general(left, right, (((0,), (0,)), ((), ())), preferred_element_...  22.1 us
    pallas_call x1, Pallas kernels, attend(): pl.pallas_call(functools.partial(attend_kernel, spans, span_len, tokens),...  20 us
    pallas_call x2, Pallas kernels, with_blocks(): pl.pallas_call(functools.partial(kernel, seqs, count), grid_spec=pltpu.Pr...  18.2 us
  transfers between devices with their start and end apart: 60, of which 26 were waited for; matrix products, arithmetic and copies ran while one was open for 22% of the time, Pallas kernels for 30%

profile of v5, /device:TPU:0, one launch (start us, length us, event | category | flops | bytes accessed | tf_op | source)
XLA Modules:
  0.0 642.7 jit_solution(6554715913486277042)
XLA Ops:
  7.2 3.0 collective-permute-start.1
  13.1 1.9 collective-permute-start.13
  17.8 2.3 fusion.119
  20.1 4.1 fusion.115
  24.2 1.9 fusion.114
  28.6 2.1 select_bitcast_fusion
  33.4 3.3 fusion.10
  48.7 2.0 convolution_convert_fusion.17.eo_ref.oe_ref
  50.7 3.0 all-gather.5.cloned.1.call-done.w_ref
  53.7 4.3 keys_values.1
  63.8 11.6 %collective-permute-done.5.refs_6_ = bf16[192,1536]{1,0:T(8,128)(2,1)S(1)} collective-permute-done((bf16[192,1536]{1,0:T(8,128)(2,1)S(1)}, bf16[192,1536]{1,0:T(8,128)(2,1)S(1)}, u32[]{:S(2)}, u32[]{:S(2)}) %collective-permute-start.5) | collective-permute-done | bytes 589856 | tf_op jit(solution)/shard_map/ppermute | solution.py:806
  75.4 12.7 %collective-permute-done.4.refs_4_ = bf16[192,1536]{1,0:T(8,128)(2,1)} collective-permute-done((bf16[192,1536]{1,0:T(8,128)(2,1)S(1)}, bf16[192,1536]{1,0:T(8,128)(2,1)}, u32[]{:S(2)}, u32[]{:S(2)}) %collective-permute-start.4) | collective-permute-done | bytes 589856 | tf_op jit(solution)/shard_map/ppermute | solution.py:806
  88.1 3.4 collective-permute-done.3.refs_2_
  92.4 8.3 %collective-permute-done.6.refs_10_ = bf16[192,1536]{1,0:T(8,128)(2,1)S(1)} collective-permute-done((bf16[192,1536]{1,0:T(8,128)(2,1)}, bf16[192,1536]{1,0:T(8,128)(2,1)S(1)}, u32[]{:S(2)}, u32[]{:S(2)}) %collective-permute-start.6) | collective-permute-done | bytes 589856 | tf_op jit(solution)/shard_map/ppermute | solution.py:806
  103.4 9.3 %collective-permute-done.7.refs_11_ = bf16[192,1536]{1,0:T(8,128)(2,1)} collective-permute-done((bf16[192,1536]{1,0:T(8,128)(2,1)}, bf16[192,1536]{1,0:T(8,128)(2,1)}, u32[]{:S(2)}, u32[]{:S(2)}) %collective-permute-start.7) | collective-permute-done | bytes 589856 | tf_op jit(solution)/shard_map/ppermute | solution.py:806
  116.3 7.6 %queries.1 = (bf16[384,1536]{1,0:T(8,128)(2,1)}, bf16[384,64]{1,0:T(8,128)(2,1)}, bf16[1536,1536]{1,0:T(8,128)(2,1)}) custom-call(s32[1]{0:T(128)} %bitcast.info, bf16[384,1536]{1,0:T(8,128)(2,1)} %get-tuple-element.176.normed_ref, bf16[1536,64]{1,0:T(8,128)(2,1)} %bitcast.194, bf16[64,1536]{1,0:T(8,128)(2,1)} %convolution_convert_fusion.16.eq_ref, ...), custom_call_target="tpu_custom_call" | custom-call | flops 1811939328 | bytes 9437184 | tf_op jit(solution)/shard_map/queries/pallas_call | solution.py:482
  130.5 2.0 select_bitcast_fusion.2
  135.2 1.8 copy.102
  137.0 1.8 copy.103
  148.1 5.0 assemble.1.refs_14_
  153.2 20.0 %attend.1 = (bf16[384,1536]{1,0:T(8,128)(2,1)}, f32[6,8,768]{2,1,0:T(8,128)}) custom-call(s32[29]{0:T(128)} %pad_add_fusion.info, bf16[384,1536]{1,0:T(8,128)(2,1)} %get-tuple-element.198.q_ref, bf16[3,2048,512]{2,1,0:T(8,128)(2,1)} %all-gather.7.cloned.1.call-done.k_ref.v_ref, bf16[3,2048,512]{2,1,0:T(8,128)(2,1)} %all-gather.7.cloned.1.call-done.k_ref.v_ref), custom_call_target="tpu_custom_call" | custom-call | flops 4831838208 | bytes 6291456 | tf_op jit(solution)/shard_map/attend/pallas_call | solution.py:152
  174.1 10.6 %outputs.1 = (f32[384,1536]{1,0:T(8,128)}, bf16[384,1536]{1,0:T(8,128)(2,1)}, bf16[192,1536]{1,0:T(8,128)(2,1)}, bf16[192,1536]{1,0:T(8,128)(2,1)}, bf16[384,64]{1,0:T(8,128)(2,1)}, /*index=5*/bf16[1536,1536]{1,0:T(8,128)(2,1)}) custom-call(s32[1]{0:T(128)} %bitcast.info, bf16[384,1536]{1,0:T(8,128)(2,1)} %get-tuple-element.199.attended_ref.o_ref, ...), custom_call_target="tpu_custom_call" | custom-call | flops 1811939328 | bytes 9437184 | tf_op jit(solution)/shard_map/outputs/pallas_call | solution.py:482
  184.7 7.5 %collective-permute-done.23.refs_6_ = bf16[2,192,2304]{2,1,0:T(8,128)(2,1)} collective-permute-done((bf16[2,192,2304]{2,1,0:T(8,128)(2,1)}, bf16[2,192,2304]{2,1,0:T(8,128)(2,1)}, u32[]{:S(2)}, u32[]{:S(2)}) %collective-permute-start.23) | collective-permute-done | bytes 1769504 | tf_op jit(solution)/shard_map/ppermute | solution.py:806
  194.0 3.9 collective-permute-done.20.refs_3_
  198.7 2.5 collective-permute-done.24.refs_7_
  201.9 7.8 %collective-permute-start.25 = (bf16[192,1536]{1,0:T(8,128)(2,1)}, bf16[192,1536]{1,0:T(8,128)(2,1)}, u32[]{:S(2)}, u32[]{:S(2)}) collective-permute-start(bf16[192,1536]{1,0:T(8,128)(2,1)} %get-tuple-element.221.refs_8_), channel_id=1, source_target_pairs={{0,8},{4,12},{8,0},{12,4},{16,24},{20,28},{24,16},{28,20},{1,9},{5... | collective-permute-start | bytes 1769480 | tf_op jit(solution)/shard_map/ppermute | solution.py:806
  209.7 2.0 collective-permute-start.28
  212.6 29.7 %feed.4 = (bf16[384,1664]{1,0:T(8,128)(2,1)}, bf16[384,1664]{1,0:T(8,128)(2,1)}, f32[64,2304]{1,0:T(8,128)}, f32[64,2304]{1,0:T(8,128)}, f32[64,2304]{1,0:T(8,128)}) custom-call(s32[2]{0:T(128)} %pad_add_fusion.1.info, bf16[2,192,2304]{2,1,0:T(8,128)(2,1)} %get-tuple-element.208.refs_0_, bf16[2,192,2304]{2,1,0:T(8,128)(2,1)} %collective-permute-done.18.refs_1_, ...), custom_call_target="tpu_custom_call" | custom-call | flops 16986931200 | bytes 21233664 | tf_op jit(solution)/shard_map/feed/pallas_call | solution.py:608
  242.2 2.1 collective-permute-start.29
  246.0 29.9 %feed.5 = (bf16[384,1664]{1,0:T(8,128)(2,1)}, bf16[384,1664]{1,0:T(8,128)(2,1)}, f32[64,2304]{1,0:T(8,128)}, f32[64,2304]{1,0:T(8,128)}, f32[64,2304]{1,0:T(8,128)}) custom-call(s32[2]{0:T(128)} %pad_add_fusion.1.info, bf16[2,192,2304]{2,1,0:T(8,128)(2,1)} %get-tuple-element.208.refs_0_, bf16[2,192,2304]{2,1,0:T(8,128)(2,1)} %collective-permute-done.18.refs_1_, ...), custom_call_target="tpu_custom_call" | custom-call | flops 16986931200 | bytes 21233664 | tf_op jit(solution)/shard_map/feed/pallas_call | solution.py:608
  275.9 2.0 collective-permute-start.31
  278.1 1.9 collective-permute-start.34
  280.1 30.1 %feed.6 = (bf16[384,1664]{1,0:T(8,128)(2,1)}, bf16[384,1664]{1,0:T(8,128)(2,1)}, f32[64,2304]{1,0:T(8,128)}, f32[64,2304]{1,0:T(8,128)}, f32[64,2304]{1,0:T(8,128)}) custom-call(s32[2]{0:T(128)} %pad_add_fusion.1.info, bf16[2,192,2304]{2,1,0:T(8,128)(2,1)} %get-tuple-element.208.refs_0_, bf16[2,192,2304]{2,1,0:T(8,128)(2,1)} %collective-permute-done.18.refs_1_, ...), custom_call_target="tpu_custom_call" | custom-call | flops 16986931200 | bytes 21233664 | tf_op jit(solution)/shard_map/feed/pallas_call | solution.py:608
  310.2 2.0 collective-permute-start.36
  313.0 30.0 %feed.7 = (bf16[384,1664]{1,0:T(8,128)(2,1)}, bf16[384,1664]{1,0:T(8,128)(2,1)}, f32[64,2304]{1,0:T(8,128)}, f32[64,2304]{1,0:T(8,128)}, f32[64,2304]{1,0:T(8,128)}) custom-call(s32[2]{0:T(128)} %pad_add_fusion.1.info, bf16[2,192,2304]{2,1,0:T(8,128)(2,1)} %get-tuple-element.208.refs_0_, bf16[2,192,2304]{2,1,0:T(8,128)(2,1)} %collective-permute-done.18.refs_1_, ...), custom_call_target="tpu_custom_call" | custom-call | flops 16986931200 | bytes 21233664 | tf_op jit(solution)/shard_map/feed/pallas_call | solution.py:608
  345.4 3.0 convert_add_fusion.1.most_ref
  348.5 22.9 %collective-permute-done.37.last_ref = bf16[384,1664]{1,0:T(8,128)(2,1)} collective-permute-done((bf16[384,1664]{1,0:T(8,128)(2,1)}, bf16[384,1664]{1,0:T(8,128)(2,1)}, u32[]{:S(2)}, u32[]{:S(2)}) %collective-permute-start.37) | collective-permute-done | bytes 1277984 | tf_op jit(solution)/shard_map/ppermute | solution.py:806
  371.4 11.5 %before_attention.1 = (f32[384,1536]{1,0:T(8,128)}, bf16[384,1536]{1,0:T(8,128)(2,1)}, bf16[384,64]{1,0:T(8,128)(2,1)}, bf16[384,64]{1,0:T(8,128)(2,1)}, bf16[38...) custom-call(f32[384,1664]{1,0:T(8,128)} %convert_add_fusion.1.most_ref, bf16[384,1664]{1,0:T(8,128)(2,1)} %collective-permute-done.37.last_ref, ...), custom_call_target="tpu_custom_call" | custom-call | flops 1811939328 | bytes 17694720 | tf_op jit(solution)/shard_map/before_attention/pallas_call | solution.py:401
  385.7 26.4 %attend_back.1 = (bf16[384,1536]{1,0:T(8,128)(2,1)}, bf16[3,2048,512]{2,1,0:T(8,128)(2,1)}) custom-call(s32[29]{0:T(128)} %pad_add_fusion.info, bf16[384,1536]{1,0:T(8,128)(2,1)} %get-tuple-element.198.q_ref, bf16[384,1536]{1,0:T(8,128)(2,1)} %get-tuple-element.261.do_ref, bf16[384,1536]{1,0:T(8,128)(2,1)} %get-tuple-element.199.attended_ref.o_ref, ...), custom_call_target="tpu_custom_call" | custom-call | flops 12079595520 | bytes 12582912 | tf_op jit(solution)/shard_map/attend_back/pallas_call | solution.py:253
  413.0 12.8 %collective-permute-start.40 = (bf16[384,1664]{1,0:T(8,128)(2,1)}, bf16[384,1664]{1,0:T(8,128)(2,1)}, u32[]{:S(2)}, u32[]{:S(2)}) collective-permute-start(bf16[384,1664]{1,0:T(8,128)(2,1)} %get-tuple-element.264), channel_id=1, source_target_pairs={{0,24},{4,28},{8,16},{12,20},{16,8},{20,12},{24,0},{28,4},{1,25},{... | collective-permute-start | bytes 3833864 | tf_op jit(solution)/shard_map/ppermute | solution.py:806
  427.3 2.0 copy.106
  429.5 2.4 fusion.123
  433.6 1.9 broadcast_multiply_fusion
  437.3 3.0 copy.109
  444.8 10.0 %collective-permute-done.40 = bf16[384,1664]{1,0:T(8,128)(2,1)} collective-permute-done((bf16[384,1664]{1,0:T(8,128)(2,1)}, bf16[384,1664]{1,0:T(8,128)(2,1)}, u32[]{:S(2)}, u32[]{:S(2)}) %collective-permute-start.40) | collective-permute-done | bytes 1277984 | tf_op jit(solution)/shard_map/ppermute | solution.py:806
  454.8 2.9 convert_add_fusion
  479.7 12.3 %collective-permute-done.42 = bf16[1,4,48,768]{3,2,1,0:T(8,128)(2,1)S(1)} collective-permute-done((bf16[1,4,48,768]{3,2,1,0:T(8,128)(2,1)S(1)}, bf16[1,4,48,768]{3,2,1,0:T(8,128)(2,1)S(1)}, u32[]{:S(2)}, u32[]{:S(2)}) %collective-permute-start.42) | collective-permute-done | bytes 294944 | tf_op jit(solution)/shard_map/ppermute | solution.py:806
  494.3 10.8 %collective-permute-done.43 = bf16[2,48,768]{2,1,0:T(8,128)(2,1)S(1)} collective-permute-done((bf16[2,48,768]{2,1,0:T(8,128)(2,1)S(1)}, bf16[2,48,768]{2,1,0:T(8,128)(2,1)S(1)}, u32[]{:S(2)}, u32[]{:S(2)}) %collective-permute-start.43) | collective-permute-done | bytes 147488 | tf_op jit(solution)/shard_map/ppermute | solution.py:809
  505.3 10.0 %collective-permute-done.46 = bf16[2,48,1792]{2,1,0:T(8,128)(2,1)S(1)} collective-permute-done((bf16[2,48,1792]{2,1,0:T(8,128)(2,1)S(1)}, bf16[2,48,1792]{2,1,0:T(8,128)(2,1)S(1)}, u32[]{:S(2)}, u32[]{:S(2)}) %collective-permute-start.46) | collective-permute-done | bytes 344096 | tf_op jit(solution)/shard_map/ppermute | solution.py:809
  515.6 19.8 %collective-permute-done.47 = bf16[1,48,1792]{2,1,0:T(8,128)(2,1)S(1)} collective-permute-done((bf16[1,48,1792]{2,1,0:T(8,128)(2,1)S(1)}, bf16[1,48,1792]{2,1,0:T(8,128)(2,1)S(1)}, u32[]{:S(2)}, u32[]{:S(2)}) %collective-permute-start.47) | collective-permute-done | bytes 172064 | tf_op jit(solution)/shard_map/ppermute | solution.py:809
  536.2 3.7 reduce-scatter.2.cloned.1.call-done
  547.8 2.0 gather_fusion
  551.3 3.6 fusion.8
  554.9 4.4 fusion.120
  559.8 3.3 last_grads.1
  567.6 4.9 collective-permute-done.49
  572.6 3.8 collective-permute-start.51
  577.4 3.9 collective-permute-done.52
  581.4 8.5 %collective-permute-done.51 = bf16[48,896]{1,0:T(8,128)(2,1)S(1)} collective-permute-done((bf16[48,896]{1,0:T(8,128)(2,1)S(1)}, bf16[48,896]{1,0:T(8,128)(2,1)S(1)}, u32[]{:S(2)}, u32[]{:S(2)}) %collective-permute-start.51) | collective-permute-done | bytes 86048 | tf_op jit(solution)/shard_map/ppermute | solution.py:809
  592.0 2.5 collective-permute-done.53
  595.2 9.4 %collective-permute-done.54 = bf16[2,48,896]{2,1,0:T(8,128)(2,1)S(1)} collective-permute-done((bf16[2,48,896]{2,1,0:T(8,128)(2,1)S(1)}, bf16[2,48,896]{2,1,0:T(8,128)(2,1)S(1)}, u32[]{:S(2)}, u32[]{:S(2)}) %collective-permute-start.54) | collective-permute-done | bytes 172064 | tf_op jit(solution)/shard_map/ppermute | solution.py:806
  604.8 2.0 fusion.5
  612.4 11.2 %all-gather.9.cloned.1.call-done = bf16[1536,2560]{1,0:T(8,128)(2,1)} async-done(((bf16[48,2560]{1,0:T(8,128)(2,1)}), bf16[1536,2560]{1,0:T(8,128)(2,1)}) %all-gather.9.cloned.1.call-update) | async-done | bytes 7864336 | tf_op jit(solution)/shard_map/all_gather | solution.py:1117
  623.6 12.1 %expand.1 = (f32[128,8960]{1,0:T(8,128)}, f32[128,8960]{1,0:T(8,128)}, f32[8960,128]{1,0:T(8,128)}, f32[1536,128]{1,0:T(8,128)}, f32[1536,128]{1,0:T(8,128)}, /*...) custom-call(bf16[32,48,2560]{2,1,0:T(8,128)(2,1)} %bitcast.191, ...), custom_call_target="tpu_custom_call" | custom-call | flops 660602880 | bytes 13762560 | tf_op jit(solution)/shard_map/expand/pallas_call | solution.py:746
  (445 shorter events, 125.9 us)
Async XLA Ops:
  7.2 126.8 %copy-start = (bf16[8960,128]{1,0:T(8,128)(2,1)S(1)}, bf16[8960,128]{1,0:T(8,128)(2,1)}, u32[]{:S(2)}) copy-start(bf16[8960,128]{1,0:T(8,128)(2,1)} %param.59) | copy-start | bytes 6881284
  7.2 46.5 %all-gather.5.cloned.1.call-start = ((), (), s32[]{:S(2)}) async-start(), calls=%async_computation.1 | async-start | bytes 1769472 | tf_op jit(solution)/shard_map/all_gather | solution.py:848
  7.2 43.5 %collective-permute-start.1 = (bf16[192,1536]{1,0:T(8,128)(2,1)}, bf16[192,1536]{1,0:T(8,128)(2,1)}, u32[]{:S(2)}, u32[]{:S(2)}) collective-permute-start(bf16[192,1536]{1,0:T(8,128)(2,1)} %refs_0_), channel_id=1, source_target_pairs={{0,16},{4,20},{8,24},{12,28},{16,0},{20,4},{24,8},{28,12},{1,17},{... | collective-permute-start | bytes 1769480 | tf_op jit(solution)/shard_map/ppermute | solution.py:806
  10.2 40.5 %collective-permute-start = (bf16[192,1536]{1,0:T(8,128)(2,1)}, bf16[192,1536]{1,0:T(8,128)(2,1)}, u32[]{:S(2)}, u32[]{:S(2)}) collective-permute-start(bf16[192,1536]{1,0:T(8,128)(2,1)} %refs_0_), channel_id=1, source_target_pairs={{0,8},{4,12},{8,0},{12,4},{16,24},{20,28},{24,16},{28,20},{1,9},{5... | collective-permute-start | bytes 1769480 | tf_op jit(solution)/shard_map/ppermute | solution.py:806
  11.8 38.9 %collective-permute-start.2 = (bf16[192,1536]{1,0:T(8,128)(2,1)}, bf16[192,1536]{1,0:T(8,128)(2,1)}, u32[]{:S(2)}, u32[]{:S(2)}) collective-permute-start(bf16[192,1536]{1,0:T(8,128)(2,1)} %refs_0_), channel_id=1, source_target_pairs={{0,24},{4,28},{8,16},{12,20},{16,8},{20,12},{24,0},{28,4},{1,25},{... | collective-permute-start | bytes 1769480 | tf_op jit(solution)/shard_map/ppermute | solution.py:806
  13.1 27.0 %collective-permute-start.13 = (f32[8,128]{0,1:T(8,128)}, f32[8,128]{0,1:T(8,128)}, u32[]{:S(2)}, u32[]{:S(2)}) collective-permute-start(f32[8,128]{0,1:T(8,128)} %broadcast_in_dim.83), channel_id=1, source_target_pairs={{0,16},{4,20},{8,24},{12,28},{16,0},{20,4},{24,8},{28,12},{1,17},{... | collective-permute-start | bytes 12296 | tf_op jit(solution)/shard_map/ppermute | solution.py:806
  16.7 136.5 %all-gather.7.cloned.1.call-start = ((), (), s32[]{:S(2)}) async-start(), calls=%async_computation.2 | async-start | bytes 6684672 | tf_op jit(solution)/shard_map/all_gather | solution.py:910
  58.0 481.9 %reduce-scatter.2.cloned.1.call-start = ((), (), s32[]{:S(2)}) async-start(), calls=%async_computation.3 | async-start | bytes 6684672 | tf_op jit(solution)/shard_map/reduce_scatter | solution.py:1050
  58.2 17.2 %collective-permute-start.5 = (bf16[192,1536]{1,0:T(8,128)(2,1)S(1)}, bf16[192,1536]{1,0:T(8,128)(2,1)S(1)}, u32[]{:S(2)}, u32[]{:S(2)}) collective-permute-start(bf16[192,1536]{1,0:T(8,128)(2,1)S(1)} %copy-done.50), channel_id=1, source_target_pairs={{0,24},{4,28},{8,16},{12,20},{16,8},{20,12},{24,0},{28,4},{1,25},{... | collective-permute-start | bytes 1769480 | tf_op jit(solution)/shard_map/ppermute | solution.py:806
  59.7 28.4 %collective-permute-start.4 = (bf16[192,1536]{1,0:T(8,128)(2,1)S(1)}, bf16[192,1536]{1,0:T(8,128)(2,1)}, u32[]{:S(2)}, u32[]{:S(2)}) collective-permute-start(bf16[192,1536]{1,0:T(8,128)(2,1)S(1)} %copy-done.50), channel_id=1, source_target_pairs={{0,16},{4,20},{8,24},{12,28},{16,0},{20,4},{24,8},{28,12},{1,17},{... | collective-permute-start | bytes 1769480 | tf_op jit(solution)/shard_map/ppermute | solution.py:806
  61.2 30.4 %collective-permute-start.3 = (bf16[192,1536]{1,0:T(8,128)(2,1)S(1)}, bf16[192,1536]{1,0:T(8,128)(2,1)S(1)}, u32[]{:S(2)}, u32[]{:S(2)}) collective-permute-start(bf16[192,1536]{1,0:T(8,128)(2,1)S(1)} %copy-done.50), channel_id=1, source_target_pairs={{0,8},{4,12},{8,0},{12,4},{16,24},{20,28},{24,16},{28,20},{1,9},{5... | collective-permute-start | bytes 1769480 | tf_op jit(solution)/shard_map/ppermute | solution.py:806
  61.8 38.9 %collective-permute-start.6 = (bf16[192,1536]{1,0:T(8,128)(2,1)}, bf16[192,1536]{1,0:T(8,128)(2,1)S(1)}, u32[]{:S(2)}, u32[]{:S(2)}) collective-permute-start(bf16[192,1536]{1,0:T(8,128)(2,1)} %get-tuple-element.231.refs_10_), channel_id=1, source_target_pairs={{0,16},{4,20},{8,24},{12,28},{16,0},{20,4},{24,8},{28,12},{1,17},{... | collective-permute-start | bytes 1769480 | tf_op jit(solution)/shard_map/ppermute | solution.py:806
  63.2 49.4 %collective-permute-start.7 = (bf16[192,1536]{1,0:T(8,128)(2,1)}, bf16[192,1536]{1,0:T(8,128)(2,1)}, u32[]{:S(2)}, u32[]{:S(2)}) collective-permute-start(bf16[192,1536]{1,0:T(8,128)(2,1)} %get-tuple-element.232.refs_11_), channel_id=1, source_target_pairs={{0,16},{4,20},{8,24},{12,28},{16,0},{20,4},{24,8},{28,12},{1,17},{... | collective-permute-start | bytes 1769480 | tf_op jit(solution)/shard_map/ppermute | solution.py:806
  75.4 37.3 %collective-permute-start.8 = (bf16[192,1536]{1,0:T(8,128)(2,1)S(1)}, bf16[192,1536]{1,0:T(8,128)(2,1)}, u32[]{:S(2)}, u32[]{:S(2)}) collective-permute-start(bf16[192,1536]{1,0:T(8,128)(2,1)S(1)} %copy-done.49), channel_id=1, source_target_pairs={{0,4},{4,0},{8,12},{12,8},{16,20},{20,16},{24,28},{28,24},{1,5},{5... | collective-permute-start | bytes 1769480 | tf_op jit(solution)/shard_map/ppermute | solution.py:806
  88.1 24.6 %collective-permute-start.9 = (bf16[192,1536]{1,0:T(8,128)(2,1)}, bf16[192,1536]{1,0:T(8,128)(2,1)}, u32[]{:S(2)}, u32[]{:S(2)}) collective-permute-start(bf16[192,1536]{1,0:T(8,128)(2,1)} %collective-permute-done.refs_2_), channel_id=1, source_target_pairs={{0,4},{4,0},{8,12},{12,8},{16,20},{20,16},{24,28},{28,24},{1,5},{5... | collective-permute-start | bytes 1769480 | tf_op jit(solution)/shard_map/ppermute | solution.py:806
  91.6 21.1 %collective-permute-start.10 = (bf16[192,1536]{1,0:T(8,128)(2,1)}, bf16[192,1536]{1,0:T(8,128)(2,1)S(1)}, u32[]{:S(2)}, u32[]{:S(2)}) collective-permute-start(bf16[192,1536]{1,0:T(8,128)(2,1)} %collective-permute-done.1.refs_4_), channel_id=1, source_target_pairs={{0,4},{4,0},{8,12},{12,8},{16,20},{20,16},{24,28},{28,24},{1,5},{5... | collective-permute-start | bytes 1769480 | tf_op jit(solution)/shard_map/ppermute | solution.py:806
  101.4 11.3 %collective-permute-start.11 = (bf16[192,1536]{1,0:T(8,128)(2,1)}, bf16[192,1536]{1,0:T(8,128)(2,1)}, u32[]{:S(2)}, u32[]{:S(2)}) collective-permute-start(bf16[192,1536]{1,0:T(8,128)(2,1)} %collective-permute-done.2.refs_6_), channel_id=1, source_target_pairs={{0,4},{4,0},{8,12},{12,8},{16,20},{20,16},{24,28},{28,24},{1,5},{5... | collective-permute-start | bytes 1769480 | tf_op jit(solution)/shard_map/ppermute | solution.py:806
  112.7 79.4 %collective-permute-start.19 = (bf16[2,192,2304]{2,1,0:T(8,128)(2,1)}, bf16[2,192,2304]{2,1,0:T(8,128)(2,1)}, u32[]{:S(2)}, u32[]{:S(2)}) collective-permute-start(bf16[2,192,2304]{2,1,0:T(8,128)(2,1)} %get-tuple-element.210), channel_id=1, source_target_pairs={{0,8},{4,12},{8,0},{12,4},{16,24},{20,28},{24,16},{28,20},{1,9},{5... | collective-permute-start | bytes 5308424 | tf_op jit(solution)/shard_map/ppermute | solution.py:806
  113.4 78.7 %collective-permute-start.21 = (bf16[2,192,2304]{2,1,0:T(8,128)(2,1)}, bf16[2,192,2304]{2,1,0:T(8,128)(2,1)}, u32[]{:S(2)}, u32[]{:S(2)}) collective-permute-start(bf16[2,192,2304]{2,1,0:T(8,128)(2,1)} %get-tuple-element.213), channel_id=1, source_target_pairs={{0,16},{4,20},{8,24},{12,28},{16,0},{20,4},{24,8},{28,12},{1,17},{... | collective-permute-start | bytes 5308424 | tf_op jit(solution)/shard_map/ppermute | solution.py:806
  114.9 77.2 %collective-permute-start.23 = (bf16[2,192,2304]{2,1,0:T(8,128)(2,1)}, bf16[2,192,2304]{2,1,0:T(8,128)(2,1)}, u32[]{:S(2)}, u32[]{:S(2)}) collective-permute-start(bf16[2,192,2304]{2,1,0:T(8,128)(2,1)} %get-tuple-element.216), channel_id=1, source_target_pairs={{0,24},{4,28},{8,16},{12,20},{16,8},{20,12},{24,0},{28,4},{1,25},{... | collective-permute-start | bytes 5308424 | tf_op jit(solution)/shard_map/ppermute | solution.py:806
  123.9 23.1 %collective-permute-start.12 = (bf16[1120,1536]{1,0:T(8,128)(2,1)}, bf16[1120,1536]{1,0:T(8,128)(2,1)}, u32[]{:S(2)}, u32[]{:S(2)}) collective-permute-start(bf16[1120,1536]{1,0:T(8,128)(2,1)} %refs_0_.1), channel_id=1, source_target_pairs={{0,4},{4,0},{8,12},{12,8},{16,20},{20,16},{24,28},{28,24},{1,5},{5... | collective-permute-start | bytes 10321928 | tf_op jit(solution)/shard_map/ppermute | solution.py:806
  138.9 4.6 collective-permute-start.14
  143.5 3.1 collective-permute-start.15
  146.6 26.7 %collective-permute-start.16 = (bf16[192,1536]{1,0:T(8,128)(2,1)}, bf16[192,1536]{1,0:T(8,128)(2,1)S(1)}, u32[]{:S(2)}, u32[]{:S(2)}) collective-permute-start(bf16[192,1536]{1,0:T(8,128)(2,1)} %collective-permute-done.4.refs_4_), channel_id=1, source_target_pairs={{0,4},{4,0},{8,12},{12,8},{16,20},{20,16},{24,28},{28,24},{1,5},{5... | collective-permute-start | bytes 1769480 | tf_op jit(solution)/shard_map/ppermute | solution.py:806
  147.1 26.3 %collective-permute-start.17 = (bf16[192,1536]{1,0:T(8,128)(2,1)S(1)}, bf16[192,1536]{1,0:T(8,128)(2,1)}, u32[]{:S(2)}, u32[]{:S(2)}) collective-permute-start(bf16[192,1536]{1,0:T(8,128)(2,1)S(1)} %copy-done.52), channel_id=1, source_target_pairs={{0,4},{4,0},{8,12},{12,8},{16,20},{20,16},{24,28},{28,24},{1,5},{5... | collective-permute-start | bytes 1769480 | tf_op jit(solution)/shard_map/ppermute | solution.py:806
  173.3 20.7 %collective-permute-start.18 = (bf16[2,192,2304]{2,1,0:T(8,128)(2,1)S(1)}, bf16[2,192,2304]{2,1,0:T(8,128)(2,1)}, u32[]{:S(2)}, u32[]{:S(2)}) collective-permute-start(bf16[2,192,2304]{2,1,0:T(8,128)(2,1)S(1)} %copy-done.31), channel_id=1, source_target_pairs={{0,4},{4,0},{8,12},{12,8},{16,20},{20,16},{24,28},{28,24},{1,5},{5... | collective-permute-start | bytes 5308424 | tf_op jit(solution)/shard_map/ppermute | solution.py:806
  192.1 5.7 collective-permute-start.20
  192.1 6.6 %collective-permute-start.22 = (bf16[2,192,2304]{2,1,0:T(8,128)(2,1)}, bf16[2,192,2304]{2,1,0:T(8,128)(2,1)}, u32[]{:S(2)}, u32[]{:S(2)}) collective-permute-start(bf16[2,192,2304]{2,1,0:T(8,128)(2,1)} %collective-permute-done.21.refs_4_), channel_id=1, source_target_pairs={{0,4},{4,0},{8,12},{12,8},{16,20},{20,16},{24,28},{28,24},{1,5},{5... | collective-permute-start | bytes 5308424 | tf_op jit(solution)/shard_map/ppermute | solution.py:806
  192.6 8.6 %collective-permute-start.24 = (bf16[2,192,2304]{2,1,0:T(8,128)(2,1)}, bf16[2,192,2304]{2,1,0:T(8,128)(2,1)}, u32[]{:S(2)}, u32[]{:S(2)}) collective-permute-start(bf16[2,192,2304]{2,1,0:T(8,128)(2,1)} %collective-permute-done.23.refs_6_), channel_id=1, source_target_pairs={{0,4},{4,0},{8,12},{12,8},{16,20},{20,16},{24,28},{28,24},{1,5},{5... | collective-permute-start | bytes 5308424 | tf_op jit(solution)/shard_map/ppermute | solution.py:806
  193.4 264.9 %copy-start.84 = (pred[64]{0:T(512)(128)(4,1)}, pred[64]{0:T(512)(128)(4,1)S(1)}, u32[]{:S(2)}) copy-start(pred[64]{0:T(512)(128)(4,1)S(1)} %compare_and_fusion.2) | copy-start | bytes 196
  194.0 264.3 %copy-start.76 = (s32[384]{0:T(512)}, s32[384]{0:T(512)S(1)}, u32[]{:S(2)}) copy-start(s32[384]{0:T(512)S(1)} %get-tuple-element.353) | copy-start | bytes 4612
  194.0 264.3 %copy-start.77 = (s32[384]{0:T(512)}, s32[384]{0:T(512)S(1)}, u32[]{:S(2)}) copy-start(s32[384]{0:T(512)S(1)} %get-tuple-element.354) | copy-start | bytes 4612
  201.2 44.6 %collective-permute-start.27 = (bf16[192,1536]{1,0:T(8,128)(2,1)}, bf16[192,1536]{1,0:T(8,128)(2,1)}, u32[]{:S(2)}, u32[]{:S(2)}) collective-permute-start(bf16[192,1536]{1,0:T(8,128)(2,1)} %get-tuple-element.221.refs_8_), channel_id=1, source_target_pairs={{0,16},{4,20},{8,24},{12,28},{16,0},{20,4},{24,8},{28,12},{1,17},{... | collective-permute-start | bytes 1769480 | tf_op jit(solution)/shard_map/ppermute | solution.py:806
  201.9 44.0 %collective-permute-start.25 = (bf16[192,1536]{1,0:T(8,128)(2,1)}, bf16[192,1536]{1,0:T(8,128)(2,1)}, u32[]{:S(2)}, u32[]{:S(2)}) collective-permute-start(bf16[192,1536]{1,0:T(8,128)(2,1)} %get-tuple-element.221.refs_8_), channel_id=1, source_target_pairs={{0,8},{4,12},{8,0},{12,4},{16,24},{20,28},{24,16},{28,20},{1,9},{5... | collective-permute-start | bytes 1769480 | tf_op jit(solution)/shard_map/ppermute | solution.py:806
  209.7 36.3 %collective-permute-start.28 = (bf16[192,1536]{1,0:T(8,128)(2,1)}, bf16[192,1536]{1,0:T(8,128)(2,1)}, u32[]{:S(2)}, u32[]{:S(2)}) collective-permute-start(bf16[192,1536]{1,0:T(8,128)(2,1)} %get-tuple-element.222.refs_9_), channel_id=1, source_target_pairs={{0,16},{4,20},{8,24},{12,28},{16,0},{20,4},{24,8},{28,12},{1,17},{... | collective-permute-start | bytes 1769480 | tf_op jit(solution)/shard_map/ppermute | solution.py:806
  211.7 34.3 %collective-permute-start.26 = (bf16[192,1536]{1,0:T(8,128)(2,1)}, bf16[192,1536]{1,0:T(8,128)(2,1)}, u32[]{:S(2)}, u32[]{:S(2)}) collective-permute-start(bf16[192,1536]{1,0:T(8,128)(2,1)} %get-tuple-element.222.refs_9_), channel_id=1, source_target_pairs={{0,8},{4,12},{8,0},{12,4},{16,24},{20,28},{24,16},{28,20},{1,9},{5... | collective-permute-start | bytes 1769480 | tf_op jit(solution)/shard_map/ppermute | solution.py:806
  242.2 33.7 %collective-permute-start.29 = (bf16[192,1536]{1,0:T(8,128)(2,1)}, bf16[192,1536]{1,0:T(8,128)(2,1)}, u32[]{:S(2)}, u32[]{:S(2)}) collective-permute-start(bf16[192,1536]{1,0:T(8,128)(2,1)} %get-tuple-element.231.refs_10_), channel_id=1, source_target_pairs={{0,8},{4,12},{8,0},{12,4},{16,24},{20,28},{24,16},{28,20},{1,9},{5... | collective-permute-start | bytes 1769480 | tf_op jit(solution)/shard_map/ppermute | solution.py:806
  245.8 30.1 %collective-permute-start.30 = (bf16[192,1536]{1,0:T(8,128)(2,1)S(1)}, bf16[192,1536]{1,0:T(8,128)(2,1)}, u32[]{:S(2)}, u32[]{:S(2)}) collective-permute-start(bf16[192,1536]{1,0:T(8,128)(2,1)S(1)} %copy-done.59), channel_id=1, source_target_pairs={{0,8},{4,12},{8,0},{12,4},{16,24},{20,28},{24,16},{28,20},{1,9},{5... | collective-permute-start | bytes 1769480 | tf_op jit(solution)/shard_map/ppermute | solution.py:806
  275.9 36.3 %collective-permute-start.31 = (bf16[192,1536]{1,0:T(8,128)(2,1)}, bf16[192,1536]{1,0:T(8,128)(2,1)S(1)}, u32[]{:S(2)}, u32[]{:S(2)}) collective-permute-start(bf16[192,1536]{1,0:T(8,128)(2,1)} %collective-permute-done.27.refs_8_), channel_id=1, source_target_pairs={{0,8},{4,12},{8,0},{12,4},{16,24},{20,28},{24,16},{28,20},{1,9},{5... | collective-permute-start | bytes 1769480 | tf_op jit(solution)/shard_map/ppermute | solution.py:806
  277.9 34.3 %collective-permute-start.32 = (bf16[192,1536]{1,0:T(8,128)(2,1)}, bf16[192,1536]{1,0:T(8,128)(2,1)}, u32[]{:S(2)}, u32[]{:S(2)}) collective-permute-start(bf16[192,1536]{1,0:T(8,128)(2,1)} %collective-permute-done.26.refs_9_), channel_id=1, source_target_pairs={{0,16},{4,20},{8,24},{12,28},{16,0},{20,4},{24,8},{28,12},{1,17},{... | collective-permute-start | bytes 1769480 | tf_op jit(solution)/shard_map/ppermute | solution.py:806
  278.0 34.3 %collective-permute-start.33 = (bf16[192,1536]{1,0:T(8,128)(2,1)}, bf16[192,1536]{1,0:T(8,128)(2,1)}, u32[]{:S(2)}, u32[]{:S(2)}) collective-permute-start(bf16[192,1536]{1,0:T(8,128)(2,1)} %copy-done.90), channel_id=1, source_target_pairs={{0,8},{4,12},{8,0},{12,4},{16,24},{20,28},{24,16},{28,20},{1,9},{5... | collective-permute-start | bytes 1769480 | tf_op jit(solution)/shard_map/ppermute | solution.py:806
  278.1 34.1 %collective-permute-start.34 = (bf16[192,1536]{1,0:T(8,128)(2,1)}, bf16[192,1536]{1,0:T(8,128)(2,1)}, u32[]{:S(2)}, u32[]{:S(2)}) collective-permute-start(bf16[192,1536]{1,0:T(8,128)(2,1)} %collective-permute-done.30.refs_11_), channel_id=1, source_target_pairs={{0,16},{4,20},{8,24},{12,28},{16,0},{20,4},{24,8},{28,12},{1,17},{... | collective-permute-start | bytes 1769480 | tf_op jit(solution)/shard_map/ppermute | solution.py:806
  310.2 35.2 %collective-permute-start.36 = (bf16[384,1664]{1,0:T(8,128)(2,1)}, bf16[384,1664]{1,0:T(8,128)(2,1)}, u32[]{:S(2)}, u32[]{:S(2)}) collective-permute-start(bf16[384,1664]{1,0:T(8,128)(2,1)} %get-tuple-element.253), channel_id=1, source_target_pairs={{0,8},{4,12},{8,0},{12,4},{16,24},{20,28},{24,16},{28,20},{1,9},{5... | collective-permute-start | bytes 3833864 | tf_op jit(solution)/shard_map/ppermute | solution.py:806
  312.2 31.7 %collective-permute-start.35 = (bf16[384,1664]{1,0:T(8,128)(2,1)}, bf16[384,1664]{1,0:T(8,128)(2,1)}, u32[]{:S(2)}, u32[]{:S(2)}) collective-permute-start(bf16[384,1664]{1,0:T(8,128)(2,1)} %get-tuple-element.252), channel_id=1, source_target_pairs={{0,16},{4,20},{8,24},{12,28},{16,0},{20,4},{24,8},{28,12},{1,17},{... | collective-permute-start | bytes 3833864 | tf_op jit(solution)/shard_map/ppermute | solution.py:806
  343.0 28.3 %collective-permute-start.37 = (bf16[384,1664]{1,0:T(8,128)(2,1)}, bf16[384,1664]{1,0:T(8,128)(2,1)}, u32[]{:S(2)}, u32[]{:S(2)}) collective-permute-start(bf16[384,1664]{1,0:T(8,128)(2,1)} %get-tuple-element.254), channel_id=1, source_target_pairs={{0,24},{4,28},{8,16},{12,20},{16,8},{20,12},{24,0},{28,4},{1,25},{... | collective-permute-start | bytes 3833864 | tf_op jit(solution)/shard_map/ppermute | solution.py:806
  382.9 46.5 %collective-permute-start.38 = (bf16[384,1664]{1,0:T(8,128)(2,1)}, bf16[384,1664]{1,0:T(8,128)(2,1)}, u32[]{:S(2)}, u32[]{:S(2)}) collective-permute-start(bf16[384,1664]{1,0:T(8,128)(2,1)} %get-tuple-element.258), channel_id=1, source_target_pairs={{0,16},{4,20},{8,24},{12,28},{16,0},{20,4},{24,8},{28,12},{1,17},{... | collective-permute-start | bytes 3833864 | tf_op jit(solution)/shard_map/ppermute | solution.py:806
  383.9 45.5 %collective-permute-start.39 = (bf16[384,1664]{1,0:T(8,128)(2,1)}, bf16[384,1664]{1,0:T(8,128)(2,1)}, u32[]{:S(2)}, u32[]{:S(2)}) collective-permute-start(bf16[384,1664]{1,0:T(8,128)(2,1)} %get-tuple-element.259), channel_id=1, source_target_pairs={{0,8},{4,12},{8,0},{12,4},{16,24},{20,28},{24,16},{28,20},{1,9},{5... | collective-permute-start | bytes 3833864 | tf_op jit(solution)/shard_map/ppermute | solution.py:806
  413.0 41.8 %collective-permute-start.40 = (bf16[384,1664]{1,0:T(8,128)(2,1)}, bf16[384,1664]{1,0:T(8,128)(2,1)}, u32[]{:S(2)}, u32[]{:S(2)}) collective-permute-start(bf16[384,1664]{1,0:T(8,128)(2,1)} %get-tuple-element.264), channel_id=1, source_target_pairs={{0,24},{4,28},{8,16},{12,20},{16,8},{20,12},{24,0},{28,4},{1,25},{... | collective-permute-start | bytes 3833864 | tf_op jit(solution)/shard_map/ppermute | solution.py:806
  429.4 194.2 %all-gather.9.cloned.1.call-start = ((), (), s32[]{:S(2)}) async-start(), calls=%async_computation.4 | async-start | bytes 8110080 | tf_op jit(solution)/shard_map/all_gather | solution.py:1117
  472.9 2.2 collective-permute-start.41
  475.0 2.5 collective-permute-start.45
  476.4 15.6 %collective-permute-start.42 = (bf16[1,4,48,768]{3,2,1,0:T(8,128)(2,1)S(1)}, bf16[1,4,48,768]{3,2,1,0:T(8,128)(2,1)S(1)}, u32[]{:S(2)}, u32[]{:S(2)}) collective-permute-start(bf16[1,4,48,768]{3,2,1,0:T(8,128)(2,1)S(1)} %constant_dynamic-slice_fusion.2), channel_id=1, source_target_pairs={{0,8},{4,12},{8,0},{12,4},{16,24},{20,28},{24,16},{28,20},{1,9},{5... | collective-permute-start | bytes 884744 | tf_op jit(solution)/shard_map/ppermute | solution.py:806
  492.2 13.0 %collective-permute-start.43 = (bf16[2,48,768]{2,1,0:T(8,128)(2,1)S(1)}, bf16[2,48,768]{2,1,0:T(8,128)(2,1)S(1)}, u32[]{:S(2)}, u32[]{:S(2)}) collective-permute-start(bf16[2,48,768]{2,1,0:T(8,128)(2,1)S(1)} %dynamic-slice_bitcast_fusion.2), channel_id=1, source_target_pairs={{0,1},{1,0},{2,3},{3,2},{4,5},{5,4},{6,7},{7,6},{8,9},{9,8},{10,11... | collective-permute-start | bytes 442376 | tf_op jit(solution)/shard_map/ppermute | solution.py:809
  493.7 21.6 %collective-permute-start.46 = (bf16[2,48,1792]{2,1,0:T(8,128)(2,1)S(1)}, bf16[2,48,1792]{2,1,0:T(8,128)(2,1)S(1)}, u32[]{:S(2)}, u32[]{:S(2)}) collective-permute-start(bf16[2,48,1792]{2,1,0:T(8,128)(2,1)S(1)} %dynamic-slice_bitcast_fusion.1), channel_id=1, source_target_pairs={{0,1},{1,0},{2,3},{3,2},{4,5},{5,4},{6,7},{7,6},{8,9},{9,8},{10,11... | collective-permute-start | bytes 1032200 | tf_op jit(solution)/shard_map/ppermute | solution.py:809
  505.2 10.3 %collective-permute-start.44 = (bf16[1,48,768]{2,1,0:T(8,128)(2,1)S(1)}, bf16[1,48,768]{2,1,0:T(8,128)(2,1)S(1)}, u32[]{:S(2)}, u32[]{:S(2)}) collective-permute-start(bf16[1,48,768]{2,1,0:T(8,128)(2,1)S(1)} %constant_dynamic-slice_fusion.1), channel_id=1, source_target_pairs={{0,2},{1,3},{2,0},{3,1},{4,6},{5,7},{6,4},{7,5},{8,10},{9,11},{10,... | collective-permute-start | bytes 221192 | tf_op jit(solution)/shard_map/ppermute | solution.py:809
  515.4 20.0 %collective-permute-start.47 = (bf16[1,48,1792]{2,1,0:T(8,128)(2,1)S(1)}, bf16[1,48,1792]{2,1,0:T(8,128)(2,1)S(1)}, u32[]{:S(2)}, u32[]{:S(2)}) collective-permute-start(bf16[1,48,1792]{2,1,0:T(8,128)(2,1)S(1)} %constant_dynamic-slice_fusion), channel_id=1, source_target_pairs={{0,2},{1,3},{2,0},{3,1},{4,6},{5,7},{6,4},{7,5},{8,10},{9,11},{10,... | collective-permute-start | bytes 516104 | tf_op jit(solution)/shard_map/ppermute | solution.py:809
  564.1 2.0 collective-permute-start.48
  566.2 6.3 collective-permute-start.49
  572.5 8.9 %collective-permute-start.52 = (bf16[48,896]{1,0:T(8,128)(2,1)S(1)}, bf16[48,896]{1,0:T(8,128)(2,1)S(1)}, u32[]{:S(2)}, u32[]{:S(2)}) collective-permute-start(bf16[48,896]{1,0:T(8,128)(2,1)S(1)} %fusion.65), channel_id=1, source_target_pairs={{0,3},{1,2},{2,1},{3,0},{4,7},{5,6},{6,5},{7,4},{8,11},{9,10},{10,... | collective-permute-start | bytes 258056 | tf_op jit(solution)/shard_map/ppermute | solution.py:809
  572.6 17.3 %collective-permute-start.51 = (bf16[48,896]{1,0:T(8,128)(2,1)S(1)}, bf16[48,896]{1,0:T(8,128)(2,1)S(1)}, u32[]{:S(2)}, u32[]{:S(2)}) collective-permute-start(bf16[48,896]{1,0:T(8,128)(2,1)S(1)} %fusion.65), channel_id=1, source_target_pairs={{0,2},{1,3},{2,0},{3,1},{4,6},{5,7},{6,4},{7,5},{8,10},{9,11},{10,... | collective-permute-start | bytes 258056 | tf_op jit(solution)/shard_map/ppermute | solution.py:809
  576.4 13.5 %collective-permute-start.50 = (bf16[48,896]{1,0:T(8,128)(2,1)S(1)}, bf16[48,896]{1,0:T(8,128)(2,1)S(1)}, u32[]{:S(2)}, u32[]{:S(2)}) collective-permute-start(bf16[48,896]{1,0:T(8,128)(2,1)S(1)} %fusion.65), channel_id=1, source_target_pairs={{0,1},{1,0},{2,3},{3,2},{4,5},{5,4},{6,7},{7,6},{8,9},{9,8},{10,11... | collective-permute-start | bytes 258056 | tf_op jit(solution)/shard_map/ppermute | solution.py:809
  590.0 4.6 collective-permute-start.53
  594.5 10.1 %collective-permute-start.54 = (bf16[2,48,896]{2,1,0:T(8,128)(2,1)S(1)}, bf16[2,48,896]{2,1,0:T(8,128)(2,1)S(1)}, u32[]{:S(2)}, u32[]{:S(2)}) collective-permute-start(bf16[2,48,896]{2,1,0:T(8,128)(2,1)S(1)} %pad_maximum_fusion.10), channel_id=1, source_target_pairs={{0,16},{4,20},{8,24},{12,28},{16,0},{20,4},{24,8},{28,12},{1,17},{... | collective-permute-start | bytes 516104 | tf_op jit(solution)/shard_map/ppermute | solution.py:806
  604.7 2.1 collective-permute-start.55
  (91 other events, 877.6 us)
Sparse Core Ops, SparseCore 0:
  16.8 36.8 all-gather.4
  58.1 73.0 all-gather.6
  429.6 110.2 reduce-scatter.1
  543.6 79.9 all-gather.8

commit v6 on v5

--- a/solution.py
+++ b/solution.py
@@ -371,13 +371,14 @@
 
 
 def before_attention_kernel(
-    seqs, most_ref, last_ref, grad_ref, middle_ref, gain_ref, gs_ref, us_ref, os_ref, oe_ref, w_ref,
-    mg_ref, low_ref, gb_ref, ub_ref, ob_ref, ag_ref,
+    seqs, count, *refs
 ):
+    grad_ref, middle_ref, gain_ref, gs_ref, us_ref, os_ref, oe_ref, w_ref = refs[count : count + 8]
+    mg_ref, low_ref, gb_ref, ub_ref, ob_ref, ag_ref = refs[count + 8 :]
     tokens, model = mg_ref.shape
     lanes = oe_ref.shape[0]
     mix = token_mask(tokens, lanes, seqs)
-    total = most_ref[...] + last_ref[...].astype(F32)
+    total = sum(ref[...].astype(F32) for ref in refs[:count])
     gate_back = (total[:, model : model + lanes] * mix).astype(BF)
     up_back = (total[:, model + lanes :] * mix).astype(BF)
     gb_ref[...] = gate_back
@@ -394,12 +395,12 @@
     ag_ref[...] = (mm_nt(low, w_ref[...]) + mm_nt(output_back, os_ref[...])).astype(BF)
 
 
-def before_attention(most, last, grad, middle, gain, gs, us, os, oe, w_output, seqs):
+def before_attention(parts, grad, middle, gain, gs, us, os, oe, w_output, seqs):
     tokens, model = middle.shape
     lanes = oe.shape[0]
     low = lambda n: jax.ShapeDtypeStruct((tokens, n), BF)
     return pl.pallas_call(
-        functools.partial(before_attention_kernel, seqs),
+        functools.partial(before_attention_kernel, seqs, len(parts)),
         out_shape=[
             jax.ShapeDtypeStruct((tokens, model), F32),
             low(model), low(lanes), low(lanes), low(lanes), low(model),
@@ -408,7 +409,7 @@
         cost_estimate=pl.CostEstimate(
             flops=2 * tokens * model * model, bytes_accessed=30 * tokens * model, transcendentals=0
         ),
-    )(most, last, grad, middle, gain, gs, us, os, oe, w_output)
+    )(*parts, grad, middle, gain, gs, us, os, oe, w_output)
 
 
 def last_grads_kernel(
@@ -989,21 +990,17 @@
     for k in range(1, chips):
         if k < 3:
             n2_pieces.append(swap_both(after(normed_halves, wide), 2 * k))
-    if chips > 2:
-        n2_pieces[1:3] = lax.optimization_barrier(n2_pieces[1:3])
+            if k not in g0_pieces:
+                g0_pieces[k] = swap_both(after(grad_halves, wide), 2 * k)
     zero = jnp.zeros((lanes, hp), F32)
     sums = [(zero, zero, zero)] * fsdp_n
     out_raw = []
     grad_parts = []
-    early_first = [0] + sorted(range(1, chips), key=lambda k: (k > 2, -k if k < 3 else k))
+    early_first = sorted(range(1, chips), key=lambda k: (k > 2, -k if k < 3 else k)) + [0]
     for k in early_first:
         f = 2 * k // cp_n
         sgu, ed, eg, eu, sd = feed_factors[f]
         if len(out_raw) == 1:
-            for other in range(1, min(chips, 3)):
-                if other not in g0_pieces:
-                    g0_pieces[other] = swap_both(after(grad_halves, out_raw[0]), 2 * other)
-        if len(out_raw) == 2:
             for other in range(3, chips):
                 for pieces in (n2_pieces, g0_pieces):
                     first, second, own_pair = after((pieces[2], pieces[1], pieces[0]), out_raw[-1])
@@ -1016,23 +1013,19 @@
                     else:
                         g0_pieces[other] = piece
         if out_raw:
-            sums[f] = after(sums[f], out_raw[-1])
+            sums[f] = after(sums[f], out_raw[-1], [] if k else grad_parts[:-1])
         out_k, ng_k, *sums[f] = feed(
             feed_index, kinds, wide, n2_pieces[k], g0_pieces[k], sgu, ed, w_down, eg, eu, sd, sums[f], seqs
         )
         out_raw.append(out_k)
         grad_parts.append(ng_k if k == 0 else swap(ng_k, 2 * k))
 
-    grad_most = grad_parts[0].astype(F32)
-    for part in grad_parts[1:-1]:
-        grad_most = lax.optimization_barrier(grad_most) + part.astype(F32)
-
     def pack(values, tiles):
         value = jnp.concatenate([value[:rank].astype(BF) for value in values], axis=1)
         return jnp.pad(value, ((0, 0), (0, -value.shape[1] % (128 * tiles))))
 
     middle_grad, middle_low, gate_back, up_back, output_back, attended_grad = before_attention(
-        grad_most, grad_parts[-1], grad_low, middle, second_scales[None],
+        grad_parts, grad_low, middle, second_scales[None],
         gate_shrink, up_shrink, output_shrink, output_expand, w_output, seqs,
     )
 
@@ -1040,12 +1033,13 @@
         return (mm_nt(grad, expand) * mixing).astype(BF)
 
     out_raw = after(out_raw, middle_low)
-    out_parts = [swap(part, 2 * k) if k else part for k, part in zip(early_first[:3], out_raw)]
+    out_of = dict(zip(early_first, out_raw))
+    out_parts = [out_of[0]] + [swap(out_of[k], 2 * k) for k in range(1, min(chips, 3))]
     query_rot_grad, pair_part = attend_back(
         info, query_rot, attended_grad, attended, pair_all, lse, seqs, spans, span_len
     )
     out_parts += [
-        swap(after(part, pair_part), 2 * k) for k, part in zip(early_first[3:], out_raw[3:])
+        swap(after(out_of[k], pair_part), 2 * k) for k in range(3, chips)
     ]
     pair_grad = lax.psum_scatter(
         after(pair_part, out_parts[:3]), ("cp", "seq"), scatter_dimension=1, tiled=True

time: 647 us -> 659 us (1.019)
  starting transfers between devices: 61.5 us -> 70.4 us
    all_gather x1, waiting for transfers between devices: 0.02 us -> 17.8 us  [body(): lax.all_gather(pair.reshape(seqs, tok_rows, 2 * kv_width), ('cp', 'seq'),...]
    ppermute x49, waiting for transfers between devices: 124 us -> 114 us  [swap(): return lax.ppermute(value, PLANE, [(i, i ^ k) for i in range(plane)])]
    ppermute x49, starting transfers between devices: 54.4 us -> 63.3 us  [swap(): return lax.ppermute(value, PLANE, [(i, i ^ k) for i in range(plane)])]
  transfers between devices with their start and end apart: 60 -> 60, of which waited for: 26 -> 22; matrix products, arithmetic and copies ran while one was open for 22% -> 20% of each run, Pallas kernels for 30% -> 31%
where the time goes in v6:
time: 659 us; the launch traced here: 649 us
  Pallas kernels  226 us (34%)
  waiting for transfers between devices  199 us (30%)
  starting transfers between devices  70.4 us (11%)
  local copies, waits for them, and re-layouts  54.5 us (8%)
  other arithmetic  46.3 us (7%)
  matrix products  37.2 us (6%)
  between operations  15.6 us (2%)
    pallas_call x4, Pallas kernels, feed(): pl.pallas_call(functools.partial(feed_kernel, seqs, tuple(kinds)), grid_s...  120 us
    ppermute x49, waiting for transfers between devices, swap(): return lax.ppermute(value, PLANE, [(i, i ^ k) for i in range(plane)])  114 us
    ppermute x49, starting transfers between devices, swap(): return lax.ppermute(value, PLANE, [(i, i ^ k) for i in range(plane)])  63.3 us
    ppermute x7, waiting for transfers between devices, swap_seq(): return lax.ppermute(value, 'seq', [(i, i ^ k) for i in range(seq_n)])  49.1 us
    pallas_call x1, Pallas kernels, attend_back(): pl.pallas_call(functools.partial(attend_back_kernel, spans, span_len, tok...  29.4 us
    pallas_call x1, Pallas kernels, attend(): pl.pallas_call(functools.partial(attend_kernel, spans, span_len, tokens),...  22.7 us
    pallas_call x2, Pallas kernels, with_blocks(): pl.pallas_call(functools.partial(kernel, seqs, count), grid_spec=pltpu.Pr...  18.2 us
    all_gather x1, waiting for transfers between devices, body(): lax.all_gather(pair.reshape(seqs, tok_rows, 2 * kv_width), ('cp', 'seq'),...  17.8 us
  transfers between devices with their start and end apart: 60, of which 22 were waited for; matrix products, arithmetic and copies ran while one was open for 20% of the time, Pallas kernels for 31%

profile of v6, /device:TPU:0, one launch (start us, length us, event | category | flops | bytes accessed | tf_op | source)
XLA Modules:
  0.0 649.2 jit_solution(13260731886443084998)
XLA Ops:
  7.2 3.0 collective-permute-start
  14.8 1.9 collective-permute-start.13
  16.8 4.1 fusion.115
  20.8 1.9 fusion.114
  27.2 1.9 select_bitcast_fusion
  33.3 3.3 fusion.10
  38.5 7.2 %collective-permute-done.13 = f32[8,128]{0,1:T(8,128)} collective-permute-done((f32[8,128]{0,1:T(8,128)}, f32[8,128]{0,1:T(8,128)}, u32[]{:S(2)}, u32[]{:S(2)}) %collective-permute-start.13) | collective-permute-done | bytes 4128 | tf_op jit(solution)/shard_map/ppermute | solution.py:807
  54.6 2.0 convolution_convert_fusion.17.eo_ref.refs_10_
  56.7 4.3 keys_values.1
  61.3 2.0 collective-permute-start.4
  65.3 23.8 %collective-permute-done.3.refs_2_ = bf16[192,1536]{1,0:T(8,128)(2,1)S(1)} collective-permute-done((bf16[192,1536]{1,0:T(8,128)(2,1)S(1)}, bf16[192,1536]{1,0:T(8,128)(2,1)S(1)}, u32[]{:S(2)}, u32[]{:S(2)}) %collective-permute-start.3) | collective-permute-done | bytes 589856 | tf_op jit(solution)/shard_map/ppermute | solution.py:807
  89.9 3.8 collective-permute-start.6
  97.5 10.6 %collective-permute-done.6.refs_10_ = bf16[192,1536]{1,0:T(8,128)(2,1)S(1)} collective-permute-done((bf16[192,1536]{1,0:T(8,128)(2,1)}, bf16[192,1536]{1,0:T(8,128)(2,1)S(1)}, u32[]{:S(2)}, u32[]{:S(2)}) %collective-permute-start.6) | collective-permute-done | bytes 589856 | tf_op jit(solution)/shard_map/ppermute | solution.py:807
  108.1 12.7 %collective-permute-done.7.refs_11_ = bf16[192,1536]{1,0:T(8,128)(2,1)} collective-permute-done((bf16[192,1536]{1,0:T(8,128)(2,1)}, bf16[192,1536]{1,0:T(8,128)(2,1)}, u32[]{:S(2)}, u32[]{:S(2)}) %collective-permute-start.7) | collective-permute-done | bytes 589856 | tf_op jit(solution)/shard_map/ppermute | solution.py:807
  120.8 7.5 %queries.1 = (bf16[384,1536]{1,0:T(8,128)(2,1)}, bf16[384,64]{1,0:T(8,128)(2,1)}, bf16[1536,1536]{1,0:T(8,128)(2,1)}) custom-call(s32[1]{0:T(128)} %bitcast.info, bf16[384,1536]{1,0:T(8,128)(2,1)} %get-tuple-element.172.normed_ref, bf16[1536,64]{1,0:T(8,128)(2,1)} %bitcast.194, bf16[64,1536]{1,0:T(8,128)(2,1)} %convolution_convert_fusion.16.eq_ref, ...), custom_call_target="tpu_custom_call" | custom-call | flops 1811939328 | bytes 9437184 | tf_op jit(solution)/shard_map/queries/pallas_call | solution.py:483
  135.5 2.0 select_bitcast_fusion.2
  143.8 2.1 collective-permute-start.21
  154.8 5.0 assemble.1.refs_14_
  159.9 17.8 %all-gather.7.cloned.1.call-done.k_ref.v_ref = bf16[3,2048,512]{2,1,0:T(8,128)(2,1)} async-done(((bf16[3,128,512]{2,1,0:T(8,128)(2,1)}), bf16[3,2048,512]{2,1,0:T(8,128)(2,1)}) %all-gather.7.cloned.1.call-update) | async-done | bytes 6291472 | tf_op jit(solution)/shard_map/all_gather | solution.py:911
  177.7 22.7 %attend.1 = (bf16[384,1536]{1,0:T(8,128)(2,1)}, f32[6,8,768]{2,1,0:T(8,128)}) custom-call(s32[29]{0:T(128)} %pad_add_fusion.info, bf16[384,1536]{1,0:T(8,128)(2,1)} %get-tuple-element.194.q_ref, bf16[3,2048,512]{2,1,0:T(8,128)(2,1)} %all-gather.7.cloned.1.call-done.k_ref.v_ref, bf16[3,2048,512]{2,1,0:T(8,128)(2,1)} %all-gather.7.cloned.1.call-done.k_ref.v_ref), custom_call_target="tpu_custom_call" | custom-call | flops 4831838208 | bytes 6291456 | tf_op jit(solution)/shard_map/attend/pallas_call | solution.py:152
  201.4 10.6 %outputs.1 = (f32[384,1536]{1,0:T(8,128)}, bf16[384,1536]{1,0:T(8,128)(2,1)}, bf16[192,1536]{1,0:T(8,128)(2,1)}, bf16[192,1536]{1,0:T(8,128)(2,1)}, bf16[384,64]{1,0:T(8,128)(2,1)}, /*index=5*/bf16[1536,1536]{1,0:T(8,128)(2,1)}) custom-call(s32[1]{0:T(128)} %bitcast.info, bf16[384,1536]{1,0:T(8,128)(2,1)} %get-tuple-element.195.attended_ref.o_ref, ...), custom_call_target="tpu_custom_call" | custom-call | flops 1811939328 | bytes 9437184 | tf_op jit(solution)/shard_map/outputs/pallas_call | solution.py:483
  213.0 3.1 collective-permute-done.24.refs_7_
  216.2 2.5 collective-permute-done.22.refs_5_
  218.7 2.5 collective-permute-done.20.refs_3_
  221.2 7.5 %collective-permute-start.25 = (bf16[192,1536]{1,0:T(8,128)(2,1)}, bf16[192,1536]{1,0:T(8,128)(2,1)S(1)}, u32[]{:S(2)}, u32[]{:S(2)}) collective-permute-start(bf16[192,1536]{1,0:T(8,128)(2,1)} %get-tuple-element.216.refs_8_), channel_id=1, source_target_pairs={{0,16},{4,20},{8,24},{12,28},{16,0},{20,4},{24,8},{28,12},{1,17},{... | collective-permute-start | bytes 1769480 | tf_op jit(solution)/shard_map/ppermute | solution.py:807
  229.9 2.0 collective-permute-start.27
  232.0 1.9 collective-permute-start.29
  234.0 9.1 %collective-permute-done.25.refs_8_ = bf16[192,1536]{1,0:T(8,128)(2,1)S(1)} collective-permute-done((bf16[192,1536]{1,0:T(8,128)(2,1)}, bf16[192,1536]{1,0:T(8,128)(2,1)S(1)}, u32[]{:S(2)}, u32[]{:S(2)}) %collective-permute-start.25) | collective-permute-done | bytes 589856 | tf_op jit(solution)/shard_map/ppermute | solution.py:807
  243.1 2.0 collective-permute-start.30
  245.1 10.2 %collective-permute-done.26.refs_9_ = bf16[192,1536]{1,0:T(8,128)(2,1)S(1)} collective-permute-done((bf16[192,1536]{1,0:T(8,128)(2,1)}, bf16[192,1536]{1,0:T(8,128)(2,1)S(1)}, u32[]{:S(2)}, u32[]{:S(2)}) %collective-permute-start.26) | collective-permute-done | bytes 589856 | tf_op jit(solution)/shard_map/ppermute | solution.py:807
  256.3 30.4 %feed.4 = (bf16[384,1664]{1,0:T(8,128)(2,1)}, bf16[384,1664]{1,0:T(8,128)(2,1)}, f32[64,2304]{1,0:T(8,128)}, f32[64,2304]{1,0:T(8,128)}, f32[64,2304]{1,0:T(8,128)}) custom-call(s32[2]{0:T(128)} %pad_add_fusion.1.info, bf16[2,192,2304]{2,1,0:T(8,128)(2,1)} %get-tuple-element.204.refs_0_, bf16[2,192,2304]{2,1,0:T(8,128)(2,1)} %collective-permute-done.18.refs_1_, ...), custom_call_target="tpu_custom_call" | custom-call | flops 16986931200 | bytes 21233664 | tf_op jit(solution)/shard_map/feed/pallas_call | solution.py:609
  287.5 2.0 collective-permute-start.33
  292.1 29.7 %feed.5 = (bf16[384,1664]{1,0:T(8,128)(2,1)}, bf16[384,1664]{1,0:T(8,128)(2,1)}, f32[64,2304]{1,0:T(8,128)}, f32[64,2304]{1,0:T(8,128)}, f32[64,2304]{1,0:T(8,128)}) custom-call(s32[2]{0:T(128)} %pad_add_fusion.1.info, bf16[2,192,2304]{2,1,0:T(8,128)(2,1)} %get-tuple-element.204.refs_0_, bf16[2,192,2304]{2,1,0:T(8,128)(2,1)} %collective-permute-done.18.refs_1_, ...), custom_call_target="tpu_custom_call" | custom-call | flops 16986931200 | bytes 21233664 | tf_op jit(solution)/shard_map/feed/pallas_call | solution.py:609
  326.0 29.7 %feed.6 = (bf16[384,1664]{1,0:T(8,128)(2,1)}, bf16[384,1664]{1,0:T(8,128)(2,1)}, f32[64,2304]{1,0:T(8,128)}, f32[64,2304]{1,0:T(8,128)}, f32[64,2304]{1,0:T(8,128)}) custom-call(s32[2]{0:T(128)} %pad_add_fusion.1.info, bf16[2,192,2304]{2,1,0:T(8,128)(2,1)} %get-tuple-element.204.refs_0_, bf16[2,192,2304]{2,1,0:T(8,128)(2,1)} %collective-permute-done.18.refs_1_, ...), custom_call_target="tpu_custom_call" | custom-call | flops 16986931200 | bytes 21233664 | tf_op jit(solution)/shard_map/feed/pallas_call | solution.py:609
  355.9 29.9 %feed.7 = (bf16[384,1664]{1,0:T(8,128)(2,1)}, bf16[384,1664]{1,0:T(8,128)(2,1)}, f32[64,2304]{1,0:T(8,128)}, f32[64,2304]{1,0:T(8,128)}, f32[64,2304]{1,0:T(8,128)}) custom-call(s32[2]{0:T(128)} %pad_add_fusion.1.info, bf16[2,192,2304]{2,1,0:T(8,128)(2,1)} %get-tuple-element.204.refs_0_, bf16[2,192,2304]{2,1,0:T(8,128)(2,1)} %collective-permute-done.18.refs_1_, ...), custom_call_target="tpu_custom_call" | custom-call | flops 16986931200 | bytes 21233664 | tf_op jit(solution)/shard_map/feed/pallas_call | solution.py:609
  385.9 11.8 %before_attention.1 = (f32[384,1536]{1,0:T(8,128)}, bf16[384,1536]{1,0:T(8,128)(2,1)}, bf16[384,64]{1,0:T(8,128)(2,1)}, bf16[384,64]{1,0:T(8,128)(2,1)}, bf16[38...) custom-call(bf16[384,1664]{1,0:T(8,128)(2,1)} %copy-done.40, bf16[384,1664]{1,0:T(8,128)(2,1)} %copy-done.39, ...), custom_call_target="tpu_custom_call" | custom-call | flops 1811939328 | bytes 17694720 | tf_op jit(solution)/shard_map/before_attention/pallas_call | solution.py:402
  402.4 29.4 %attend_back.1 = (bf16[384,1536]{1,0:T(8,128)(2,1)}, bf16[3,2048,512]{2,1,0:T(8,128)(2,1)}) custom-call(s32[29]{0:T(128)} %pad_add_fusion.info, bf16[384,1536]{1,0:T(8,128)(2,1)} %get-tuple-element.194.q_ref, bf16[384,1536]{1,0:T(8,128)(2,1)} %get-tuple-element.253.do_ref, bf16[384,1536]{1,0:T(8,128)(2,1)} %get-tuple-element.195.attended_ref.o_ref, ...), custom_call_target="tpu_custom_call" | custom-call | flops 12079595520 | bytes 12582912 | tf_op jit(solution)/shard_map/attend_back/pallas_call | solution.py:253
  434.3 2.0 copy.106
  436.3 3.4 collective-permute-start.40
  445.2 3.0 copy.109
  448.3 2.5 add_convert_fusion
  454.6 9.5 %collective-permute-done.40 = bf16[384,1664]{1,0:T(8,128)(2,1)} collective-permute-done((bf16[384,1664]{1,0:T(8,128)(2,1)}, bf16[384,1664]{1,0:T(8,128)(2,1)}, u32[]{:S(2)}, u32[]{:S(2)}) %collective-permute-start.40) | collective-permute-done | bytes 1277984 | tf_op jit(solution)/shard_map/ppermute | solution.py:807
  464.0 2.8 convert_add_fusion
  471.9 4.6 collective-permute-start.41
  485.2 3.7 collective-permute-start.42
  491.1 9.3 %collective-permute-done.42 = bf16[1,4,48,768]{3,2,1,0:T(8,128)(2,1)S(1)} collective-permute-done((bf16[1,4,48,768]{3,2,1,0:T(8,128)(2,1)S(1)}, bf16[1,4,48,768]{3,2,1,0:T(8,128)(2,1)S(1)}, u32[]{:S(2)}, u32[]{:S(2)}) %collective-permute-start.42) | collective-permute-done | bytes 294944 | tf_op jit(solution)/shard_map/ppermute | solution.py:807
  502.7 11.3 %collective-permute-done.43 = bf16[2,48,768]{2,1,0:T(8,128)(2,1)S(1)} collective-permute-done((bf16[2,48,768]{2,1,0:T(8,128)(2,1)S(1)}, bf16[2,48,768]{2,1,0:T(8,128)(2,1)S(1)}, u32[]{:S(2)}, u32[]{:S(2)}) %collective-permute-start.43) | collective-permute-done | bytes 147488 | tf_op jit(solution)/shard_map/ppermute | solution.py:810
  514.1 9.4 %collective-permute-done.46 = bf16[2,48,1792]{2,1,0:T(8,128)(2,1)S(1)} collective-permute-done((bf16[2,48,1792]{2,1,0:T(8,128)(2,1)S(1)}, bf16[2,48,1792]{2,1,0:T(8,128)(2,1)S(1)}, u32[]{:S(2)}, u32[]{:S(2)}) %collective-permute-start.46) | collective-permute-done | bytes 344096 | tf_op jit(solution)/shard_map/ppermute | solution.py:810
  523.8 19.0 %collective-permute-done.47 = bf16[1,48,1792]{2,1,0:T(8,128)(2,1)S(1)} collective-permute-done((bf16[1,48,1792]{2,1,0:T(8,128)(2,1)S(1)}, bf16[1,48,1792]{2,1,0:T(8,128)(2,1)S(1)}, u32[]{:S(2)}, u32[]{:S(2)}) %collective-permute-start.47) | collective-permute-done | bytes 172064 | tf_op jit(solution)/shard_map/ppermute | solution.py:810
  543.6 2.4 reduce-scatter.2.cloned.1.call-done
  553.9 2.0 gather_fusion
  557.5 3.6 fusion.8
  561.1 4.4 fusion.120
  566.0 3.3 last_grads.1
  573.6 4.9 collective-permute-done.49
  579.1 3.8 collective-permute-start.52
  583.5 3.4 collective-permute-done.50
  586.8 6.1 collective-permute-done.51
  592.9 1.9 collective-permute-start.53
  597.5 2.8 collective-permute-start.54
  600.3 6.4 collective-permute-done.54
  606.9 2.0 fusion.5
  614.5 15.9 %all-gather.9.cloned.1.call-done = bf16[1536,2560]{1,0:T(8,128)(2,1)} async-done(((bf16[48,2560]{1,0:T(8,128)(2,1)}), bf16[1536,2560]{1,0:T(8,128)(2,1)}) %all-gather.9.cloned.1.call-update) | async-done | bytes 7864336 | tf_op jit(solution)/shard_map/all_gather | solution.py:1111
  630.4 12.1 %expand.1 = (f32[128,8960]{1,0:T(8,128)}, f32[128,8960]{1,0:T(8,128)}, f32[8960,128]{1,0:T(8,128)}, f32[1536,128]{1,0:T(8,128)}, f32[1536,128]{1,0:T(8,128)}, /*...) custom-call(bf16[32,48,2560]{2,1,0:T(8,128)(2,1)} %bitcast.191, ...), custom_call_target="tpu_custom_call" | custom-call | flops 660602880 | bytes 13762560 | tf_op jit(solution)/shard_map/expand/pallas_call | solution.py:747
  (446 shorter events, 123.9 us)
Async XLA Ops:
  7.2 131.8 %copy-start = (bf16[8960,128]{1,0:T(8,128)(2,1)S(1)}, bf16[8960,128]{1,0:T(8,128)(2,1)}, u32[]{:S(2)}) copy-start(bf16[8960,128]{1,0:T(8,128)(2,1)} %param.59) | copy-start | bytes 6881284
  7.2 49.5 %all-gather.5.cloned.1.call-start = ((), (), s32[]{:S(2)}) async-start(), calls=%async_computation.1 | async-start | bytes 1769472 | tf_op jit(solution)/shard_map/all_gather | solution.py:849
  7.2 49.4 %collective-permute-start = (bf16[192,1536]{1,0:T(8,128)(2,1)}, bf16[192,1536]{1,0:T(8,128)(2,1)}, u32[]{:S(2)}, u32[]{:S(2)}) collective-permute-start(bf16[192,1536]{1,0:T(8,128)(2,1)} %refs_0_), channel_id=1, source_target_pairs={{0,8},{4,12},{8,0},{12,4},{16,24},{20,28},{24,16},{28,20},{1,9},{5... | collective-permute-start | bytes 1769480 | tf_op jit(solution)/shard_map/ppermute | solution.py:807
  10.3 46.4 %collective-permute-start.1 = (bf16[192,1536]{1,0:T(8,128)(2,1)}, bf16[192,1536]{1,0:T(8,128)(2,1)}, u32[]{:S(2)}, u32[]{:S(2)}) collective-permute-start(bf16[192,1536]{1,0:T(8,128)(2,1)} %refs_0_), channel_id=1, source_target_pairs={{0,16},{4,20},{8,24},{12,28},{16,0},{20,4},{24,8},{28,12},{1,17},{... | collective-permute-start | bytes 1769480 | tf_op jit(solution)/shard_map/ppermute | solution.py:807
  11.8 44.9 %collective-permute-start.2 = (bf16[192,1536]{1,0:T(8,128)(2,1)}, bf16[192,1536]{1,0:T(8,128)(2,1)}, u32[]{:S(2)}, u32[]{:S(2)}) collective-permute-start(bf16[192,1536]{1,0:T(8,128)(2,1)} %refs_0_), channel_id=1, source_target_pairs={{0,24},{4,28},{8,16},{12,20},{16,8},{20,12},{24,0},{28,4},{1,25},{... | collective-permute-start | bytes 1769480 | tf_op jit(solution)/shard_map/ppermute | solution.py:807
  13.5 164.2 %all-gather.7.cloned.1.call-start = ((), (), s32[]{:S(2)}) async-start(), calls=%async_computation.2 | async-start | bytes 6684672 | tf_op jit(solution)/shard_map/all_gather | solution.py:911
  14.8 30.9 %collective-permute-start.13 = (f32[8,128]{0,1:T(8,128)}, f32[8,128]{0,1:T(8,128)}, u32[]{:S(2)}, u32[]{:S(2)}) collective-permute-start(f32[8,128]{0,1:T(8,128)} %broadcast_in_dim.83), channel_id=1, source_target_pairs={{0,16},{4,20},{8,24},{12,28},{16,0},{20,4},{24,8},{28,12},{1,17},{... | collective-permute-start | bytes 12296 | tf_op jit(solution)/shard_map/ppermute | solution.py:807
  61.0 485.0 %reduce-scatter.2.cloned.1.call-start = ((), (), s32[]{:S(2)}) async-start(), calls=%async_computation.3 | async-start | bytes 6684672 | tf_op jit(solution)/shard_map/reduce_scatter | solution.py:1044
  61.2 27.9 %collective-permute-start.3 = (bf16[192,1536]{1,0:T(8,128)(2,1)S(1)}, bf16[192,1536]{1,0:T(8,128)(2,1)S(1)}, u32[]{:S(2)}, u32[]{:S(2)}) collective-permute-start(bf16[192,1536]{1,0:T(8,128)(2,1)S(1)} %copy-done.47), channel_id=1, source_target_pairs={{0,8},{4,12},{8,0},{12,4},{16,24},{20,28},{24,16},{28,20},{1,9},{5... | collective-permute-start | bytes 1769480 | tf_op jit(solution)/shard_map/ppermute | solution.py:807
  61.3 27.8 %collective-permute-start.4 = (bf16[192,1536]{1,0:T(8,128)(2,1)S(1)}, bf16[192,1536]{1,0:T(8,128)(2,1)}, u32[]{:S(2)}, u32[]{:S(2)}) collective-permute-start(bf16[192,1536]{1,0:T(8,128)(2,1)S(1)} %copy-done.47), channel_id=1, source_target_pairs={{0,16},{4,20},{8,24},{12,28},{16,0},{20,4},{24,8},{28,12},{1,17},{... | collective-permute-start | bytes 1769480 | tf_op jit(solution)/shard_map/ppermute | solution.py:807
  63.3 26.3 %collective-permute-start.5 = (bf16[192,1536]{1,0:T(8,128)(2,1)S(1)}, bf16[192,1536]{1,0:T(8,128)(2,1)}, u32[]{:S(2)}, u32[]{:S(2)}) collective-permute-start(bf16[192,1536]{1,0:T(8,128)(2,1)S(1)} %copy-done.47), channel_id=1, source_target_pairs={{0,24},{4,28},{8,16},{12,20},{16,8},{20,12},{24,0},{28,4},{1,25},{... | collective-permute-start | bytes 1769480 | tf_op jit(solution)/shard_map/ppermute | solution.py:807
  64.8 28.9 %collective-permute-start.10 = (bf16[192,1536]{1,0:T(8,128)(2,1)}, bf16[192,1536]{1,0:T(8,128)(2,1)}, u32[]{:S(2)}, u32[]{:S(2)}) collective-permute-start(bf16[192,1536]{1,0:T(8,128)(2,1)} %collective-permute-done.1.refs_4_), channel_id=1, source_target_pairs={{0,4},{4,0},{8,12},{12,8},{16,20},{20,16},{24,28},{28,24},{1,5},{5... | collective-permute-start | bytes 1769480 | tf_op jit(solution)/shard_map/ppermute | solution.py:807
  64.8 30.9 %collective-permute-start.11 = (bf16[192,1536]{1,0:T(8,128)(2,1)}, bf16[192,1536]{1,0:T(8,128)(2,1)}, u32[]{:S(2)}, u32[]{:S(2)}) collective-permute-start(bf16[192,1536]{1,0:T(8,128)(2,1)} %collective-permute-done.2.refs_6_), channel_id=1, source_target_pairs={{0,4},{4,0},{8,12},{12,8},{16,20},{20,16},{24,28},{28,24},{1,5},{5... | collective-permute-start | bytes 1769480 | tf_op jit(solution)/shard_map/ppermute | solution.py:807
  89.1 8.4 %collective-permute-start.8 = (bf16[192,1536]{1,0:T(8,128)(2,1)S(1)}, bf16[192,1536]{1,0:T(8,128)(2,1)}, u32[]{:S(2)}, u32[]{:S(2)}) collective-permute-start(bf16[192,1536]{1,0:T(8,128)(2,1)S(1)} %copy-done.46), channel_id=1, source_target_pairs={{0,4},{4,0},{8,12},{12,8},{16,20},{20,16},{24,28},{28,24},{1,5},{5... | collective-permute-start | bytes 1769480 | tf_op jit(solution)/shard_map/ppermute | solution.py:807
  89.1 8.3 %collective-permute-start.9 = (bf16[192,1536]{1,0:T(8,128)(2,1)}, bf16[192,1536]{1,0:T(8,128)(2,1)}, u32[]{:S(2)}, u32[]{:S(2)}) collective-permute-start(bf16[192,1536]{1,0:T(8,128)(2,1)} %collective-permute-done.refs_2_), channel_id=1, source_target_pairs={{0,4},{4,0},{8,12},{12,8},{16,20},{20,16},{24,28},{28,24},{1,5},{5... | collective-permute-start | bytes 1769480 | tf_op jit(solution)/shard_map/ppermute | solution.py:807
  89.9 18.1 %collective-permute-start.6 = (bf16[192,1536]{1,0:T(8,128)(2,1)}, bf16[192,1536]{1,0:T(8,128)(2,1)S(1)}, u32[]{:S(2)}, u32[]{:S(2)}) collective-permute-start(bf16[192,1536]{1,0:T(8,128)(2,1)} %get-tuple-element.219.refs_10_), channel_id=1, source_target_pairs={{0,16},{4,20},{8,24},{12,28},{16,0},{20,4},{24,8},{28,12},{1,17},{... | collective-permute-start | bytes 1769480 | tf_op jit(solution)/shard_map/ppermute | solution.py:807
  93.7 27.1 %collective-permute-start.7 = (bf16[192,1536]{1,0:T(8,128)(2,1)}, bf16[192,1536]{1,0:T(8,128)(2,1)}, u32[]{:S(2)}, u32[]{:S(2)}) collective-permute-start(bf16[192,1536]{1,0:T(8,128)(2,1)} %get-tuple-element.220.refs_11_), channel_id=1, source_target_pairs={{0,16},{4,20},{8,24},{12,28},{16,0},{20,4},{24,8},{28,12},{1,17},{... | collective-permute-start | bytes 1769480 | tf_op jit(solution)/shard_map/ppermute | solution.py:807
  95.7 116.4 %collective-permute-start.23 = (bf16[2,192,2304]{2,1,0:T(8,128)(2,1)}, bf16[2,192,2304]{2,1,0:T(8,128)(2,1)}, u32[]{:S(2)}, u32[]{:S(2)}) collective-permute-start(bf16[2,192,2304]{2,1,0:T(8,128)(2,1)} %get-tuple-element.212), channel_id=1, source_target_pairs={{0,24},{4,28},{8,16},{12,20},{16,8},{20,12},{24,0},{28,4},{1,25},{... | collective-permute-start | bytes 5308424 | tf_op jit(solution)/shard_map/ppermute | solution.py:807
  128.4 21.9 %collective-permute-start.14 = (bf16[192,1536]{1,0:T(8,128)(2,1)}, bf16[192,1536]{1,0:T(8,128)(2,1)}, u32[]{:S(2)}, u32[]{:S(2)}) collective-permute-start(bf16[192,1536]{1,0:T(8,128)(2,1)} %refs_0_.2), channel_id=1, source_target_pairs={{0,4},{4,0},{8,12},{12,8},{16,20},{20,16},{24,28},{28,24},{1,5},{5... | collective-permute-start | bytes 1769480 | tf_op jit(solution)/shard_map/ppermute | solution.py:807
  128.5 25.3 %collective-permute-start.12 = (bf16[1120,1536]{1,0:T(8,128)(2,1)}, bf16[1120,1536]{1,0:T(8,128)(2,1)}, u32[]{:S(2)}, u32[]{:S(2)}) collective-permute-start(bf16[1120,1536]{1,0:T(8,128)(2,1)} %refs_0_.1), channel_id=1, source_target_pairs={{0,4},{4,0},{8,12},{12,8},{16,20},{20,16},{24,28},{28,24},{1,5},{5... | collective-permute-start | bytes 10321928 | tf_op jit(solution)/shard_map/ppermute | solution.py:807
  143.8 68.7 %collective-permute-start.21 = (bf16[2,192,2304]{2,1,0:T(8,128)(2,1)}, bf16[2,192,2304]{2,1,0:T(8,128)(2,1)}, u32[]{:S(2)}, u32[]{:S(2)}) collective-permute-start(bf16[2,192,2304]{2,1,0:T(8,128)(2,1)} %get-tuple-element.209), channel_id=1, source_target_pairs={{0,16},{4,20},{8,24},{12,28},{16,0},{20,4},{24,8},{28,12},{1,17},{... | collective-permute-start | bytes 5308424 | tf_op jit(solution)/shard_map/ppermute | solution.py:807
  145.9 66.8 %collective-permute-start.19 = (bf16[2,192,2304]{2,1,0:T(8,128)(2,1)}, bf16[2,192,2304]{2,1,0:T(8,128)(2,1)}, u32[]{:S(2)}, u32[]{:S(2)}) collective-permute-start(bf16[2,192,2304]{2,1,0:T(8,128)(2,1)} %get-tuple-element.206), channel_id=1, source_target_pairs={{0,8},{4,12},{8,0},{12,4},{16,24},{20,28},{24,16},{28,20},{1,9},{5... | collective-permute-start | bytes 5308424 | tf_op jit(solution)/shard_map/ppermute | solution.py:807
  150.3 3.0 collective-permute-start.15
  153.3 47.1 %collective-permute-start.16 = (bf16[192,1536]{1,0:T(8,128)(2,1)}, bf16[192,1536]{1,0:T(8,128)(2,1)S(1)}, u32[]{:S(2)}, u32[]{:S(2)}) collective-permute-start(bf16[192,1536]{1,0:T(8,128)(2,1)} %collective-permute-done.4.refs_4_), channel_id=1, source_target_pairs={{0,4},{4,0},{8,12},{12,8},{16,20},{20,16},{24,28},{28,24},{1,5},{5... | collective-permute-start | bytes 1769480 | tf_op jit(solution)/shard_map/ppermute | solution.py:807
  153.8 46.7 %collective-permute-start.17 = (bf16[192,1536]{1,0:T(8,128)(2,1)}, bf16[192,1536]{1,0:T(8,128)(2,1)S(1)}, u32[]{:S(2)}, u32[]{:S(2)}) collective-permute-start(bf16[192,1536]{1,0:T(8,128)(2,1)} %collective-permute-done.5.refs_6_), channel_id=1, source_target_pairs={{0,4},{4,0},{8,12},{12,8},{16,20},{20,16},{24,28},{28,24},{1,5},{5... | collective-permute-start | bytes 1769480 | tf_op jit(solution)/shard_map/ppermute | solution.py:807
  200.4 12.6 %collective-permute-start.18 = (bf16[2,192,2304]{2,1,0:T(8,128)(2,1)S(1)}, bf16[2,192,2304]{2,1,0:T(8,128)(2,1)}, u32[]{:S(2)}, u32[]{:S(2)}) collective-permute-start(bf16[2,192,2304]{2,1,0:T(8,128)(2,1)S(1)} %copy-done.33), channel_id=1, source_target_pairs={{0,4},{4,0},{8,12},{12,8},{16,20},{20,16},{24,28},{28,24},{1,5},{5... | collective-permute-start | bytes 5308424 | tf_op jit(solution)/shard_map/ppermute | solution.py:807
  212.1 4.1 collective-permute-start.24
  212.5 6.2 collective-permute-start.22
  212.6 8.6 %collective-permute-start.20 = (bf16[2,192,2304]{2,1,0:T(8,128)(2,1)}, bf16[2,192,2304]{2,1,0:T(8,128)(2,1)}, u32[]{:S(2)}, u32[]{:S(2)}) collective-permute-start(bf16[2,192,2304]{2,1,0:T(8,128)(2,1)} %collective-permute-done.19.refs_2_), channel_id=1, source_target_pairs={{0,4},{4,0},{8,12},{12,8},{16,20},{20,16},{24,28},{28,24},{1,5},{5... | collective-permute-start | bytes 5308424 | tf_op jit(solution)/shard_map/ppermute | solution.py:807
  221.2 21.9 %collective-permute-start.25 = (bf16[192,1536]{1,0:T(8,128)(2,1)}, bf16[192,1536]{1,0:T(8,128)(2,1)S(1)}, u32[]{:S(2)}, u32[]{:S(2)}) collective-permute-start(bf16[192,1536]{1,0:T(8,128)(2,1)} %get-tuple-element.216.refs_8_), channel_id=1, source_target_pairs={{0,16},{4,20},{8,24},{12,28},{16,0},{20,4},{24,8},{28,12},{1,17},{... | collective-permute-start | bytes 1769480 | tf_op jit(solution)/shard_map/ppermute | solution.py:807
  228.8 26.5 %collective-permute-start.26 = (bf16[192,1536]{1,0:T(8,128)(2,1)}, bf16[192,1536]{1,0:T(8,128)(2,1)S(1)}, u32[]{:S(2)}, u32[]{:S(2)}) collective-permute-start(bf16[192,1536]{1,0:T(8,128)(2,1)} %get-tuple-element.217.refs_9_), channel_id=1, source_target_pairs={{0,16},{4,20},{8,24},{12,28},{16,0},{20,4},{24,8},{28,12},{1,17},{... | collective-permute-start | bytes 1769480 | tf_op jit(solution)/shard_map/ppermute | solution.py:807
  229.4 237.5 %copy-start.81 = (pred[64]{0:T(512)(128)(4,1)}, pred[64]{0:T(512)(128)(4,1)S(1)}, u32[]{:S(2)}) copy-start(pred[64]{0:T(512)(128)(4,1)S(1)} %compare_and_fusion.2) | copy-start | bytes 196
  229.9 236.9 %copy-start.73 = (s32[384]{0:T(512)}, s32[384]{0:T(512)S(1)}, u32[]{:S(2)}) copy-start(s32[384]{0:T(512)S(1)} %get-tuple-element.345) | copy-start | bytes 4612
  229.9 236.9 %copy-start.74 = (s32[384]{0:T(512)}, s32[384]{0:T(512)S(1)}, u32[]{:S(2)}) copy-start(s32[384]{0:T(512)S(1)} %get-tuple-element.346) | copy-start | bytes 4612
  229.9 61.3 %collective-permute-start.27 = (bf16[192,1536]{1,0:T(8,128)(2,1)}, bf16[192,1536]{1,0:T(8,128)(2,1)S(1)}, u32[]{:S(2)}, u32[]{:S(2)}) collective-permute-start(bf16[192,1536]{1,0:T(8,128)(2,1)} %get-tuple-element.216.refs_8_), channel_id=1, source_target_pairs={{0,8},{4,12},{8,0},{12,4},{16,24},{20,28},{24,16},{28,20},{1,9},{5... | collective-permute-start | bytes 1769480 | tf_op jit(solution)/shard_map/ppermute | solution.py:807
  232.0 59.3 %collective-permute-start.28 = (bf16[192,1536]{1,0:T(8,128)(2,1)}, bf16[192,1536]{1,0:T(8,128)(2,1)}, u32[]{:S(2)}, u32[]{:S(2)}) collective-permute-start(bf16[192,1536]{1,0:T(8,128)(2,1)} %get-tuple-element.217.refs_9_), channel_id=1, source_target_pairs={{0,8},{4,12},{8,0},{12,4},{16,24},{20,28},{24,16},{28,20},{1,9},{5... | collective-permute-start | bytes 1769480 | tf_op jit(solution)/shard_map/ppermute | solution.py:807
  232.0 54.6 %collective-permute-start.29 = (bf16[192,1536]{1,0:T(8,128)(2,1)}, bf16[192,1536]{1,0:T(8,128)(2,1)S(1)}, u32[]{:S(2)}, u32[]{:S(2)}) collective-permute-start(bf16[192,1536]{1,0:T(8,128)(2,1)} %get-tuple-element.219.refs_10_), channel_id=1, source_target_pairs={{0,8},{4,12},{8,0},{12,4},{16,24},{20,28},{24,16},{28,20},{1,9},{5... | collective-permute-start | bytes 1769480 | tf_op jit(solution)/shard_map/ppermute | solution.py:807
  243.1 44.4 %collective-permute-start.30 = (bf16[192,1536]{1,0:T(8,128)(2,1)S(1)}, bf16[192,1536]{1,0:T(8,128)(2,1)}, u32[]{:S(2)}, u32[]{:S(2)}) collective-permute-start(bf16[192,1536]{1,0:T(8,128)(2,1)S(1)} %copy-done.53), channel_id=1, source_target_pairs={{0,8},{4,12},{8,0},{12,4},{16,24},{20,28},{24,16},{28,20},{1,9},{5... | collective-permute-start | bytes 1769480 | tf_op jit(solution)/shard_map/ppermute | solution.py:807
  287.5 35.9 %collective-permute-start.33 = (bf16[192,1536]{1,0:T(8,128)(2,1)S(1)}, bf16[192,1536]{1,0:T(8,128)(2,1)S(1)}, u32[]{:S(2)}, u32[]{:S(2)}) collective-permute-start(bf16[192,1536]{1,0:T(8,128)(2,1)S(1)} %copy-done.88), channel_id=1, source_target_pairs={{0,8},{4,12},{8,0},{12,4},{16,24},{20,28},{24,16},{28,20},{1,9},{5... | collective-permute-start | bytes 1769480 | tf_op jit(solution)/shard_map/ppermute | solution.py:807
  289.5 36.5 %collective-permute-start.34 = (bf16[192,1536]{1,0:T(8,128)(2,1)}, bf16[192,1536]{1,0:T(8,128)(2,1)}, u32[]{:S(2)}, u32[]{:S(2)}) collective-permute-start(bf16[192,1536]{1,0:T(8,128)(2,1)} %collective-permute-done.30.refs_11_), channel_id=1, source_target_pairs={{0,16},{4,20},{8,24},{12,28},{16,0},{20,4},{24,8},{28,12},{1,17},{... | collective-permute-start | bytes 1769480 | tf_op jit(solution)/shard_map/ppermute | solution.py:807
  291.3 34.7 %collective-permute-start.31 = (bf16[192,1536]{1,0:T(8,128)(2,1)}, bf16[192,1536]{1,0:T(8,128)(2,1)}, u32[]{:S(2)}, u32[]{:S(2)}) collective-permute-start(bf16[192,1536]{1,0:T(8,128)(2,1)} %copy-done.89), channel_id=1, source_target_pairs={{0,8},{4,12},{8,0},{12,4},{16,24},{20,28},{24,16},{28,20},{1,9},{5... | collective-permute-start | bytes 1769480 | tf_op jit(solution)/shard_map/ppermute | solution.py:807
  291.4 34.6 %collective-permute-start.32 = (bf16[192,1536]{1,0:T(8,128)(2,1)}, bf16[192,1536]{1,0:T(8,128)(2,1)}, u32[]{:S(2)}, u32[]{:S(2)}) collective-permute-start(bf16[192,1536]{1,0:T(8,128)(2,1)} %collective-permute-done.28.refs_9_), channel_id=1, source_target_pairs={{0,16},{4,20},{8,24},{12,28},{16,0},{20,4},{24,8},{28,12},{1,17},{... | collective-permute-start | bytes 1769480 | tf_op jit(solution)/shard_map/ppermute | solution.py:807
  321.8 34.1 %collective-permute-start.36 = (bf16[384,1664]{1,0:T(8,128)(2,1)}, bf16[384,1664]{1,0:T(8,128)(2,1)S(1)}, u32[]{:S(2)}, u32[]{:S(2)}) collective-permute-start(bf16[384,1664]{1,0:T(8,128)(2,1)} %get-tuple-element.240), channel_id=1, source_target_pairs={{0,8},{4,12},{8,0},{12,4},{16,24},{20,28},{24,16},{28,20},{1,9},{5... | collective-permute-start | bytes 3833864 | tf_op jit(solution)/shard_map/ppermute | solution.py:807
  324.3 31.7 %collective-permute-start.35 = (bf16[384,1664]{1,0:T(8,128)(2,1)}, bf16[384,1664]{1,0:T(8,128)(2,1)S(1)}, u32[]{:S(2)}, u32[]{:S(2)}) collective-permute-start(bf16[384,1664]{1,0:T(8,128)(2,1)} %get-tuple-element.239), channel_id=1, source_target_pairs={{0,16},{4,20},{8,24},{12,28},{16,0},{20,4},{24,8},{28,12},{1,17},{... | collective-permute-start | bytes 3833864 | tf_op jit(solution)/shard_map/ppermute | solution.py:807
  355.7 30.2 %collective-permute-start.37 = (bf16[384,1664]{1,0:T(8,128)(2,1)}, bf16[384,1664]{1,0:T(8,128)(2,1)}, u32[]{:S(2)}, u32[]{:S(2)}) collective-permute-start(bf16[384,1664]{1,0:T(8,128)(2,1)} %get-tuple-element.245), channel_id=1, source_target_pairs={{0,24},{4,28},{8,16},{12,20},{16,8},{20,12},{24,0},{28,4},{1,25},{... | collective-permute-start | bytes 3833864 | tf_op jit(solution)/shard_map/ppermute | solution.py:807
  397.7 42.0 %collective-permute-start.38 = (bf16[384,1664]{1,0:T(8,128)(2,1)}, bf16[384,1664]{1,0:T(8,128)(2,1)}, u32[]{:S(2)}, u32[]{:S(2)}) collective-permute-start(bf16[384,1664]{1,0:T(8,128)(2,1)} %get-tuple-element.250), channel_id=1, source_target_pairs={{0,8},{4,12},{8,0},{12,4},{16,24},{20,28},{24,16},{28,20},{1,9},{5... | collective-permute-start | bytes 3833864 | tf_op jit(solution)/shard_map/ppermute | solution.py:807
  399.3 40.4 %collective-permute-start.39 = (bf16[384,1664]{1,0:T(8,128)(2,1)}, bf16[384,1664]{1,0:T(8,128)(2,1)}, u32[]{:S(2)}, u32[]{:S(2)}) collective-permute-start(bf16[384,1664]{1,0:T(8,128)(2,1)} %get-tuple-element.251), channel_id=1, source_target_pairs={{0,16},{4,20},{8,24},{12,28},{16,0},{20,4},{24,8},{28,12},{1,17},{... | collective-permute-start | bytes 3833864 | tf_op jit(solution)/shard_map/ppermute | solution.py:807
  436.3 27.7 %collective-permute-start.40 = (bf16[384,1664]{1,0:T(8,128)(2,1)}, bf16[384,1664]{1,0:T(8,128)(2,1)}, u32[]{:S(2)}, u32[]{:S(2)}) collective-permute-start(bf16[384,1664]{1,0:T(8,128)(2,1)} %get-tuple-element.256), channel_id=1, source_target_pairs={{0,24},{4,28},{8,16},{12,20},{16,8},{20,12},{24,0},{28,4},{1,25},{... | collective-permute-start | bytes 3833864 | tf_op jit(solution)/shard_map/ppermute | solution.py:807
  439.8 190.6 %all-gather.9.cloned.1.call-start = ((), (), s32[]{:S(2)}) async-start(), calls=%async_computation.4 | async-start | bytes 8110080 | tf_op jit(solution)/shard_map/all_gather | solution.py:1111
  471.9 12.1 %collective-permute-start.41 = (bf16[2,4,48,768]{3,2,1,0:T(8,128)(2,1)}, bf16[2,4,48,768]{3,2,1,0:T(8,128)(2,1)}, u32[]{:S(2)}, u32[]{:S(2)}) collective-permute-start(bf16[2,4,48,768]{3,2,1,0:T(8,128)(2,1)} %dynamic-slice_bitcast_fusion), channel_id=1, source_target_pairs={{0,4},{4,0},{8,12},{12,8},{16,20},{20,16},{24,28},{28,24},{1,5},{5... | collective-permute-start | bytes 1769480 | tf_op jit(solution)/shard_map/ppermute | solution.py:807
  484.0 5.0 collective-permute-start.45
  485.2 15.2 %collective-permute-start.42 = (bf16[1,4,48,768]{3,2,1,0:T(8,128)(2,1)S(1)}, bf16[1,4,48,768]{3,2,1,0:T(8,128)(2,1)S(1)}, u32[]{:S(2)}, u32[]{:S(2)}) collective-permute-start(bf16[1,4,48,768]{3,2,1,0:T(8,128)(2,1)S(1)} %constant_dynamic-slice_fusion.2), channel_id=1, source_target_pairs={{0,8},{4,12},{8,0},{12,4},{16,24},{20,28},{24,16},{28,20},{1,9},{5... | collective-permute-start | bytes 884744 | tf_op jit(solution)/shard_map/ppermute | solution.py:807
  500.5 13.4 %collective-permute-start.43 = (bf16[2,48,768]{2,1,0:T(8,128)(2,1)S(1)}, bf16[2,48,768]{2,1,0:T(8,128)(2,1)S(1)}, u32[]{:S(2)}, u32[]{:S(2)}) collective-permute-start(bf16[2,48,768]{2,1,0:T(8,128)(2,1)S(1)} %dynamic-slice_bitcast_fusion.2), channel_id=1, source_target_pairs={{0,1},{1,0},{2,3},{3,2},{4,5},{5,4},{6,7},{7,6},{8,9},{9,8},{10,11... | collective-permute-start | bytes 442376 | tf_op jit(solution)/shard_map/ppermute | solution.py:810
  502.1 21.4 %collective-permute-start.46 = (bf16[2,48,1792]{2,1,0:T(8,128)(2,1)S(1)}, bf16[2,48,1792]{2,1,0:T(8,128)(2,1)S(1)}, u32[]{:S(2)}, u32[]{:S(2)}) collective-permute-start(bf16[2,48,1792]{2,1,0:T(8,128)(2,1)S(1)} %dynamic-slice_bitcast_fusion.1), channel_id=1, source_target_pairs={{0,1},{1,0},{2,3},{3,2},{4,5},{5,4},{6,7},{7,6},{8,9},{9,8},{10,11... | collective-permute-start | bytes 1032200 | tf_op jit(solution)/shard_map/ppermute | solution.py:810
  514.1 9.7 %collective-permute-start.44 = (bf16[1,48,768]{2,1,0:T(8,128)(2,1)S(1)}, bf16[1,48,768]{2,1,0:T(8,128)(2,1)S(1)}, u32[]{:S(2)}, u32[]{:S(2)}) collective-permute-start(bf16[1,48,768]{2,1,0:T(8,128)(2,1)S(1)} %constant_dynamic-slice_fusion.1), channel_id=1, source_target_pairs={{0,2},{1,3},{2,0},{3,1},{4,6},{5,7},{6,4},{7,5},{8,10},{9,11},{10,... | collective-permute-start | bytes 221192 | tf_op jit(solution)/shard_map/ppermute | solution.py:810
  523.7 19.2 %collective-permute-start.47 = (bf16[1,48,1792]{2,1,0:T(8,128)(2,1)S(1)}, bf16[1,48,1792]{2,1,0:T(8,128)(2,1)S(1)}, u32[]{:S(2)}, u32[]{:S(2)}) collective-permute-start(bf16[1,48,1792]{2,1,0:T(8,128)(2,1)S(1)} %constant_dynamic-slice_fusion), channel_id=1, source_target_pairs={{0,2},{1,3},{2,0},{3,1},{4,6},{5,7},{6,4},{7,5},{8,10},{9,11},{10,... | collective-permute-start | bytes 516104 | tf_op jit(solution)/shard_map/ppermute | solution.py:810
  570.2 2.0 collective-permute-start.48
  572.3 6.2 collective-permute-start.49
  578.5 8.3 %collective-permute-start.50 = (bf16[48,896]{1,0:T(8,128)(2,1)S(1)}, bf16[48,896]{1,0:T(8,128)(2,1)S(1)}, u32[]{:S(2)}, u32[]{:S(2)}) collective-permute-start(bf16[48,896]{1,0:T(8,128)(2,1)S(1)} %fusion.65), channel_id=1, source_target_pairs={{0,1},{1,0},{2,3},{3,2},{4,5},{5,4},{6,7},{7,6},{8,9},{9,8},{10,11... | collective-permute-start | bytes 258056 | tf_op jit(solution)/shard_map/ppermute | solution.py:810
  578.7 14.1 %collective-permute-start.51 = (bf16[48,896]{1,0:T(8,128)(2,1)S(1)}, bf16[48,896]{1,0:T(8,128)(2,1)S(1)}, u32[]{:S(2)}, u32[]{:S(2)}) collective-permute-start(bf16[48,896]{1,0:T(8,128)(2,1)S(1)} %fusion.65), channel_id=1, source_target_pairs={{0,2},{1,3},{2,0},{3,1},{4,6},{5,7},{6,4},{7,5},{8,10},{9,11},{10,... | collective-permute-start | bytes 258056 | tf_op jit(solution)/shard_map/ppermute | solution.py:810
  579.1 13.7 %collective-permute-start.52 = (bf16[48,896]{1,0:T(8,128)(2,1)S(1)}, bf16[48,896]{1,0:T(8,128)(2,1)S(1)}, u32[]{:S(2)}, u32[]{:S(2)}) collective-permute-start(bf16[48,896]{1,0:T(8,128)(2,1)S(1)} %fusion.65), channel_id=1, source_target_pairs={{0,3},{1,2},{2,1},{3,0},{4,7},{5,6},{6,5},{7,4},{8,11},{9,10},{10,... | collective-permute-start | bytes 258056 | tf_op jit(solution)/shard_map/ppermute | solution.py:810
  592.9 4.6 collective-permute-start.53
  597.5 9.2 %collective-permute-start.54 = (bf16[2,48,896]{2,1,0:T(8,128)(2,1)S(1)}, bf16[2,48,896]{2,1,0:T(8,128)(2,1)S(1)}, u32[]{:S(2)}, u32[]{:S(2)}) collective-permute-start(bf16[2,48,896]{2,1,0:T(8,128)(2,1)S(1)} %pad_maximum_fusion.10), channel_id=1, source_target_pairs={{0,16},{4,20},{8,24},{12,28},{16,0},{20,4},{24,8},{28,12},{1,17},{... | collective-permute-start | bytes 516104 | tf_op jit(solution)/shard_map/ppermute | solution.py:807
  606.8 2.1 collective-permute-start.55
  (93 other events, 966.1 us)
Sparse Core Ops, SparseCore 0:
  13.6 32.9 all-gather.4
  61.1 116.5 all-gather.6
  439.9 106.0 reduce-scatter.1
  549.7 80.6 all-gather.8

commit v7 on v6

--- a/solution.py
+++ b/solution.py
@@ -935,7 +935,7 @@
         gate_lift_factors, upper_lift_factors, down_reduce_factors, down_lift_factors,
         gate_reduce_factors, upper_reduce_factors,
         ),
-        query_rot,
+        pair_all,
     )
     gate_shrink, up_shrink = shrink_of(late_lift[4]), shrink_of(late_lift[5])
     down_expand = expand_of(late_lift[3])
@@ -989,7 +989,7 @@
     n2_pieces = [normed_halves]
     for k in range(1, chips):
         if k < 3:
-            n2_pieces.append(swap_both(after(normed_halves, wide), 2 * k))
+            n2_pieces.append(swap_both(after(normed_halves, blocks), 2 * k))
             if k not in g0_pieces:
                 g0_pieces[k] = swap_both(after(grad_halves, wide), 2 * k)
     zero = jnp.zeros((lanes, hp), F32)

time: 659 us -> 654 us (level)
  Pallas kernels: 226 us -> 218 us
    ppermute x49, waiting for transfers between devices: 114 us -> 135 us  [swap(): return lax.ppermute(value, PLANE, [(i, i ^ k) for i in range(plane)])]
    all_gather x1, waiting for transfers between devices: 17.8 us -> 1.07 us  [body(): lax.all_gather(pair.reshape(seqs, tok_rows, 2 * kv_width), ('cp', 'seq'),...]
  transfers between devices with their start and end apart: 60 -> 60, of which waited for: 22 -> 28; matrix products, arithmetic and copies ran while one was open for 20% -> 20% of each run, Pallas kernels for 31% -> 29%
where the time goes in v7:
time: 654 us; the launch traced here: 642 us
  Pallas kernels  218 us (33%)
  waiting for transfers between devices  202 us (31%)
  starting transfers between devices  70.7 us (11%)
  local copies, waits for them, and re-layouts  55.9 us (9%)
  other arithmetic  44.5 us (7%)
  matrix products  36.4 us (6%)
  between operations  15.5 us (2%)
    ppermute x49, waiting for transfers between devices, swap(): return lax.ppermute(value, PLANE, [(i, i ^ k) for i in range(plane)])  135 us
    pallas_call x4, Pallas kernels, feed(): pl.pallas_call(functools.partial(feed_kernel, seqs, tuple(kinds)), grid_s...  120 us
    ppermute x49, starting transfers between devices, swap(): return lax.ppermute(value, PLANE, [(i, i ^ k) for i in range(plane)])  62.1 us
    ppermute x7, waiting for transfers between devices, swap_seq(): return lax.ppermute(value, 'seq', [(i, i ^ k) for i in range(seq_n)])  45.5 us
    pallas_call x1, Pallas kernels, attend_back(): pl.pallas_call(functools.partial(attend_back_kernel, spans, span_len, tok...  24.4 us
    pallas_call x1, Pallas kernels, attend(): pl.pallas_call(functools.partial(attend_kernel, spans, span_len, tokens),...  18.6 us
    pallas_call x2, Pallas kernels, with_blocks(): pl.pallas_call(functools.partial(kernel, seqs, count), grid_spec=pltpu.Pr...  18 us
    dot_general x21, matrix products, mm_tn(): lax.dot_general(left, right, (((0,), (0,)), ((), ())), preferred_element_...  17.1 us
  transfers between devices with their start and end apart: 60, of which 28 were waited for; matrix products, arithmetic and copies ran while one was open for 20% of the time, Pallas kernels for 29%

profile of v7, /device:TPU:0, one launch (start us, length us, event | category | flops | bytes accessed | tf_op | source)
XLA Modules:
  0.0 642.5 jit_solution(13636645276355928890)
XLA Ops:
  7.2 3.0 collective-permute-start
  11.8 1.6 pad_maximum_fusion.7
  14.8 1.9 collective-permute-start.13
  16.8 4.1 fusion.115
  20.8 1.9 fusion.114
  26.7 1.9 select_bitcast_fusion
  32.2 3.3 fusion.10
  36.8 8.9 %collective-permute-done.13 = f32[8,128]{0,1:T(8,128)} collective-permute-done((f32[8,128]{0,1:T(8,128)}, f32[8,128]{0,1:T(8,128)}, u32[]{:S(2)}, u32[]{:S(2)}) %collective-permute-start.13) | collective-permute-done | bytes 4128 | tf_op jit(solution)/shard_map/ppermute | solution.py:807
  53.9 2.0 convolution_convert_fusion.17.eo_ref.refs_10_
  55.9 4.3 keys_values.1
  69.4 24.6 %collective-permute-done.3.refs_2_ = bf16[192,1536]{1,0:T(8,128)(2,1)} collective-permute-done((bf16[192,1536]{1,0:T(8,128)(2,1)}, bf16[192,1536]{1,0:T(8,128)(2,1)}, u32[]{:S(2)}, u32[]{:S(2)}) %collective-permute-start.3) | collective-permute-done | bytes 589856 | tf_op jit(solution)/shard_map/ppermute | solution.py:807
  94.1 10.4 %collective-permute-done.6.refs_10_ = bf16[192,1536]{1,0:T(8,128)(2,1)S(1)} collective-permute-done((bf16[192,1536]{1,0:T(8,128)(2,1)}, bf16[192,1536]{1,0:T(8,128)(2,1)S(1)}, u32[]{:S(2)}, u32[]{:S(2)}) %collective-permute-start.6) | collective-permute-done | bytes 589856 | tf_op jit(solution)/shard_map/ppermute | solution.py:807
  104.5 11.8 %collective-permute-done.7.refs_11_ = bf16[192,1536]{1,0:T(8,128)(2,1)S(1)} collective-permute-done((bf16[192,1536]{1,0:T(8,128)(2,1)}, bf16[192,1536]{1,0:T(8,128)(2,1)S(1)}, u32[]{:S(2)}, u32[]{:S(2)}) %collective-permute-start.7) | collective-permute-done | bytes 589856 | tf_op jit(solution)/shard_map/ppermute | solution.py:807
  117.2 7.5 %queries.1 = (bf16[384,1536]{1,0:T(8,128)(2,1)}, bf16[384,64]{1,0:T(8,128)(2,1)}, bf16[1536,1536]{1,0:T(8,128)(2,1)}) custom-call(s32[1]{0:T(128)} %bitcast.info, bf16[384,1536]{1,0:T(8,128)(2,1)} %get-tuple-element.172.normed_ref, bf16[1536,64]{1,0:T(8,128)(2,1)} %bitcast.194, bf16[64,1536]{1,0:T(8,128)(2,1)} %convolution_convert_fusion.16.eq_ref, ...), custom_call_target="tpu_custom_call" | custom-call | flops 1811939328 | bytes 9437184 | tf_op jit(solution)/shard_map/queries/pallas_call | solution.py:483
  128.5 2.9 collective-permute-done.12.refs_1_
  131.9 5.1 assemble.1.refs_14_
  138.0 2.0 fusion.117
  153.6 2.0 copy.102
  155.6 1.8 copy.103
  157.7 2.1 pad_maximum_fusion.4.refs_12_
  162.3 18.6 %attend.1 = (bf16[384,1536]{1,0:T(8,128)(2,1)}, f32[6,8,768]{2,1,0:T(8,128)}) custom-call(s32[29]{0:T(128)} %pad_add_fusion.info, bf16[384,1536]{1,0:T(8,128)(2,1)} %get-tuple-element.194.q_ref, bf16[3,2048,512]{2,1,0:T(8,128)(2,1)} %all-gather.7.cloned.1.call-done.k_ref.v_ref, bf16[3,2048,512]{2,1,0:T(8,128)(2,1)} %all-gather.7.cloned.1.call-done.k_ref.v_ref), custom_call_target="tpu_custom_call" | custom-call | flops 4831838208 | bytes 6291456 | tf_op jit(solution)/shard_map/attend/pallas_call | solution.py:152
  181.7 10.6 %outputs.1 = (f32[384,1536]{1,0:T(8,128)}, bf16[384,1536]{1,0:T(8,128)(2,1)}, bf16[192,1536]{1,0:T(8,128)(2,1)}, bf16[192,1536]{1,0:T(8,128)(2,1)}, bf16[384,64]{1,0:T(8,128)(2,1)}, /*index=5*/bf16[1536,1536]{1,0:T(8,128)(2,1)}) custom-call(s32[1]{0:T(128)} %bitcast.info, bf16[384,1536]{1,0:T(8,128)(2,1)} %get-tuple-element.195.attended_ref.o_ref, ...), custom_call_target="tpu_custom_call" | custom-call | flops 1811939328 | bytes 9437184 | tf_op jit(solution)/shard_map/outputs/pallas_call | solution.py:483
  192.3 11.9 %collective-permute-start.24 = (bf16[2,192,2304]{2,1,0:T(8,128)(2,1)}, bf16[2,192,2304]{2,1,0:T(8,128)(2,1)}, u32[]{:S(2)}, u32[]{:S(2)}) collective-permute-start(bf16[2,192,2304]{2,1,0:T(8,128)(2,1)} %collective-permute-done.23.refs_6_), channel_id=1, source_target_pairs={{0,4},{4,0},{8,12},{12,8},{16,20},{20,16},{24,28},{28,24},{1,5},{5... | collective-permute-start | bytes 5308424 | tf_op jit(solution)/shard_map/ppermute | solution.py:807
  213.3 9.2 %collective-permute-done.25.refs_8_ = bf16[192,1536]{1,0:T(8,128)(2,1)S(1)} collective-permute-done((bf16[192,1536]{1,0:T(8,128)(2,1)}, bf16[192,1536]{1,0:T(8,128)(2,1)S(1)}, u32[]{:S(2)}, u32[]{:S(2)}) %collective-permute-start.25) | collective-permute-done | bytes 589856 | tf_op jit(solution)/shard_map/ppermute | solution.py:807
  223.7 11.1 %collective-permute-done.26.refs_9_ = bf16[192,1536]{1,0:T(8,128)(2,1)S(1)} collective-permute-done((bf16[192,1536]{1,0:T(8,128)(2,1)}, bf16[192,1536]{1,0:T(8,128)(2,1)S(1)}, u32[]{:S(2)}, u32[]{:S(2)}) %collective-permute-start.26) | collective-permute-done | bytes 589856 | tf_op jit(solution)/shard_map/ppermute | solution.py:807
  235.8 30.5 %feed.4 = (bf16[384,1664]{1,0:T(8,128)(2,1)}, bf16[384,1664]{1,0:T(8,128)(2,1)}, f32[64,2304]{1,0:T(8,128)}, f32[64,2304]{1,0:T(8,128)}, f32[64,2304]{1,0:T(8,128)}) custom-call(s32[2]{0:T(128)} %pad_add_fusion.1.info, bf16[2,192,2304]{2,1,0:T(8,128)(2,1)} %get-tuple-element.204.refs_0_, bf16[2,192,2304]{2,1,0:T(8,128)(2,1)} %collective-permute-done.18.refs_1_, ...), custom_call_target="tpu_custom_call" | custom-call | flops 16986931200 | bytes 21233664 | tf_op jit(solution)/shard_map/feed/pallas_call | solution.py:609
  271.9 29.9 %feed.5 = (bf16[384,1664]{1,0:T(8,128)(2,1)}, bf16[384,1664]{1,0:T(8,128)(2,1)}, f32[64,2304]{1,0:T(8,128)}, f32[64,2304]{1,0:T(8,128)}, f32[64,2304]{1,0:T(8,128)}) custom-call(s32[2]{0:T(128)} %pad_add_fusion.1.info, bf16[2,192,2304]{2,1,0:T(8,128)(2,1)} %get-tuple-element.204.refs_0_, bf16[2,192,2304]{2,1,0:T(8,128)(2,1)} %collective-permute-done.18.refs_1_, ...), custom_call_target="tpu_custom_call" | custom-call | flops 16986931200 | bytes 21233664 | tf_op jit(solution)/shard_map/feed/pallas_call | solution.py:609
  303.3 18.5 %collective-permute-done.34.refs_11_ = bf16[192,1536]{1,0:T(8,128)(2,1)} collective-permute-done((bf16[192,1536]{1,0:T(8,128)(2,1)}, bf16[192,1536]{1,0:T(8,128)(2,1)}, u32[]{:S(2)}, u32[]{:S(2)}) %collective-permute-start.34) | collective-permute-done | bytes 589856 | tf_op jit(solution)/shard_map/ppermute | solution.py:807
  321.7 29.7 %feed.6 = (bf16[384,1664]{1,0:T(8,128)(2,1)}, bf16[384,1664]{1,0:T(8,128)(2,1)}, f32[64,2304]{1,0:T(8,128)}, f32[64,2304]{1,0:T(8,128)}, f32[64,2304]{1,0:T(8,128)}) custom-call(s32[2]{0:T(128)} %pad_add_fusion.1.info, bf16[2,192,2304]{2,1,0:T(8,128)(2,1)} %get-tuple-element.204.refs_0_, bf16[2,192,2304]{2,1,0:T(8,128)(2,1)} %collective-permute-done.18.refs_1_, ...), custom_call_target="tpu_custom_call" | custom-call | flops 16986931200 | bytes 21233664 | tf_op jit(solution)/shard_map/feed/pallas_call | solution.py:609
  351.4 2.7 collective-permute-start.37
  354.1 29.9 %feed.7 = (bf16[384,1664]{1,0:T(8,128)(2,1)}, bf16[384,1664]{1,0:T(8,128)(2,1)}, f32[64,2304]{1,0:T(8,128)}, f32[64,2304]{1,0:T(8,128)}, f32[64,2304]{1,0:T(8,128)}) custom-call(s32[2]{0:T(128)} %pad_add_fusion.1.info, bf16[2,192,2304]{2,1,0:T(8,128)(2,1)} %get-tuple-element.204.refs_0_, bf16[2,192,2304]{2,1,0:T(8,128)(2,1)} %collective-permute-done.18.refs_1_, ...), custom_call_target="tpu_custom_call" | custom-call | flops 16986931200 | bytes 21233664 | tf_op jit(solution)/shard_map/feed/pallas_call | solution.py:609
  384.0 11.8 %before_attention.1 = (f32[384,1536]{1,0:T(8,128)}, bf16[384,1536]{1,0:T(8,128)(2,1)}, bf16[384,64]{1,0:T(8,128)(2,1)}, bf16[384,64]{1,0:T(8,128)(2,1)}, bf16[38...) custom-call(bf16[384,1664]{1,0:T(8,128)(2,1)} %copy-done.35, bf16[384,1664]{1,0:T(8,128)(2,1)} %copy-done.36, ...), custom_call_target="tpu_custom_call" | custom-call | flops 1811939328 | bytes 17694720 | tf_op jit(solution)/shard_map/before_attention/pallas_call | solution.py:402
  398.0 24.4 %attend_back.1 = (bf16[384,1536]{1,0:T(8,128)(2,1)}, bf16[3,2048,512]{2,1,0:T(8,128)(2,1)}) custom-call(s32[29]{0:T(128)} %pad_add_fusion.info, bf16[384,1536]{1,0:T(8,128)(2,1)} %get-tuple-element.194.q_ref, bf16[384,1536]{1,0:T(8,128)(2,1)} %get-tuple-element.253.do_ref, bf16[384,1536]{1,0:T(8,128)(2,1)} %get-tuple-element.195.attended_ref.o_ref, ...), custom_call_target="tpu_custom_call" | custom-call | flops 12079595520 | bytes 12582912 | tf_op jit(solution)/shard_map/attend_back/pallas_call | solution.py:253
  423.4 1.6 mul.173
  425.0 2.0 copy.106
  427.1 10.7 %collective-permute-start.40 = (bf16[384,1664]{1,0:T(8,128)(2,1)}, bf16[384,1664]{1,0:T(8,128)(2,1)}, u32[]{:S(2)}, u32[]{:S(2)}) collective-permute-start(bf16[384,1664]{1,0:T(8,128)(2,1)} %get-tuple-element.256), channel_id=1, source_target_pairs={{0,24},{4,28},{8,16},{12,20},{16,8},{20,12},{24,0},{28,4},{1,25},{... | collective-permute-start | bytes 3833864 | tf_op jit(solution)/shard_map/ppermute | solution.py:807
  437.9 1.7 copy.107
  439.6 1.9 broadcast_multiply_fusion
  443.3 3.2 copy.109
  446.5 2.5 add_convert_fusion
  452.7 13.0 %collective-permute-done.40 = bf16[384,1664]{1,0:T(8,128)(2,1)} collective-permute-done((bf16[384,1664]{1,0:T(8,128)(2,1)}, bf16[384,1664]{1,0:T(8,128)(2,1)}, u32[]{:S(2)}, u32[]{:S(2)}) %collective-permute-start.40) | collective-permute-done | bytes 1277984 | tf_op jit(solution)/shard_map/ppermute | solution.py:807
  465.7 2.7 convert_add_fusion
  469.0 1.6 copy-done.38
  486.7 7.7 %collective-permute-done.42 = bf16[1,4,48,768]{3,2,1,0:T(8,128)(2,1)S(1)} collective-permute-done((bf16[1,4,48,768]{3,2,1,0:T(8,128)(2,1)S(1)}, bf16[1,4,48,768]{3,2,1,0:T(8,128)(2,1)S(1)}, u32[]{:S(2)}, u32[]{:S(2)}) %collective-permute-start.42) | collective-permute-done | bytes 294944 | tf_op jit(solution)/shard_map/ppermute | solution.py:807
  496.7 9.0 %collective-permute-done.43 = bf16[2,48,768]{2,1,0:T(8,128)(2,1)S(1)} collective-permute-done((bf16[2,48,768]{2,1,0:T(8,128)(2,1)S(1)}, bf16[2,48,768]{2,1,0:T(8,128)(2,1)S(1)}, u32[]{:S(2)}, u32[]{:S(2)}) %collective-permute-start.43) | collective-permute-done | bytes 147488 | tf_op jit(solution)/shard_map/ppermute | solution.py:810
  506.7 8.0 %collective-permute-done.46 = bf16[2,48,1792]{2,1,0:T(8,128)(2,1)S(1)} collective-permute-done((bf16[2,48,1792]{2,1,0:T(8,128)(2,1)S(1)}, bf16[2,48,1792]{2,1,0:T(8,128)(2,1)S(1)}, u32[]{:S(2)}, u32[]{:S(2)}) %collective-permute-start.46) | collective-permute-done | bytes 344096 | tf_op jit(solution)/shard_map/ppermute | solution.py:810
  515.2 17.5 %collective-permute-done.47 = bf16[1,48,1792]{2,1,0:T(8,128)(2,1)S(1)} collective-permute-done((bf16[1,48,1792]{2,1,0:T(8,128)(2,1)S(1)}, bf16[1,48,1792]{2,1,0:T(8,128)(2,1)S(1)}, u32[]{:S(2)}, u32[]{:S(2)}) %collective-permute-start.47) | collective-permute-done | bytes 172064 | tf_op jit(solution)/shard_map/ppermute | solution.py:810
  533.5 4.3 reduce-scatter.2.cloned.1.call-done
  545.7 2.0 gather_fusion
  549.3 3.6 fusion.8
  552.9 4.4 fusion.120
  557.9 3.3 last_grads.1
  562.2 1.8 convolution_add_fusion.1
  565.4 3.7 collective-permute-done.49
  569.1 2.4 collective-permute-start.50
  574.5 5.1 collective-permute-done.50
  579.6 5.5 collective-permute-done.51
  585.4 1.7 collective-permute-start.53
  588.2 1.8 collective-permute-done.53
  590.0 3.7 collective-permute-start.54
  593.7 6.4 collective-permute-done.54
  600.3 2.0 fusion.5
  607.9 15.8 %all-gather.9.cloned.1.call-done = bf16[1536,2560]{1,0:T(8,128)(2,1)} async-done(((bf16[48,2560]{1,0:T(8,128)(2,1)}), bf16[1536,2560]{1,0:T(8,128)(2,1)}) %all-gather.9.cloned.1.call-update) | async-done | bytes 7864336 | tf_op jit(solution)/shard_map/all_gather | solution.py:1111
  623.6 12.1 %expand.1 = (f32[128,8960]{1,0:T(8,128)}, f32[128,8960]{1,0:T(8,128)}, f32[8960,128]{1,0:T(8,128)}, f32[1536,128]{1,0:T(8,128)}, f32[1536,128]{1,0:T(8,128)}, /*...) custom-call(bf16[32,48,2560]{2,1,0:T(8,128)(2,1)} %bitcast.191, ...), custom_call_target="tpu_custom_call" | custom-call | flops 660602880 | bytes 13762560 | tf_op jit(solution)/shard_map/expand/pallas_call | solution.py:747
  (432 shorter events, 122.5 us)
Async XLA Ops:
  7.2 143.2 %copy-start = (bf16[8960,128]{1,0:T(8,128)(2,1)S(1)}, bf16[8960,128]{1,0:T(8,128)(2,1)}, u32[]{:S(2)}) copy-start(bf16[8960,128]{1,0:T(8,128)(2,1)} %param.59) | copy-start | bytes 6881284
  7.2 48.7 %all-gather.5.cloned.1.call-start = ((), (), s32[]{:S(2)}) async-start(), calls=%async_computation.1 | async-start | bytes 1769472 | tf_op jit(solution)/shard_map/all_gather | solution.py:849
  7.2 48.7 %collective-permute-start = (bf16[192,1536]{1,0:T(8,128)(2,1)}, bf16[192,1536]{1,0:T(8,128)(2,1)}, u32[]{:S(2)}, u32[]{:S(2)}) collective-permute-start(bf16[192,1536]{1,0:T(8,128)(2,1)} %refs_0_), channel_id=1, source_target_pairs={{0,8},{4,12},{8,0},{12,4},{16,24},{20,28},{24,16},{28,20},{1,9},{5... | collective-permute-start | bytes 1769480 | tf_op jit(solution)/shard_map/ppermute | solution.py:807
  10.3 45.6 %collective-permute-start.1 = (bf16[192,1536]{1,0:T(8,128)(2,1)}, bf16[192,1536]{1,0:T(8,128)(2,1)}, u32[]{:S(2)}, u32[]{:S(2)}) collective-permute-start(bf16[192,1536]{1,0:T(8,128)(2,1)} %refs_0_), channel_id=1, source_target_pairs={{0,16},{4,20},{8,24},{12,28},{16,0},{20,4},{24,8},{28,12},{1,17},{... | collective-permute-start | bytes 1769480 | tf_op jit(solution)/shard_map/ppermute | solution.py:807
  11.8 44.1 %collective-permute-start.2 = (bf16[192,1536]{1,0:T(8,128)(2,1)}, bf16[192,1536]{1,0:T(8,128)(2,1)}, u32[]{:S(2)}, u32[]{:S(2)}) collective-permute-start(bf16[192,1536]{1,0:T(8,128)(2,1)} %refs_0_), channel_id=1, source_target_pairs={{0,24},{4,28},{8,16},{12,20},{16,8},{20,12},{24,0},{28,4},{1,25},{... | collective-permute-start | bytes 1769480 | tf_op jit(solution)/shard_map/ppermute | solution.py:807
  13.5 124.5 %all-gather.7.cloned.1.call-start = ((), (), s32[]{:S(2)}) async-start(), calls=%async_computation.2 | async-start | bytes 6684672 | tf_op jit(solution)/shard_map/all_gather | solution.py:911
  14.8 30.9 %collective-permute-start.13 = (f32[8,128]{0,1:T(8,128)}, f32[8,128]{0,1:T(8,128)}, u32[]{:S(2)}, u32[]{:S(2)}) collective-permute-start(f32[8,128]{0,1:T(8,128)} %broadcast_in_dim.83), channel_id=1, source_target_pairs={{0,16},{4,20},{8,24},{12,28},{16,0},{20,4},{24,8},{28,12},{1,17},{... | collective-permute-start | bytes 12296 | tf_op jit(solution)/shard_map/ppermute | solution.py:807
  60.2 477.5 %reduce-scatter.2.cloned.1.call-start = ((), (), s32[]{:S(2)}) async-start(), calls=%async_computation.3 | async-start | bytes 6684672 | tf_op jit(solution)/shard_map/reduce_scatter | solution.py:1044
  60.5 2.3 collective-permute-start.10
  60.6 3.9 collective-permute-start.11
  61.1 4.8 collective-permute-start.8
  61.2 5.5 collective-permute-start.9
  61.6 32.5 %collective-permute-start.3 = (bf16[192,1536]{1,0:T(8,128)(2,1)}, bf16[192,1536]{1,0:T(8,128)(2,1)}, u32[]{:S(2)}, u32[]{:S(2)}) collective-permute-start(bf16[192,1536]{1,0:T(8,128)(2,1)} %refs_0_.2), channel_id=1, source_target_pairs={{0,8},{4,12},{8,0},{12,4},{16,24},{20,28},{24,16},{28,20},{1,9},{5... | collective-permute-start | bytes 1769480 | tf_op jit(solution)/shard_map/ppermute | solution.py:807
  62.8 31.3 %collective-permute-start.4 = (bf16[192,1536]{1,0:T(8,128)(2,1)}, bf16[192,1536]{1,0:T(8,128)(2,1)}, u32[]{:S(2)}, u32[]{:S(2)}) collective-permute-start(bf16[192,1536]{1,0:T(8,128)(2,1)} %refs_0_.2), channel_id=1, source_target_pairs={{0,16},{4,20},{8,24},{12,28},{16,0},{20,4},{24,8},{28,12},{1,17},{... | collective-permute-start | bytes 1769480 | tf_op jit(solution)/shard_map/ppermute | solution.py:807
  64.5 29.6 %collective-permute-start.5 = (bf16[192,1536]{1,0:T(8,128)(2,1)}, bf16[192,1536]{1,0:T(8,128)(2,1)}, u32[]{:S(2)}, u32[]{:S(2)}) collective-permute-start(bf16[192,1536]{1,0:T(8,128)(2,1)} %refs_0_.2), channel_id=1, source_target_pairs={{0,24},{4,28},{8,16},{12,20},{16,8},{20,12},{24,0},{28,4},{1,25},{... | collective-permute-start | bytes 1769480 | tf_op jit(solution)/shard_map/ppermute | solution.py:807
  65.9 38.6 %collective-permute-start.6 = (bf16[192,1536]{1,0:T(8,128)(2,1)}, bf16[192,1536]{1,0:T(8,128)(2,1)S(1)}, u32[]{:S(2)}, u32[]{:S(2)}) collective-permute-start(bf16[192,1536]{1,0:T(8,128)(2,1)} %get-tuple-element.219.refs_10_), channel_id=1, source_target_pairs={{0,16},{4,20},{8,24},{12,28},{16,0},{20,4},{24,8},{28,12},{1,17},{... | collective-permute-start | bytes 1769480 | tf_op jit(solution)/shard_map/ppermute | solution.py:807
  67.5 48.8 %collective-permute-start.7 = (bf16[192,1536]{1,0:T(8,128)(2,1)}, bf16[192,1536]{1,0:T(8,128)(2,1)S(1)}, u32[]{:S(2)}, u32[]{:S(2)}) collective-permute-start(bf16[192,1536]{1,0:T(8,128)(2,1)} %get-tuple-element.220.refs_11_), channel_id=1, source_target_pairs={{0,16},{4,20},{8,24},{12,28},{16,0},{20,4},{24,8},{28,12},{1,17},{... | collective-permute-start | bytes 1769480 | tf_op jit(solution)/shard_map/ppermute | solution.py:807
  124.6 6.8 %collective-permute-start.12 = (bf16[1120,1536]{1,0:T(8,128)(2,1)}, bf16[1120,1536]{1,0:T(8,128)(2,1)}, u32[]{:S(2)}, u32[]{:S(2)}) collective-permute-start(bf16[1120,1536]{1,0:T(8,128)(2,1)} %refs_0_.1), channel_id=1, source_target_pairs={{0,4},{4,0},{8,12},{12,8},{16,20},{20,16},{24,28},{28,24},{1,5},{5... | collective-permute-start | bytes 10321928 | tf_op jit(solution)/shard_map/ppermute | solution.py:807
  126.0 66.3 %collective-permute-start.23 = (bf16[2,192,2304]{2,1,0:T(8,128)(2,1)}, bf16[2,192,2304]{2,1,0:T(8,128)(2,1)}, u32[]{:S(2)}, u32[]{:S(2)}) collective-permute-start(bf16[2,192,2304]{2,1,0:T(8,128)(2,1)} %get-tuple-element.212), channel_id=1, source_target_pairs={{0,24},{4,28},{8,16},{12,20},{16,8},{20,12},{24,0},{28,4},{1,25},{... | collective-permute-start | bytes 5308424 | tf_op jit(solution)/shard_map/ppermute | solution.py:807
  127.4 30.0 %collective-permute-start.14 = (bf16[192,1536]{1,0:T(8,128)(2,1)}, bf16[192,1536]{1,0:T(8,128)(2,1)}, u32[]{:S(2)}, u32[]{:S(2)}) collective-permute-start(bf16[192,1536]{1,0:T(8,128)(2,1)} %refs_0_.2), channel_id=1, source_target_pairs={{0,4},{4,0},{8,12},{12,8},{16,20},{20,16},{24,28},{28,24},{1,5},{5... | collective-permute-start | bytes 1769480 | tf_op jit(solution)/shard_map/ppermute | solution.py:807
  127.6 33.1 %collective-permute-start.15 = (bf16[192,1536]{1,0:T(8,128)(2,1)}, bf16[192,1536]{1,0:T(8,128)(2,1)}, u32[]{:S(2)}, u32[]{:S(2)}) collective-permute-start(bf16[192,1536]{1,0:T(8,128)(2,1)} %collective-permute-done.3.refs_2_), channel_id=1, source_target_pairs={{0,4},{4,0},{8,12},{12,8},{16,20},{20,16},{24,28},{28,24},{1,5},{5... | collective-permute-start | bytes 1769480 | tf_op jit(solution)/shard_map/ppermute | solution.py:807
  128.0 77.3 %collective-permute-start.21 = (bf16[2,192,2304]{2,1,0:T(8,128)(2,1)}, bf16[2,192,2304]{2,1,0:T(8,128)(2,1)}, u32[]{:S(2)}, u32[]{:S(2)}) collective-permute-start(bf16[2,192,2304]{2,1,0:T(8,128)(2,1)} %get-tuple-element.209), channel_id=1, source_target_pairs={{0,16},{4,20},{8,24},{12,28},{16,0},{20,4},{24,8},{28,12},{1,17},{... | collective-permute-start | bytes 5308424 | tf_op jit(solution)/shard_map/ppermute | solution.py:807
  131.4 74.7 %collective-permute-start.19 = (bf16[2,192,2304]{2,1,0:T(8,128)(2,1)}, bf16[2,192,2304]{2,1,0:T(8,128)(2,1)}, u32[]{:S(2)}, u32[]{:S(2)}) collective-permute-start(bf16[2,192,2304]{2,1,0:T(8,128)(2,1)} %get-tuple-element.206), channel_id=1, source_target_pairs={{0,8},{4,12},{8,0},{12,4},{16,24},{20,28},{24,16},{28,20},{1,9},{5... | collective-permute-start | bytes 5308424 | tf_op jit(solution)/shard_map/ppermute | solution.py:807
  157.4 4.6 collective-permute-start.16
  160.8 20.1 %collective-permute-start.17 = (bf16[192,1536]{1,0:T(8,128)(2,1)}, bf16[192,1536]{1,0:T(8,128)(2,1)S(1)}, u32[]{:S(2)}, u32[]{:S(2)}) collective-permute-start(bf16[192,1536]{1,0:T(8,128)(2,1)} %collective-permute-done.5.refs_6_), channel_id=1, source_target_pairs={{0,4},{4,0},{8,12},{12,8},{16,20},{20,16},{24,28},{28,24},{1,5},{5... | collective-permute-start | bytes 1769480 | tf_op jit(solution)/shard_map/ppermute | solution.py:807
  162.0 45.7 %collective-permute-start.18 = (bf16[2,192,2304]{2,1,0:T(8,128)(2,1)S(1)}, bf16[2,192,2304]{2,1,0:T(8,128)(2,1)}, u32[]{:S(2)}, u32[]{:S(2)}) collective-permute-start(bf16[2,192,2304]{2,1,0:T(8,128)(2,1)S(1)} %copy-done.31), channel_id=1, source_target_pairs={{0,4},{4,0},{8,12},{12,8},{16,20},{20,16},{24,28},{28,24},{1,5},{5... | collective-permute-start | bytes 5308424 | tf_op jit(solution)/shard_map/ppermute | solution.py:807
  192.3 17.2 %collective-permute-start.24 = (bf16[2,192,2304]{2,1,0:T(8,128)(2,1)}, bf16[2,192,2304]{2,1,0:T(8,128)(2,1)}, u32[]{:S(2)}, u32[]{:S(2)}) collective-permute-start(bf16[2,192,2304]{2,1,0:T(8,128)(2,1)} %collective-permute-done.23.refs_6_), channel_id=1, source_target_pairs={{0,4},{4,0},{8,12},{12,8},{16,20},{20,16},{24,28},{28,24},{1,5},{5... | collective-permute-start | bytes 5308424 | tf_op jit(solution)/shard_map/ppermute | solution.py:807
  205.2 5.4 collective-permute-start.22
  206.1 6.8 %collective-permute-start.20 = (bf16[2,192,2304]{2,1,0:T(8,128)(2,1)}, bf16[2,192,2304]{2,1,0:T(8,128)(2,1)}, u32[]{:S(2)}, u32[]{:S(2)}) collective-permute-start(bf16[2,192,2304]{2,1,0:T(8,128)(2,1)} %collective-permute-done.19.refs_2_), channel_id=1, source_target_pairs={{0,4},{4,0},{8,12},{12,8},{16,20},{20,16},{24,28},{28,24},{1,5},{5... | collective-permute-start | bytes 5308424 | tf_op jit(solution)/shard_map/ppermute | solution.py:807
  206.2 16.3 %collective-permute-start.25 = (bf16[192,1536]{1,0:T(8,128)(2,1)}, bf16[192,1536]{1,0:T(8,128)(2,1)S(1)}, u32[]{:S(2)}, u32[]{:S(2)}) collective-permute-start(bf16[192,1536]{1,0:T(8,128)(2,1)} %get-tuple-element.216.refs_8_), channel_id=1, source_target_pairs={{0,16},{4,20},{8,24},{12,28},{16,0},{20,4},{24,8},{28,12},{1,17},{... | collective-permute-start | bytes 1769480 | tf_op jit(solution)/shard_map/ppermute | solution.py:807
  207.7 27.0 %collective-permute-start.26 = (bf16[192,1536]{1,0:T(8,128)(2,1)}, bf16[192,1536]{1,0:T(8,128)(2,1)S(1)}, u32[]{:S(2)}, u32[]{:S(2)}) collective-permute-start(bf16[192,1536]{1,0:T(8,128)(2,1)} %get-tuple-element.217.refs_9_), channel_id=1, source_target_pairs={{0,16},{4,20},{8,24},{12,28},{16,0},{20,4},{24,8},{28,12},{1,17},{... | collective-permute-start | bytes 1769480 | tf_op jit(solution)/shard_map/ppermute | solution.py:807
  208.9 259.4 %copy-start.74 = (pred[64]{0:T(512)(128)(4,1)}, pred[64]{0:T(512)(128)(4,1)S(1)}, u32[]{:S(2)}) copy-start(pred[64]{0:T(512)(128)(4,1)S(1)} %compare_and_fusion.2) | copy-start | bytes 196
  209.5 258.8 %copy-start.66 = (s32[384]{0:T(512)}, s32[384]{0:T(512)S(1)}, u32[]{:S(2)}) copy-start(s32[384]{0:T(512)S(1)} %get-tuple-element.345) | copy-start | bytes 4612
  209.5 258.9 %copy-start.67 = (s32[384]{0:T(512)}, s32[384]{0:T(512)S(1)}, u32[]{:S(2)}) copy-start(s32[384]{0:T(512)S(1)} %get-tuple-element.346) | copy-start | bytes 4612
  209.5 56.7 %collective-permute-start.27 = (bf16[192,1536]{1,0:T(8,128)(2,1)}, bf16[192,1536]{1,0:T(8,128)(2,1)S(1)}, u32[]{:S(2)}, u32[]{:S(2)}) collective-permute-start(bf16[192,1536]{1,0:T(8,128)(2,1)} %get-tuple-element.216.refs_8_), channel_id=1, source_target_pairs={{0,8},{4,12},{8,0},{12,4},{16,24},{20,28},{24,16},{28,20},{1,9},{5... | collective-permute-start | bytes 1769480 | tf_op jit(solution)/shard_map/ppermute | solution.py:807
  210.6 55.6 %collective-permute-start.28 = (bf16[192,1536]{1,0:T(8,128)(2,1)}, bf16[192,1536]{1,0:T(8,128)(2,1)}, u32[]{:S(2)}, u32[]{:S(2)}) collective-permute-start(bf16[192,1536]{1,0:T(8,128)(2,1)} %get-tuple-element.217.refs_9_), channel_id=1, source_target_pairs={{0,8},{4,12},{8,0},{12,4},{16,24},{20,28},{24,16},{28,20},{1,9},{5... | collective-permute-start | bytes 1769480 | tf_op jit(solution)/shard_map/ppermute | solution.py:807
  212.9 56.1 %collective-permute-start.29 = (bf16[192,1536]{1,0:T(8,128)(2,1)}, bf16[192,1536]{1,0:T(8,128)(2,1)}, u32[]{:S(2)}, u32[]{:S(2)}) collective-permute-start(bf16[192,1536]{1,0:T(8,128)(2,1)} %get-tuple-element.219.refs_10_), channel_id=1, source_target_pairs={{0,8},{4,12},{8,0},{12,4},{16,24},{20,28},{24,16},{28,20},{1,9},{5... | collective-permute-start | bytes 1769480 | tf_op jit(solution)/shard_map/ppermute | solution.py:807
  222.5 46.4 %collective-permute-start.30 = (bf16[192,1536]{1,0:T(8,128)(2,1)}, bf16[192,1536]{1,0:T(8,128)(2,1)}, u32[]{:S(2)}, u32[]{:S(2)}) collective-permute-start(bf16[192,1536]{1,0:T(8,128)(2,1)} %get-tuple-element.220.refs_11_), channel_id=1, source_target_pairs={{0,8},{4,12},{8,0},{12,4},{16,24},{20,28},{24,16},{28,20},{1,9},{5... | collective-permute-start | bytes 1769480 | tf_op jit(solution)/shard_map/ppermute | solution.py:807
  266.3 35.6 %collective-permute-start.31 = (bf16[192,1536]{1,0:T(8,128)(2,1)S(1)}, bf16[192,1536]{1,0:T(8,128)(2,1)S(1)}, u32[]{:S(2)}, u32[]{:S(2)}) collective-permute-start(bf16[192,1536]{1,0:T(8,128)(2,1)S(1)} %copy-done.83), channel_id=1, source_target_pairs={{0,8},{4,12},{8,0},{12,4},{16,24},{20,28},{24,16},{28,20},{1,9},{5... | collective-permute-start | bytes 1769480 | tf_op jit(solution)/shard_map/ppermute | solution.py:807
  266.9 36.3 %collective-permute-start.32 = (bf16[192,1536]{1,0:T(8,128)(2,1)}, bf16[192,1536]{1,0:T(8,128)(2,1)}, u32[]{:S(2)}, u32[]{:S(2)}) collective-permute-start(bf16[192,1536]{1,0:T(8,128)(2,1)} %collective-permute-done.28.refs_9_), channel_id=1, source_target_pairs={{0,16},{4,20},{8,24},{12,28},{16,0},{20,4},{24,8},{28,12},{1,17},{... | collective-permute-start | bytes 1769480 | tf_op jit(solution)/shard_map/ppermute | solution.py:807
  268.4 85.7 %collective-permute-start.35 = (bf16[384,1664]{1,0:T(8,128)(2,1)}, bf16[384,1664]{1,0:T(8,128)(2,1)S(1)}, u32[]{:S(2)}, u32[]{:S(2)}) collective-permute-start(bf16[384,1664]{1,0:T(8,128)(2,1)} %get-tuple-element.239), channel_id=1, source_target_pairs={{0,16},{4,20},{8,24},{12,28},{16,0},{20,4},{24,8},{28,12},{1,17},{... | collective-permute-start | bytes 3833864 | tf_op jit(solution)/shard_map/ppermute | solution.py:807
  269.0 34.3 %collective-permute-start.33 = (bf16[192,1536]{1,0:T(8,128)(2,1)S(1)}, bf16[192,1536]{1,0:T(8,128)(2,1)}, u32[]{:S(2)}, u32[]{:S(2)}) collective-permute-start(bf16[192,1536]{1,0:T(8,128)(2,1)S(1)} %copy-done.80), channel_id=1, source_target_pairs={{0,8},{4,12},{8,0},{12,4},{16,24},{20,28},{24,16},{28,20},{1,9},{5... | collective-permute-start | bytes 1769480 | tf_op jit(solution)/shard_map/ppermute | solution.py:807
  270.5 51.3 %collective-permute-start.34 = (bf16[192,1536]{1,0:T(8,128)(2,1)}, bf16[192,1536]{1,0:T(8,128)(2,1)}, u32[]{:S(2)}, u32[]{:S(2)}) collective-permute-start(bf16[192,1536]{1,0:T(8,128)(2,1)} %collective-permute-done.30.refs_11_), channel_id=1, source_target_pairs={{0,16},{4,20},{8,24},{12,28},{16,0},{20,4},{24,8},{28,12},{1,17},{... | collective-permute-start | bytes 1769480 | tf_op jit(solution)/shard_map/ppermute | solution.py:807
  302.6 51.4 %collective-permute-start.36 = (bf16[384,1664]{1,0:T(8,128)(2,1)}, bf16[384,1664]{1,0:T(8,128)(2,1)S(1)}, u32[]{:S(2)}, u32[]{:S(2)}) collective-permute-start(bf16[384,1664]{1,0:T(8,128)(2,1)} %get-tuple-element.240), channel_id=1, source_target_pairs={{0,8},{4,12},{8,0},{12,4},{16,24},{20,28},{24,16},{28,20},{1,9},{5... | collective-permute-start | bytes 3833864 | tf_op jit(solution)/shard_map/ppermute | solution.py:807
  351.4 32.6 %collective-permute-start.37 = (bf16[384,1664]{1,0:T(8,128)(2,1)}, bf16[384,1664]{1,0:T(8,128)(2,1)}, u32[]{:S(2)}, u32[]{:S(2)}) collective-permute-start(bf16[384,1664]{1,0:T(8,128)(2,1)} %get-tuple-element.245), channel_id=1, source_target_pairs={{0,24},{4,28},{8,16},{12,20},{16,8},{20,12},{24,0},{28,4},{1,25},{... | collective-permute-start | bytes 3833864 | tf_op jit(solution)/shard_map/ppermute | solution.py:807
  395.9 41.9 %collective-permute-start.38 = (bf16[384,1664]{1,0:T(8,128)(2,1)}, bf16[384,1664]{1,0:T(8,128)(2,1)}, u32[]{:S(2)}, u32[]{:S(2)}) collective-permute-start(bf16[384,1664]{1,0:T(8,128)(2,1)} %get-tuple-element.250), channel_id=1, source_target_pairs={{0,8},{4,12},{8,0},{12,4},{16,24},{20,28},{24,16},{28,20},{1,9},{5... | collective-permute-start | bytes 3833864 | tf_op jit(solution)/shard_map/ppermute | solution.py:807
  396.2 41.5 %collective-permute-start.39 = (bf16[384,1664]{1,0:T(8,128)(2,1)}, bf16[384,1664]{1,0:T(8,128)(2,1)}, u32[]{:S(2)}, u32[]{:S(2)}) collective-permute-start(bf16[384,1664]{1,0:T(8,128)(2,1)} %get-tuple-element.251), channel_id=1, source_target_pairs={{0,16},{4,20},{8,24},{12,28},{16,0},{20,4},{24,8},{28,12},{1,17},{... | collective-permute-start | bytes 3833864 | tf_op jit(solution)/shard_map/ppermute | solution.py:807
  427.1 38.6 %collective-permute-start.40 = (bf16[384,1664]{1,0:T(8,128)(2,1)}, bf16[384,1664]{1,0:T(8,128)(2,1)}, u32[]{:S(2)}, u32[]{:S(2)}) collective-permute-start(bf16[384,1664]{1,0:T(8,128)(2,1)} %get-tuple-element.256), channel_id=1, source_target_pairs={{0,24},{4,28},{8,16},{12,20},{16,8},{20,12},{24,0},{28,4},{1,25},{... | collective-permute-start | bytes 3833864 | tf_op jit(solution)/shard_map/ppermute | solution.py:807
  437.8 185.8 %all-gather.9.cloned.1.call-start = ((), (), s32[]{:S(2)}) async-start(), calls=%async_computation.4 | async-start | bytes 8110080 | tf_op jit(solution)/shard_map/all_gather | solution.py:1111
  473.4 8.6 %collective-permute-start.41 = (bf16[2,4,48,768]{3,2,1,0:T(8,128)(2,1)}, bf16[2,4,48,768]{3,2,1,0:T(8,128)(2,1)}, u32[]{:S(2)}, u32[]{:S(2)}) collective-permute-start(bf16[2,4,48,768]{3,2,1,0:T(8,128)(2,1)} %dynamic-slice_bitcast_fusion), channel_id=1, source_target_pairs={{0,4},{4,0},{8,12},{12,8},{16,20},{20,16},{24,28},{28,24},{1,5},{5... | collective-permute-start | bytes 1769480 | tf_op jit(solution)/shard_map/ppermute | solution.py:807
  482.1 2.5 collective-permute-start.45
  483.3 11.1 %collective-permute-start.42 = (bf16[1,4,48,768]{3,2,1,0:T(8,128)(2,1)S(1)}, bf16[1,4,48,768]{3,2,1,0:T(8,128)(2,1)S(1)}, u32[]{:S(2)}, u32[]{:S(2)}) collective-permute-start(bf16[1,4,48,768]{3,2,1,0:T(8,128)(2,1)S(1)} %constant_dynamic-slice_fusion.2), channel_id=1, source_target_pairs={{0,8},{4,12},{8,0},{12,4},{16,24},{20,28},{24,16},{28,20},{1,9},{5... | collective-permute-start | bytes 884744 | tf_op jit(solution)/shard_map/ppermute | solution.py:807
  494.5 11.2 %collective-permute-start.43 = (bf16[2,48,768]{2,1,0:T(8,128)(2,1)S(1)}, bf16[2,48,768]{2,1,0:T(8,128)(2,1)S(1)}, u32[]{:S(2)}, u32[]{:S(2)}) collective-permute-start(bf16[2,48,768]{2,1,0:T(8,128)(2,1)S(1)} %dynamic-slice_bitcast_fusion.2), channel_id=1, source_target_pairs={{0,1},{1,0},{2,3},{3,2},{4,5},{5,4},{6,7},{7,6},{8,9},{9,8},{10,11... | collective-permute-start | bytes 442376 | tf_op jit(solution)/shard_map/ppermute | solution.py:810
  496.1 18.6 %collective-permute-start.46 = (bf16[2,48,1792]{2,1,0:T(8,128)(2,1)S(1)}, bf16[2,48,1792]{2,1,0:T(8,128)(2,1)S(1)}, u32[]{:S(2)}, u32[]{:S(2)}) collective-permute-start(bf16[2,48,1792]{2,1,0:T(8,128)(2,1)S(1)} %dynamic-slice_bitcast_fusion.1), channel_id=1, source_target_pairs={{0,1},{1,0},{2,3},{3,2},{4,5},{5,4},{6,7},{7,6},{8,9},{9,8},{10,11... | collective-permute-start | bytes 1032200 | tf_op jit(solution)/shard_map/ppermute | solution.py:810
  505.8 9.3 %collective-permute-start.44 = (bf16[1,48,768]{2,1,0:T(8,128)(2,1)S(1)}, bf16[1,48,768]{2,1,0:T(8,128)(2,1)S(1)}, u32[]{:S(2)}, u32[]{:S(2)}) collective-permute-start(bf16[1,48,768]{2,1,0:T(8,128)(2,1)S(1)} %constant_dynamic-slice_fusion.1), channel_id=1, source_target_pairs={{0,2},{1,3},{2,0},{3,1},{4,6},{5,7},{6,4},{7,5},{8,10},{9,11},{10,... | collective-permute-start | bytes 221192 | tf_op jit(solution)/shard_map/ppermute | solution.py:810
  514.8 17.9 %collective-permute-start.47 = (bf16[1,48,1792]{2,1,0:T(8,128)(2,1)S(1)}, bf16[1,48,1792]{2,1,0:T(8,128)(2,1)S(1)}, u32[]{:S(2)}, u32[]{:S(2)}) collective-permute-start(bf16[1,48,1792]{2,1,0:T(8,128)(2,1)S(1)} %constant_dynamic-slice_fusion), channel_id=1, source_target_pairs={{0,2},{1,3},{2,0},{3,1},{4,6},{5,7},{6,4},{7,5},{8,10},{9,11},{10,... | collective-permute-start | bytes 516104 | tf_op jit(solution)/shard_map/ppermute | solution.py:810
  562.1 2.0 collective-permute-start.48
  564.1 5.0 collective-permute-start.49
  569.1 10.4 %collective-permute-start.50 = (bf16[48,896]{1,0:T(8,128)(2,1)S(1)}, bf16[48,896]{1,0:T(8,128)(2,1)S(1)}, u32[]{:S(2)}, u32[]{:S(2)}) collective-permute-start(bf16[48,896]{1,0:T(8,128)(2,1)S(1)} %fusion.65), channel_id=1, source_target_pairs={{0,1},{1,0},{2,3},{3,2},{4,5},{5,4},{6,7},{7,6},{8,9},{9,8},{10,11... | collective-permute-start | bytes 258056 | tf_op jit(solution)/shard_map/ppermute | solution.py:810
  571.6 13.5 %collective-permute-start.51 = (bf16[48,896]{1,0:T(8,128)(2,1)S(1)}, bf16[48,896]{1,0:T(8,128)(2,1)S(1)}, u32[]{:S(2)}, u32[]{:S(2)}) collective-permute-start(bf16[48,896]{1,0:T(8,128)(2,1)S(1)} %fusion.65), channel_id=1, source_target_pairs={{0,2},{1,3},{2,0},{3,1},{4,6},{5,7},{6,4},{7,5},{8,10},{9,11},{10,... | collective-permute-start | bytes 258056 | tf_op jit(solution)/shard_map/ppermute | solution.py:810
  572.7 12.7 %collective-permute-start.52 = (bf16[48,896]{1,0:T(8,128)(2,1)S(1)}, bf16[48,896]{1,0:T(8,128)(2,1)S(1)}, u32[]{:S(2)}, u32[]{:S(2)}) collective-permute-start(bf16[48,896]{1,0:T(8,128)(2,1)S(1)} %fusion.65), channel_id=1, source_target_pairs={{0,3},{1,2},{2,1},{3,0},{4,7},{5,6},{6,5},{7,4},{8,11},{9,10},{10,... | collective-permute-start | bytes 258056 | tf_op jit(solution)/shard_map/ppermute | solution.py:810
  585.4 4.6 collective-permute-start.53
  590.0 10.1 %collective-permute-start.54 = (bf16[2,48,896]{2,1,0:T(8,128)(2,1)S(1)}, bf16[2,48,896]{2,1,0:T(8,128)(2,1)S(1)}, u32[]{:S(2)}, u32[]{:S(2)}) collective-permute-start(bf16[2,48,896]{2,1,0:T(8,128)(2,1)S(1)} %pad_maximum_fusion.10), channel_id=1, source_target_pairs={{0,16},{4,20},{8,24},{12,28},{16,0},{20,4},{24,8},{28,12},{1,17},{... | collective-permute-start | bytes 516104 | tf_op jit(solution)/shard_map/ppermute | solution.py:807
  600.2 2.1 collective-permute-start.55
  (86 other events, 735.7 us)
Sparse Core Ops, SparseCore 0:
  13.6 32.9 all-gather.4
  60.4 77.6 all-gather.6
  437.9 99.8 reduce-scatter.1
  541.5 82.0 all-gather.8

commit v8 on v5

--- a/solution.py
+++ b/solution.py
@@ -988,7 +988,7 @@
     n2_pieces = [normed_halves]
     for k in range(1, chips):
         if k < 3:
-            n2_pieces.append(swap_both(after(normed_halves, wide), 2 * k))
+            n2_pieces.append(swap_both(after(normed_halves, wide[:-1]), 2 * k))
     if chips > 2:
         n2_pieces[1:3] = lax.optimization_barrier(n2_pieces[1:3])
     zero = jnp.zeros((lanes, hp), F32)

time: 647 us -> 638 us (0.986)
  waiting for transfers between devices: 195 us -> 178 us
    ppermute x49, waiting for transfers between devices: 124 us -> 110 us  [swap(): return lax.ppermute(value, PLANE, [(i, i ^ k) for i in range(plane)])]
    ppermute x49, starting transfers between devices: 54.4 us -> 47.7 us  [swap(): return lax.ppermute(value, PLANE, [(i, i ^ k) for i in range(plane)])]
  transfers between devices with their start and end apart: 60 -> 60, of which waited for: 26 -> 23; matrix products, arithmetic and copies ran while one was open for 22% -> 22% of each run, Pallas kernels for 30% -> 31%
where the time goes in v8:
time: 638 us; the launch traced here: 628 us
  Pallas kernels  225 us (35%)
  waiting for transfers between devices  178 us (28%)
  starting transfers between devices  58.9 us (9%)
  local copies, waits for them, and re-layouts  55.5 us (9%)
  other arithmetic  51.3 us (8%)
  matrix products  42.1 us (7%)
  between operations  16 us (3%)
    pallas_call x4, Pallas kernels, feed(): pl.pallas_call(functools.partial(feed_kernel, seqs, tuple(kinds)), grid_s...  120 us
    ppermute x49, waiting for transfers between devices, swap(): return lax.ppermute(value, PLANE, [(i, i ^ k) for i in range(plane)])  110 us
    ppermute x7, waiting for transfers between devices, swap_seq(): return lax.ppermute(value, 'seq', [(i, i ^ k) for i in range(seq_n)])  49.4 us
    ppermute x49, starting transfers between devices, swap(): return lax.ppermute(value, PLANE, [(i, i ^ k) for i in range(plane)])  47.7 us
    pallas_call x1, Pallas kernels, attend_back(): pl.pallas_call(functools.partial(attend_back_kernel, spans, span_len, tok...  28.9 us
    pallas_call x1, Pallas kernels, attend(): pl.pallas_call(functools.partial(attend_kernel, spans, span_len, tokens),...  22.4 us
    dot_general x21, matrix products, mm_tn(): lax.dot_general(left, right, (((0,), (0,)), ((), ())), preferred_element_...  22 us
    pallas_call x2, Pallas kernels, with_blocks(): pl.pallas_call(functools.partial(kernel, seqs, count), grid_spec=pltpu.Pr...  18.2 us
  transfers between devices with their start and end apart: 60, of which 23 were waited for; matrix products, arithmetic and copies ran while one was open for 22% of the time, Pallas kernels for 31%

profile of v8, /device:TPU:0, one launch (start us, length us, event | category | flops | bytes accessed | tf_op | source)
XLA Modules:
  0.0 627.9 jit_solution(11275799353680692344)
XLA Ops:
  7.2 3.0 collective-permute-start.1
  13.1 1.9 collective-permute-start.13
  17.8 2.3 fusion.119
  20.1 4.1 fusion.115
  24.2 1.9 fusion.114
  28.6 2.1 select_bitcast_fusion
  33.4 3.3 fusion.10
  48.7 2.0 convolution_convert_fusion.17.eo_ref.oe_ref
  50.7 3.0 all-gather.5.cloned.1.call-done.w_ref
  53.7 4.3 keys_values.1
  63.8 11.6 %collective-permute-done.5.refs_6_ = bf16[192,1536]{1,0:T(8,128)(2,1)S(1)} collective-permute-done((bf16[192,1536]{1,0:T(8,128)(2,1)S(1)}, bf16[192,1536]{1,0:T(8,128)(2,1)S(1)}, u32[]{:S(2)}, u32[]{:S(2)}) %collective-permute-start.5) | collective-permute-done | bytes 589856 | tf_op jit(solution)/shard_map/ppermute | solution.py:806
  75.4 12.7 %collective-permute-done.4.refs_4_ = bf16[192,1536]{1,0:T(8,128)(2,1)} collective-permute-done((bf16[192,1536]{1,0:T(8,128)(2,1)S(1)}, bf16[192,1536]{1,0:T(8,128)(2,1)}, u32[]{:S(2)}, u32[]{:S(2)}) %collective-permute-start.4) | collective-permute-done | bytes 589856 | tf_op jit(solution)/shard_map/ppermute | solution.py:806
  88.1 3.4 collective-permute-done.3.refs_2_
  92.4 8.3 %collective-permute-done.6.refs_10_ = bf16[192,1536]{1,0:T(8,128)(2,1)S(1)} collective-permute-done((bf16[192,1536]{1,0:T(8,128)(2,1)}, bf16[192,1536]{1,0:T(8,128)(2,1)S(1)}, u32[]{:S(2)}, u32[]{:S(2)}) %collective-permute-start.6) | collective-permute-done | bytes 589856 | tf_op jit(solution)/shard_map/ppermute | solution.py:806
  103.4 9.3 %collective-permute-done.7.refs_11_ = bf16[192,1536]{1,0:T(8,128)(2,1)} collective-permute-done((bf16[192,1536]{1,0:T(8,128)(2,1)}, bf16[192,1536]{1,0:T(8,128)(2,1)}, u32[]{:S(2)}, u32[]{:S(2)}) %collective-permute-start.7) | collective-permute-done | bytes 589856 | tf_op jit(solution)/shard_map/ppermute | solution.py:806
  116.3 7.6 %queries.1 = (bf16[384,1536]{1,0:T(8,128)(2,1)}, bf16[384,64]{1,0:T(8,128)(2,1)}, bf16[1536,1536]{1,0:T(8,128)(2,1)}) custom-call(s32[1]{0:T(128)} %bitcast.info, bf16[384,1536]{1,0:T(8,128)(2,1)} %get-tuple-element.176.normed_ref, bf16[1536,64]{1,0:T(8,128)(2,1)} %bitcast.194, bf16[64,1536]{1,0:T(8,128)(2,1)} %convolution_convert_fusion.16.eq_ref, ...), custom_call_target="tpu_custom_call" | custom-call | flops 1811939328 | bytes 9437184 | tf_op jit(solution)/shard_map/queries/pallas_call | solution.py:482
  130.5 2.0 select_bitcast_fusion.2
  148.1 5.0 assemble.1.refs_14_
  153.2 22.4 %attend.1 = (bf16[384,1536]{1,0:T(8,128)(2,1)}, f32[6,8,768]{2,1,0:T(8,128)}) custom-call(s32[29]{0:T(128)} %pad_add_fusion.info, bf16[384,1536]{1,0:T(8,128)(2,1)} %get-tuple-element.198.q_ref, bf16[3,2048,512]{2,1,0:T(8,128)(2,1)} %all-gather.7.cloned.1.call-done.k_ref.v_ref, bf16[3,2048,512]{2,1,0:T(8,128)(2,1)} %all-gather.7.cloned.1.call-done.k_ref.v_ref), custom_call_target="tpu_custom_call" | custom-call | flops 4831838208 | bytes 6291456 | tf_op jit(solution)/shard_map/attend/pallas_call | solution.py:152
  176.4 10.6 %outputs.1 = (f32[384,1536]{1,0:T(8,128)}, bf16[384,1536]{1,0:T(8,128)(2,1)}, bf16[192,1536]{1,0:T(8,128)(2,1)}, bf16[192,1536]{1,0:T(8,128)(2,1)}, bf16[384,64]{1,0:T(8,128)(2,1)}, /*index=5*/bf16[1536,1536]{1,0:T(8,128)(2,1)}) custom-call(s32[1]{0:T(128)} %bitcast.info, bf16[384,1536]{1,0:T(8,128)(2,1)} %get-tuple-element.199.attended_ref.o_ref, ...), custom_call_target="tpu_custom_call" | custom-call | flops 1811939328 | bytes 9437184 | tf_op jit(solution)/shard_map/outputs/pallas_call | solution.py:482
  187.6 4.5 collective-permute-done.23.refs_6_
  193.7 4.6 collective-permute-start.27
  198.3 2.4 collective-permute-start.25
  200.7 2.0 collective-permute-start.28
  203.6 29.7 %feed.4 = (bf16[384,1664]{1,0:T(8,128)(2,1)}, bf16[384,1664]{1,0:T(8,128)(2,1)}, f32[64,2304]{1,0:T(8,128)}, f32[64,2304]{1,0:T(8,128)}, f32[64,2304]{1,0:T(8,128)}) custom-call(s32[2]{0:T(128)} %pad_add_fusion.1.info, bf16[2,192,2304]{2,1,0:T(8,128)(2,1)} %get-tuple-element.208.refs_0_, bf16[2,192,2304]{2,1,0:T(8,128)(2,1)} %collective-permute-done.18.refs_1_, ...), custom_call_target="tpu_custom_call" | custom-call | flops 16986931200 | bytes 21233664 | tf_op jit(solution)/shard_map/feed/pallas_call | solution.py:608
  233.3 2.1 collective-permute-start.29
  237.0 29.9 %feed.5 = (bf16[384,1664]{1,0:T(8,128)(2,1)}, bf16[384,1664]{1,0:T(8,128)(2,1)}, f32[64,2304]{1,0:T(8,128)}, f32[64,2304]{1,0:T(8,128)}, f32[64,2304]{1,0:T(8,128)}) custom-call(s32[2]{0:T(128)} %pad_add_fusion.1.info, bf16[2,192,2304]{2,1,0:T(8,128)(2,1)} %get-tuple-element.208.refs_0_, bf16[2,192,2304]{2,1,0:T(8,128)(2,1)} %collective-permute-done.18.refs_1_, ...), custom_call_target="tpu_custom_call" | custom-call | flops 16986931200 | bytes 21233664 | tf_op jit(solution)/shard_map/feed/pallas_call | solution.py:608
  267.0 2.0 collective-permute-start.31
  269.2 1.9 collective-permute-start.34
  271.1 30.2 %feed.6 = (bf16[384,1664]{1,0:T(8,128)(2,1)}, bf16[384,1664]{1,0:T(8,128)(2,1)}, f32[64,2304]{1,0:T(8,128)}, f32[64,2304]{1,0:T(8,128)}, f32[64,2304]{1,0:T(8,128)}) custom-call(s32[2]{0:T(128)} %pad_add_fusion.1.info, bf16[2,192,2304]{2,1,0:T(8,128)(2,1)} %get-tuple-element.208.refs_0_, bf16[2,192,2304]{2,1,0:T(8,128)(2,1)} %collective-permute-done.18.refs_1_, ...), custom_call_target="tpu_custom_call" | custom-call | flops 16986931200 | bytes 21233664 | tf_op jit(solution)/shard_map/feed/pallas_call | solution.py:608
  301.3 2.0 collective-permute-start.36
  304.1 30.0 %feed.7 = (bf16[384,1664]{1,0:T(8,128)(2,1)}, bf16[384,1664]{1,0:T(8,128)(2,1)}, f32[64,2304]{1,0:T(8,128)}, f32[64,2304]{1,0:T(8,128)}, f32[64,2304]{1,0:T(8,128)}) custom-call(s32[2]{0:T(128)} %pad_add_fusion.1.info, bf16[2,192,2304]{2,1,0:T(8,128)(2,1)} %get-tuple-element.208.refs_0_, bf16[2,192,2304]{2,1,0:T(8,128)(2,1)} %collective-permute-done.18.refs_1_, ...), custom_call_target="tpu_custom_call" | custom-call | flops 16986931200 | bytes 21233664 | tf_op jit(solution)/shard_map/feed/pallas_call | solution.py:608
  336.5 3.0 convert_add_fusion.1.most_ref
  339.6 22.9 %collective-permute-done.37.last_ref = bf16[384,1664]{1,0:T(8,128)(2,1)} collective-permute-done((bf16[384,1664]{1,0:T(8,128)(2,1)}, bf16[384,1664]{1,0:T(8,128)(2,1)}, u32[]{:S(2)}, u32[]{:S(2)}) %collective-permute-start.37) | collective-permute-done | bytes 1277984 | tf_op jit(solution)/shard_map/ppermute | solution.py:806
  362.5 11.5 %before_attention.1 = (f32[384,1536]{1,0:T(8,128)}, bf16[384,1536]{1,0:T(8,128)(2,1)}, bf16[384,64]{1,0:T(8,128)(2,1)}, bf16[384,64]{1,0:T(8,128)(2,1)}, bf16[38...) custom-call(f32[384,1664]{1,0:T(8,128)} %convert_add_fusion.1.most_ref, bf16[384,1664]{1,0:T(8,128)(2,1)} %collective-permute-done.37.last_ref, ...), custom_call_target="tpu_custom_call" | custom-call | flops 1811939328 | bytes 17694720 | tf_op jit(solution)/shard_map/before_attention/pallas_call | solution.py:401
  376.7 28.9 %attend_back.1 = (bf16[384,1536]{1,0:T(8,128)(2,1)}, bf16[3,2048,512]{2,1,0:T(8,128)(2,1)}) custom-call(s32[29]{0:T(128)} %pad_add_fusion.info, bf16[384,1536]{1,0:T(8,128)(2,1)} %get-tuple-element.198.q_ref, bf16[384,1536]{1,0:T(8,128)(2,1)} %get-tuple-element.261.do_ref, bf16[384,1536]{1,0:T(8,128)(2,1)} %get-tuple-element.199.attended_ref.o_ref, ...), custom_call_target="tpu_custom_call" | custom-call | flops 12079595520 | bytes 12582912 | tf_op jit(solution)/shard_map/attend_back/pallas_call | solution.py:253
  408.2 2.0 copy.106
  410.4 2.4 fusion.123
  414.5 1.9 broadcast_multiply_fusion
  418.2 3.0 copy.109
  425.5 9.0 %collective-permute-done.40 = bf16[384,1664]{1,0:T(8,128)(2,1)} collective-permute-done((bf16[384,1664]{1,0:T(8,128)(2,1)}, bf16[384,1664]{1,0:T(8,128)(2,1)}, u32[]{:S(2)}, u32[]{:S(2)}) %collective-permute-start.40) | collective-permute-done | bytes 1277984 | tf_op jit(solution)/shard_map/ppermute | solution.py:806
  434.5 3.0 convert_add_fusion
  456.3 5.0 collective-permute-start.42
  463.5 11.9 %collective-permute-done.42 = bf16[1,4,48,768]{3,2,1,0:T(8,128)(2,1)S(1)} collective-permute-done((bf16[1,4,48,768]{3,2,1,0:T(8,128)(2,1)S(1)}, bf16[1,4,48,768]{3,2,1,0:T(8,128)(2,1)S(1)}, u32[]{:S(2)}, u32[]{:S(2)}) %collective-permute-start.42) | collective-permute-done | bytes 294944 | tf_op jit(solution)/shard_map/ppermute | solution.py:806
  477.7 12.4 %collective-permute-done.43 = bf16[2,48,768]{2,1,0:T(8,128)(2,1)S(1)} collective-permute-done((bf16[2,48,768]{2,1,0:T(8,128)(2,1)S(1)}, bf16[2,48,768]{2,1,0:T(8,128)(2,1)S(1)}, u32[]{:S(2)}, u32[]{:S(2)}) %collective-permute-start.43) | collective-permute-done | bytes 147488 | tf_op jit(solution)/shard_map/ppermute | solution.py:809
  490.2 2.2 collective-permute-start.44
  492.4 8.3 %collective-permute-done.46 = bf16[2,48,1792]{2,1,0:T(8,128)(2,1)S(1)} collective-permute-done((bf16[2,48,1792]{2,1,0:T(8,128)(2,1)S(1)}, bf16[2,48,1792]{2,1,0:T(8,128)(2,1)S(1)}, u32[]{:S(2)}, u32[]{:S(2)}) %collective-permute-start.46) | collective-permute-done | bytes 344096 | tf_op jit(solution)/shard_map/ppermute | solution.py:809
  500.9 2.0 collective-permute-start.47
  502.9 15.3 %collective-permute-done.47 = bf16[1,48,1792]{2,1,0:T(8,128)(2,1)S(1)} collective-permute-done((bf16[1,48,1792]{2,1,0:T(8,128)(2,1)S(1)}, bf16[1,48,1792]{2,1,0:T(8,128)(2,1)S(1)}, u32[]{:S(2)}, u32[]{:S(2)}) %collective-permute-start.47) | collective-permute-done | bytes 172064 | tf_op jit(solution)/shard_map/ppermute | solution.py:809
  519.0 5.0 reduce-scatter.2.cloned.1.call-done
  532.0 2.0 gather_fusion
  535.5 3.7 fusion.8
  539.2 4.4 fusion.120
  544.1 3.3 last_grads.1
  550.4 2.6 collective-permute-start.49
  553.4 3.6 collective-permute-done.49
  558.9 2.3 collective-permute-start.51
  562.0 4.1 collective-permute-done.52
  566.2 9.2 %collective-permute-done.51 = bf16[48,896]{1,0:T(8,128)(2,1)S(1)} collective-permute-done((bf16[48,896]{1,0:T(8,128)(2,1)S(1)}, bf16[48,896]{1,0:T(8,128)(2,1)S(1)}, u32[]{:S(2)}, u32[]{:S(2)}) %collective-permute-start.51) | collective-permute-done | bytes 86048 | tf_op jit(solution)/shard_map/ppermute | solution.py:809
  577.8 2.2 collective-permute-done.53
  581.4 8.7 %collective-permute-done.54 = bf16[2,48,896]{2,1,0:T(8,128)(2,1)S(1)} collective-permute-done((bf16[2,48,896]{2,1,0:T(8,128)(2,1)S(1)}, bf16[2,48,896]{2,1,0:T(8,128)(2,1)S(1)}, u32[]{:S(2)}, u32[]{:S(2)}) %collective-permute-start.54) | collective-permute-done | bytes 172064 | tf_op jit(solution)/shard_map/ppermute | solution.py:806
  590.3 2.0 fusion.5
  597.8 10.9 %all-gather.9.cloned.1.call-done = bf16[1536,2560]{1,0:T(8,128)(2,1)} async-done(((bf16[48,2560]{1,0:T(8,128)(2,1)}), bf16[1536,2560]{1,0:T(8,128)(2,1)}) %all-gather.9.cloned.1.call-update) | async-done | bytes 7864336 | tf_op jit(solution)/shard_map/all_gather | solution.py:1117
  608.8 12.1 %expand.1 = (f32[128,8960]{1,0:T(8,128)}, f32[128,8960]{1,0:T(8,128)}, f32[8960,128]{1,0:T(8,128)}, f32[1536,128]{1,0:T(8,128)}, f32[1536,128]{1,0:T(8,128)}, /*...) custom-call(bf16[32,48,2560]{2,1,0:T(8,128)(2,1)} %bitcast.191, ...), custom_call_target="tpu_custom_call" | custom-call | flops 660602880 | bytes 13762560 | tf_op jit(solution)/shard_map/expand/pallas_call | solution.py:746
  (445 shorter events, 128.6 us)
Async XLA Ops:
  7.2 126.8 %copy-start = (bf16[8960,128]{1,0:T(8,128)(2,1)S(1)}, bf16[8960,128]{1,0:T(8,128)(2,1)}, u32[]{:S(2)}) copy-start(bf16[8960,128]{1,0:T(8,128)(2,1)} %param.59) | copy-start | bytes 6881284
  7.2 46.5 %all-gather.5.cloned.1.call-start = ((), (), s32[]{:S(2)}) async-start(), calls=%async_computation.1 | async-start | bytes 1769472 | tf_op jit(solution)/shard_map/all_gather | solution.py:848
  7.2 43.5 %collective-permute-start.1 = (bf16[192,1536]{1,0:T(8,128)(2,1)}, bf16[192,1536]{1,0:T(8,128)(2,1)}, u32[]{:S(2)}, u32[]{:S(2)}) collective-permute-start(bf16[192,1536]{1,0:T(8,128)(2,1)} %refs_0_), channel_id=1, source_target_pairs={{0,16},{4,20},{8,24},{12,28},{16,0},{20,4},{24,8},{28,12},{1,17},{... | collective-permute-start | bytes 1769480 | tf_op jit(solution)/shard_map/ppermute | solution.py:806
  10.2 40.5 %collective-permute-start = (bf16[192,1536]{1,0:T(8,128)(2,1)}, bf16[192,1536]{1,0:T(8,128)(2,1)}, u32[]{:S(2)}, u32[]{:S(2)}) collective-permute-start(bf16[192,1536]{1,0:T(8,128)(2,1)} %refs_0_), channel_id=1, source_target_pairs={{0,8},{4,12},{8,0},{12,4},{16,24},{20,28},{24,16},{28,20},{1,9},{5... | collective-permute-start | bytes 1769480 | tf_op jit(solution)/shard_map/ppermute | solution.py:806
  11.8 38.9 %collective-permute-start.2 = (bf16[192,1536]{1,0:T(8,128)(2,1)}, bf16[192,1536]{1,0:T(8,128)(2,1)}, u32[]{:S(2)}, u32[]{:S(2)}) collective-permute-start(bf16[192,1536]{1,0:T(8,128)(2,1)} %refs_0_), channel_id=1, source_target_pairs={{0,24},{4,28},{8,16},{12,20},{16,8},{20,12},{24,0},{28,4},{1,25},{... | collective-permute-start | bytes 1769480 | tf_op jit(solution)/shard_map/ppermute | solution.py:806
  13.1 27.0 %collective-permute-start.13 = (f32[8,128]{0,1:T(8,128)}, f32[8,128]{0,1:T(8,128)}, u32[]{:S(2)}, u32[]{:S(2)}) collective-permute-start(f32[8,128]{0,1:T(8,128)} %broadcast_in_dim.83), channel_id=1, source_target_pairs={{0,16},{4,20},{8,24},{12,28},{16,0},{20,4},{24,8},{28,12},{1,17},{... | collective-permute-start | bytes 12296 | tf_op jit(solution)/shard_map/ppermute | solution.py:806
  16.7 136.5 %all-gather.7.cloned.1.call-start = ((), (), s32[]{:S(2)}) async-start(), calls=%async_computation.2 | async-start | bytes 6684672 | tf_op jit(solution)/shard_map/all_gather | solution.py:910
  58.0 466.1 %reduce-scatter.2.cloned.1.call-start = ((), (), s32[]{:S(2)}) async-start(), calls=%async_computation.3 | async-start | bytes 6684672 | tf_op jit(solution)/shard_map/reduce_scatter | solution.py:1050
  58.2 17.2 %collective-permute-start.5 = (bf16[192,1536]{1,0:T(8,128)(2,1)S(1)}, bf16[192,1536]{1,0:T(8,128)(2,1)S(1)}, u32[]{:S(2)}, u32[]{:S(2)}) collective-permute-start(bf16[192,1536]{1,0:T(8,128)(2,1)S(1)} %copy-done.50), channel_id=1, source_target_pairs={{0,24},{4,28},{8,16},{12,20},{16,8},{20,12},{24,0},{28,4},{1,25},{... | collective-permute-start | bytes 1769480 | tf_op jit(solution)/shard_map/ppermute | solution.py:806
  59.7 28.4 %collective-permute-start.4 = (bf16[192,1536]{1,0:T(8,128)(2,1)S(1)}, bf16[192,1536]{1,0:T(8,128)(2,1)}, u32[]{:S(2)}, u32[]{:S(2)}) collective-permute-start(bf16[192,1536]{1,0:T(8,128)(2,1)S(1)} %copy-done.50), channel_id=1, source_target_pairs={{0,16},{4,20},{8,24},{12,28},{16,0},{20,4},{24,8},{28,12},{1,17},{... | collective-permute-start | bytes 1769480 | tf_op jit(solution)/shard_map/ppermute | solution.py:806
  61.2 30.4 %collective-permute-start.3 = (bf16[192,1536]{1,0:T(8,128)(2,1)S(1)}, bf16[192,1536]{1,0:T(8,128)(2,1)S(1)}, u32[]{:S(2)}, u32[]{:S(2)}) collective-permute-start(bf16[192,1536]{1,0:T(8,128)(2,1)S(1)} %copy-done.50), channel_id=1, source_target_pairs={{0,8},{4,12},{8,0},{12,4},{16,24},{20,28},{24,16},{28,20},{1,9},{5... | collective-permute-start | bytes 1769480 | tf_op jit(solution)/shard_map/ppermute | solution.py:806
  61.8 38.9 %collective-permute-start.6 = (bf16[192,1536]{1,0:T(8,128)(2,1)}, bf16[192,1536]{1,0:T(8,128)(2,1)S(1)}, u32[]{:S(2)}, u32[]{:S(2)}) collective-permute-start(bf16[192,1536]{1,0:T(8,128)(2,1)} %get-tuple-element.231.refs_10_), channel_id=1, source_target_pairs={{0,16},{4,20},{8,24},{12,28},{16,0},{20,4},{24,8},{28,12},{1,17},{... | collective-permute-start | bytes 1769480 | tf_op jit(solution)/shard_map/ppermute | solution.py:806
  63.2 49.4 %collective-permute-start.7 = (bf16[192,1536]{1,0:T(8,128)(2,1)}, bf16[192,1536]{1,0:T(8,128)(2,1)}, u32[]{:S(2)}, u32[]{:S(2)}) collective-permute-start(bf16[192,1536]{1,0:T(8,128)(2,1)} %get-tuple-element.232.refs_11_), channel_id=1, source_target_pairs={{0,16},{4,20},{8,24},{12,28},{16,0},{20,4},{24,8},{28,12},{1,17},{... | collective-permute-start | bytes 1769480 | tf_op jit(solution)/shard_map/ppermute | solution.py:806
  75.4 37.3 %collective-permute-start.8 = (bf16[192,1536]{1,0:T(8,128)(2,1)S(1)}, bf16[192,1536]{1,0:T(8,128)(2,1)}, u32[]{:S(2)}, u32[]{:S(2)}) collective-permute-start(bf16[192,1536]{1,0:T(8,128)(2,1)S(1)} %copy-done.49), channel_id=1, source_target_pairs={{0,4},{4,0},{8,12},{12,8},{16,20},{20,16},{24,28},{28,24},{1,5},{5... | collective-permute-start | bytes 1769480 | tf_op jit(solution)/shard_map/ppermute | solution.py:806
  88.1 24.6 %collective-permute-start.9 = (bf16[192,1536]{1,0:T(8,128)(2,1)}, bf16[192,1536]{1,0:T(8,128)(2,1)}, u32[]{:S(2)}, u32[]{:S(2)}) collective-permute-start(bf16[192,1536]{1,0:T(8,128)(2,1)} %collective-permute-done.refs_2_), channel_id=1, source_target_pairs={{0,4},{4,0},{8,12},{12,8},{16,20},{20,16},{24,28},{28,24},{1,5},{5... | collective-permute-start | bytes 1769480 | tf_op jit(solution)/shard_map/ppermute | solution.py:806
  91.6 21.1 %collective-permute-start.10 = (bf16[192,1536]{1,0:T(8,128)(2,1)}, bf16[192,1536]{1,0:T(8,128)(2,1)S(1)}, u32[]{:S(2)}, u32[]{:S(2)}) collective-permute-start(bf16[192,1536]{1,0:T(8,128)(2,1)} %collective-permute-done.1.refs_4_), channel_id=1, source_target_pairs={{0,4},{4,0},{8,12},{12,8},{16,20},{20,16},{24,28},{28,24},{1,5},{5... | collective-permute-start | bytes 1769480 | tf_op jit(solution)/shard_map/ppermute | solution.py:806
  101.4 11.3 %collective-permute-start.11 = (bf16[192,1536]{1,0:T(8,128)(2,1)}, bf16[192,1536]{1,0:T(8,128)(2,1)}, u32[]{:S(2)}, u32[]{:S(2)}) collective-permute-start(bf16[192,1536]{1,0:T(8,128)(2,1)} %collective-permute-done.2.refs_6_), channel_id=1, source_target_pairs={{0,4},{4,0},{8,12},{12,8},{16,20},{20,16},{24,28},{28,24},{1,5},{5... | collective-permute-start | bytes 1769480 | tf_op jit(solution)/shard_map/ppermute | solution.py:806
  112.7 74.3 %collective-permute-start.19 = (bf16[2,192,2304]{2,1,0:T(8,128)(2,1)}, bf16[2,192,2304]{2,1,0:T(8,128)(2,1)}, u32[]{:S(2)}, u32[]{:S(2)}) collective-permute-start(bf16[2,192,2304]{2,1,0:T(8,128)(2,1)} %get-tuple-element.210), channel_id=1, source_target_pairs={{0,8},{4,12},{8,0},{12,4},{16,24},{20,28},{24,16},{28,20},{1,9},{5... | collective-permute-start | bytes 5308424 | tf_op jit(solution)/shard_map/ppermute | solution.py:806
  113.4 73.6 %collective-permute-start.21 = (bf16[2,192,2304]{2,1,0:T(8,128)(2,1)}, bf16[2,192,2304]{2,1,0:T(8,128)(2,1)}, u32[]{:S(2)}, u32[]{:S(2)}) collective-permute-start(bf16[2,192,2304]{2,1,0:T(8,128)(2,1)} %get-tuple-element.213), channel_id=1, source_target_pairs={{0,16},{4,20},{8,24},{12,28},{16,0},{20,4},{24,8},{28,12},{1,17},{... | collective-permute-start | bytes 5308424 | tf_op jit(solution)/shard_map/ppermute | solution.py:806
  114.9 77.2 %collective-permute-start.23 = (bf16[2,192,2304]{2,1,0:T(8,128)(2,1)}, bf16[2,192,2304]{2,1,0:T(8,128)(2,1)}, u32[]{:S(2)}, u32[]{:S(2)}) collective-permute-start(bf16[2,192,2304]{2,1,0:T(8,128)(2,1)} %get-tuple-element.216), channel_id=1, source_target_pairs={{0,24},{4,28},{8,16},{12,20},{16,8},{20,12},{24,0},{28,4},{1,25},{... | collective-permute-start | bytes 5308424 | tf_op jit(solution)/shard_map/ppermute | solution.py:806
  123.9 23.1 %collective-permute-start.12 = (bf16[1120,1536]{1,0:T(8,128)(2,1)}, bf16[1120,1536]{1,0:T(8,128)(2,1)}, u32[]{:S(2)}, u32[]{:S(2)}) collective-permute-start(bf16[1120,1536]{1,0:T(8,128)(2,1)} %refs_0_.1), channel_id=1, source_target_pairs={{0,4},{4,0},{8,12},{12,8},{16,20},{20,16},{24,28},{28,24},{1,5},{5... | collective-permute-start | bytes 10321928 | tf_op jit(solution)/shard_map/ppermute | solution.py:806
  138.9 4.6 collective-permute-start.14
  143.5 3.1 collective-permute-start.15
  146.6 29.0 %collective-permute-start.16 = (bf16[192,1536]{1,0:T(8,128)(2,1)}, bf16[192,1536]{1,0:T(8,128)(2,1)S(1)}, u32[]{:S(2)}, u32[]{:S(2)}) collective-permute-start(bf16[192,1536]{1,0:T(8,128)(2,1)} %collective-permute-done.4.refs_4_), channel_id=1, source_target_pairs={{0,4},{4,0},{8,12},{12,8},{16,20},{20,16},{24,28},{28,24},{1,5},{5... | collective-permute-start | bytes 1769480 | tf_op jit(solution)/shard_map/ppermute | solution.py:806
  147.1 28.6 %collective-permute-start.17 = (bf16[192,1536]{1,0:T(8,128)(2,1)S(1)}, bf16[192,1536]{1,0:T(8,128)(2,1)}, u32[]{:S(2)}, u32[]{:S(2)}) collective-permute-start(bf16[192,1536]{1,0:T(8,128)(2,1)S(1)} %copy-done.52), channel_id=1, source_target_pairs={{0,4},{4,0},{8,12},{12,8},{16,20},{20,16},{24,28},{28,24},{1,5},{5... | collective-permute-start | bytes 1769480 | tf_op jit(solution)/shard_map/ppermute | solution.py:806
  175.6 17.7 %collective-permute-start.18 = (bf16[2,192,2304]{2,1,0:T(8,128)(2,1)S(1)}, bf16[2,192,2304]{2,1,0:T(8,128)(2,1)}, u32[]{:S(2)}, u32[]{:S(2)}) collective-permute-start(bf16[2,192,2304]{2,1,0:T(8,128)(2,1)S(1)} %copy-done.31), channel_id=1, source_target_pairs={{0,4},{4,0},{8,12},{12,8},{16,20},{20,16},{24,28},{28,24},{1,5},{5... | collective-permute-start | bytes 5308424 | tf_op jit(solution)/shard_map/ppermute | solution.py:806
  187.0 6.4 %collective-permute-start.20 = (bf16[2,192,2304]{2,1,0:T(8,128)(2,1)}, bf16[2,192,2304]{2,1,0:T(8,128)(2,1)S(1)}, u32[]{:S(2)}, u32[]{:S(2)}) collective-permute-start(bf16[2,192,2304]{2,1,0:T(8,128)(2,1)} %collective-permute-done.19.refs_2_), channel_id=1, source_target_pairs={{0,4},{4,0},{8,12},{12,8},{16,20},{20,16},{24,28},{28,24},{1,5},{5... | collective-permute-start | bytes 5308424 | tf_op jit(solution)/shard_map/ppermute | solution.py:806
  187.1 6.6 %collective-permute-start.22 = (bf16[2,192,2304]{2,1,0:T(8,128)(2,1)}, bf16[2,192,2304]{2,1,0:T(8,128)(2,1)}, u32[]{:S(2)}, u32[]{:S(2)}) collective-permute-start(bf16[2,192,2304]{2,1,0:T(8,128)(2,1)} %collective-permute-done.21.refs_4_), channel_id=1, source_target_pairs={{0,4},{4,0},{8,12},{12,8},{16,20},{20,16},{24,28},{28,24},{1,5},{5... | collective-permute-start | bytes 5308424 | tf_op jit(solution)/shard_map/ppermute | solution.py:806
  192.1 10.6 %collective-permute-start.24 = (bf16[2,192,2304]{2,1,0:T(8,128)(2,1)}, bf16[2,192,2304]{2,1,0:T(8,128)(2,1)}, u32[]{:S(2)}, u32[]{:S(2)}) collective-permute-start(bf16[2,192,2304]{2,1,0:T(8,128)(2,1)} %collective-permute-done.23.refs_6_), channel_id=1, source_target_pairs={{0,4},{4,0},{8,12},{12,8},{16,20},{20,16},{24,28},{28,24},{1,5},{5... | collective-permute-start | bytes 5308424 | tf_op jit(solution)/shard_map/ppermute | solution.py:806
  192.8 245.3 %copy-start.84 = (pred[64]{0:T(512)(128)(4,1)}, pred[64]{0:T(512)(128)(4,1)S(1)}, u32[]{:S(2)}) copy-start(pred[64]{0:T(512)(128)(4,1)S(1)} %compare_and_fusion.2) | copy-start | bytes 196
  193.4 244.7 %copy-start.76 = (s32[384]{0:T(512)}, s32[384]{0:T(512)S(1)}, u32[]{:S(2)}) copy-start(s32[384]{0:T(512)S(1)} %get-tuple-element.353) | copy-start | bytes 4612
  193.4 244.7 %copy-start.77 = (s32[384]{0:T(512)}, s32[384]{0:T(512)S(1)}, u32[]{:S(2)}) copy-start(s32[384]{0:T(512)S(1)} %get-tuple-element.354) | copy-start | bytes 4612
  193.7 43.2 %collective-permute-start.27 = (bf16[192,1536]{1,0:T(8,128)(2,1)}, bf16[192,1536]{1,0:T(8,128)(2,1)}, u32[]{:S(2)}, u32[]{:S(2)}) collective-permute-start(bf16[192,1536]{1,0:T(8,128)(2,1)} %get-tuple-element.221.refs_8_), channel_id=1, source_target_pairs={{0,16},{4,20},{8,24},{12,28},{16,0},{20,4},{24,8},{28,12},{1,17},{... | collective-permute-start | bytes 1769480 | tf_op jit(solution)/shard_map/ppermute | solution.py:806
  198.3 38.7 %collective-permute-start.25 = (bf16[192,1536]{1,0:T(8,128)(2,1)}, bf16[192,1536]{1,0:T(8,128)(2,1)}, u32[]{:S(2)}, u32[]{:S(2)}) collective-permute-start(bf16[192,1536]{1,0:T(8,128)(2,1)} %get-tuple-element.221.refs_8_), channel_id=1, source_target_pairs={{0,8},{4,12},{8,0},{12,4},{16,24},{20,28},{24,16},{28,20},{1,9},{5... | collective-permute-start | bytes 1769480 | tf_op jit(solution)/shard_map/ppermute | solution.py:806
  200.7 36.3 %collective-permute-start.28 = (bf16[192,1536]{1,0:T(8,128)(2,1)}, bf16[192,1536]{1,0:T(8,128)(2,1)}, u32[]{:S(2)}, u32[]{:S(2)}) collective-permute-start(bf16[192,1536]{1,0:T(8,128)(2,1)} %get-tuple-element.222.refs_9_), channel_id=1, source_target_pairs={{0,16},{4,20},{8,24},{12,28},{16,0},{20,4},{24,8},{28,12},{1,17},{... | collective-permute-start | bytes 1769480 | tf_op jit(solution)/shard_map/ppermute | solution.py:806
  202.7 34.3 %collective-permute-start.26 = (bf16[192,1536]{1,0:T(8,128)(2,1)}, bf16[192,1536]{1,0:T(8,128)(2,1)}, u32[]{:S(2)}, u32[]{:S(2)}) collective-permute-start(bf16[192,1536]{1,0:T(8,128)(2,1)} %get-tuple-element.222.refs_9_), channel_id=1, source_target_pairs={{0,8},{4,12},{8,0},{12,4},{16,24},{20,28},{24,16},{28,20},{1,9},{5... | collective-permute-start | bytes 1769480 | tf_op jit(solution)/shard_map/ppermute | solution.py:806
  233.3 33.7 %collective-permute-start.29 = (bf16[192,1536]{1,0:T(8,128)(2,1)}, bf16[192,1536]{1,0:T(8,128)(2,1)}, u32[]{:S(2)}, u32[]{:S(2)}) collective-permute-start(bf16[192,1536]{1,0:T(8,128)(2,1)} %get-tuple-element.231.refs_10_), channel_id=1, source_target_pairs={{0,8},{4,12},{8,0},{12,4},{16,24},{20,28},{24,16},{28,20},{1,9},{5... | collective-permute-start | bytes 1769480 | tf_op jit(solution)/shard_map/ppermute | solution.py:806
  236.9 30.1 %collective-permute-start.30 = (bf16[192,1536]{1,0:T(8,128)(2,1)S(1)}, bf16[192,1536]{1,0:T(8,128)(2,1)}, u32[]{:S(2)}, u32[]{:S(2)}) collective-permute-start(bf16[192,1536]{1,0:T(8,128)(2,1)S(1)} %copy-done.59), channel_id=1, source_target_pairs={{0,8},{4,12},{8,0},{12,4},{16,24},{20,28},{24,16},{28,20},{1,9},{5... | collective-permute-start | bytes 1769480 | tf_op jit(solution)/shard_map/ppermute | solution.py:806
  267.0 36.3 %collective-permute-start.31 = (bf16[192,1536]{1,0:T(8,128)(2,1)}, bf16[192,1536]{1,0:T(8,128)(2,1)S(1)}, u32[]{:S(2)}, u32[]{:S(2)}) collective-permute-start(bf16[192,1536]{1,0:T(8,128)(2,1)} %collective-permute-done.27.refs_8_), channel_id=1, source_target_pairs={{0,8},{4,12},{8,0},{12,4},{16,24},{20,28},{24,16},{28,20},{1,9},{5... | collective-permute-start | bytes 1769480 | tf_op jit(solution)/shard_map/ppermute | solution.py:806
  269.0 34.3 %collective-permute-start.32 = (bf16[192,1536]{1,0:T(8,128)(2,1)}, bf16[192,1536]{1,0:T(8,128)(2,1)}, u32[]{:S(2)}, u32[]{:S(2)}) collective-permute-start(bf16[192,1536]{1,0:T(8,128)(2,1)} %collective-permute-done.26.refs_9_), channel_id=1, source_target_pairs={{0,16},{4,20},{8,24},{12,28},{16,0},{20,4},{24,8},{28,12},{1,17},{... | collective-permute-start | bytes 1769480 | tf_op jit(solution)/shard_map/ppermute | solution.py:806
  269.0 34.3 %collective-permute-start.33 = (bf16[192,1536]{1,0:T(8,128)(2,1)}, bf16[192,1536]{1,0:T(8,128)(2,1)}, u32[]{:S(2)}, u32[]{:S(2)}) collective-permute-start(bf16[192,1536]{1,0:T(8,128)(2,1)} %copy-done.90), channel_id=1, source_target_pairs={{0,8},{4,12},{8,0},{12,4},{16,24},{20,28},{24,16},{28,20},{1,9},{5... | collective-permute-start | bytes 1769480 | tf_op jit(solution)/shard_map/ppermute | solution.py:806
  269.2 34.2 %collective-permute-start.34 = (bf16[192,1536]{1,0:T(8,128)(2,1)}, bf16[192,1536]{1,0:T(8,128)(2,1)}, u32[]{:S(2)}, u32[]{:S(2)}) collective-permute-start(bf16[192,1536]{1,0:T(8,128)(2,1)} %collective-permute-done.30.refs_11_), channel_id=1, source_target_pairs={{0,16},{4,20},{8,24},{12,28},{16,0},{20,4},{24,8},{28,12},{1,17},{... | collective-permute-start | bytes 1769480 | tf_op jit(solution)/shard_map/ppermute | solution.py:806
  301.3 35.2 %collective-permute-start.36 = (bf16[384,1664]{1,0:T(8,128)(2,1)}, bf16[384,1664]{1,0:T(8,128)(2,1)}, u32[]{:S(2)}, u32[]{:S(2)}) collective-permute-start(bf16[384,1664]{1,0:T(8,128)(2,1)} %get-tuple-element.253), channel_id=1, source_target_pairs={{0,8},{4,12},{8,0},{12,4},{16,24},{20,28},{24,16},{28,20},{1,9},{5... | collective-permute-start | bytes 3833864 | tf_op jit(solution)/shard_map/ppermute | solution.py:806
  303.3 31.7 %collective-permute-start.35 = (bf16[384,1664]{1,0:T(8,128)(2,1)}, bf16[384,1664]{1,0:T(8,128)(2,1)}, u32[]{:S(2)}, u32[]{:S(2)}) collective-permute-start(bf16[384,1664]{1,0:T(8,128)(2,1)} %get-tuple-element.252), channel_id=1, source_target_pairs={{0,16},{4,20},{8,24},{12,28},{16,0},{20,4},{24,8},{28,12},{1,17},{... | collective-permute-start | bytes 3833864 | tf_op jit(solution)/shard_map/ppermute | solution.py:806
  334.1 28.3 %collective-permute-start.37 = (bf16[384,1664]{1,0:T(8,128)(2,1)}, bf16[384,1664]{1,0:T(8,128)(2,1)}, u32[]{:S(2)}, u32[]{:S(2)}) collective-permute-start(bf16[384,1664]{1,0:T(8,128)(2,1)} %get-tuple-element.254), channel_id=1, source_target_pairs={{0,24},{4,28},{8,16},{12,20},{16,8},{20,12},{24,0},{28,4},{1,25},{... | collective-permute-start | bytes 3833864 | tf_op jit(solution)/shard_map/ppermute | solution.py:806
  374.0 36.3 %collective-permute-start.38 = (bf16[384,1664]{1,0:T(8,128)(2,1)}, bf16[384,1664]{1,0:T(8,128)(2,1)}, u32[]{:S(2)}, u32[]{:S(2)}) collective-permute-start(bf16[384,1664]{1,0:T(8,128)(2,1)} %get-tuple-element.258), channel_id=1, source_target_pairs={{0,16},{4,20},{8,24},{12,28},{16,0},{20,4},{24,8},{28,12},{1,17},{... | collective-permute-start | bytes 3833864 | tf_op jit(solution)/shard_map/ppermute | solution.py:806
  375.0 35.3 %collective-permute-start.39 = (bf16[384,1664]{1,0:T(8,128)(2,1)}, bf16[384,1664]{1,0:T(8,128)(2,1)}, u32[]{:S(2)}, u32[]{:S(2)}) collective-permute-start(bf16[384,1664]{1,0:T(8,128)(2,1)} %get-tuple-element.259), channel_id=1, source_target_pairs={{0,8},{4,12},{8,0},{12,4},{16,24},{20,28},{24,16},{28,20},{1,9},{5... | collective-permute-start | bytes 3833864 | tf_op jit(solution)/shard_map/ppermute | solution.py:806
  406.6 27.9 %collective-permute-start.40 = (bf16[384,1664]{1,0:T(8,128)(2,1)}, bf16[384,1664]{1,0:T(8,128)(2,1)}, u32[]{:S(2)}, u32[]{:S(2)}) collective-permute-start(bf16[384,1664]{1,0:T(8,128)(2,1)} %get-tuple-element.264), channel_id=1, source_target_pairs={{0,24},{4,28},{8,16},{12,20},{16,8},{20,12},{24,0},{28,4},{1,25},{... | collective-permute-start | bytes 3833864 | tf_op jit(solution)/shard_map/ppermute | solution.py:806
  410.3 198.5 %all-gather.9.cloned.1.call-start = ((), (), s32[]{:S(2)}) async-start(), calls=%async_computation.4 | async-start | bytes 8110080 | tf_op jit(solution)/shard_map/all_gather | solution.py:1117
  452.9 2.2 collective-permute-start.41
  455.0 6.3 %collective-permute-start.45 = (bf16[1,48,7168]{2,1,0:T(8,128)(2,1)}, bf16[1,48,7168]{2,1,0:T(8,128)(2,1)}, u32[]{:S(2)}, u32[]{:S(2)}) collective-permute-start(bf16[1,48,7168]{2,1,0:T(8,128)(2,1)} %fusion.33), channel_id=1, source_target_pairs={{0,4},{4,0},{8,12},{12,8},{16,20},{20,16},{24,28},{28,24},{1,5},{5... | collective-permute-start | bytes 2064392 | tf_op jit(solution)/shard_map/ppermute | solution.py:806
  456.3 19.0 %collective-permute-start.42 = (bf16[1,4,48,768]{3,2,1,0:T(8,128)(2,1)S(1)}, bf16[1,4,48,768]{3,2,1,0:T(8,128)(2,1)S(1)}, u32[]{:S(2)}, u32[]{:S(2)}) collective-permute-start(bf16[1,4,48,768]{3,2,1,0:T(8,128)(2,1)S(1)} %constant_dynamic-slice_fusion.2), channel_id=1, source_target_pairs={{0,8},{4,12},{8,0},{12,4},{16,24},{20,28},{24,16},{28,20},{1,9},{5... | collective-permute-start | bytes 884744 | tf_op jit(solution)/shard_map/ppermute | solution.py:806
  475.5 14.6 %collective-permute-start.43 = (bf16[2,48,768]{2,1,0:T(8,128)(2,1)S(1)}, bf16[2,48,768]{2,1,0:T(8,128)(2,1)S(1)}, u32[]{:S(2)}, u32[]{:S(2)}) collective-permute-start(bf16[2,48,768]{2,1,0:T(8,128)(2,1)S(1)} %dynamic-slice_bitcast_fusion.2), channel_id=1, source_target_pairs={{0,1},{1,0},{2,3},{3,2},{4,5},{5,4},{6,7},{7,6},{8,9},{9,8},{10,11... | collective-permute-start | bytes 442376 | tf_op jit(solution)/shard_map/ppermute | solution.py:809
  477.2 23.6 %collective-permute-start.46 = (bf16[2,48,1792]{2,1,0:T(8,128)(2,1)S(1)}, bf16[2,48,1792]{2,1,0:T(8,128)(2,1)S(1)}, u32[]{:S(2)}, u32[]{:S(2)}) collective-permute-start(bf16[2,48,1792]{2,1,0:T(8,128)(2,1)S(1)} %dynamic-slice_bitcast_fusion.1), channel_id=1, source_target_pairs={{0,1},{1,0},{2,3},{3,2},{4,5},{5,4},{6,7},{7,6},{8,9},{9,8},{10,11... | collective-permute-start | bytes 1032200 | tf_op jit(solution)/shard_map/ppermute | solution.py:809
  490.2 12.7 %collective-permute-start.44 = (bf16[1,48,768]{2,1,0:T(8,128)(2,1)S(1)}, bf16[1,48,768]{2,1,0:T(8,128)(2,1)S(1)}, u32[]{:S(2)}, u32[]{:S(2)}) collective-permute-start(bf16[1,48,768]{2,1,0:T(8,128)(2,1)S(1)} %constant_dynamic-slice_fusion.1), channel_id=1, source_target_pairs={{0,2},{1,3},{2,0},{3,1},{4,6},{5,7},{6,4},{7,5},{8,10},{9,11},{10,... | collective-permute-start | bytes 221192 | tf_op jit(solution)/shard_map/ppermute | solution.py:809
  500.9 17.4 %collective-permute-start.47 = (bf16[1,48,1792]{2,1,0:T(8,128)(2,1)S(1)}, bf16[1,48,1792]{2,1,0:T(8,128)(2,1)S(1)}, u32[]{:S(2)}, u32[]{:S(2)}) collective-permute-start(bf16[1,48,1792]{2,1,0:T(8,128)(2,1)S(1)} %constant_dynamic-slice_fusion), channel_id=1, source_target_pairs={{0,2},{1,3},{2,0},{3,1},{4,6},{5,7},{6,4},{7,5},{8,10},{9,11},{10,... | collective-permute-start | bytes 516104 | tf_op jit(solution)/shard_map/ppermute | solution.py:809
  548.3 2.0 collective-permute-start.48
  550.4 6.7 %collective-permute-start.49 = (bf16[1,48,896]{2,1,0:T(8,128)(2,1)S(1)}, bf16[1,48,896]{2,1,0:T(8,128)(2,1)S(1)}, u32[]{:S(2)}, u32[]{:S(2)}) collective-permute-start(bf16[1,48,896]{2,1,0:T(8,128)(2,1)S(1)} %slice.323), channel_id=1, source_target_pairs={{0,8},{4,12},{8,0},{12,4},{16,24},{20,28},{24,16},{28,20},{1,9},{5... | collective-permute-start | bytes 258056 | tf_op jit(solution)/shard_map/ppermute | solution.py:806
  557.1 9.1 %collective-permute-start.52 = (bf16[48,896]{1,0:T(8,128)(2,1)S(1)}, bf16[48,896]{1,0:T(8,128)(2,1)S(1)}, u32[]{:S(2)}, u32[]{:S(2)}) collective-permute-start(bf16[48,896]{1,0:T(8,128)(2,1)S(1)} %fusion.65), channel_id=1, source_target_pairs={{0,3},{1,2},{2,1},{3,0},{4,7},{5,6},{6,5},{7,4},{8,11},{9,10},{10,... | collective-permute-start | bytes 258056 | tf_op jit(solution)/shard_map/ppermute | solution.py:809
  558.9 16.5 %collective-permute-start.51 = (bf16[48,896]{1,0:T(8,128)(2,1)S(1)}, bf16[48,896]{1,0:T(8,128)(2,1)S(1)}, u32[]{:S(2)}, u32[]{:S(2)}) collective-permute-start(bf16[48,896]{1,0:T(8,128)(2,1)S(1)} %fusion.65), channel_id=1, source_target_pairs={{0,2},{1,3},{2,0},{3,1},{4,6},{5,7},{6,4},{7,5},{8,10},{9,11},{10,... | collective-permute-start | bytes 258056 | tf_op jit(solution)/shard_map/ppermute | solution.py:809
  561.2 14.2 %collective-permute-start.50 = (bf16[48,896]{1,0:T(8,128)(2,1)S(1)}, bf16[48,896]{1,0:T(8,128)(2,1)S(1)}, u32[]{:S(2)}, u32[]{:S(2)}) collective-permute-start(bf16[48,896]{1,0:T(8,128)(2,1)S(1)} %fusion.65), channel_id=1, source_target_pairs={{0,1},{1,0},{2,3},{3,2},{4,5},{5,4},{6,7},{7,6},{8,9},{9,8},{10,11... | collective-permute-start | bytes 258056 | tf_op jit(solution)/shard_map/ppermute | solution.py:809
  575.4 4.6 collective-permute-start.53
  580.0 10.1 %collective-permute-start.54 = (bf16[2,48,896]{2,1,0:T(8,128)(2,1)S(1)}, bf16[2,48,896]{2,1,0:T(8,128)(2,1)S(1)}, u32[]{:S(2)}, u32[]{:S(2)}) collective-permute-start(bf16[2,48,896]{2,1,0:T(8,128)(2,1)S(1)} %pad_maximum_fusion.10), channel_id=1, source_target_pairs={{0,16},{4,20},{8,24},{12,28},{16,0},{20,4},{24,8},{28,12},{1,17},{... | collective-permute-start | bytes 516104 | tf_op jit(solution)/shard_map/ppermute | solution.py:806
  590.2 2.1 collective-permute-start.55
  (91 other events, 877.5 us)
Sparse Core Ops, SparseCore 0:
  16.8 36.8 all-gather.4
  58.1 73.0 all-gather.6
  410.4 113.5 reduce-scatter.1
  527.8 80.9 all-gather.8
